TPU v7x, 32 devices: a whole 2x2x4 slice. The times are simulated.
32 devices in a mesh: dp: 16 (over z, y, x), tensor: 2 (over core).
Axes of the slice: x: 2, y: 2, z: 4, core: 2. Of those that a mesh axis runs over, the one named last changes fastest.
Arguments:
- inputs: bfloat16 [17664, 1024], P(('dp', 'tensor')), may hold values from -6 to 6
- cotangent: bfloat16 [17664, 1024], P(('dp', 'tensor')), may hold values from -6 to 6
- slot_live: int32 [16], P('dp'), may hold values from 0 to 1, as said below
- token_type: int32 [17664], P(('dp', 'tensor')), may hold values from 0 to 3, as said below
- attn_norm_gain: bfloat16 [1024], P('dp'), may hold values from 0.25 to 1.75
- attn_norm_bias: bfloat16 [1024], P('dp'), may hold values from -4 to 4
- qkv_weight: bfloat16 [3, 1024, 1024], P(None, 'dp', 'tensor'), may hold values from -0.1875 to 0.1875
- proj_weight: bfloat16 [1024, 1024], P('tensor', 'dp'), may hold values from -1 to 1
- proj_bias: bfloat16 [1024], P('dp'), may hold values from -4 to 4
- mlp_norm_gain: bfloat16 [1024], P('dp'), may hold values from 0.25 to 1.75
- mlp_norm_bias: bfloat16 [1024], P('dp'), may hold values from -4 to 4
- fc1_weight: bfloat16 [1024, 4096], P('dp', 'tensor'), may hold values from -0.1875 to 0.1875
- fc1_bias: bfloat16 [4096], P(('tensor', 'dp')), may hold values from -6 to 6
- fc2_weight: bfloat16 [4096, 1024], P('tensor', 'dp'), may hold values from -0.09375 to 0.09375
- fc2_bias: bfloat16 [1024], P('dp'), may hold values from -4 to 4
Outputs:
- outputs: bfloat16 [17664, 1024], P(('dp', 'tensor'))
- grad_inputs: bfloat16 [17664, 1024], P(('dp', 'tensor'))
- grad_attn_norm_gain: float32 [1024], P('dp')
- grad_attn_norm_bias: float32 [1024], P('dp')
- grad_qkv_weight: float32 [3, 1024, 1024], P(None, 'dp', 'tensor')
- grad_proj_weight: float32 [1024, 1024], P('tensor', 'dp')
- grad_proj_bias: float32 [1024], P('dp')
- grad_mlp_norm_gain: float32 [1024], P('dp')
- grad_mlp_norm_bias: float32 [1024], P('dp')
- grad_fc1_weight: float32 [1024, 4096], P('dp', 'tensor')
- grad_fc1_bias: float32 [4096], P(('tensor', 'dp'))
- grad_fc2_weight: float32 [4096, 1024], P('tensor', 'dp')
- grad_fc2_bias: float32 [1024], P('dp')
Inputs may be any that keep to these rules, and one draw needn't show every extreme that they name: `slot_live`: the ones of each data group's 1 entries come first; some data group holds 1 sequence. `token_type`: in each sequence position 0 is 0; positions 1 to 77 are 1 up to a caption length of at least one and 3 after it; later positions are 2, except the last two, which are 3.
All inputs are finite; a program needn't handle non-finite values.
Results may differ from a plain program's by a relative error of at most 0.02.
Values may be sent and summed in bfloat16 or wider, within the bound.
No kernel may reach another device: no remote copies, remote signals or barrier semaphores. Data moves between devices by JAX's collectives and lax.ppermute only.
A program may use at most 256 MiB of HBM per device.

v0:
```python
import jax
import jax.numpy as jnp
from jax import lax
from jax.sharding import PartitionSpec as P

HEAD_DIM = 64
SEQ_LEN = 1104


def layer_norm(values, norm_gain, norm_shift):
    row_mean = jnp.mean(values, axis=-1, keepdims=True)
    centered = values - row_mean
    variance = jnp.mean(centered * centered, axis=-1, keepdims=True)
    return centered * lax.rsqrt(variance + 1e-05) * norm_gain + norm_shift


def exact_gelu(values):
    return jax.nn.gelu(values, approximate=False)


def masked_scores(query, keys, key_valid, score_scale):
    scores = (
        jnp.einsum("qhd,khd->hqk", query, keys, preferred_element_type=jnp.float32) * score_scale
    )
    return jnp.where(key_valid[None, None, :] > 0, scores, -1e30)


def attend_forward(query, keys, values, key_valid, score_scale):
    scores = masked_scores(query, keys, key_valid, score_scale)
    row_max = jnp.max(scores, axis=-1, keepdims=True)
    exp_scores = jnp.exp(scores - row_max)
    row_sum = jnp.sum(exp_scores, axis=-1, keepdims=True)
    attn_prob = (exp_scores / row_sum).astype(jnp.bfloat16)
    mixed = jnp.einsum("hqk,khd->qhd", attn_prob, values, preferred_element_type=jnp.float32)
    return (mixed.astype(jnp.bfloat16), row_max + jnp.log(row_sum))


def attend_backward(query, keys, values, key_valid, log_total, grad_mixed, score_scale):
    scores = masked_scores(query, keys, key_valid, score_scale)
    attn_prob = jnp.exp(scores - log_total)
    grad_prob = jnp.einsum("qhd,khd->hqk", grad_mixed, values, preferred_element_type=jnp.float32)
    row_dot = jnp.sum(attn_prob * grad_prob, axis=-1, keepdims=True)
    grad_scores = (attn_prob * (grad_prob - row_dot)).astype(jnp.bfloat16)
    grad_query = (
        jnp.einsum("hqk,khd->qhd", grad_scores, keys, preferred_element_type=jnp.float32)
        * score_scale
    )
    grad_keys = (
        jnp.einsum("hqk,qhd->khd", grad_scores, query, preferred_element_type=jnp.float32)
        * score_scale
    )
    grad_values = jnp.einsum(
        "hqk,qhd->khd",
        attn_prob.astype(jnp.bfloat16),
        grad_mixed,
        preferred_element_type=jnp.float32,
    )
    return (
        grad_query.astype(jnp.bfloat16),
        grad_keys.astype(jnp.bfloat16),
        grad_values.astype(jnp.bfloat16),
    )


def contract_rows(left, right):
    return lax.dot_general(
        left, right, (((0,), (0,)), ((), ())), preferred_element_type=jnp.float32
    )


def contract_cols(left, right):
    return lax.dot_general(
        left, right, (((1,), (1,)), ((), ())), preferred_element_type=jnp.float32
    )


def on_device(
    inputs,
    cotangent,
    slot_live,
    token_type,
    attn_norm_gain,
    attn_norm_bias,
    qkv_weight,
    proj_weight,
    proj_bias,
    mlp_norm_gain,
    mlp_norm_bias,
    fc1_weight,
    fc1_bias,
    fc2_weight,
    fc2_bias,
):
    tensor_size = lax.axis_size("tensor")
    tensor_rank = lax.axis_index("tensor")
    local_rows = inputs.shape[0]
    slot_count = slot_live.shape[0]
    whole_rows = local_rows * tensor_size
    width_here = qkv_weight.shape[2]
    heads_here = width_here // HEAD_DIM
    score_scale = HEAD_DIM ** (-0.5)
    position = tensor_rank * local_rows + jnp.arange(local_rows, dtype=jnp.int32)
    slot_of_row = position // SEQ_LEN
    slot_match = slot_of_row[:, None] == jnp.arange(slot_count, dtype=jnp.int32)[None, :]
    live_rows = jnp.sum(jnp.where(slot_match, slot_live.astype(jnp.float32)[None, :], 0.0), axis=1)
    live_col = live_rows[:, None]
    valid_local = (token_type != 3).astype(jnp.bfloat16)
    (
        qkv_full,
        proj_full,
        proj_bias_full,
        gain_one,
        shift_one,
        fc1_full,
        fc1_bias_full,
        fc2_full,
        gain_two,
        shift_two,
        fc2_bias_full,
    ) = (
        lax.all_gather(qkv_weight, "dp", axis=1, tiled=True),
        lax.all_gather(proj_weight, "dp", axis=1, tiled=True),
        lax.all_gather(proj_bias, "dp", axis=0, tiled=True),
        lax.all_gather(attn_norm_gain, "dp", axis=0, tiled=True),
        lax.all_gather(attn_norm_bias, "dp", axis=0, tiled=True),
        lax.all_gather(fc1_weight, "dp", axis=0, tiled=True),
        lax.all_gather(fc1_bias, "dp", axis=0, tiled=True),
        lax.all_gather(fc2_weight, "dp", axis=1, tiled=True),
        lax.all_gather(mlp_norm_gain, "dp", axis=0, tiled=True),
        lax.all_gather(mlp_norm_bias, "dp", axis=0, tiled=True),
        lax.all_gather(fc2_bias, "dp", axis=0, tiled=True),
    )
    gain_one_f = gain_one.astype(jnp.float32)
    shift_one_f = shift_one.astype(jnp.float32)
    rows_in = inputs.astype(jnp.float32)
    norm_one = layer_norm(rows_in, gain_one_f, shift_one_f).astype(jnp.bfloat16)
    whole_one, whole_valid = (
        lax.all_gather(norm_one, "tensor", axis=0, tiled=True),
        lax.all_gather(valid_local, "tensor", axis=0, tiled=True),
    )
    packed = jnp.einsum("nd,jdc->jnc", whole_one, qkv_full, preferred_element_type=jnp.float32)
    packed = packed.astype(jnp.bfloat16).reshape(3, slot_count, SEQ_LEN, heads_here, HEAD_DIM)
    valid_seq = whole_valid.reshape(slot_count, SEQ_LEN)

    def forward_slot(slot_index):
        slot_qkv = lax.dynamic_index_in_dim(packed, slot_index, 1, keepdims=False)
        slot_valid = lax.dynamic_index_in_dim(valid_seq, slot_index, 0, keepdims=False)
        return attend_forward(slot_qkv[0], slot_qkv[1], slot_qkv[2], slot_valid, score_scale)

    heads_out, log_total = lax.map(forward_slot, jnp.arange(slot_count, dtype=jnp.int32))
    mixed_flat = heads_out.reshape(whole_rows, width_here)
    row_block = mixed_flat
    attn_out = lax.psum_scatter(
        jnp.dot(row_block, proj_full, preferred_element_type=jnp.float32).astype(jnp.bfloat16),
        "tensor",
        scatter_dimension=0,
        tiled=True,
    ).astype(jnp.float32)
    middle = rows_in + live_col * (attn_out + proj_bias_full.astype(jnp.float32))
    gain_two_f = gain_two.astype(jnp.float32)
    shift_two_f = shift_two.astype(jnp.float32)
    fc1_bias_f = fc1_bias_full.astype(jnp.float32)
    norm_two = layer_norm(middle, gain_two_f, shift_two_f).astype(jnp.bfloat16)
    whole_two = lax.all_gather(norm_two, "tensor", axis=0, tiled=True)
    hidden_pre = jnp.dot(whole_two, fc1_full, preferred_element_type=jnp.float32) + fc1_bias_f
    hidden_act = exact_gelu(hidden_pre).astype(jnp.bfloat16)
    row_block = hidden_act
    mlp_out = lax.psum_scatter(
        jnp.dot(row_block, fc2_full, preferred_element_type=jnp.float32).astype(jnp.bfloat16),
        "tensor",
        scatter_dimension=0,
        tiled=True,
    ).astype(jnp.float32)
    result = middle + live_col * (mlp_out + fc2_bias_full.astype(jnp.float32))
    outputs = result.astype(jnp.bfloat16)
    grad_out = cotangent.astype(jnp.float32)
    grad_mlp = (live_col * grad_out).astype(jnp.bfloat16)
    grad_fc2_bias = jnp.sum(grad_mlp, axis=0, dtype=jnp.float32)
    whole_grad_mlp = lax.all_gather(grad_mlp, "tensor", axis=0, tiled=True)
    whole_two = lax.all_gather(norm_two, "tensor", axis=0, tiled=True)
    hidden_pre = jnp.dot(whole_two, fc1_full, preferred_element_type=jnp.float32) + fc1_bias_f
    hidden_act = exact_gelu(hidden_pre).astype(jnp.bfloat16)
    grad_fc2 = contract_rows(hidden_act, whole_grad_mlp)
    grad_act = contract_cols(whole_grad_mlp, fc2_full)
    unused, gelu_pull = jax.vjp(exact_gelu, hidden_pre)
    grad_pre = gelu_pull(grad_act)[0].astype(jnp.bfloat16)
    grad_fc1_bias = jnp.sum(grad_pre, axis=0, dtype=jnp.float32)
    grad_fc1 = contract_rows(whole_two, grad_pre)
    row_block = grad_pre
    grad_two = lax.psum_scatter(
        contract_cols(row_block, fc1_full).astype(jnp.bfloat16),
        "tensor",
        scatter_dimension=0,
        tiled=True,
    ).astype(jnp.float32)
    unused, norm_pull_two = jax.vjp(layer_norm, middle, gain_two_f, shift_two_f)
    grad_mid_norm, grad_gain_two, grad_shift_two = norm_pull_two(grad_two)
    grad_middle = grad_out + grad_mid_norm
    grad_branch = (live_col * grad_middle).astype(jnp.bfloat16)
    grad_proj_bias = jnp.sum(grad_branch, axis=0, dtype=jnp.float32)
    whole_grad_branch = lax.all_gather(grad_branch, "tensor", axis=0, tiled=True)
    grad_proj = contract_rows(mixed_flat, whole_grad_branch)
    grad_mixed = contract_cols(whole_grad_branch, proj_full).astype(jnp.bfloat16)
    grad_mixed_seq = grad_mixed.reshape(slot_count, SEQ_LEN, heads_here, HEAD_DIM)

    def backward_slot(slot_index):
        slot_qkv = lax.dynamic_index_in_dim(packed, slot_index, 1, keepdims=False)
        slot_valid = lax.dynamic_index_in_dim(valid_seq, slot_index, 0, keepdims=False)
        slot_total = lax.dynamic_index_in_dim(log_total, slot_index, 0, keepdims=False)
        slot_grad = lax.dynamic_index_in_dim(grad_mixed_seq, slot_index, 0, keepdims=False)
        return attend_backward(
            slot_qkv[0], slot_qkv[1], slot_qkv[2], slot_valid, slot_total, slot_grad, score_scale
        )

    grad_query, grad_keys, grad_values = lax.map(
        backward_slot, jnp.arange(slot_count, dtype=jnp.int32)
    )
    grad_packed = jnp.stack((grad_query, grad_keys, grad_values)).reshape(3, whole_rows, width_here)
    whole_one = lax.all_gather(norm_one, "tensor", axis=0, tiled=True)
    grad_qkv = jnp.einsum("nd,jnc->jdc", whole_one, grad_packed, preferred_element_type=jnp.float32)
    row_block = grad_packed
    grad_one = lax.psum_scatter(
        jnp.einsum("jnc,jdc->nd", row_block, qkv_full, preferred_element_type=jnp.float32).astype(
            jnp.bfloat16
        ),
        "tensor",
        scatter_dimension=0,
        tiled=True,
    ).astype(jnp.float32)
    unused, norm_pull_one = jax.vjp(layer_norm, rows_in, gain_one_f, shift_one_f)
    grad_in_norm, grad_gain_one, grad_shift_one = norm_pull_one(grad_one)
    grad_inputs = (grad_middle + grad_in_norm).astype(jnp.bfloat16)
    (
        out_qkv,
        out_proj,
        sum_proj_bias,
        sum_gain_one,
        sum_shift_one,
        out_fc1,
        out_fc1_bias,
        out_fc2,
        sum_gain_two,
        sum_shift_two,
        sum_fc2_bias,
    ) = (
        lax.psum_scatter(
            grad_qkv.astype(jnp.bfloat16), "dp", scatter_dimension=1, tiled=True
        ).astype(jnp.float32),
        lax.psum_scatter(
            grad_proj.astype(jnp.bfloat16), "dp", scatter_dimension=1, tiled=True
        ).astype(jnp.float32),
        lax.psum_scatter(
            grad_proj_bias.astype(jnp.bfloat16), "dp", scatter_dimension=0, tiled=True
        ).astype(jnp.float32),
        lax.psum_scatter(
            grad_gain_one.astype(jnp.bfloat16), "dp", scatter_dimension=0, tiled=True
        ).astype(jnp.float32),
        lax.psum_scatter(
            grad_shift_one.astype(jnp.bfloat16), "dp", scatter_dimension=0, tiled=True
        ).astype(jnp.float32),
        lax.psum_scatter(
            grad_fc1.astype(jnp.bfloat16), "dp", scatter_dimension=0, tiled=True
        ).astype(jnp.float32),
        lax.psum_scatter(
            grad_fc1_bias.astype(jnp.bfloat16), "dp", scatter_dimension=0, tiled=True
        ).astype(jnp.float32),
        lax.psum_scatter(
            grad_fc2.astype(jnp.bfloat16), "dp", scatter_dimension=1, tiled=True
        ).astype(jnp.float32),
        lax.psum_scatter(
            grad_gain_two.astype(jnp.bfloat16), "dp", scatter_dimension=0, tiled=True
        ).astype(jnp.float32),
        lax.psum_scatter(
            grad_shift_two.astype(jnp.bfloat16), "dp", scatter_dimension=0, tiled=True
        ).astype(jnp.float32),
        lax.psum_scatter(
            grad_fc2_bias.astype(jnp.bfloat16), "dp", scatter_dimension=0, tiled=True
        ).astype(jnp.float32),
    )
    sum_gain_one, sum_shift_one, sum_proj_bias, sum_gain_two, sum_shift_two, sum_fc2_bias = (
        lax.psum(
            (sum_gain_one, sum_shift_one, sum_proj_bias, sum_gain_two, sum_shift_two, sum_fc2_bias),
            "tensor",
        )
    )
    return (
        outputs,
        grad_inputs,
        sum_gain_one,
        sum_shift_one,
        out_qkv,
        out_proj,
        sum_proj_bias,
        sum_gain_two,
        sum_shift_two,
        out_fc1,
        out_fc1_bias,
        out_fc2,
        sum_fc2_bias,
    )


def solution(mesh):
    in_specs = (
        P(("dp", "tensor"), None),
        P(("dp", "tensor"), None),
        P("dp"),
        P(("dp", "tensor")),
        P("dp"),
        P("dp"),
        P(None, "dp", "tensor"),
        P("tensor", "dp"),
        P("dp"),
        P("dp"),
        P("dp"),
        P("dp", "tensor"),
        P(("tensor", "dp")),
        P("tensor", "dp"),
        P("dp"),
    )
    out_specs = (
        P(("dp", "tensor"), None),
        P(("dp", "tensor"), None),
        P("dp"),
        P("dp"),
        P(None, "dp", "tensor"),
        P("tensor", "dp"),
        P("dp"),
        P("dp"),
        P("dp"),
        P("dp", "tensor"),
        P(("tensor", "dp")),
        P("tensor", "dp"),
        P("dp"),
    )
    return jax.shard_map(
        on_device, mesh=mesh, in_specs=in_specs, out_specs=out_specs, check_vma=False
    )
```

profile of v0, /device:TPU:0, one launch (start us, length us, event | category | flops | bytes accessed | tf_op | source)
XLA Modules:
  0.0 1062.3 jit_solution(11267200392812141874)
XLA Ops:
  13.4 78.6 %all-reduce.17 = (bf16[1024]{0:T(1024)(128)(2,1)S(1)}, bf16[1024]{0:T(1024)(128)(2,1)S(1)}, bf16[1024]{0:T(1024)(128)(2,1)S(1)}, bf16[1024]{0:T(1024)(128)(2,1)S(1)}, bf16[1024]{0:T(1024)(128)(2,1)S(1)}) all-reduce(bf16[1024]{0:T(1024)(128)(2,1)S(1)} %dynamic-update-slice.5, ...), channel_id=1, replica_groups=mesh['dp'=16,'tensor'=2] {'dp'}, use_global_device_ids=true, to_apply=%add.5 | all-reduce | flops 5120 | bytes 20480
  104.8 71.6 %all-gather.12.cloned.1.call-done = bf16[3,1024,512]{2,1,0:T(8,128)(2,1)} async-done(((bf16[3,64,512]{2,1,0:T(8,128)(2,1)}), bf16[3,1024,512]{2,1,0:T(8,128)(2,1)}) %all-gather.12.cloned.1.call-update) | async-done | bytes 3145744 | tf_op jit(solution)/shard_map/all_gather | solution.py:121
  176.4 6.2 fusion.13
  190.0 15.7 %fusion.55 = (f32[8,1104]{1,0:T(8,128)S(1)}, f32[8,1104,1104]{1,2,0:T(8,128)}) fusion(bf16[1104,8,64]{0,2,1:T(8,128)(2,1)S(1)} %bitcast.65, bf16[1104,8,64]{0,2,1:T(8,128)(2,1)S(1)} %bitcast.67, pred[1104]{0:T(1024)(128)(4,1)S(1)} %broadcast_compare_fusion), kind=kOutput, calls=%fused_computation.120 | convolution fusion | flops 1277310336 | bytes 41299536 | tf_op jit(solution)/shard_map/while/body/eval_jaxpr/qhd,khd->hqk/dot_general | solution.py:23
  205.7 16.2 %fusion.1 = f32[8,1104]{1,0:T(8,128)S(1)} fusion(f32[8,1104,1104]{1,2,0:T(8,128)} %get-tuple-element.131, f32[8,1104]{1,0:T(8,128)S(1)} %get-tuple-element.130), kind=kLoop, calls=%fused_computation.7 | loop fusion | flops 19492224 | bytes 39072768 | tf_op jit(solution)/shard_map/while/body/eval_jaxpr/reduce_sum | solution.py:32
  221.9 15.8 %fusion.23 = bf16[8,64,1104]{2,1,0:T(8,128)(2,1)S(1)} fusion(bf16[1104,8,64]{0,2,1:T(8,128)(2,1)S(1)} %bitcast.69, f32[8,1104,1104]{1,2,0:T(8,128)} %get-tuple-element.131, f32[8,1104]{1,0:T(8,128)S(1)} %fusion.1, f32[8,1104]{1,0:T(8,128)S(1)} %get-tuple-element.130), kind=kOutput, calls=%fused_computation.55 | convolution fusion | flops 1277884416 | bytes 41333760 | tf_op jit(solution)/shard_map/while/body/eval_jaxpr/hqk,khd->qhd/dot_general | solution.py:34
  244.2 7.2 reduce-scatter.8.cloned.1.call-done
  258.7 40.7 %all-gather = bf16[16,1,128]{2,1,0:T(2,128)(2,1)S(1)} all-gather(bf16[1,1,128]{2,1,0:T(2,128)(2,1)S(1)} %bitcast.75), channel_id=1, replica_groups=mesh['dp'=16,'tensor'=2] {'dp'}, dimensions={0}, use_global_device_ids=true | all-gather | bytes 4352 | tf_op jit(solution)/shard_map/all_gather | solution.py:127
  299.4 31.8 %all-gather.18.cloned.1.call-done = bf16[1024,2048]{1,0:T(8,128)(2,1)} async-done(((bf16[64,2048]{1,0:T(8,128)(2,1)}), bf16[1024,2048]{1,0:T(8,128)(2,1)}) %all-gather.18.cloned.1.call-update) | async-done | bytes 4194320 | tf_op jit(solution)/shard_map/all_gather | solution.py:126
  331.2 11.4 %all-gather.16.cloned.1.call-done = bf16[1104,1024]{1,0:T(8,128)(2,1)} async-done(((bf16[552,1024]{1,0:T(8,128)(2,1)}), bf16[1104,1024]{1,0:T(8,128)(2,1)}) %all-gather.16.cloned.1.call-update) | async-done | bytes 2261008 | tf_op jit(solution)/shard_map/all_gather | solution.py:164
  342.6 11.6 %convolution_add_fusion = f32[1104,2048]{1,0:T(8,128)} fusion(bf16[1104,1024]{1,0:T(8,128)(2,1)} %all-gather.16.cloned.1.call-done, bf16[1024,2048]{1,0:T(8,128)(2,1)} %all-gather.18.cloned.1.call-done, f32[2048]{0:T(1024)S(1)} %bitcast.74), kind=kOutput, calls=%fused_computation.13 | convolution fusion | flops 4632772608 | bytes 15507456 | tf_op jit(solution)/shard_map/dot_general | solution.py:165
  356.8 80.1 %all-gather.20.cloned.1.call-done = bf16[2048,1024]{0,1:T(8,128)(2,1)} async-done(((bf16[2048,64]{0,1:T(8,128)(2,1)}), bf16[2048,1024]{0,1:T(8,128)(2,1)}) %all-gather.20.cloned.1.call-update) | async-done | bytes 4194320 | tf_op jit(solution)/shard_map/all_gather | solution.py:128
  436.8 29.1 %fusion.47 = (bf16[2048]{0:T(1024)(128)(2,1)}, bf16[1104,2048]{1,0:T(8,128)(2,1)S(1)}, f32[1104,2048]{1,0:T(8,128)}) fusion(f32[1104,2048]{1,0:T(8,128)} %convolution_add_fusion, bf16[1104,1024]{1,0:T(8,128)(2,1)} %all-gather.22.cloned.1.call-done, bf16[2048,1024]{0,1:T(8,128)(2,1)} %all-gather.20.cloned.1.call-done), kind=kOutput, calls=%fused_computation.114 | convolution fusion | flops 4795561984 | bytes 29069312 | tf_op jit(solution)/shard_map/dot_general | solution.py:72
  468.1 6.2 convolution_convert_fusion.4
  474.5 8.3 reduce-scatter.12.cloned.1.call-done
  489.8 10.7 %multiply_convert_fusion.1 = bf16[1104,2048]{1,0:T(8,128)(2,1)} fusion(f32[1104,2048]{1,0:T(8,128)} %get-tuple-element.116, f32[1104,2048]{1,0:T(8,128)} %convolution_add_fusion), kind=kLoop, calls=%fused_computation.16 | loop fusion | flops 6782976 | bytes 22609920 | tf_op jit(solution)/shard_map/convert_element_type | solution.py:166
  500.5 9.5 convolution_convert_fusion.2
  511.7 9.5 convolution_convert_fusion.3
  526.1 16.6 %fusion.20 = bf16[8,64,1104]{2,1,0:T(8,128)(2,1)} fusion(bf16[1104,8,64]{0,2,1:T(8,128)(2,1)S(1)} %bitcast.63, f32[8,1104,1104]{1,2,0:T(8,128)} %get-tuple-element.131, f32[8,1104]{1,0:T(8,128)S(1)} %log_add_fusion), kind=kOutput, calls=%fused_computation.53 | convolution fusion | flops 1268133888 | bytes 41298432 | tf_op jit(solution)/shard_map/while/body/eval_jaxpr/hqk,qhd->khd/dot_general | solution.py:52
  542.7 30.0 %multiply_reduce_fusion = (f32[8,1104]{1,0:T(8,128)S(1)}, f32[8,1104,1104]{1,2,0:T(8,128)}) fusion(f32[8,1104,1104]{1,2,0:T(8,128)} %get-tuple-element.131, f32[8,1104]{1,0:T(8,128)S(1)} %log_add_fusion, bf16[1104,8,64]{0,2,1:T(8,128)(2,1)S(1)} %bitcast.64, bf16[1104,8,64]{0,2,1:T(8,128)(2,1)S(1)} %bitcast.70), kind=kOutput, calls=%fused_computation.3 | convolution fusion | flops 1277310336 | bytes 80335872 | tf_op jit(solution)/shard_map/while/body/eval_jaxpr/qhd,khd->hqk/dot_general | solution.py:41
  575.0 33.6 %multiply_convert_fusion = bf16[8,1104,1104]{1,2,0:T(8,128)(2,1)} fusion(f32[8,1104,1104]{1,2,0:T(8,128)} %get-tuple-element.133, f32[8,1104,1104]{1,2,0:T(8,128)} %get-tuple-element.131, f32[8,1104]{1,0:T(8,128)S(1)} %get-tuple-element.132, f32[8,1104]{1,0:T(8,128)S(1)} %log_add_fusion), kind=kLoop, calls=%fused_computation.2 | loop fusion | flops 39002112 | bytes 97575936 | tf_op jit(solution)/shard_map/while/body/eval_jaxpr/convert_element_type | solution.py:43
  608.6 10.4 fusion.18
  625.6 10.3 fusion.19
  637.9 8.0 convert_bitcast_fusion
  645.9 7.6 copy.67
  654.8 6.8 bitcast_convert_fusion
  661.9 9.8 convolution_convert_fusion.5
  675.5 27.9 %reduce-scatter.18.cloned.1.call-done = bf16[64,2048]{1,0:T(8,128)(2,1)} async-done(((bf16[1024,2048]{1,0:T(8,128)(2,1)}), bf16[64,2048]{1,0:T(8,128)(2,1)}) %reduce-scatter.18.cloned.1.call-update) | async-done | bytes 262160 | tf_op jit(solution)/shard_map/reduce_scatter | solution.py:261
  705.2 77.7 %reduce-scatter.16.cloned.1.call-done = bf16[512,64]{0,1:T(8,128)(2,1)} async-done(((bf16[512,1024]{0,1:T(8,128)(2,1)}), bf16[512,64]{0,1:T(8,128)(2,1)}) %reduce-scatter.16.cloned.1.call-update) | async-done | bytes 65552 | tf_op jit(solution)/shard_map/reduce_scatter | solution.py:249
  784.4 169.8 %all-reduce.20.cloned.1.call-done = bf16[3,1024,512]{2,0,1:T(4,128)(2,1)} async-done(((bf16[3,1024,512]{2,0,1:T(4,128)(2,1)}), bf16[3,1024,512]{2,0,1:T(4,128)(2,1)}) %all-reduce.20.cloned.1.call-update) | async-done | bytes 3145744
  956.1 9.0 reduce-scatter.14.cloned.1.call-done
  970.1 77.0 %all-reduce.16 = (bf16[1024]{0:T(1024)(128)(2,1)S(1)}, bf16[1024]{0:T(1024)(128)(2,1)S(1)}, bf16[1024]{0:T(1024)(128)(2,1)S(1)}, bf16[1024]{0:T(1024)(128)(2,1)S...) all-reduce(bf16[1024]{0:T(1024)(128)(2,1)S(1)} %dynamic-update-slic, ...), channel_id=1, replica_groups=mesh['dp'=16,'tensor'=2] {'dp'}, use_global_device_ids=true, to_apply=%add.6 | all-reduce | flops 9216 | bytes 36864
  (202 shorter events, 89.3 us)
Async XLA Ops:
  7.2 89.3 %copy-start = (bf16[552,1024]{1,0:T(8,128)(2,1)S(1)}, bf16[552,1024]{1,0:T(8,128)(2,1)}, u32[]{:S(2)}) copy-start(bf16[552,1024]{1,0:T(8,128)(2,1)} %param.15) | copy-start | bytes 3391492
  7.2 97.6 %all-gather.10.cloned.1.call-start = ((), (), s32[]{:S(2)}) async-start(), calls=%async_computation.7 | async-start | bytes 3391488 | tf_op jit(solution)/shard_map/all_gather | solution.py:138
  98.0 78.4 %all-gather.12.cloned.1.call-start = ((), (), s32[]{:S(2)}) async-start(), calls=%async_computation.8 | async-start | bytes 3342336 | tf_op jit(solution)/shard_map/all_gather | solution.py:121
  98.7 139.1 %all-gather.14.cloned.1.call-start = ((), (), s32[]{:S(2)}) async-start(), calls=%async_computation.9 | async-start | bytes 1114112 | tf_op jit(solution)/shard_map/all_gather | solution.py:122
  99.4 152.0 %reduce-scatter.8.cloned.1.call-start = ((), (), s32[]{:S(2)}) async-start(), calls=%async_computation.10 | async-start | bytes 3391488 | tf_op jit(solution)/shard_map/reduce_scatter | solution.py:153
  187.1 18.6 %copy-start.6 = (bf16[1,1104,512]{1,2,0:T(8,128)(2,1)}, bf16[1,1104,512]{1,2,0:T(8,128)(2,1)S(1)}, u32[]{:S(2)}) copy-start(bf16[1,1104,512]{1,2,0:T(8,128)(2,1)S(1)} %copy.57) | copy-start | bytes 3391492
  205.7 16.2 %copy-start.13 = (bf16[1,1104,512]{1,2,0:T(8,128)(2,1)S(1)}, bf16[1,1104,512]{1,2,0:T(8,128)(2,1)}, u32[]{:S(2)}) copy-start(bf16[1,1104,512]{1,2,0:T(8,128)(2,1)} %copy.56) | copy-start | bytes 3391492
  242.3 88.9 %all-gather.18.cloned.1.call-start = ((), (), s32[]{:S(2)}) async-start(), calls=%async_computation.12 | async-start | bytes 4456448 | tf_op jit(solution)/shard_map/all_gather | solution.py:126
  242.9 99.8 %all-gather.16.cloned.1.call-start = ((), (), s32[]{:S(2)}) async-start(), calls=%async_computation.11 | async-start | bytes 3391488 | tf_op jit(solution)/shard_map/all_gather | solution.py:164
  244.1 242.0 %copy-start.20 = (f32[1024]{0:T(1024)}, f32[1024]{0:T(1024)S(1)}, u32[]{:S(2)}) copy-start(f32[1024]{0:T(1024)S(1)} %convert_element_type.206) | copy-start | bytes 12292
  244.2 243.2 %copy-start.18 = (f32[552]{0:T(1024)}, f32[552]{0:T(1024)S(1)}, u32[]{:S(2)}) copy-start(f32[552]{0:T(1024)S(1)} %fusion.40) | copy-start | bytes 6628
  255.9 100.9 %all-gather.22.cloned.1.call-start = ((), (), s32[]{:S(2)}) async-start(), calls=%async_computation.15 | async-start | bytes 3391488 | tf_op jit(solution)/shard_map/all_gather | solution.py:179
  257.9 178.9 %all-gather.20.cloned.1.call-start = ((), (), s32[]{:S(2)}) async-start(), calls=%async_computation.13 | async-start | bytes 4456448 | tf_op jit(solution)/shard_map/all_gather | solution.py:128
  258.7 224.2 %reduce-scatter.12.cloned.1.call-start = ((), (), s32[]{:S(2)}) async-start(), calls=%async_computation.16 | async-start | bytes 3391488 | tf_op jit(solution)/shard_map/reduce_scatter | solution.py:190
  436.8 31.2 %copy-start.38 = (bf16[1024,2048]{1,0:T(8,128)(2,1)S(1)}, bf16[1024,2048]{1,0:T(8,128)(2,1)}, u32[]{:S(2)}) copy-start(bf16[1024,2048]{1,0:T(8,128)(2,1)} %all-gather.18.cloned.1.call-done) | copy-start | bytes 12582916
  474.3 47.2 %all-gather.24.cloned.1.call-start = ((), (), s32[]{:S(2)}) async-start(), calls=%async_computation.17 | async-start | bytes 3391488 | tf_op jit(solution)/shard_map/all_gather | solution.py:201
  489.8 183.9 %reduce-scatter.20.cloned.1.call-start = ((), (), s32[]{:S(2)}) async-start(), calls=%async_computation.21 | async-start | bytes 4456448 | tf_op jit(solution)/shard_map/reduce_scatter | solution.py:267
  510.1 193.3 %reduce-scatter.18.cloned.1.call-start = ((), (), s32[]{:S(2)}) async-start(), calls=%async_computation.20 | async-start | bytes 4456448 | tf_op jit(solution)/shard_map/reduce_scatter | solution.py:261
  521.2 261.7 %reduce-scatter.16.cloned.1.call-start = ((), (), s32[]{:S(2)}) async-start(), calls=%async_computation.19 | async-start | bytes 1114112 | tf_op jit(solution)/shard_map/reduce_scatter | solution.py:249
  526.1 16.6 %copy-start.14 = (bf16[1,1104,512]{1,2,0:T(8,128)(2,1)S(1)}, bf16[1,1104,512]{1,2,0:T(8,128)(2,1)}, u32[]{:S(2)}) copy-start(bf16[1,1104,512]{1,2,0:T(8,128)(2,1)} %copy.56) | copy-start | bytes 3391492
  575.0 33.6 %copy-start.9 = (bf16[1,1104,512]{1,2,0:T(8,128)(2,1)S(1)}, bf16[1,1104,512]{1,2,0:T(8,128)(2,1)}, u32[]{:S(2)}) copy-start(bf16[1,1104,512]{1,2,0:T(8,128)(2,1)} %copy-done.8) | copy-start | bytes 3391492
  625.1 329.2 %all-reduce.20.cloned.1.call-start = ((), (), s32[]{:S(2)}) async-start(), calls=%async_computation.22 | async-start | bytes 8388608
  653.5 311.6 %reduce-scatter.14.cloned.1.call-start = ((), (), s32[]{:S(2)}) async-start(), calls=%async_computation.18 | async-start | bytes 3391488 | tf_op jit(solution)/shard_map/reduce_scatter | solution.py:222
  661.6 389.3 %reduce-scatter.10.cloned.1.call-start = ((), (), s32[]{:S(2)}) async-start(), calls=%async_computation.14 | async-start | bytes 3391488 | tf_op jit(solution)/shard_map/reduce_scatter | solution.py:168
  673.6 293.1 %copy-start.1 = (bf16[552,1024]{1,0:T(8,128)(2,1)S(1)}, bf16[552,1024]{1,0:T(8,128)(2,1)}, u32[]{:S(2)}) copy-start(bf16[552,1024]{1,0:T(8,128)(2,1)} %param.15) | copy-start | bytes 3391492
  673.6 293.1 %copy-start.23 = (f32[552]{0:T(1024)S(1)}, f32[552]{0:T(1024)}, u32[]{:S(2)}) copy-start(f32[552]{0:T(1024)} %copy-done.22) | copy-start | bytes 6628
  673.6 293.1 %copy-start.25 = (f32[1024]{0:T(1024)S(1)}, f32[1024]{0:T(1024)}, u32[]{:S(2)}) copy-start(f32[1024]{0:T(1024)} %copy-done.24) | copy-start | bytes 12292
  955.3 13.5 %copy-start.27 = (f32[552]{0:T(1024)S(1)}, f32[552]{0:T(1024)}, u32[]{:S(2)}) copy-start(f32[552]{0:T(1024)} %copy-done.26) | copy-start | bytes 6628
  966.8 84.1 %copy-start.3 = (bf16[552,1024]{1,0:T(8,128)(2,1)S(1)}, bf16[552,1024]{1,0:T(8,128)(2,1)}, u32[]{:S(2)}) copy-start(bf16[552,1024]{1,0:T(8,128)(2,1)} %reduce-scatter.8.cloned.1.call-done) | copy-start | bytes 3391492
  966.8 84.1 %copy-start.19 = (f32[552]{0:T(1024)S(1)}, f32[552]{0:T(1024)}, u32[]{:S(2)}) copy-start(f32[552]{0:T(1024)} %copy-done.18) | copy-start | bytes 6628
  966.8 84.1 %copy-start.21 = (f32[1024]{0:T(1024)S(1)}, f32[1024]{0:T(1024)}, u32[]{:S(2)}) copy-start(f32[1024]{0:T(1024)} %copy-done.20) | copy-start | bytes 12292
  966.8 84.1 %copy-start.31 = (f32[552]{0:T(1024)S(1)}, f32[552]{0:T(1024)}, u32[]{:S(2)}) copy-start(f32[552]{0:T(1024)} %copy-done.30) | copy-start | bytes 6628
  (30 other events, 103.1 us)
Sparse Core Ops, SparseCore 0:
  98.1 6.6 all-gather.9
  107.6 68.7 all-gather.11
  179.1 54.3 all-gather.13
  242.4 8.9 reduce-scatter.7
  254.0 77.1 all-gather.17
  333.2 9.4 all-gather.15
  344.8 11.9 all-gather.21
  359.6 77.2 all-gather.19
  474.4 8.3 reduce-scatter.11
  489.9 11.9 all-gather.23
  510.2 96.2 reduce-scatter.19
  608.6 94.7 reduce-scatter.17
  705.7 77.2 reduce-scatter.15
  789.3 164.8 all-reduce.19
  956.4 8.7 reduce-scatter.13
  967.3 10.9 reduce-scatter.9
where the time goes:
time: 1070 us; the launch traced here: 1060 us
  waiting for transfers between devices  501 us (47%)
  matrix products  208 us (19%)
  blocking collectives  202 us (19%)
  other arithmetic  95 us (9%)
  local copies, waits for them, and re-layouts  36 us (3%)
  between operations  18.1 us (2%)
    unnamed x17, waiting for transfers between devices  173 us
    unnamed x3, blocking collectives  158 us
    all_gather x1, waiting for transfers between devices, on_device(): lax.all_gather(fc2_weight, 'dp', axis=1, tiled=True)  80.1 us
    reduce_scatter x1, waiting for transfers between devices, on_device(): lax.psum_scatter(grad_proj.astype(jnp.bfloat16), 'dp', scatter_dimension=...  77.7 us
    all_gather x1, waiting for transfers between devices, on_device(): lax.all_gather(qkv_weight, 'dp', axis=1, tiled=True)  71.6 us
    all_gather x1, blocking collectives, on_device(): lax.all_gather(fc1_bias, 'dp', axis=0, tiled=True)  40.7 us
    dot_general x3, matrix products, contract_cols(): lax.dot_general(left, right, (((1,), (1,)), ((), ())), preferred_element_...  38.3 us
    convert_element_type x1, other arithmetic, attend_backward(): grad_scores = (attn_prob * (grad_prob - row_dot)).astype(jnp.bfloat16)  33.6 us
  transfers between devices with their start and end apart: 16, of which 12 were waited for; matrix products, arithmetic and copies ran while one was open for 25% of the time, Pallas kernels for 0%

commit v1 on v0

v1 whole, which is shorter than its diff:
```python
import jax
import jax.numpy as jnp
from jax import lax
from jax.sharding import PartitionSpec as P

HEAD_DIM = 64
SEQ_LEN = 1104
F32 = jnp.float32
BF16 = jnp.bfloat16


def dp_factors(size):
    if size % 8 == 0:
        return (4, 2, size // 8)
    return (1, 1, size)


class DpGrid:
    def __init__(self, size):
        self.size = size
        self.factors = dp_factors(size)

    def coords(self, index):
        _, second, third = self.factors
        return (index // (second * third), (index // third) % second, index % third)

    def index(self, coords):
        _, second, third = self.factors
        return (coords[0] * second + coords[1]) * third + coords[2]

    def ahead(self, index, axis, step):
        coords = list(self.coords(index))
        coords[axis] = (coords[axis] + step) % self.factors[axis]
        return self.index(coords)

    def fetch(self, value, axis, step):
        pairs = [(self.ahead(i, axis, step), i) for i in range(self.size)]
        return lax.ppermute(value, "dp", pairs)

    def push(self, value, axis, step):
        pairs = [(i, self.ahead(i, axis, step)) for i in range(self.size)]
        return lax.ppermute(value, "dp", pairs)

    def gather(self, value, order):
        done = []
        for axis in order:
            pieces = [value] + [
                self.fetch(value, axis, step) for step in range(1, self.factors[axis])
            ]
            place = sum(1 for other in done if other < axis)
            value = jnp.stack(pieces, axis=place)
            done.append(axis)
        return value

    def scatter(self, value, order):
        left = [0, 1, 2]
        for axis in order:
            place = left.index(axis)
            total = lax.index_in_dim(value, 0, place, keepdims=False).astype(F32)
            for step in range(1, self.factors[axis]):
                piece = lax.index_in_dim(value, step, place, keepdims=False)
                total = total + self.push(piece, axis, step).astype(F32)
            left.remove(axis)
            value = total.astype(BF16) if left else total
        return value

    def block_order(self):
        here = self.coords(lax.axis_index("dp"))
        rel = self.coords(jnp.arange(self.size, dtype=jnp.int32))
        return self.index([(h + r) % f for h, r, f in zip(here, rel, self.factors)])


class TensorPair:
    def __init__(self, size, slot_count, local_rows):
        self.size = size
        self.relative = size == 2 and slot_count == 1
        self.local_rows = local_rows

    def swap(self, value):
        return lax.ppermute(value, "tensor", [(0, 1), (1, 0)])

    def whole(self, value):
        if self.relative:
            return jnp.concatenate([value, self.swap(value)], axis=0)
        return lax.all_gather(value, "tensor", axis=0, tiled=True)

    def own(self, value):
        if self.relative:
            return value[: self.local_rows]
        start = lax.axis_index("tensor") * self.local_rows
        return lax.dynamic_slice_in_dim(value, start, self.local_rows, axis=0)

    def total(self, value):
        if self.relative:
            other = self.swap(value)
            other = jnp.concatenate([other[self.local_rows :], other[: self.local_rows]], axis=0)
            return value.astype(F32) + other.astype(F32)
        return lax.psum(value.astype(F32), "tensor")

    def own_total(self, value):
        if self.relative:
            kept = value[: self.local_rows].astype(F32)
            return kept + self.swap(value[self.local_rows :]).astype(F32)
        return lax.psum_scatter(value, "tensor", scatter_dimension=0, tiled=True).astype(F32)

    def small_total(self, value):
        if self.size == 2:
            return value + self.swap(value)
        return lax.psum(value, "tensor")


def normalize(values):
    row_mean = jnp.mean(values, axis=-1, keepdims=True)
    centered = values - row_mean
    variance = jnp.mean(centered * centered, axis=-1, keepdims=True)
    inverse = lax.rsqrt(variance + 1e-05)
    return centered * inverse, inverse


def norm_input_grad(grad, gain, normed, inverse):
    scaled = grad * gain
    first = jnp.mean(scaled, axis=-1, keepdims=True)
    second = jnp.mean(scaled * normed, axis=-1, keepdims=True)
    return inverse * (scaled - first - normed * second)


def masked_scores(query, keys, key_valid, score_scale):
    scores = jnp.einsum("qhd,khd->hqk", query, keys, preferred_element_type=F32) * score_scale
    return jnp.where(key_valid[None, None, :] > 0, scores, -1e30)


def attend_forward(query, keys, values, key_valid, score_scale):
    scores = masked_scores(query, keys, key_valid, score_scale)
    row_max = jnp.max(scores, axis=-1, keepdims=True)
    exp_scores = jnp.exp(scores - row_max)
    row_sum = jnp.sum(exp_scores, axis=-1, keepdims=True)
    attn_prob = (exp_scores / row_sum).astype(BF16)
    mixed = jnp.einsum("hqk,khd->qhd", attn_prob, values, preferred_element_type=F32)
    return (mixed.astype(BF16), row_max + jnp.log(row_sum))


def attend_backward(query, keys, values, key_valid, log_total, grad_mixed, score_scale):
    scores = masked_scores(query, keys, key_valid, score_scale)
    attn_prob = jnp.exp(scores - log_total)
    grad_prob = jnp.einsum("qhd,khd->hqk", grad_mixed, values, preferred_element_type=F32)
    row_dot = jnp.sum(attn_prob * grad_prob, axis=-1, keepdims=True)
    grad_scores = (attn_prob * (grad_prob - row_dot)).astype(BF16)
    grad_query = (
        jnp.einsum("hqk,khd->qhd", grad_scores, keys, preferred_element_type=F32) * score_scale
    )
    grad_keys = (
        jnp.einsum("hqk,qhd->khd", grad_scores, query, preferred_element_type=F32) * score_scale
    )
    grad_values = jnp.einsum(
        "hqk,qhd->khd", attn_prob.astype(BF16), grad_mixed, preferred_element_type=F32
    )
    return (grad_query.astype(BF16), grad_keys.astype(BF16), grad_values.astype(BF16))


def dot_nn(left, right):
    return lax.dot_general(left, right, (((1,), (0,)), ((), ())), preferred_element_type=F32)


def dot_tn(left, right):
    return lax.dot_general(left, right, (((0,), (0,)), ((), ())), preferred_element_type=F32)


def dot_nt(left, right):
    return lax.dot_general(left, right, (((1,), (1,)), ((), ())), preferred_element_type=F32)


def gelu_and_slope(values):
    cdf = 0.5 * (1.0 + lax.erf(values * (0.5**0.5)))
    density = jnp.exp(-0.5 * values * values) * 0.3989422804014327
    return values * cdf, cdf + values * density


def on_device(
    inputs,
    cotangent,
    slot_live,
    token_type,
    attn_norm_gain,
    attn_norm_bias,
    qkv_weight,
    proj_weight,
    proj_bias,
    mlp_norm_gain,
    mlp_norm_bias,
    fc1_weight,
    fc1_bias,
    fc2_weight,
    fc2_bias,
):
    dp_size = lax.axis_size("dp")
    tensor_size = lax.axis_size("tensor")
    local_rows, width = inputs.shape
    slot_count = slot_live.shape[0]
    whole_rows = local_rows * tensor_size
    block = fc1_weight.shape[0]
    width_here = qkv_weight.shape[2]
    heads_here = width_here // HEAD_DIM
    hidden_here = fc1_weight.shape[1]
    hidden_block = fc1_bias.shape[0]
    hidden_cut = hidden_here // 2
    score_scale = HEAD_DIM ** (-0.5)
    grid = DpGrid(dp_size)
    pair = TensorPair(tensor_size, slot_count, local_rows)
    first_order, second_order = (0, 2, 1), (0, 1, 2)

    smalls = jnp.stack(
        (attn_norm_gain, attn_norm_bias, proj_bias, mlp_norm_gain, mlp_norm_bias, fc2_bias)
    )
    bias_rows = -(-hidden_block // block)
    bias_pad = bias_rows * block - hidden_block
    bias_block = jnp.pad(fc1_bias, (0, bias_pad)).reshape(bias_rows, block)
    smalls = jnp.concatenate([smalls, bias_block], axis=0)
    smalls = grid.gather(smalls, second_order).reshape(dp_size, 6 + bias_rows, block)

    def rows_of(weight):
        return weight.reshape(width, weight.shape[-1])

    weight_q, weight_k, weight_v = qkv_weight[0], qkv_weight[1], qkv_weight[2]
    query_key = rows_of(grid.gather(jnp.concatenate([weight_q, weight_k], axis=1), first_order))
    value_proj = rows_of(
        grid.gather(jnp.concatenate([weight_v, proj_weight.T], axis=1), second_order)
    )
    fc2_t = fc2_weight.T
    fc1_parts, fc2_parts = [], []
    for start in (0, hidden_cut):
        cut = slice(start, start + hidden_cut)
        fc1_parts.append(rows_of(grid.gather(fc1_weight[:, cut], first_order)))
        fc2_parts.append(rows_of(grid.gather(fc2_t[:, cut], second_order)))

    order = grid.block_order()
    feature = jnp.repeat(order * block, block) + jnp.tile(
        jnp.arange(block, dtype=jnp.int32), dp_size
    )
    select = (jnp.arange(width, dtype=jnp.int32)[:, None] == feature[None, :]).astype(BF16)
    rows_in_b = pair.whole(dot_nn(inputs, select).astype(BF16))
    grad_out_b = pair.whole(dot_nn(cotangent, select).astype(BF16))
    rows_in = rows_in_b.astype(F32)
    valid_whole = pair.whole((token_type != 3).astype(F32))
    valid_seq = valid_whole.reshape(slot_count, SEQ_LEN)
    live_col = jnp.repeat(slot_live.astype(F32), SEQ_LEN)[:, None]

    vectors = smalls[:, :6].transpose(1, 0, 2).reshape(6, width).astype(F32)
    gain_one, shift_one, proj_shift, gain_two, shift_two, fc2_shift = (
        vectors[i : i + 1] for i in range(6)
    )
    place = (jnp.arange(dp_size, dtype=jnp.int32)[:, None] == order[None, :]).astype(BF16)
    fc1_shift = smalls[:, 6:].reshape(dp_size, bias_rows * block)[:, :hidden_block]
    fc1_shift = dot_nn(place, fc1_shift).reshape(1, hidden_here)

    hat_one, inverse_one = normalize(rows_in)
    norm_one = (hat_one * gain_one + shift_one).astype(BF16)
    packed_qk = dot_nn(norm_one, query_key).astype(BF16)
    packed_v = dot_nn(norm_one, value_proj[:, :width_here]).astype(BF16)
    proj_t = value_proj[:, width_here:]
    split = (slot_count, SEQ_LEN, heads_here, HEAD_DIM)
    query = packed_qk[:, :width_here].reshape(split)
    keys = packed_qk[:, width_here:].reshape(split)
    values = packed_v.reshape(split)

    forward = [
        attend_forward(query[s], keys[s], values[s], valid_seq[s], score_scale)
        for s in range(slot_count)
    ]
    mixed = jnp.concatenate([f[0] for f in forward], axis=0).reshape(whole_rows, width_here)

    attn_out = pair.total(dot_nt(mixed, proj_t).astype(BF16))
    middle = rows_in + live_col * (attn_out + proj_shift)
    hat_two, inverse_two = normalize(middle)
    norm_two = (hat_two * gain_two + shift_two).astype(BF16)
    grad_out = grad_out_b.astype(F32)
    grad_mlp = (live_col * grad_out).astype(BF16)

    mlp_out, grad_two = 0.0, 0.0
    out_fc1, out_fc2, fc1_bias_parts = [], [], []
    block_shape = grid.factors + (block,)
    for part in range(2):
        cut = slice(part * hidden_cut, (part + 1) * hidden_cut)
        hidden_pre = dot_nn(norm_two, fc1_parts[part]) + fc1_shift[:, cut]
        hidden_act, slope = gelu_and_slope(hidden_pre)
        hidden_act = hidden_act.astype(BF16)
        mlp_out = mlp_out + dot_nt(hidden_act, fc2_parts[part])
        grad_pre = (dot_nn(grad_mlp, fc2_parts[part]) * slope).astype(BF16)
        grad_fc2 = dot_tn(grad_mlp, hidden_act).astype(BF16).reshape(block_shape + (hidden_cut,))
        grad_fc1 = dot_tn(norm_two, grad_pre).astype(BF16).reshape(block_shape + (hidden_cut,))
        fc1_bias_parts.append(jnp.sum(grad_pre, axis=0, dtype=F32))
        grad_two = grad_two + dot_nt(grad_pre, fc1_parts[part])
        out_fc1.append(grid.scatter(grad_fc1, first_order[::-1]))
        out_fc2.append(grid.scatter(grad_fc2, second_order[::-1]))
    grad_fc1_bias = jnp.concatenate(fc1_bias_parts)

    result = pair.own(middle) + pair.own(live_col) * (
        pair.own_total(mlp_out.astype(BF16)) + fc2_shift
    )
    outputs = dot_nt(result.astype(BF16), select).astype(BF16)

    grad_two = pair.total(grad_two.astype(BF16))
    grad_gain_two = jnp.sum(grad_two * hat_two, axis=0)
    grad_shift_two = jnp.sum(grad_two, axis=0)
    grad_middle = grad_out + norm_input_grad(grad_two, gain_two, hat_two, inverse_two)
    grad_branch = (live_col * grad_middle).astype(BF16)
    grad_proj_bias = jnp.sum(grad_branch, axis=0, dtype=F32)
    grad_fc2_bias = jnp.sum(grad_mlp, axis=0, dtype=F32)
    grad_proj = dot_tn(grad_branch, mixed).astype(BF16)
    grad_mixed = dot_nn(grad_branch, proj_t).astype(BF16).reshape(split)
    backward = [
        attend_backward(
            query[s], keys[s], values[s], valid_seq[s], forward[s][1], grad_mixed[s], score_scale
        )
        for s in range(slot_count)
    ]
    grad_q, grad_k, grad_v = (
        jnp.concatenate([b[i] for b in backward], axis=0).reshape(whole_rows, width_here)
        for i in range(3)
    )
    grad_qk = jnp.concatenate([grad_q, grad_k], axis=1)
    grad_weight_qk = dot_tn(norm_one, grad_qk).astype(BF16)
    grad_weight_v = dot_tn(norm_one, grad_v).astype(BF16)
    out_qk = grid.scatter(
        grad_weight_qk.reshape(block_shape + (2 * width_here,)), first_order[::-1]
    )
    out_vp = grid.scatter(
        jnp.concatenate([grad_weight_v, grad_proj], axis=1).reshape(
            block_shape + (2 * width_here,)
        ),
        second_order[::-1],
    )
    grad_one = dot_nt(grad_qk, query_key) + dot_nt(grad_v, value_proj[:, :width_here])
    grad_one = pair.own_total(grad_one.astype(BF16))
    own_hat, own_inverse = pair.own(hat_one), pair.own(inverse_one)
    grad_gain_one = pair.small_total(jnp.sum(grad_one * own_hat, axis=0))
    grad_shift_one = pair.small_total(jnp.sum(grad_one, axis=0))
    grad_rows = pair.own(grad_middle) + norm_input_grad(grad_one, gain_one, own_hat, own_inverse)
    grad_inputs = dot_nt(grad_rows.astype(BF16), select).astype(BF16)

    vector_grads = jnp.stack(
        (
            grad_gain_one,
            grad_shift_one,
            grad_proj_bias,
            grad_gain_two,
            grad_shift_two,
            grad_fc2_bias,
        )
    ).astype(BF16)
    vector_grads = vector_grads.reshape(6, dp_size, block).transpose(1, 0, 2)
    bias_grads = dot_tn(place, grad_fc1_bias.astype(BF16).reshape(dp_size, hidden_block))
    bias_grads = jnp.pad(bias_grads.astype(BF16), ((0, 0), (0, bias_pad)))
    bias_grads = bias_grads.reshape(dp_size, bias_rows, block)
    small_grads = jnp.concatenate([vector_grads, bias_grads], axis=1)
    small_grads = grid.scatter(
        small_grads.reshape(grid.factors + (6 + bias_rows, block)), second_order[::-1]
    )
    out_qkv = jnp.stack([out_qk[:, :width_here], out_qk[:, width_here:], out_vp[:, :width_here]])
    return (
        outputs,
        grad_inputs,
        small_grads[0],
        small_grads[1],
        out_qkv,
        out_vp[:, width_here:].T,
        small_grads[2],
        small_grads[3],
        small_grads[4],
        jnp.concatenate(out_fc1, axis=1),
        small_grads[6:].reshape(-1)[:hidden_block],
        jnp.concatenate(out_fc2, axis=1).T,
        small_grads[5],
    )


def solution(mesh):
    in_specs = (
        P(("dp", "tensor"), None),
        P(("dp", "tensor"), None),
        P("dp"),
        P(("dp", "tensor")),
        P("dp"),
        P("dp"),
        P(None, "dp", "tensor"),
        P("tensor", "dp"),
        P("dp"),
        P("dp"),
        P("dp"),
        P("dp", "tensor"),
        P(("tensor", "dp")),
        P("tensor", "dp"),
        P("dp"),
    )
    out_specs = (
        P(("dp", "tensor"), None),
        P(("dp", "tensor"), None),
        P("dp"),
        P("dp"),
        P(None, "dp", "tensor"),
        P("tensor", "dp"),
        P("dp"),
        P("dp"),
        P("dp"),
        P("dp", "tensor"),
        P(("tensor", "dp")),
        P("tensor", "dp"),
        P("dp"),
    )
    return jax.shard_map(
        on_device, mesh=mesh, in_specs=in_specs, out_specs=out_specs, check_vma=False
    )
```

time: 1070 us -> 645 us (0.60)
  waiting for transfers between devices: 501 us -> 157 us
  blocking collectives: 202 us -> 0 us
  starting transfers between devices: 2.14 us -> 126 us
  other arithmetic: 95 us -> 113 us
  between operations: 18.1 us -> 3.21 us
    all_gather x8 -> x0, waiting for transfers between devices: 199 us -> none  [the longest x1 80.1 us: on_device(): lax.all_gather(fc2_weight, 'dp', axis=1, tiled=True)]
    unnamed x17 -> x0, waiting for transfers between devices: 173 us -> none
    unnamed x3 -> x0, blocking collectives: 158 us -> none
    ppermute x0 -> x79, waiting for transfers between devices: none -> 157 us  [the longest x35 81.5 us: push(): return lax.ppermute(value, 'dp', pairs)]
    reduce_scatter x7 -> x0, waiting for transfers between devices: 130 us -> none  [the longest x1 77.7 us: on_device(): lax.psum_scatter(grad_proj.astype(jnp.bfloat16), 'dp', scatter_dimension=...]
    ppermute x0 -> x79, starting transfers between devices: none -> 126 us  [the longest x35 69.5 us: fetch(): return lax.ppermute(value, 'dp', pairs)]
    all_gather x1 -> x0, blocking collectives: 40.7 us -> none  [on_device(): lax.all_gather(fc1_bias, 'dp', axis=0, tiled=True)]
    another operation x0 -> x26, other arithmetic: none -> 26.4 us  [the longest x23 25.7 us: gather(): value = jnp.stack(pieces, axis=place)]
  transfers between devices with their start and end apart: 16 -> 79, of which waited for: 12 -> 28; matrix products, arithmetic and copies ran while one was open for 25% -> 31% of each run, Pallas kernels for 0% -> 0%
where the time goes in v1:
time: 645 us; the launch traced here: 640 us
  matrix products  198 us (31%)
  waiting for transfers between devices  157 us (24%)
  starting transfers between devices  126 us (20%)
  other arithmetic  113 us (18%)
  local copies, waits for them, and re-layouts  42.9 us (7%)
    ppermute x35, waiting for transfers between devices, push(): return lax.ppermute(value, 'dp', pairs)  81.5 us
    ppermute x35, waiting for transfers between devices, fetch(): return lax.ppermute(value, 'dp', pairs)  74.2 us
    ppermute x35, starting transfers between devices, fetch(): return lax.ppermute(value, 'dp', pairs)  69.5 us
    ppermute x35, starting transfers between devices, push(): return lax.ppermute(value, 'dp', pairs)  55.7 us
    dot_general x9, matrix products, dot_nt(): lax.dot_general(left, right, (((1,), (1,)), ((), ())), preferred_element_...  39.7 us
    dot_general x1, matrix products, attend_backward(): jnp.einsum('qhd,khd->hqk', grad_mixed, values, preferred_element_type=F32)  32.8 us
    convert_element_type x1, other arithmetic, attend_backward(): grad_scores = (attn_prob * (grad_prob - row_dot)).astype(BF16)  32.6 us
    dot_general x10, matrix products, dot_nn(): lax.dot_general(left, right, (((1,), (0,)), ((), ())), preferred_element_...  29 us
  transfers between devices with their start and end apart: 79, of which 28 were waited for; matrix products, arithmetic and copies ran while one was open for 31% of the time, Pallas kernels for 0%

profile of v1, /device:TPU:0, one launch (start us, length us, event | category | flops | bytes accessed | tf_op | source)
XLA Modules:
  0.0 639.6 jit_solution(15184068943807710580)
XLA Ops:
  45.0 4.7 collective-permute-done.29
  56.3 6.8 %collective-permute-start.25 = (bf16[64,1024]{1,0:T(8,128)(2,1)}, bf16[64,1024]{1,0:T(8,128)(2,1)S(1)}, u32[]{:S(2)}, u32[]{:S(2)}) collective-permute-start(bf16[64,1024]{1,0:T(8,128)(2,1)} %get-tuple-element.102), channel_id=1, source_target_pairs={{24,0},{26,2},{28,4},{30,6},{0,8},{2,10},{4,12},{6,14},{8,16},{10,... | collective-permute-start | bytes 393224 | tf_op jit(solution)/shard_map/ppermute | solution.py:38
  102.1 24.6 %collective-permute-done.10 = bf16[4,2,64,1024]{3,2,1,0:T(8,128)(2,1)S(1)} collective-permute-done((bf16[4,2,64,1024]{3,2,1,0:T(8,128)(2,1)S(1)}, bf16[4,2,64,1024]{3,2,1,0:T(8,128)(2,1)S(1)}, u32[]{:S(2)}, u32[]{:S(2)}) %collective-permute-start.10) | collective-permute-done | bytes 1048608 | tf_op jit(solution)/shard_map/ppermute | solution.py:38
  134.5 5.8 collective-permute-done.16
  148.5 17.7 %select_reduce_fusion = (f32[8,1104]{1,0:T(8,128)S(1)}, f32[8,1104,1104]{1,2,0:T(8,128)}) fusion(pred[1104]{0:T(1024)(128)(4,1)S(1)} %maximum_compare_fusion, bf16[1104,8,64]{0,2,1:T(8,128)(2,1)S(1)} %bitcast.400, bf16[1104,8,64]{0,2,1:T(8,128)(2,1)} %bitcast.402), kind=kOutput, calls=%fused_computation.7 | convolution fusion | flops 1277310336 | bytes 41299536 | tf_op jit(solution)/shard_map/qhd,khd->hqk/dot_general | solution.py:128
  166.1 17.1 %fusion = f32[8,1104]{1,0:T(8,128)S(1)} fusion(f32[8,1104,1104]{1,2,0:T(8,128)} %get-tuple-element.135, f32[8,1104]{1,0:T(8,128)S(1)} %get-tuple-element.134, pred[1104]{0:T(1024)(128)(4,1)S(1)} %maximum_compare_fusion), kind=kLoop, calls=%fused_computation.6 | loop fusion | flops 29242752 | bytes 39073872 | tf_op jit(solution)/shard_map/reduce_sum | solution.py:136
  183.3 17.0 %fusion.35 = bf16[8,64,1104]{2,1,0:T(8,128)(2,1)S(1)} fusion(bf16[1104,8,64]{0,2,1:T(8,128)(2,1)S(1)} %bitcast.406, f32[8,1104,1104]{1,2,0:T(8,128)} %get-tuple-element.135, f32[8,1104]{1,0:T(8,128)S(1)} %fusion, f32[8,1104]{1,0:T(8,128)S(1)} %get-tuple-element.134, pred[1104]{0:T(1024)(128)(4,1)S(1)} %maximum_compare_fusion), kind=kOutput, calls=%fused_computation.72 | convolution fusion | flops 1287634944 | bytes 41334864 | tf_op jit(solution)/shard_map/hqk,khd->qhd/dot_general | solution.py:138
  217.6 14.5 %collective-permute-done.37 = bf16[4,2,64,1024]{3,2,0,1:T(8,128)(2,1)} collective-permute-done((bf16[4,2,64,1024]{3,2,0,1:T(8,128)(2,1)}, bf16[4,2,64,1024]{3,2,0,1:T(8,128)(2,1)}, u32[]{:S(2)}, u32[]{:S(2)}) %collective-permute-start.37) | collective-permute-done | bytes 1048608 | tf_op jit(solution)/shard_map/ppermute | solution.py:38
  238.0 16.1 %collective-permute-done.27 = bf16[4,2,64,1024]{3,2,1,0:T(8,128)(2,1)} collective-permute-done((bf16[4,2,64,1024]{3,2,1,0:T(8,128)(2,1)}, bf16[4,2,64,1024]{3,2,1,0:T(8,128)(2,1)}, u32[]{:S(2)}, u32[]{:S(2)}) %collective-permute-start.27) | collective-permute-done | bytes 1048608 | tf_op jit(solution)/shard_map/ppermute | solution.py:38
  267.5 5.5 fusion.147
  283.5 4.7 fusion.149
  297.4 5.3 fusion.148
  310.3 6.3 fusion.24
  335.0 12.9 %collective-permute-done.69 = bf16[4,2,64,1024]{3,2,0,1:T(8,128)(2,1)S(1)} collective-permute-done((bf16[4,2,64,1024]{3,2,0,1:T(8,128)(2,1)S(1)}, bf16[4,2,64,1024]{3,2,0,1:T(8,128)(2,1)S(1)}, u32[]{:S(2)}, u32[]{:S(2)}) %collective-permute-start.69) | collective-permute-done | bytes 1048608 | tf_op jit(solution)/shard_map/ppermute | solution.py:42
  354.1 5.0 collective-permute-done.65
  363.6 4.8 collective-permute-done.60
  376.1 6.0 collective-permute-done.67
  399.1 6.5 %collective-permute-done.62 = bf16[64,1024]{1,0:T(8,128)(2,1)S(1)} collective-permute-done((bf16[64,1024]{1,0:T(8,128)(2,1)S(1)}, bf16[64,1024]{1,0:T(8,128)(2,1)S(1)}, u32[]{:S(2)}, u32[]{:S(2)}) %collective-permute-start.62) | collective-permute-done | bytes 131104 | tf_op jit(solution)/shard_map/ppermute | solution.py:42
  415.0 5.3 fusion.133
  424.9 16.0 %fusion.32 = bf16[8,64,1104]{2,1,0:T(8,128)(2,1)S(1)} fusion(bf16[1104,8,64]{0,2,1:T(8,128)(2,1)S(1)} %bitcast.408, f32[8,1104,1104]{1,2,0:T(8,128)} %get-tuple-element.135, f32[8,1104]{1,0:T(8,128)S(1)} %log_add_fusion, pred[1104]{0:T(1024)(128)(4,1)S(1)} %maximum_compare_fusion), kind=kOutput, calls=%fused_computation.69 | convolution fusion | flops 1277884416 | bytes 41299536 | tf_op jit(solution)/shard_map/hqk,qhd->khd/dot_general | solution.py:154
  444.5 4.9 fusion.74
  449.4 32.8 %multiply_reduce_fusion = (f32[8,1104]{1,0:T(8,128)S(1)}, f32[8,1104,1104]{1,2,0:T(8,128)}) fusion(f32[8,1104,1104]{1,2,0:T(8,128)} %get-tuple-element.135, f32[8,1104]{1,0:T(8,128)S(1)} %log_add_fusion, pred[1104]{0:T(1024)(128)(4,1)S(1)} %maximum_compare_fusion, bf16[1104,8,64]{0,2,1:T(8,128)(2,1)S(1)} %bitcast.409, bf16[1104,8,64]{0,2,1:T(8,128)(2,1)S(1)} %bitcast.407), kind=kOutput, calls=%fused_computation.2 | convolution fusion | flops 1287060864 | bytes 80336976 | tf_op jit(solution)/shard_map/qhd,khd->hqk/dot_general | solution.py:145
  482.2 32.6 %multiply_convert_fusion = bf16[8,1104,1104]{1,2,0:T(8,128)(2,1)} fusion(f32[8,1104,1104]{1,2,0:T(8,128)} %get-tuple-element.141, f32[8,1104,1104]{1,2,0:T(8,128)} %get-tuple-element.135, f32[8,1104]{1,0:T(8,128)S(1)} %get-tuple-element.140, f32[8,1104]{1,0:T(8,128)S(1)} %log_add_fusion, pred[1104]{0:T(1024)(128)(4,1)S(1)} %maximum_compare_fusion), kind=kLoop, calls=%fused_computation.1 | loop fusion | flops 48752640 | bytes 97577040 | tf_op jit(solution)/shard_map/convert_element_type | solution.py:147
  514.8 11.1 %fusion.31 = bf16[8,64,1104]{2,1,0:T(8,128)(2,1)} fusion(bf16[1104,8,64]{0,2,1:T(8,128)(2,1)S(1)} %bitcast.401, bf16[8,1104,1104]{1,2,0:T(8,128)(2,1)} %multiply_convert_fusion), kind=kOutput, calls=%fused_computation.68 | convolution fusion | flops 1249198080 | bytes 21762048 | tf_op jit(solution)/shard_map/hqk,qhd->khd/dot_general | solution.py:152
  525.9 11.4 %fusion.30 = bf16[8,64,1104]{2,1,0:T(8,128)(2,1)} fusion(bf16[1104,8,64]{0,2,1:T(8,128)(2,1)S(1)} %bitcast.403, bf16[8,1104,1104]{1,2,0:T(8,128)(2,1)} %multiply_convert_fusion), kind=kOutput, calls=%fused_computation.67 | convolution fusion | flops 1249198080 | bytes 21762048 | tf_op jit(solution)/shard_map/hqk,khd->qhd/dot_general | solution.py:149
  543.9 5.2 convolution_convert_fusion.8
  553.1 5.1 fusion.26
  562.7 4.6 collective-permute-done.54
  571.4 6.7 %collective-permute-done.49 = bf16[4,2,64,1024]{3,2,0,1:T(8,128)(2,1)} collective-permute-done((bf16[4,2,64,1024]{3,2,0,1:T(8,128)(2,1)}, bf16[4,2,64,1024]{3,2,0,1:T(8,128)(2,1)}, u32[]{:S(2)}, u32[]{:S(2)}) %collective-permute-start.49) | collective-permute-done | bytes 1048608 | tf_op jit(solution)/shard_map/ppermute | solution.py:42
  587.4 11.4 %collective-permute-done.44 = bf16[4,2,8,64]{3,1,0,2:T(2,128)(2,1)S(1)} collective-permute-done((bf16[4,2,8,64]{3,1,0,2:T(2,128)(2,1)S(1)}, bf16[4,2,8,64]{3,1,0,2:T(2,128)(2,1)S(1)}, u32[]{:S(2)}, u32[]{:S(2)}) %collective-permute-start.44) | collective-permute-done | bytes 8224 | tf_op jit(solution)/shard_map/ppermute | solution.py:42
  606.0 6.0 fusion.54
  625.7 8.6 %collective-permute-done.57 = bf16[64,1024]{1,0:T(8,128)(2,1)S(1)} collective-permute-done((bf16[64,1024]{1,0:T(8,128)(2,1)S(1)}, bf16[64,1024]{1,0:T(8,128)(2,1)S(1)}, u32[]{:S(2)}, u32[]{:S(2)}) %collective-permute-start.57) | collective-permute-done | bytes 131104 | tf_op jit(solution)/shard_map/ppermute | solution.py:42
  (467 shorter events, 293.6 us)
Async XLA Ops:
  29.4 20.3 %collective-permute-start.29 = (bf16[64,1024]{1,0:T(8,128)(2,1)}, bf16[64,1024]{1,0:T(8,128)(2,1)S(1)}, u32[]{:S(2)}, u32[]{:S(2)}) collective-permute-start(bf16[64,1024]{1,0:T(8,128)(2,1)} %get-tuple-element.105), channel_id=1, source_target_pairs={{16,0},{18,2},{20,4},{22,6},{24,8},{26,10},{28,12},{30,14},{0,16},... | collective-permute-start | bytes 393224 | tf_op jit(solution)/shard_map/ppermute | solution.py:38
  30.0 21.8 %collective-permute-start.28 = (bf16[64,1024]{1,0:T(8,128)(2,1)}, bf16[64,1024]{1,0:T(8,128)(2,1)S(1)}, u32[]{:S(2)}, u32[]{:S(2)}) collective-permute-start(bf16[64,1024]{1,0:T(8,128)(2,1)} %get-tuple-element.105), channel_id=1, source_target_pairs={{8,0},{10,2},{12,4},{14,6},{16,8},{18,10},{20,12},{22,14},{24,16},... | collective-permute-start | bytes 393224 | tf_op jit(solution)/shard_map/ppermute | solution.py:38
  33.8 22.1 %collective-permute-start.30 = (bf16[64,1024]{1,0:T(8,128)(2,1)}, bf16[64,1024]{1,0:T(8,128)(2,1)S(1)}, u32[]{:S(2)}, u32[]{:S(2)}) collective-permute-start(bf16[64,1024]{1,0:T(8,128)(2,1)} %get-tuple-element.105), channel_id=1, source_target_pairs={{24,0},{26,2},{28,4},{30,6},{0,8},{2,10},{4,12},{6,14},{8,16},{10,... | collective-permute-start | bytes 393224 | tf_op jit(solution)/shard_map/ppermute | solution.py:38
  41.1 21.9 %collective-permute-start.18 = (bf16[64,1024]{1,0:T(8,128)(2,1)}, bf16[64,1024]{1,0:T(8,128)(2,1)}, u32[]{:S(2)}, u32[]{:S(2)}) collective-permute-start(bf16[64,1024]{1,0:T(8,128)(2,1)} %get-tuple-element.106), channel_id=1, source_target_pairs={{8,0},{10,2},{12,4},{14,6},{16,8},{18,10},{20,12},{22,14},{24,16},... | collective-permute-start | bytes 393224 | tf_op jit(solution)/shard_map/ppermute | solution.py:38
  63.1 34.0 %collective-permute-start = (bf16[552,1024]{1,0:T(8,128)(2,1)S(1)}, bf16[552,1024]{1,0:T(8,128)(2,1)S(1)}, u32[]{:S(2)}, u32[]{:S(2)}) collective-permute-start(bf16[552,1024]{1,0:T(8,128)(2,1)S(1)} %fusion.56), channel_id=1, source_target_pairs={{0,1},{1,0},{2,3},{3,2},{4,5},{5,4},{6,7},{7,6},{8,9},{9,8},{10,11... | collective-permute-start | bytes 3391496 | tf_op jit(solution)/shard_map/ppermute | solution.py:80
  67.8 20.3 %collective-permute-start.31 = (bf16[4,64,1024]{2,1,0:T(8,128)(2,1)S(1)}, bf16[4,64,1024]{2,1,0:T(8,128)(2,1)S(1)}, u32[]{:S(2)}, u32[]{:S(2)}) collective-permute-start(bf16[4,64,1024]{2,1,0:T(8,128)(2,1)S(1)} %get-tuple-element.90), channel_id=1, source_target_pairs={{2,0},{0,2},{6,4},{4,6},{10,8},{8,10},{14,12},{12,14},{18,16},{16,... | collective-permute-start | bytes 1572872 | tf_op jit(solution)/shard_map/ppermute | solution.py:38
  73.2 20.6 %collective-permute-start.15 = (bf16[4,64,1024]{2,1,0:T(8,128)(2,1)S(1)}, bf16[4,64,1024]{2,1,0:T(8,128)(2,1)S(1)}, u32[]{:S(2)}, u32[]{:S(2)}) collective-permute-start(bf16[4,64,1024]{2,1,0:T(8,128)(2,1)S(1)} %get-tuple-element.92), channel_id=1, source_target_pairs={{2,0},{0,2},{6,4},{4,6},{10,8},{8,10},{14,12},{12,14},{18,16},{16,... | collective-permute-start | bytes 1572872 | tf_op jit(solution)/shard_map/ppermute | solution.py:38
  86.5 119.9 %collective-permute-start.21 = (bf16[4,64,1024]{2,1,0:T(8,128)(2,1)}, bf16[4,64,1024]{2,1,0:T(8,128)(2,1)}, u32[]{:S(2)}, u32[]{:S(2)}) collective-permute-start(bf16[4,64,1024]{2,1,0:T(8,128)(2,1)} %get-tuple-element.86), channel_id=1, source_target_pairs={{2,0},{0,2},{6,4},{4,6},{10,8},{8,10},{14,12},{12,14},{18,16},{16,... | collective-permute-start | bytes 1572872 | tf_op jit(solution)/shard_map/ppermute | solution.py:38
  88.0 115.2 %collective-permute-start.36 = (bf16[4,64,1024]{2,1,0:T(8,128)(2,1)}, bf16[4,64,1024]{2,1,0:T(8,128)(2,1)}, u32[]{:S(2)}, u32[]{:S(2)}) collective-permute-start(bf16[4,64,1024]{2,1,0:T(8,128)(2,1)} %get-tuple-element.88), channel_id=1, source_target_pairs={{4,0},{6,2},{0,4},{2,6},{12,8},{14,10},{8,12},{10,14},{20,16},{22,... | collective-permute-start | bytes 1572872 | tf_op jit(solution)/shard_map/ppermute | solution.py:38
  93.8 116.3 %collective-permute-start.26 = (bf16[4,64,1024]{2,1,0:T(8,128)(2,1)}, bf16[4,64,1024]{2,1,0:T(8,128)(2,1)}, u32[]{:S(2)}, u32[]{:S(2)}) collective-permute-start(bf16[4,64,1024]{2,1,0:T(8,128)(2,1)} %get-tuple-element.84), channel_id=1, source_target_pairs={{4,0},{6,2},{0,4},{2,6},{12,8},{14,10},{8,12},{10,14},{20,16},{22,... | collective-permute-start | bytes 1572872 | tf_op jit(solution)/shard_map/ppermute | solution.py:38
  96.4 43.8 %collective-permute-start.16 = (bf16[4,2,64,1024]{3,2,1,0:T(8,128)(2,1)}, bf16[4,2,64,1024]{3,2,1,0:T(8,128)(2,1)}, u32[]{:S(2)}, u32[]{:S(2)}) collective-permute-start(bf16[4,2,64,1024]{3,2,1,0:T(8,128)(2,1)} %get-tuple-element.62), channel_id=1, source_target_pairs={{4,0},{6,2},{0,4},{2,6},{12,8},{14,10},{8,12},{10,14},{20,16},{22,... | collective-permute-start | bytes 3145736 | tf_op jit(solution)/shard_map/ppermute | solution.py:38
  97.1 29.6 %collective-permute-start.10 = (bf16[4,2,64,1024]{3,2,1,0:T(8,128)(2,1)S(1)}, bf16[4,2,64,1024]{3,2,1,0:T(8,128)(2,1)S(1)}, u32[]{:S(2)}, u32[]{:S(2)}) collective-permute-start(bf16[4,2,64,1024]{3,2,1,0:T(8,128)(2,1)S(1)} %get-tuple-element.64), channel_id=1, source_target_pairs={{2,0},{0,2},{6,4},{4,6},{10,8},{8,10},{14,12},{12,14},{18,16},{16,... | collective-permute-start | bytes 3145736 | tf_op jit(solution)/shard_map/ppermute | solution.py:38
  126.7 107.4 %collective-permute-start.32 = (bf16[4,2,64,1024]{3,2,1,0:T(8,128)(2,1)}, bf16[4,2,64,1024]{3,2,1,0:T(8,128)(2,1)}, u32[]{:S(2)}, u32[]{:S(2)}) collective-permute-start(bf16[4,2,64,1024]{3,2,1,0:T(8,128)(2,1)} %get-tuple-element.60), channel_id=1, source_target_pairs={{4,0},{6,2},{0,4},{2,6},{12,8},{14,10},{8,12},{10,14},{20,16},{22,... | collective-permute-start | bytes 3145736 | tf_op jit(solution)/shard_map/ppermute | solution.py:38
  203.2 52.3 %collective-permute-start.17 = (bf16[1104,1024]{1,0:T(8,128)(2,1)}, bf16[1104,1024]{1,0:T(8,128)(2,1)}, u32[]{:S(2)}, u32[]{:S(2)}) collective-permute-start(bf16[1104,1024]{1,0:T(8,128)(2,1)} %convolution_convert_fusion), channel_id=1, source_target_pairs={{0,1},{1,0},{2,3},{3,2},{4,5},{5,4},{6,7},{7,6},{8,9},{9,8},{10,11... | collective-permute-start | bytes 6782984 | tf_op jit(solution)/shard_map/ppermute | solution.py:80
  205.8 26.3 %collective-permute-start.37 = (bf16[4,2,64,1024]{3,2,0,1:T(8,128)(2,1)}, bf16[4,2,64,1024]{3,2,0,1:T(8,128)(2,1)}, u32[]{:S(2)}, u32[]{:S(2)}) collective-permute-start(bf16[4,2,64,1024]{3,2,0,1:T(8,128)(2,1)} %get-tuple-element.58), channel_id=1, source_target_pairs={{2,0},{0,2},{6,4},{4,6},{10,8},{8,10},{14,12},{12,14},{18,16},{16,... | collective-permute-start | bytes 3145736 | tf_op jit(solution)/shard_map/ppermute | solution.py:38
  208.5 28.0 %collective-permute-start.22 = (bf16[4,2,64,1024]{3,2,1,0:T(8,128)(2,1)}, bf16[4,2,64,1024]{3,2,1,0:T(8,128)(2,1)}, u32[]{:S(2)}, u32[]{:S(2)}) collective-permute-start(bf16[4,2,64,1024]{3,2,1,0:T(8,128)(2,1)} %get-tuple-element.56), channel_id=1, source_target_pairs={{4,0},{6,2},{0,4},{2,6},{12,8},{14,10},{8,12},{10,14},{20,16},{22,... | collective-permute-start | bytes 3145736 | tf_op jit(solution)/shard_map/ppermute | solution.py:38
  212.5 41.6 %collective-permute-start.27 = (bf16[4,2,64,1024]{3,2,1,0:T(8,128)(2,1)}, bf16[4,2,64,1024]{3,2,1,0:T(8,128)(2,1)}, u32[]{:S(2)}, u32[]{:S(2)}) collective-permute-start(bf16[4,2,64,1024]{3,2,1,0:T(8,128)(2,1)} %get-tuple-element.54), channel_id=1, source_target_pairs={{2,0},{0,2},{6,4},{4,6},{10,8},{8,10},{14,12},{12,14},{18,16},{16,... | collective-permute-start | bytes 3145736 | tf_op jit(solution)/shard_map/ppermute | solution.py:38
  232.1 35.4 %collective-permute-start.39 = (bf16[552,1024]{1,0:T(8,128)(2,1)}, bf16[552,1024]{1,0:T(8,128)(2,1)S(1)}, u32[]{:S(2)}, u32[]{:S(2)}) collective-permute-start(bf16[552,1024]{1,0:T(8,128)(2,1)} %fusion.55), channel_id=1, source_target_pairs={{0,1},{1,0},{2,3},{3,2},{4,5},{5,4},{6,7},{7,6},{8,9},{9,8},{10,11... | collective-permute-start | bytes 3391496 | tf_op jit(solution)/shard_map/ppermute | solution.py:80
  282.0 44.3 %collective-permute-start.64 = (bf16[4,2,64,1024]{3,2,0,1:T(8,128)(2,1)}, bf16[4,2,64,1024]{3,2,0,1:T(8,128)(2,1)}, u32[]{:S(2)}, u32[]{:S(2)}) collective-permute-start(bf16[4,2,64,1024]{3,2,0,1:T(8,128)(2,1)} %bitcast.390), channel_id=1, source_target_pairs={{0,4},{2,6},{4,0},{6,2},{8,12},{10,14},{12,8},{14,10},{16,20},{18,... | collective-permute-start | bytes 3145736 | tf_op jit(solution)/shard_map/ppermute | solution.py:42
  292.6 35.4 %collective-permute-start.74 = (bf16[4,2,64,1024]{3,2,0,1:T(8,128)(2,1)}, bf16[4,2,64,1024]{3,2,0,1:T(8,128)(2,1)}, u32[]{:S(2)}, u32[]{:S(2)}) collective-permute-start(bf16[4,2,64,1024]{3,2,0,1:T(8,128)(2,1)} %bitcast.388), channel_id=1, source_target_pairs={{0,2},{2,0},{4,6},{6,4},{8,10},{10,8},{12,14},{14,12},{16,18},{18,... | collective-permute-start | bytes 3145736 | tf_op jit(solution)/shard_map/ppermute | solution.py:42
  309.8 24.2 %collective-permute-start.59 = (bf16[4,2,64,1024]{3,2,0,1:T(8,128)(2,1)S(1)}, bf16[4,2,64,1024]{3,2,0,1:T(8,128)(2,1)S(1)}, u32[]{:S(2)}, u32[]{:S(2)}) collective-permute-start(bf16[4,2,64,1024]{3,2,0,1:T(8,128)(2,1)S(1)} %bitcast.433), channel_id=1, source_target_pairs={{0,4},{2,6},{4,0},{6,2},{8,12},{10,14},{12,8},{14,10},{16,20},{18,... | collective-permute-start | bytes 3145736 | tf_op jit(solution)/shard_map/ppermute | solution.py:42
  316.7 33.1 %collective-permute-start.38 = (bf16[552,1024]{1,0:T(8,128)(2,1)S(1)}, bf16[552,1024]{1,0:T(8,128)(2,1)S(1)}, u32[]{:S(2)}, u32[]{:S(2)}) collective-permute-start(bf16[552,1024]{1,0:T(8,128)(2,1)S(1)} %slice.428), channel_id=1, source_target_pairs={{0,1},{1,0},{2,3},{3,2},{4,5},{5,4},{6,7},{7,6},{8,9},{9,8},{10,11... | collective-permute-start | bytes 3391496 | tf_op jit(solution)/shard_map/ppermute | solution.py:80
  321.7 26.2 %collective-permute-start.69 = (bf16[4,2,64,1024]{3,2,0,1:T(8,128)(2,1)S(1)}, bf16[4,2,64,1024]{3,2,0,1:T(8,128)(2,1)S(1)}, u32[]{:S(2)}, u32[]{:S(2)}) collective-permute-start(bf16[4,2,64,1024]{3,2,0,1:T(8,128)(2,1)S(1)} %bitcast.434), channel_id=1, source_target_pairs={{0,2},{2,0},{4,6},{6,4},{8,10},{10,8},{12,14},{14,12},{16,18},{18,... | collective-permute-start | bytes 3145736 | tf_op jit(solution)/shard_map/ppermute | solution.py:42
  326.3 84.6 %collective-permute-start.40 = (bf16[1104,1024]{1,0:T(8,128)(2,1)S(1)}, bf16[1104,1024]{1,0:T(8,128)(2,1)S(1)}, u32[]{:S(2)}, u32[]{:S(2)}) collective-permute-start(bf16[1104,1024]{1,0:T(8,128)(2,1)S(1)} %fusion.25), channel_id=1, source_target_pairs={{0,1},{1,0},{2,3},{3,2},{4,5},{5,4},{6,7},{7,6},{8,9},{9,8},{10,11... | collective-permute-start | bytes 6782984 | tf_op jit(solution)/shard_map/ppermute | solution.py:80
  328.0 31.0 %collective-permute-start.65 = (bf16[4,64,1024]{2,1,0:T(8,128)(2,1)S(1)}, bf16[4,64,1024]{2,1,0:T(8,128)(2,1)S(1)}, u32[]{:S(2)}, u32[]{:S(2)}) collective-permute-start(bf16[4,64,1024]{2,1,0:T(8,128)(2,1)S(1)} %slice_bitcast_fusion.6), channel_id=1, source_target_pairs={{0,2},{2,0},{4,6},{6,4},{8,10},{10,8},{12,14},{14,12},{16,18},{18,... | collective-permute-start | bytes 1572872 | tf_op jit(solution)/shard_map/ppermute | solution.py:42
  334.0 26.8 %collective-permute-start.75 = (bf16[4,64,1024]{2,1,0:T(8,128)(2,1)S(1)}, bf16[4,64,1024]{2,1,0:T(8,128)(2,1)S(1)}, u32[]{:S(2)}, u32[]{:S(2)}) collective-permute-start(bf16[4,64,1024]{2,1,0:T(8,128)(2,1)S(1)} %slice_bitcast_fusion.2), channel_id=1, source_target_pairs={{0,4},{2,6},{4,0},{6,2},{8,12},{10,14},{12,8},{14,10},{16,20},{18,... | collective-permute-start | bytes 1572872 | tf_op jit(solution)/shard_map/ppermute | solution.py:42
  347.8 20.6 %collective-permute-start.60 = (bf16[4,64,1024]{2,1,0:T(8,128)(2,1)S(1)}, bf16[4,64,1024]{2,1,0:T(8,128)(2,1)S(1)}, u32[]{:S(2)}, u32[]{:S(2)}) collective-permute-start(bf16[4,64,1024]{2,1,0:T(8,128)(2,1)S(1)} %slice_bitcast_fusion.8), channel_id=1, source_target_pairs={{0,2},{2,0},{4,6},{6,4},{8,10},{10,8},{12,14},{14,12},{16,18},{18,... | collective-permute-start | bytes 1572872 | tf_op jit(solution)/shard_map/ppermute | solution.py:42
  349.8 22.1 %collective-permute-start.70 = (bf16[4,64,1024]{2,1,0:T(8,128)(2,1)S(1)}, bf16[4,64,1024]{2,1,0:T(8,128)(2,1)S(1)}, u32[]{:S(2)}, u32[]{:S(2)}) collective-permute-start(bf16[4,64,1024]{2,1,0:T(8,128)(2,1)S(1)} %slice_bitcast_fusion.4), channel_id=1, source_target_pairs={{0,4},{2,6},{4,0},{6,2},{8,12},{10,14},{12,8},{14,10},{16,20},{18,... | collective-permute-start | bytes 1572872 | tf_op jit(solution)/shard_map/ppermute | solution.py:42
  543.0 24.3 %collective-permute-start.54 = (bf16[4,2,64,1024]{3,2,1,0:T(8,128)(2,1)}, bf16[4,2,64,1024]{3,2,1,0:T(8,128)(2,1)}, u32[]{:S(2)}, u32[]{:S(2)}) collective-permute-start(bf16[4,2,64,1024]{3,2,1,0:T(8,128)(2,1)} %slice_bitcast_fusion), channel_id=1, source_target_pairs={{0,2},{2,0},{4,6},{6,4},{8,10},{10,8},{12,14},{14,12},{16,18},{18,... | collective-permute-start | bytes 3145736 | tf_op jit(solution)/shard_map/ppermute | solution.py:42
  551.6 26.4 %collective-permute-start.49 = (bf16[4,2,64,1024]{3,2,0,1:T(8,128)(2,1)}, bf16[4,2,64,1024]{3,2,0,1:T(8,128)(2,1)}, u32[]{:S(2)}, u32[]{:S(2)}) collective-permute-start(bf16[4,2,64,1024]{3,2,0,1:T(8,128)(2,1)} %bitcast.392), channel_id=1, source_target_pairs={{0,4},{2,6},{4,0},{6,2},{8,12},{10,14},{12,8},{14,10},{16,20},{18,... | collective-permute-start | bytes 3145736 | tf_op jit(solution)/shard_map/ppermute | solution.py:42
  569.8 43.3 %collective-permute-start.55 = (bf16[4,64,1024]{2,1,0:T(8,128)(2,1)}, bf16[4,64,1024]{2,1,0:T(8,128)(2,1)S(1)}, u32[]{:S(2)}, u32[]{:S(2)}) collective-permute-start(bf16[4,64,1024]{2,1,0:T(8,128)(2,1)} %slice_bitcast_fusion.10), channel_id=1, source_target_pairs={{0,4},{2,6},{4,0},{6,2},{8,12},{10,14},{12,8},{14,10},{16,20},{18,... | collective-permute-start | bytes 1572872 | tf_op jit(solution)/shard_map/ppermute | solution.py:42
  583.9 33.4 %collective-permute-start.50 = (bf16[4,64,1024]{2,1,0:T(8,128)(2,1)}, bf16[4,64,1024]{2,1,0:T(8,128)(2,1)S(1)}, u32[]{:S(2)}, u32[]{:S(2)}) collective-permute-start(bf16[4,64,1024]{2,1,0:T(8,128)(2,1)} %slice_bitcast_fusion.12), channel_id=1, source_target_pairs={{0,2},{2,0},{4,6},{6,4},{8,10},{10,8},{12,14},{14,12},{16,18},{18,... | collective-permute-start | bytes 1572872 | tf_op jit(solution)/shard_map/ppermute | solution.py:42
  (123 other events, 1546.6 us)

commit v2 on v1

v2 whole, which is shorter than its diff:
```python
import functools

import jax
import jax.numpy as jnp
import numpy as np
from jax import lax
from jax.experimental import pallas as pl
from jax.experimental.pallas import tpu as pltpu
from jax.sharding import PartitionSpec as P

HEAD_DIM = 64
SEQ_LEN = 1104
F32 = jnp.float32
BF16 = jnp.bfloat16
MIB = 2**20


def dp_factors(size):
    if size % 8 == 0:
        return (4, 2, size // 8)
    return (1, 1, size)


class DpGrid:
    def __init__(self, size, block):
        self.size = size
        self.block = block
        self.half = block // 2
        self.factors = dp_factors(size)
        self.routes = ((2, 1), (1, 2))

    def coords(self, index):
        _, second, third = self.factors
        return (index // (second * third), (index // third) % second, index % third)

    def index(self, coords):
        _, second, third = self.factors
        return (coords[0] * second + coords[1]) * third + coords[2]

    def ahead(self, index, axis, step):
        coords = list(self.coords(index))
        coords[axis] = (coords[axis] + step) % self.factors[axis]
        return self.index(coords)

    def fetch(self, value, axis, step):
        pairs = [(self.ahead(i, axis, step), i) for i in range(self.size)]
        return lax.ppermute(value, "dp", pairs)

    def push(self, value, axis, step):
        pairs = [(i, self.ahead(i, axis, step)) for i in range(self.size)]
        return lax.ppermute(value, "dp", pairs)

    def gather(self, shard):
        along = [shard] + [self.fetch(shard, 0, s) for s in range(1, self.factors[0])]
        pieces = []
        for part, (middle, last) in enumerate(self.routes):
            rows = slice(part * self.half, (part + 1) * self.half)
            value = jnp.concatenate([a[rows] for a in along], axis=0)
            steps = range(1, self.factors[middle])
            value = jnp.concatenate([value] + [self.fetch(value, middle, s) for s in steps], axis=0)
            pieces.append(value)
            pieces.extend(self.fetch(value, last, s) for s in range(1, self.factors[last]))
        return pieces

    def scatter(self, pieces):
        pieces = list(pieces)
        halves = []
        for middle, last in self.routes:
            mine, pieces = pieces[: self.factors[last]], pieces[self.factors[last] :]
            total = mine[0].astype(F32)
            for step in range(1, self.factors[last]):
                total = total + self.push(mine[step], last, step).astype(F32)
            value = total.astype(BF16)
            rows = self.factors[0] * self.half
            total = value[:rows].astype(F32)
            for step in range(1, self.factors[middle]):
                piece = value[step * rows : (step + 1) * rows]
                total = total + self.push(piece, middle, step).astype(F32)
            halves.append(total)

        def along(step):
            rows = slice(step * self.half, (step + 1) * self.half)
            return jnp.concatenate([h[rows] for h in halves], axis=0)

        total = along(0)
        for step in range(1, self.factors[0]):
            total = total + self.push(along(step).astype(BF16), 0, step).astype(F32)
        return total

    def piece_rows(self):
        full = self.size * self.half
        rows = []
        for _, last in self.routes:
            rows.extend([full // self.factors[last]] * self.factors[last])
        return rows

    def cut(self, value, axis=0):
        edges = np.cumsum(self.piece_rows())[:-1].tolist()
        return jnp.split(value, edges, axis=axis)

    def features(self):
        here = self.coords(lax.axis_index("dp"))
        indices = []
        for part, (middle, last) in enumerate(self.routes):
            shape = (self.factors[last], self.factors[middle], self.factors[0], self.half)
            steps = [None, None, None]
            steps[last], steps[middle], steps[0], sub = (
                jnp.asarray(g.reshape(-1), jnp.int32) for g in np.indices(shape)
            )
            coords = [(h + s) % f for h, s, f in zip(here, steps, self.factors)]
            indices.append(self.index(coords) * self.block + part * self.half + sub)
        return jnp.concatenate(indices)


class TensorPair:
    def __init__(self, size, slot_count, local_rows):
        self.size = size
        self.relative = size == 2 and slot_count == 1
        self.local_rows = local_rows

    def swap(self, value):
        return lax.ppermute(value, "tensor", [(0, 1), (1, 0)])

    def whole(self, value):
        if self.relative:
            return jnp.concatenate([value, self.swap(value)], axis=0)
        return lax.all_gather(value, "tensor", axis=0, tiled=True)

    def own(self, value):
        if self.relative:
            return value[: self.local_rows]
        start = lax.axis_index("tensor") * self.local_rows
        return lax.dynamic_slice_in_dim(value, start, self.local_rows, axis=0)

    def total(self, value):
        if self.relative:
            other = self.swap(value)
            other = jnp.concatenate([other[self.local_rows :], other[: self.local_rows]], axis=0)
            return value.astype(F32) + other.astype(F32)
        return lax.psum(value.astype(F32), "tensor")

    def own_total(self, value):
        if self.relative:
            kept = value[: self.local_rows].astype(F32)
            return kept + self.swap(value[self.local_rows :]).astype(F32)
        return lax.psum_scatter(value, "tensor", scatter_dimension=0, tiled=True).astype(F32)

    def small_total(self, value):
        if self.size == 2:
            return value + self.swap(value)
        return lax.psum(value, "tensor")


def normalize(values):
    row_mean = jnp.mean(values, axis=-1, keepdims=True)
    centered = values - row_mean
    variance = jnp.mean(centered * centered, axis=-1, keepdims=True)
    inverse = lax.rsqrt(variance + 1e-05)
    return centered * inverse, inverse


def norm_input_grad(grad, gain, normed, inverse):
    scaled = grad * gain
    first = jnp.mean(scaled, axis=-1, keepdims=True)
    second = jnp.mean(scaled * normed, axis=-1, keepdims=True)
    return inverse * (scaled - first - normed * second)


def dot_nn(left, right):
    return lax.dot_general(left, right, (((1,), (0,)), ((), ())), preferred_element_type=F32)


def dot_nt(left, right):
    return lax.dot_general(left, right, (((1,), (1,)), ((), ())), preferred_element_type=F32)


def dot_tn(left, right):
    return lax.dot_general(left, right, (((0,), (0,)), ((), ())), preferred_element_type=F32)


def gelu_and_slope(values):
    cdf = 0.5 + 0.5 * lax.erf(values * (0.5**0.5))
    density = jnp.exp(-0.5 * values * values) * 0.3989422804014327
    return values * cdf, cdf + values * density


def params(limit):
    return pltpu.CompilerParams(vmem_limit_bytes=limit * MIB)


def whole_spec(array):
    return pl.BlockSpec(array.shape, lambda *grid: (0,) * len(array.shape))


def stack_rows(refs):
    return jnp.concatenate([r[...] for r in refs], axis=0)


def head_lanes(seq, head):
    lane = lax.broadcasted_iota(jnp.int32, (seq, 2 * HEAD_DIM), 1)
    mine = (lane >= HEAD_DIM) if head else (lane < HEAD_DIM)
    return mine, lane == (0 if head else HEAD_DIM)


def head_operands(query_ref, key_ref, invalid, head):
    seq = query_ref.shape[0]
    mine, extra = head_lanes(seq, head)
    one, zero = jnp.asarray(1, BF16), jnp.asarray(0, BF16)
    scaled = query_ref[...] * jnp.asarray(HEAD_DIM**-0.5, BF16)
    query = jnp.where(mine, scaled, jnp.where(extra, one, zero))
    keys = jnp.where(mine, key_ref[...], jnp.where(extra, invalid, zero))
    return query, keys


def key_column(invalid_ref):
    seq = invalid_ref.shape[-1]
    return jnp.broadcast_to(invalid_ref[0], (2 * HEAD_DIM, seq)).T.astype(BF16)


def attend_kernel(query_ref, key_ref, value_ref, invalid_ref, mixed_ref, total_ref, turned_ref):
    seq = query_ref.shape[0]
    invalid = key_column(invalid_ref)
    values = value_ref[...].T
    for head in range(2):
        rows = slice(head * HEAD_DIM, (head + 1) * HEAD_DIM)
        query, keys = head_operands(query_ref, key_ref, invalid, head)
        with_ones = jnp.concatenate([values[rows], jnp.ones((16, seq), BF16)], axis=0)
        scores = dot_nt(keys, query)
        largest = jnp.max(scores, axis=0, keepdims=True)
        weights = jnp.exp(scores - largest)
        mixed = dot_nn(with_ones, weights.astype(BF16))
        weight_sum = mixed[HEAD_DIM : HEAD_DIM + 1]
        turned_ref[rows] = mixed[:HEAD_DIM] * (1.0 / weight_sum)
        total_ref[0, 0, head : head + 1] = largest + jnp.log(weight_sum)
    mixed_ref[...] = turned_ref[...].T.astype(BF16)


def attend_back_kernel(
    query_ref,
    key_ref,
    value_ref,
    invalid_ref,
    mixed_ref,
    total_ref,
    grad_ref,
    grad_query_ref,
    grad_key_ref,
    grad_value_ref,
    turned_ref,
    prob_ref,
    score_ref,
):
    seq = query_ref.shape[0]
    invalid = key_column(invalid_ref)
    keys_turned = key_ref[...].T
    product = mixed_ref[...].astype(F32).T * grad_ref[...].astype(F32).T
    for head in range(2):
        rows = slice(head * HEAD_DIM, (head + 1) * HEAD_DIM)
        mine, _ = head_lanes(seq, head)
        query, keys = head_operands(query_ref, key_ref, invalid, head)
        grad = jnp.where(mine, grad_ref[...], jnp.asarray(0, BF16))
        row_dot = jnp.sum(product[rows], axis=0, keepdims=True)
        for start in range(0, seq, 256):
            cut = slice(start, min(start + 256, seq))
            prob = jnp.exp(dot_nt(keys, query[cut]) - total_ref[0, 0, head : head + 1, cut])
            grad_prob = dot_nt(value_ref[...], grad[cut]) - row_dot[:, cut]
            grad_score = (prob * grad_prob).astype(BF16)
            prob_ref[:, cut] = prob.astype(BF16)
            score_ref[:, cut] = grad_score
            turned_ref[rows, cut] = dot_nn(keys_turned[rows], grad_score) * HEAD_DIM**-0.5
        grad_value = dot_nn(prob_ref[...], grad)
        grad_key = dot_nn(score_ref[...], jnp.where(mine, query, jnp.asarray(0, BF16)))
        if head == 0:
            first_value, first_key = grad_value, grad_key
    grad_value_ref[...] = (first_value + grad_value).astype(BF16)
    grad_key_ref[...] = (first_key + grad_key).astype(BF16)
    grad_query_ref[...] = turned_ref[...].T.astype(BF16)


def attend_specs(pairs):
    def columns(offset):
        return pl.BlockSpec((SEQ_LEN, 2 * HEAD_DIM), lambda s, p: (s, p + offset))

    invalid = pl.BlockSpec((1, 1, SEQ_LEN), lambda s, p: (s, 0, 0))
    total = pl.BlockSpec((1, 1, 2, SEQ_LEN), lambda s, p: (s, p, 0, 0))
    return columns, invalid, total


def attend(packed, invalid):
    slots, pairs = invalid.shape[0], packed.shape[1] // (6 * HEAD_DIM)
    columns, invalid_spec, total_spec = attend_specs(pairs)
    return pl.pallas_call(
        attend_kernel,
        grid=(slots, pairs),
        in_specs=[columns(0), columns(pairs), columns(2 * pairs), invalid_spec],
        out_specs=[columns(0), total_spec],
        out_shape=[
            jax.ShapeDtypeStruct((packed.shape[0], pairs * 2 * HEAD_DIM), BF16),
            jax.ShapeDtypeStruct((slots, pairs, 2, SEQ_LEN), F32),
        ],
        scratch_shapes=[pltpu.VMEM((2 * HEAD_DIM, SEQ_LEN), F32)],
        compiler_params=params(48),
        name="attend",
    )(packed, packed, packed, invalid)


def attend_back(packed, invalid, mixed, total, grad_mixed):
    slots, pairs = invalid.shape[0], packed.shape[1] // (6 * HEAD_DIM)
    columns, invalid_spec, total_spec = attend_specs(pairs)
    return pl.pallas_call(
        attend_back_kernel,
        grid=(slots, pairs),
        in_specs=[
            columns(0),
            columns(pairs),
            columns(2 * pairs),
            invalid_spec,
            columns(0),
            total_spec,
            columns(0),
        ],
        out_specs=[columns(0)] * 3,
        out_shape=[jax.ShapeDtypeStruct(mixed.shape, BF16)] * 3,
        scratch_shapes=[
            pltpu.VMEM((2 * HEAD_DIM, SEQ_LEN), F32),
            pltpu.VMEM((SEQ_LEN, SEQ_LEN), BF16),
            pltpu.VMEM((SEQ_LEN, SEQ_LEN), BF16),
        ],
        compiler_params=params(48),
        name="attend_back",
    )(packed, packed, packed, invalid, mixed, total, grad_mixed)


def times_pieces(rows, pieces, first, count, wide, fits):
    if not fits:
        weight = jnp.concatenate(pieces, axis=0)[:, first * wide : (first + count) * wide]
        return dot_nn(rows, weight).astype(BF16)

    def kernel(rows_ref, *refs):
        refs[-1][...] = dot_nn(rows_ref[...], stack_rows(refs[:-1])).astype(BF16)

    return pl.pallas_call(
        kernel,
        grid=(count,),
        in_specs=[whole_spec(rows)]
        + [pl.BlockSpec((p.shape[0], wide), lambda j: (0, first + j)) for p in pieces],
        out_specs=pl.BlockSpec((rows.shape[0], wide), lambda j: (0, j)),
        out_shape=jax.ShapeDtypeStruct((rows.shape[0], count * wide), BF16),
        compiler_params=params(40),
        name="times_pieces",
    )(rows, *pieces)


def times_pieces_turned(columns, pieces, first, wide, fits):
    count = len(columns)
    if not fits:
        weight = jnp.concatenate(pieces, axis=0)[:, first * wide : (first + count) * wide]
        return dot_nt(jnp.concatenate(columns, axis=1), weight).astype(BF16)
    rows = columns[0].shape[0]
    starts = np.cumsum([0] + [p.shape[0] for p in pieces]).tolist()

    def kernel(*refs):
        lefts, weights, out_ref = refs[:count], refs[count:-1], refs[-1]
        for i, start in enumerate(starts[:-1]):
            total = 0.0
            for k in range(count):
                total = total + dot_nt(lefts[k][...], weights[i * count + k][...])
            out_ref[:, start : starts[i + 1]] = total.astype(BF16)

    weight_specs, weights = [], []
    for piece in pieces:
        for k in range(count):
            weight_specs.append(
                pl.BlockSpec((piece.shape[0], wide), lambda i, k=k: (0, first + k))
            )
            weights.append(piece)
    return pl.pallas_call(
        kernel,
        grid=(1,),
        in_specs=[whole_spec(c) for c in columns] + weight_specs,
        out_specs=pl.BlockSpec((rows, starts[-1]), lambda i: (0, 0)),
        out_shape=jax.ShapeDtypeStruct((rows, starts[-1]), BF16),
        compiler_params=params(48),
        name="times_pieces_turned",
    )(*columns, *weights)


def weight_grads(lefts, rights, piece_rows, fits):
    starts = np.cumsum([0] + piece_rows).tolist()
    if not fits:
        full = [dot_tn(a, b).astype(BF16) for a, b in zip(lefts, rights)]
        full = jnp.concatenate(full, axis=1)
        return [full[s:e] for s, e in zip(starts, starts[1:])]
    count = len(rights)
    wide = rights[0].shape[1]
    names = []
    for left in lefts:
        if not any(left is other for other in names):
            names.append(left)
    which = [next(i for i, o in enumerate(names) if o is left) for left in lefts]

    def kernel(*refs):
        left_refs, right_refs = refs[: len(names)], refs[len(names) : len(names) + count]
        out_refs = refs[len(names) + count :]
        for i, (start, end) in enumerate(zip(starts, starts[1:])):
            turned = [r[:, start:end].T for r in left_refs]
            for k in range(count):
                grad = dot_nn(turned[which[k]], right_refs[k][...])
                out_refs[i][:, k * wide : (k + 1) * wide] = grad.astype(BF16)

    return pl.pallas_call(
        kernel,
        grid=(1,),
        in_specs=[whole_spec(a) for a in names + list(rights)],
        out_specs=[pl.BlockSpec((r, count * wide), lambda i: (0, 0)) for r in piece_rows],
        out_shape=[jax.ShapeDtypeStruct((r, count * wide), BF16) for r in piece_rows],
        compiler_params=params(56),
        name="weight_grads",
    )(*names, *rights)


def feed_kernel(count, tile, carried, *refs):
    normed_ref, grad_ref, shift_ref = refs[:3]
    weight_refs = refs[3 : 3 + count]
    refs = refs[3 + count :]
    before, refs = (refs[:2], refs[2:]) if carried else ((), refs)
    out_ref, grad_two_ref, shift_grad_ref = refs[:3]
    weight_grad_refs = refs[3 : 3 + count]
    normed_turned, grad_turned, out_sum, grad_sum = refs[3 + count :]
    step = pl.program_id(0)

    @pl.when(step == 0)
    def _():
        normed_turned[...] = normed_ref[...].T
        grad_turned[...] = grad_ref[...].T
        if carried:
            out_sum[...] = before[0][...].astype(F32)
            grad_sum[...] = before[1][...].astype(F32)
        else:
            out_sum[...] = jnp.zeros_like(out_sum)
            grad_sum[...] = jnp.zeros_like(grad_sum)

    first = jnp.concatenate([w[:, :tile] for w in weight_refs], axis=0)
    second = jnp.concatenate([w[:, tile:] for w in weight_refs], axis=0)
    hidden = dot_nn(normed_ref[...], first) + shift_ref[...]
    hidden_act, slope = gelu_and_slope(hidden)
    hidden_act = hidden_act.astype(BF16)
    grad_pre = (dot_nn(grad_ref[...], second) * slope).astype(BF16)
    out_sum[...] += dot_nt(hidden_act, second)
    grad_sum[...] += dot_nt(grad_pre, first)
    shift_grad_ref[...] = jnp.sum(grad_pre.astype(F32), axis=0, keepdims=True)
    start = 0
    for ref in weight_grad_refs:
        rows = slice(start, start + ref.shape[0])
        ref[:, :tile] = dot_nn(normed_turned[rows], grad_pre).astype(BF16)
        ref[:, tile:] = dot_nn(grad_turned[rows], hidden_act).astype(BF16)
        start += ref.shape[0]

    @pl.when(step == pl.num_programs(0) - 1)
    def _():
        out_ref[...] = out_sum[...].astype(BF16)
        grad_two_ref[...] = grad_sum[...].astype(BF16)


def feed_tile(normed, grad, shift, pieces, first, tile, before, fits):
    rows, width = normed.shape
    steps = shift.shape[1] // tile
    if not fits:
        weight = jnp.concatenate(pieces, axis=0)[:, first * 2 * tile :]
        weight = weight[:, : steps * 2 * tile].reshape(width, steps, 2, tile)
        first_w = weight[:, :, 0].reshape(width, steps * tile)
        second_w = weight[:, :, 1].reshape(width, steps * tile)
        hidden_act, slope = gelu_and_slope(dot_nn(normed, first_w) + shift)
        hidden_act = hidden_act.astype(BF16)
        grad_pre = (dot_nn(grad, second_w) * slope).astype(BF16)
        out, grad_two = dot_nt(hidden_act, second_w), dot_nt(grad_pre, first_w)
        if before:
            out, grad_two = out + before[0].astype(F32), grad_two + before[1].astype(F32)
        grads = jnp.stack(
            [
                dot_tn(normed, grad_pre).astype(BF16).reshape(width, steps, tile),
                dot_tn(grad, hidden_act).astype(BF16).reshape(width, steps, tile),
            ],
            axis=2,
        ).reshape(width, steps * 2 * tile)
        edges = np.cumsum([p.shape[0] for p in pieces])[:-1].tolist()
        shift_grad = jnp.sum(grad_pre, axis=0, dtype=F32, keepdims=True)
        return [out.astype(BF16), grad_two.astype(BF16), shift_grad] + jnp.split(grads, edges, 0)

    def once(array):
        return pl.BlockSpec(
            array.shape, lambda j: (0,) * len(array.shape), pipeline_mode=pl.Buffered(1)
        )

    before = tuple(before)
    return pl.pallas_call(
        functools.partial(feed_kernel, len(pieces), tile, bool(before)),
        grid=(steps,),
        in_specs=[once(normed), once(grad), pl.BlockSpec((1, tile), lambda j: (0, j))]
        + [pl.BlockSpec((p.shape[0], 2 * tile), lambda j: (0, first + j)) for p in pieces]
        + [once(b) for b in before],
        out_specs=[
            pl.BlockSpec((rows, width), lambda j: (0, 0)),
            pl.BlockSpec((rows, width), lambda j: (0, 0)),
            pl.BlockSpec((1, tile), lambda j: (0, j)),
        ]
        + [pl.BlockSpec((p.shape[0], 2 * tile), lambda j: (0, j)) for p in pieces],
        out_shape=[
            jax.ShapeDtypeStruct((rows, width), BF16),
            jax.ShapeDtypeStruct((rows, width), BF16),
            jax.ShapeDtypeStruct((1, steps * tile), F32),
        ]
        + [jax.ShapeDtypeStruct((p.shape[0], steps * 2 * tile), BF16) for p in pieces],
        scratch_shapes=[
            pltpu.VMEM((width, rows), BF16),
            pltpu.VMEM((width, rows), BF16),
            pltpu.VMEM((rows, width), F32),
            pltpu.VMEM((rows, width), F32),
        ],
        compiler_params=params(60),
        name="feed_forward",
    )(normed, grad, shift, *pieces, *before)


def on_device(
    inputs,
    cotangent,
    slot_live,
    token_type,
    attn_norm_gain,
    attn_norm_bias,
    qkv_weight,
    proj_weight,
    proj_bias,
    mlp_norm_gain,
    mlp_norm_bias,
    fc1_weight,
    fc1_bias,
    fc2_weight,
    fc2_bias,
):
    dp_size = lax.axis_size("dp")
    tensor_size = lax.axis_size("tensor")
    local_rows, width = inputs.shape
    slot_count = slot_live.shape[0]
    whole_rows = local_rows * tensor_size
    block = fc1_weight.shape[0]
    width_here = qkv_weight.shape[2]
    hidden_here = fc1_weight.shape[1]
    hidden_block = fc1_bias.shape[0]
    hidden_cut = hidden_here // 2
    tile = width_here // 2
    cut_tiles = hidden_cut // tile
    fits = whole_rows <= 2048
    grid = DpGrid(dp_size, block)
    pair = TensorPair(tensor_size, slot_count, local_rows)

    qkv_shard = jnp.concatenate([qkv_weight[0], qkv_weight[1], qkv_weight[2]], axis=1)
    qkv_pieces = grid.gather(qkv_shard)
    bias_columns = -(-hidden_block // block)
    bias_pad = bias_columns * block - hidden_block
    smalls = jnp.stack(
        (attn_norm_gain, attn_norm_bias, proj_bias, mlp_norm_gain, mlp_norm_bias, fc2_bias)
    )
    bias_block = jnp.pad(fc1_bias, (0, bias_pad)).reshape(bias_columns, block)
    smalls = jnp.concatenate([smalls, bias_block], axis=0).T
    smalls = jnp.concatenate(grid.gather(smalls), axis=0).T

    fc2_turned = fc2_weight.T

    def feed_shard(part):
        columns = []
        for j in range(part * cut_tiles, (part + 1) * cut_tiles):
            columns.append(fc1_weight[:, j * tile : (j + 1) * tile])
            columns.append(fc2_turned[:, j * tile : (j + 1) * tile])
        return columns

    first_pieces = grid.gather(jnp.concatenate([proj_weight.T] + feed_shard(0), axis=1))
    second_pieces = grid.gather(jnp.concatenate(feed_shard(1), axis=1))

    features = grid.features()
    select = (jnp.arange(width, dtype=jnp.int32)[:, None] == features[None, :]).astype(BF16)
    rows_in = pair.whole(dot_nn(inputs, select).astype(BF16)).astype(F32)
    grad_out = pair.whole(dot_nn(cotangent, select).astype(BF16)).astype(F32)
    valid_whole = pair.whole((token_type != 3).astype(F32))
    invalid = jnp.where(valid_whole > 0, 0.0, -1e30).reshape(slot_count, 1, SEQ_LEN)
    live_col = jnp.repeat(slot_live.astype(F32), SEQ_LEN)[:, None]

    gain_one, shift_one, proj_shift, gain_two, shift_two, fc2_shift = (
        smalls[i : i + 1].astype(F32) for i in range(6)
    )
    fc1_shift = dot_nt(smalls[6:], select).reshape(bias_columns, dp_size, block)
    fc1_shift = fc1_shift.transpose(1, 0, 2).reshape(dp_size, bias_columns * block)
    fc1_shift = fc1_shift[:, :hidden_block].reshape(1, hidden_here)

    hat_one, inverse_one = normalize(rows_in)
    norm_one = (hat_one * gain_one + shift_one).astype(BF16)
    packed = times_pieces(norm_one, qkv_pieces, 0, 3, width_here, fits)
    mixed, total = attend(packed, invalid)

    attn_out = pair.total(times_pieces_turned([mixed], first_pieces, 0, width_here, fits))
    middle = rows_in + live_col * (attn_out + proj_shift)
    hat_two, inverse_two = normalize(middle)
    norm_two = (hat_two * gain_two + shift_two).astype(BF16)
    grad_mlp = (live_col * grad_out).astype(BF16)

    shifts = fc1_shift[:, :hidden_cut], fc1_shift[:, hidden_cut:]
    feed_a = feed_tile(norm_two, grad_mlp, shifts[0], first_pieces, 1, tile, (), fits)
    feed_b = feed_tile(norm_two, grad_mlp, shifts[1], second_pieces, 0, tile, feed_a[:2], fits)
    mlp_out, grad_two = feed_b[:2]
    grad_fc1_bias = jnp.concatenate([feed_a[2], feed_b[2]], axis=1)
    out_feed = jnp.concatenate([grid.scatter(feed_a[3:]), grid.scatter(feed_b[3:])], axis=1)
    out_feed = out_feed.reshape(block, 2 * cut_tiles, 2, tile)
    out_fc1 = out_feed[:, :, 0].reshape(block, hidden_here)
    out_fc2 = out_feed[:, :, 1].reshape(block, hidden_here).T

    result = pair.own(middle) + pair.own(live_col) * (pair.own_total(mlp_out) + fc2_shift)
    outputs = dot_nt(result.astype(BF16), select).astype(BF16)

    grad_two = pair.total(grad_two)
    grad_gain_two = jnp.sum(grad_two * hat_two, axis=0)
    grad_shift_two = jnp.sum(grad_two, axis=0)
    grad_middle = grad_out + norm_input_grad(grad_two, gain_two, hat_two, inverse_two)
    grad_branch = (live_col * grad_middle).astype(BF16)
    grad_proj_bias = jnp.sum(grad_branch, axis=0, dtype=F32)
    grad_fc2_bias = jnp.sum(grad_mlp, axis=0, dtype=F32)
    grad_mixed = times_pieces(grad_branch, first_pieces, 0, 1, width_here, fits)
    grad_packed = attend_back(packed, invalid, mixed, total, grad_mixed)

    out_attn = grid.scatter(
        weight_grads(
            (norm_one, norm_one, norm_one, grad_branch),
            tuple(grad_packed) + (mixed,),
            grid.piece_rows(),
            fits,
        )
    )
    out_attn = out_attn.reshape(block, 4, width_here)
    grad_one = pair.own_total(
        times_pieces_turned(list(grad_packed), qkv_pieces, 0, width_here, fits)
    )
    own_hat, own_inverse = pair.own(hat_one), pair.own(inverse_one)
    grad_gain_one = pair.small_total(jnp.sum(grad_one * own_hat, axis=0))
    grad_shift_one = pair.small_total(jnp.sum(grad_one, axis=0))
    grad_rows = pair.own(grad_middle) + norm_input_grad(grad_one, gain_one, own_hat, own_inverse)
    grad_inputs = dot_nt(grad_rows.astype(BF16), select).astype(BF16)

    vector_grads = jnp.stack(
        (
            grad_gain_one,
            grad_shift_one,
            grad_proj_bias,
            grad_gain_two,
            grad_shift_two,
            grad_fc2_bias,
        )
    ).astype(BF16)
    bias_grads = grad_fc1_bias.astype(BF16).reshape(dp_size, hidden_block)
    bias_grads = jnp.pad(bias_grads, ((0, 0), (0, bias_pad))).reshape(dp_size, bias_columns, block)
    bias_grads = dot_nn(bias_grads.transpose(1, 0, 2).reshape(bias_columns, width), select)
    small_grads = jnp.concatenate([vector_grads, bias_grads.astype(BF16)], axis=0)
    small_grads = grid.scatter(grid.cut(small_grads.T)).T
    return (
        outputs,
        grad_inputs,
        small_grads[0],
        small_grads[1],
        out_attn[:, :3].transpose(1, 0, 2),
        out_attn[:, 3].T,
        small_grads[2],
        small_grads[3],
        small_grads[4],
        out_fc1,
        small_grads[6:].reshape(-1)[:hidden_block],
        out_fc2,
        small_grads[5],
    )


def solution(mesh):
    in_specs = (
        P(("dp", "tensor"), None),
        P(("dp", "tensor"), None),
        P("dp"),
        P(("dp", "tensor")),
        P("dp"),
        P("dp"),
        P(None, "dp", "tensor"),
        P("tensor", "dp"),
        P("dp"),
        P("dp"),
        P("dp"),
        P("dp", "tensor"),
        P(("tensor", "dp")),
        P("tensor", "dp"),
        P("dp"),
    )
    out_specs = (
        P(("dp", "tensor"), None),
        P(("dp", "tensor"), None),
        P("dp"),
        P("dp"),
        P(None, "dp", "tensor"),
        P("tensor", "dp"),
        P("dp"),
        P("dp"),
        P("dp"),
        P("dp", "tensor"),
        P(("tensor", "dp")),
        P("tensor", "dp"),
        P("dp"),
    )
    return jax.shard_map(
        on_device, mesh=mesh, in_specs=in_specs, out_specs=out_specs, check_vma=False
    )
```

time: 645 us -> 481 us (0.75)
  the two profiles are of different devices: /device:TPU:0 before, /device:TPU:9 now
where the time goes in v2:
time: 481 us; the launch traced here: 473 us
  waiting for transfers between devices  143 us (30%)
  Pallas kernels  128 us (27%)
  starting transfers between devices  74.8 us (16%)
  local copies, waits for them, and re-layouts  65.3 us (14%)
  other arithmetic  44.2 us (9%)
  matrix products  14.9 us (3%)
    ppermute x28, waiting for transfers between devices, fetch(): return lax.ppermute(value, 'dp', pairs)  71.3 us
    ppermute x28, waiting for transfers between devices, push(): return lax.ppermute(value, 'dp', pairs)  70.8 us
    pallas_call x2, Pallas kernels, feed_tile(): pl.pallas_call(functools.partial(feed_kernel, len(pieces), tile, bool(bef...  51.5 us
    pallas_call x1, Pallas kernels, attend_back(): pl.pallas_call(attend_back_kernel, grid=(slots, pairs), in_specs=[columns...  34.1 us
    unnamed x138, local copies, waits for them, and re-layouts  27.4 us
    ppermute x28, starting transfers between devices, push(): return lax.ppermute(value, 'dp', pairs)  27 us
    ppermute x28, starting transfers between devices, fetch(): return lax.ppermute(value, 'dp', pairs)  24.7 us
    ppermute x9, starting transfers between devices, swap(): return lax.ppermute(value, 'tensor', [(0, 1), (1, 0)])  23 us
  transfers between devices with their start and end apart: 65, of which 25 were waited for; matrix products, arithmetic and copies ran while one was open for 20% of the time, Pallas kernels for 27%

profile of v2, /device:TPU:9, one launch (start us, length us, event | category | flops | bytes accessed | tf_op | source)
XLA Modules:
  0.0 473.2 jit_solution(8327484858274484436)
XLA Ops:
  27.2 9.9 %collective-permute-done.3 = bf16[64,8]{0,1:T(8,128)(2,1)S(1)} collective-permute-done((bf16[64,8]{0,1:T(8,128)(2,1)S(1)}, bf16[64,8]{0,1:T(8,128)(2,1)S(1)}, u32[]{:S(2)}, u32[]{:S(2)}) %collective-permute-start.3) | collective-permute-done | bytes 1056 | tf_op jit(solution)/shard_map/ppermute | solution.py:47
  50.5 8.9 %collective-permute-done.8 = bf16[64,1536]{1,0:T(8,128)(2,1)} collective-permute-done((bf16[64,1536]{1,0:T(8,128)(2,1)S(1)}, bf16[64,1536]{1,0:T(8,128)(2,1)}, u32[]{:S(2)}, u32[]{:S(2)}) %collective-permute-start.8) | collective-permute-done | bytes 196640 | tf_op jit(solution)/shard_map/ppermute | solution.py:47
  60.4 5.6 %collective-permute-done.9 = bf16[64,1536]{1,0:T(8,128)(2,1)} collective-permute-done((bf16[64,1536]{1,0:T(8,128)(2,1)S(1)}, bf16[64,1536]{1,0:T(8,128)(2,1)}, u32[]{:S(2)}, u32[]{:S(2)}) %collective-permute-start.9) | collective-permute-done | bytes 196640 | tf_op jit(solution)/shard_map/ppermute | solution.py:47
  66.0 6.0 %collective-permute-start.25 = (bf16[64,2048]{1,0:T(8,128)(2,1)}, bf16[64,2048]{1,0:T(8,128)(2,1)S(1)}, u32[]{:S(2)}, u32[]{:S(2)}) collective-permute-start(bf16[64,2048]{1,0:T(8,128)(2,1)} %get-tuple-element.144), channel_id=1, source_target_pairs={{8,0},{10,2},{12,4},{14,6},{16,8},{18,10},{20,12},{22,14},{24,16},... | collective-permute-start | bytes 786440 | tf_op jit(solution)/shard_map/ppermute | solution.py:47
  73.1 3.9 collective-permute-done.25
  77.0 7.7 %collective-permute-start = (bf16[552,1024]{1,0:T(8,128)(2,1)S(1)}, bf16[552,1024]{1,0:T(8,128)(2,1)S(1)}, u32[]{:S(2)}, u32[]{:S(2)}) collective-permute-start(bf16[552,1024]{1,0:T(8,128)(2,1)S(1)} %copy-done.30), channel_id=1, source_target_pairs={{0,1},{1,0},{2,3},{3,2},{4,5},{5,4},{6,7},{7,6},{8,9},{9,8},{10,11... | collective-permute-start | bytes 3391496 | tf_op jit(solution)/shard_map/ppermute | solution.py:122
  98.2 12.1 %collective-permute-done.21 = bf16[128,2560]{1,0:T(8,128)(2,1)S(1)} collective-permute-done((bf16[128,2560]{1,0:T(8,128)(2,1)S(1)}, bf16[128,2560]{1,0:T(8,128)(2,1)S(1)}, u32[]{:S(2)}, u32[]{:S(2)}) %collective-permute-start.21) | collective-permute-done | bytes 655392 | tf_op jit(solution)/shard_map/ppermute | solution.py:47
  117.9 10.3 %collective-permute-done.14.refs_3_.refs_12_.refs_13_.refs_14_ = bf16[256,1536]{1,0:T(8,128)(2,1)S(1)} collective-permute-done((bf16[256,1536]{1,0:T(8,128)(2,1)S(1)}, bf16[256,1536]{1,0:T(8,128)(2,1)S(1)}, u32[]{:S(2)}, u32[]{:S(2)}) %collective-permute-start.14) | collective-permute-done | bytes 786464 | tf_op jit(solution)/shard_map/ppermute | solution.py:47
  128.6 3.7 collective-permute-start.24
  132.3 4.5 times_pieces.2.query_ref.key_ref.value_ref
  139.1 16.2 %attend.1 = (bf16[1104,512]{1,0:T(8,128)(2,1)S(1)}, f32[1,4,2,1104]{3,2,1,0:T(2,128)S(1)}) custom-call(bf16[1104,1536]{1,0:T(8,128)(2,1)S(1)} %times_pieces.2.query_ref.key_ref.value_ref, bf16[1104,1536]{1,0:T(8,128)(2,1)S(1)} %times_pieces.2.query_ref.key_ref.value_ref, bf16[1104,1536]{1,0:T(8,128)(2,1)S(1)} %times_pieces.2.query_ref.key_ref.value_ref, ...), custom_call_target="tpu_custom_call" | custom-call | tf_op jit(solution)/shard_map/attend/pallas_call | solution.py:292
  157.3 3.8 times_pieces_turned.2
  167.8 10.8 %collective-permute-done.30 = bf16[128,2048]{1,0:T(8,128)(2,1)} collective-permute-done((bf16[128,2048]{1,0:T(8,128)(2,1)S(1)}, bf16[128,2048]{1,0:T(8,128)(2,1)}, u32[]{:S(2)}, u32[]{:S(2)}) %collective-permute-start.30) | collective-permute-done | bytes 524320 | tf_op jit(solution)/shard_map/ppermute | solution.py:47
  183.5 3.7 fusion.76
  196.0 25.3 %feed_forward.2 = (bf16[1104,1024]{1,0:T(8,128)(2,1)}, bf16[1104,1024]{1,0:T(8,128)(2,1)}, f32[1,1024]{1,0:T(1,128)}, bf16[256,2048]{1,0:T(8,128)(2,1)}, bf16[25...) custom-call(bf16[1104,1024]{1,0:T(8,128)(2,1)} %add_convert_fusion.refs_0_, ...), custom_call_target="tpu_custom_call" | custom-call | tf_op jit(solution)/shard_map/feed_forward/pallas_call | solution.py:496
  223.1 26.2 %feed_forward.3 = (bf16[1104,1024]{1,0:T(8,128)(2,1)}, bf16[1104,1024]{1,0:T(8,128)(2,1)}, f32[1,1024]{1,0:T(1,128)}, bf16[256,2048]{1,0:T(8,128)(2,1)}, bf16[25...) custom-call(bf16[1104,1024]{1,0:T(8,128)(2,1)} %add_convert_fusion.refs_0_, ...), custom_call_target="tpu_custom_call" | custom-call | tf_op jit(solution)/shard_map/feed_forward/pallas_call | solution.py:496
  261.5 11.0 %collective-permute-done.58 = bf16[256,2048]{1,0:T(8,128)(2,1)} collective-permute-done((bf16[256,2048]{1,0:T(8,128)(2,1)}, bf16[256,2048]{1,0:T(8,128)(2,1)}, u32[]{:S(2)}, u32[]{:S(2)}) %collective-permute-start.58) | collective-permute-done | bytes 1048608 | tf_op jit(solution)/shard_map/ppermute | solution.py:51
  280.6 3.6 collective-permute-done.52
  284.8 10.6 %collective-permute-done.59 = bf16[128,2048]{1,0:T(8,128)(2,1)S(1)} collective-permute-done((bf16[128,2048]{1,0:T(8,128)(2,1)S(1)}, bf16[128,2048]{1,0:T(8,128)(2,1)S(1)}, u32[]{:S(2)}, u32[]{:S(2)}) %collective-permute-start.59) | collective-permute-done | bytes 524320 | tf_op jit(solution)/shard_map/ppermute | solution.py:51
  298.2 4.0 collective-permute-start.64
  302.2 15.7 %collective-permute-done.57 = bf16[64,2048]{1,0:T(8,128)(2,1)S(1)} collective-permute-done((bf16[64,2048]{1,0:T(8,128)(2,1)S(1)}, bf16[64,2048]{1,0:T(8,128)(2,1)S(1)}, u32[]{:S(2)}, u32[]{:S(2)}) %collective-permute-start.57) | collective-permute-done | bytes 262176 | tf_op jit(solution)/shard_map/ppermute | solution.py:51
  320.3 4.0 multiply_reduce_fusion
  324.4 6.7 %fusion.78 = (bf16[1024]{0:T(1024)(128)(2,1)S(1)}, bf16[1104,1024]{1,0:T(8,128)(2,1)S(1)}, f32[1104,1024]{1,0:T(8,128)}) fusion(f32[]{:T(128)} %bitcast.1, f32[1104]{0:T(1024)S(1)} %get-tuple-element.217, f32[1104,1024]{1,0:T(8,128)S(1)} %bitcast.70, f32[1104]{0:T(1024)S(1)} %broadcast_multiply_fusion.2, f32[1104]{0:T(1024)S(1)} %get-tuple-element.218, ...), kind=kLoop, calls=%fused_computation.246 | loop fusion | flops 23739392 | bytes 18111748 | tf_op jit(solution)/shard_map/reduce_sum | solution.py:625
  332.5 34.1 %attend_back.1 = (bf16[1104,512]{1,0:T(8,128)(2,1)S(1)}, bf16[1104,512]{1,0:T(8,128)(2,1)S(1)}, bf16[1104,512]{1,0:T(8,128)(2,1)S(1)}) custom-call(bf16[1104,1536]{1,0:T(8,128)(2,1)} %copy-done.2, bf16[1104,1536]{1,0:T(8,128)(2,1)} %copy-done.2, bf16[1104,1536]{1,0:T(8,128)(2,1)} %copy-done.2, f32[1,1,1104]{2,1,0:T(1,128)S(1)} %compare_select_fusion.invalid_ref, ...), custom_call_target="tpu_custom_call" | custom-call | tf_op jit(solution)/shard_map/attend_back/pallas_call | solution.py:310
  370.7 10.2 %weight_grads.1 = (bf16[256,2048]{1,0:T(8,128)(2,1)}, bf16[256,2048]{1,0:T(8,128)(2,1)}, bf16[256,2048]{1,0:T(8,128)(2,1)}, bf16[256,2048]{1,0:T(8,128)(2,1)}) custom-call(bf16[1104,1024]{1,0:T(8,128)(2,1)} %copy-done.3, bf16[1104,1024]{1,0:T(8,128)(2,1)} %copy-done.4, bf16[1104,512]{1,0:T(8,128)(2,1)} %copy-done.24, bf16[1104,512]{1,0:T(8,128)(2,1)} %copy-done.26, ...), custom_call_target="tpu_custom_call" | custom-call | tf_op jit(solution)/shard_map/weight_grads/pallas_call | solution.py:411
  388.1 6.4 %times_pieces_turned.3 = bf16[1104,1024]{1,0:T(8,128)(2,1)} custom-call(bf16[1104,512]{1,0:T(8,128)(2,1)S(1)} %copy-done.25, bf16[1104,512]{1,0:T(8,128)(2,1)S(1)} %copy-done.27, bf16[1104,512]{1,0:T(8,128)(2,1)} %copy-done.28, bf16[256,1536]{1,0:T(8,128)(2,1)S(1)} %copy-done.7, bf16[256,1536]{1,0:T(8,128)(2,1)S(1)} %copy-done.7, ...), custom_call_target="tpu_custom_call" | custom-call | tf_op jit(solution)/shard_map/times_pieces_turned/pallas_call | solution.py:377
  396.0 4.8 %collective-permute-start.34 = (bf16[552,1024]{1,0:T(8,128)(2,1)S(1)}, bf16[552,1024]{1,0:T(8,128)(2,1)S(1)}, u32[]{:S(2)}, u32[]{:S(2)}) collective-permute-start(bf16[552,1024]{1,0:T(8,128)(2,1)S(1)} %slice.599), channel_id=1, source_target_pairs={{0,1},{1,0},{2,3},{3,2},{4,5},{5,4},{6,7},{7,6},{8,9},{9,8},{10,11... | collective-permute-start | bytes 3391496 | tf_op jit(solution)/shard_map/ppermute | solution.py:122
  417.9 7.2 %collective-permute-done.37 = bf16[256,8]{0,1:T(8,128)(2,1)S(1)} collective-permute-done((bf16[256,8]{0,1:T(8,128)(2,1)S(1)}, bf16[256,8]{0,1:T(8,128)(2,1)S(1)}, u32[]{:S(2)}, u32[]{:S(2)}) %collective-permute-start.37) | collective-permute-done | bytes 4128 | tf_op jit(solution)/shard_map/ppermute | solution.py:51
  425.2 5.8 %fusion.27 = bf16[552,1024]{1,0:T(8,128)(2,1)} fusion(s32[1024]{0:T(1024)S(1)} %pad_add_fusion, f32[1104,1024]{1,0:T(8,128)} %get-tuple-element.73, f32[1104,1024]{1,0:T(8,128)} %get-tuple-element.76, bf16[552,1024]{1,0:T(8,128)(2,1)} %copy-done.41, f32[552]{0:T(1024)S(1)} %broadcast_multiply_fusion.4, f32[552]{0:T(1024)S(1)} %broadcast_multiply_fusion.5, ...), kind=kOutput, calls=%fused_computation.55 | convolution fusion | flops 1164894208 | bytes 7933952 | tf_op jit(solution)/shard_map/dot_general | solution.py:174
  434.3 5.1 %collective-permute-start.42 = (bf16[64,8]{0,1:T(8,128)(2,1)S(1)}, bf16[64,8]{0,1:T(8,128)(2,1)S(1)}, u32[]{:S(2)}, u32[]{:S(2)}) collective-permute-start(bf16[64,8]{0,1:T(8,128)(2,1)S(1)} %pad_maximum_fusion.23), channel_id=1, source_target_pairs={{0,16},{2,18},{4,20},{6,22},{8,24},{10,26},{12,28},{14,30},{16,0},... | collective-permute-start | bytes 3080 | tf_op jit(solution)/shard_map/ppermute | solution.py:51
  448.7 15.9 %collective-permute-done.49 = bf16[64,2048]{1,0:T(8,128)(2,1)} collective-permute-done((bf16[64,2048]{1,0:T(8,128)(2,1)}, bf16[64,2048]{1,0:T(8,128)(2,1)}, u32[]{:S(2)}, u32[]{:S(2)}) %collective-permute-start.49) | collective-permute-done | bytes 262176 | tf_op jit(solution)/shard_map/ppermute | solution.py:51
  464.5 5.3 %collective-permute-done.50 = bf16[64,2048]{1,0:T(8,128)(2,1)} collective-permute-done((bf16[64,2048]{1,0:T(8,128)(2,1)}, bf16[64,2048]{1,0:T(8,128)(2,1)}, u32[]{:S(2)}, u32[]{:S(2)}) %collective-permute-start.50) | collective-permute-done | bytes 262176 | tf_op jit(solution)/shard_map/ppermute | solution.py:51
  (400 shorter events, 161.2 us)
Async XLA Ops:
  13.5 72.0 %collective-permute-start.16 = (bf16[64,2560]{1,0:T(8,128)(2,1)}, bf16[64,2560]{1,0:T(8,128)(2,1)}, u32[]{:S(2)}, u32[]{:S(2)}) collective-permute-start(bf16[64,2560]{1,0:T(8,128)(2,1)} %get-tuple-element.145), channel_id=1, source_target_pairs={{8,0},{10,2},{12,4},{14,6},{16,8},{18,10},{20,12},{22,14},{24,16},... | collective-permute-start | bytes 983048 | tf_op jit(solution)/shard_map/ppermute | solution.py:47
  13.5 74.0 %collective-permute-start.17 = (bf16[64,2560]{1,0:T(8,128)(2,1)}, bf16[64,2560]{1,0:T(8,128)(2,1)}, u32[]{:S(2)}, u32[]{:S(2)}) collective-permute-start(bf16[64,2560]{1,0:T(8,128)(2,1)} %get-tuple-element.145), channel_id=1, source_target_pairs={{16,0},{18,2},{20,4},{22,6},{24,8},{26,10},{28,12},{30,14},{0,16},... | collective-permute-start | bytes 983048 | tf_op jit(solution)/shard_map/ppermute | solution.py:47
  17.5 19.6 %collective-permute-start.3 = (bf16[64,8]{0,1:T(8,128)(2,1)S(1)}, bf16[64,8]{0,1:T(8,128)(2,1)S(1)}, u32[]{:S(2)}, u32[]{:S(2)}) collective-permute-start(bf16[64,8]{0,1:T(8,128)(2,1)S(1)} %bitcast.96), channel_id=1, source_target_pairs={{24,0},{26,2},{28,4},{30,6},{0,8},{2,10},{4,12},{6,14},{8,16},{10,... | collective-permute-start | bytes 3080 | tf_op jit(solution)/shard_map/ppermute | solution.py:47
  44.4 45.1 %collective-permute-start.18 = (bf16[64,2560]{1,0:T(8,128)(2,1)}, bf16[64,2560]{1,0:T(8,128)(2,1)}, u32[]{:S(2)}, u32[]{:S(2)}) collective-permute-start(bf16[64,2560]{1,0:T(8,128)(2,1)} %get-tuple-element.145), channel_id=1, source_target_pairs={{24,0},{26,2},{28,4},{30,6},{0,8},{2,10},{4,12},{6,14},{8,16},{10,... | collective-permute-start | bytes 983048 | tf_op jit(solution)/shard_map/ppermute | solution.py:47
  72.9 90.3 %collective-permute-start.26 = (bf16[64,2048]{1,0:T(8,128)(2,1)}, bf16[64,2048]{1,0:T(8,128)(2,1)S(1)}, u32[]{:S(2)}, u32[]{:S(2)}) collective-permute-start(bf16[64,2048]{1,0:T(8,128)(2,1)} %get-tuple-element.144), channel_id=1, source_target_pairs={{16,0},{18,2},{20,4},{22,6},{24,8},{26,10},{28,12},{30,14},{0,16},... | collective-permute-start | bytes 786440 | tf_op jit(solution)/shard_map/ppermute | solution.py:47
  77.0 34.6 %collective-permute-start = (bf16[552,1024]{1,0:T(8,128)(2,1)S(1)}, bf16[552,1024]{1,0:T(8,128)(2,1)S(1)}, u32[]{:S(2)}, u32[]{:S(2)}) collective-permute-start(bf16[552,1024]{1,0:T(8,128)(2,1)S(1)} %copy-done.30), channel_id=1, source_target_pairs={{0,1},{1,0},{2,3},{3,2},{4,5},{5,4},{6,7},{7,6},{8,9},{9,8},{10,11... | collective-permute-start | bytes 3391496 | tf_op jit(solution)/shard_map/ppermute | solution.py:122
  97.9 30.2 %collective-permute-start.14 = (bf16[256,1536]{1,0:T(8,128)(2,1)S(1)}, bf16[256,1536]{1,0:T(8,128)(2,1)S(1)}, u32[]{:S(2)}, u32[]{:S(2)}) collective-permute-start(bf16[256,1536]{1,0:T(8,128)(2,1)S(1)} %constant_dynamic-update-slice_fusion.5.refs_2_.refs_9_.refs_10_.refs_11_), channel_id=1, source_target_pairs={{2,0},{0,2},{6,4},{4,6},{10,8},{8,10},{14,12},{12,14},{18,16},{16,... | collective-permute-start | bytes 2359304 | tf_op jit(solution)/shard_map/ppermute | solution.py:47
  111.3 44.9 %collective-permute-start.22 = (bf16[256,2560]{1,0:T(8,128)(2,1)S(1)}, bf16[256,2560]{1,0:T(8,128)(2,1)S(1)}, u32[]{:S(2)}, u32[]{:S(2)}) collective-permute-start(bf16[256,2560]{1,0:T(8,128)(2,1)S(1)} %constant_dynamic-update-slice_fusion.24.refs_3_.refs_5_.refs_2_), channel_id=1, source_target_pairs={{2,0},{0,2},{6,4},{4,6},{10,8},{8,10},{14,12},{12,14},{18,16},{16,... | collective-permute-start | bytes 3932168 | tf_op jit(solution)/shard_map/ppermute | solution.py:47
  111.6 45.0 %collective-permute-start.20 = (bf16[256,2560]{1,0:T(8,128)(2,1)S(1)}, bf16[256,2560]{1,0:T(8,128)(2,1)S(1)}, u32[]{:S(2)}, u32[]{:S(2)}) collective-permute-start(bf16[256,2560]{1,0:T(8,128)(2,1)S(1)} %constant_dynamic-update-slice_fusion.19.refs_1_.refs_3_.refs_0_), channel_id=1, source_target_pairs={{4,0},{6,2},{0,4},{2,6},{12,8},{14,10},{8,12},{10,14},{20,16},{22,... | collective-permute-start | bytes 3932168 | tf_op jit(solution)/shard_map/ppermute | solution.py:47
  128.2 35.9 %collective-permute-start.27 = (bf16[64,2048]{1,0:T(8,128)(2,1)}, bf16[64,2048]{1,0:T(8,128)(2,1)S(1)}, u32[]{:S(2)}, u32[]{:S(2)}) collective-permute-start(bf16[64,2048]{1,0:T(8,128)(2,1)} %get-tuple-element.144), channel_id=1, source_target_pairs={{24,0},{26,2},{28,4},{30,6},{0,8},{2,10},{4,12},{6,14},{8,16},{10,... | collective-permute-start | bytes 786440 | tf_op jit(solution)/shard_map/ppermute | solution.py:47
  128.6 54.9 %collective-permute-start.24 = (bf16[552,1024]{1,0:T(8,128)(2,1)}, bf16[552,1024]{1,0:T(8,128)(2,1)}, u32[]{:S(2)}, u32[]{:S(2)}) collective-permute-start(bf16[552,1024]{1,0:T(8,128)(2,1)} %fusion.28), channel_id=1, source_target_pairs={{0,1},{1,0},{2,3},{3,2},{4,5},{5,4},{6,7},{7,6},{8,9},{9,8},{10,11... | collective-permute-start | bytes 3391496 | tf_op jit(solution)/shard_map/ppermute | solution.py:122
  161.2 26.1 %collective-permute-start.23 = (bf16[1104,1024]{1,0:T(8,128)(2,1)}, bf16[1104,1024]{1,0:T(8,128)(2,1)}, u32[]{:S(2)}, u32[]{:S(2)}) collective-permute-start(bf16[1104,1024]{1,0:T(8,128)(2,1)} %times_pieces_turned.2), channel_id=1, source_target_pairs={{0,1},{1,0},{2,3},{3,2},{4,5},{5,4},{6,7},{7,6},{8,9},{9,8},{10,11... | collective-permute-start | bytes 6782984 | tf_op jit(solution)/shard_map/ppermute | solution.py:122
  180.5 42.7 %collective-permute-start.31 = (bf16[256,2048]{1,0:T(8,128)(2,1)}, bf16[256,2048]{1,0:T(8,128)(2,1)}, u32[]{:S(2)}, u32[]{:S(2)}) collective-permute-start(bf16[256,2048]{1,0:T(8,128)(2,1)} %constant_dynamic-update-slice_fusion.42.refs_5_), channel_id=1, source_target_pairs={{2,0},{0,2},{6,4},{4,6},{10,8},{8,10},{14,12},{12,14},{18,16},{16,... | collective-permute-start | bytes 3145736 | tf_op jit(solution)/shard_map/ppermute | solution.py:47
  182.6 40.5 %collective-permute-start.29 = (bf16[256,2048]{1,0:T(8,128)(2,1)}, bf16[256,2048]{1,0:T(8,128)(2,1)}, u32[]{:S(2)}, u32[]{:S(2)}) collective-permute-start(bf16[256,2048]{1,0:T(8,128)(2,1)} %constant_dynamic-update-slice_fusion.37.refs_3_), channel_id=1, source_target_pairs={{4,0},{6,2},{0,4},{2,6},{12,8},{14,10},{8,12},{10,14},{20,16},{22,... | collective-permute-start | bytes 3145736 | tf_op jit(solution)/shard_map/ppermute | solution.py:47
  221.3 34.9 %collective-permute-start.51 = (bf16[256,2048]{1,0:T(8,128)(2,1)}, bf16[256,2048]{1,0:T(8,128)(2,1)}, u32[]{:S(2)}, u32[]{:S(2)}) collective-permute-start(bf16[256,2048]{1,0:T(8,128)(2,1)} %get-tuple-element.52), channel_id=1, source_target_pairs={{0,4},{2,6},{4,0},{6,2},{8,12},{10,14},{12,8},{14,10},{16,20},{18,... | collective-permute-start | bytes 3145736 | tf_op jit(solution)/shard_map/ppermute | solution.py:51
  221.9 36.4 %collective-permute-start.53 = (bf16[256,2048]{1,0:T(8,128)(2,1)}, bf16[256,2048]{1,0:T(8,128)(2,1)}, u32[]{:S(2)}, u32[]{:S(2)}) collective-permute-start(bf16[256,2048]{1,0:T(8,128)(2,1)} %get-tuple-element.54), channel_id=1, source_target_pairs={{0,2},{2,0},{4,6},{6,4},{8,10},{10,8},{12,14},{14,12},{16,18},{18,... | collective-permute-start | bytes 3145736 | tf_op jit(solution)/shard_map/ppermute | solution.py:51
  249.4 23.1 %collective-permute-start.58 = (bf16[256,2048]{1,0:T(8,128)(2,1)}, bf16[256,2048]{1,0:T(8,128)(2,1)}, u32[]{:S(2)}, u32[]{:S(2)}) collective-permute-start(bf16[256,2048]{1,0:T(8,128)(2,1)} %get-tuple-element.56), channel_id=1, source_target_pairs={{0,4},{2,6},{4,0},{6,2},{8,12},{10,14},{12,8},{14,10},{16,20},{18,... | collective-permute-start | bytes 3145736 | tf_op jit(solution)/shard_map/ppermute | solution.py:51
  250.4 24.7 %collective-permute-start.60 = (bf16[256,2048]{1,0:T(8,128)(2,1)}, bf16[256,2048]{1,0:T(8,128)(2,1)}, u32[]{:S(2)}, u32[]{:S(2)}) collective-permute-start(bf16[256,2048]{1,0:T(8,128)(2,1)} %get-tuple-element.58), channel_id=1, source_target_pairs={{0,2},{2,0},{4,6},{6,4},{8,10},{10,8},{12,14},{14,12},{16,18},{18,... | collective-permute-start | bytes 3145736 | tf_op jit(solution)/shard_map/ppermute | solution.py:51
  250.6 67.4 %collective-permute-start.33 = (bf16[1104,1024]{1,0:T(8,128)(2,1)}, bf16[1104,1024]{1,0:T(8,128)(2,1)}, u32[]{:S(2)}, u32[]{:S(2)}) collective-permute-start(bf16[1104,1024]{1,0:T(8,128)(2,1)} %get-tuple-element.40), channel_id=1, source_target_pairs={{0,1},{1,0},{2,3},{3,2},{4,5},{5,4},{6,7},{7,6},{8,9},{9,8},{10,11... | collective-permute-start | bytes 6782984 | tf_op jit(solution)/shard_map/ppermute | solution.py:122
  256.2 21.1 %collective-permute-start.32 = (bf16[552,1024]{1,0:T(8,128)(2,1)S(1)}, bf16[552,1024]{1,0:T(8,128)(2,1)S(1)}, u32[]{:S(2)}, u32[]{:S(2)}) collective-permute-start(bf16[552,1024]{1,0:T(8,128)(2,1)S(1)} %slice.482), channel_id=1, source_target_pairs={{0,1},{1,0},{2,3},{3,2},{4,5},{5,4},{6,7},{7,6},{8,9},{9,8},{10,11... | collective-permute-start | bytes 3391496 | tf_op jit(solution)/shard_map/ppermute | solution.py:122
  258.3 25.9 %collective-permute-start.52 = (bf16[128,2048]{1,0:T(8,128)(2,1)S(1)}, bf16[128,2048]{1,0:T(8,128)(2,1)S(1)}, u32[]{:S(2)}, u32[]{:S(2)}) collective-permute-start(bf16[128,2048]{1,0:T(8,128)(2,1)S(1)} %slice.620), channel_id=1, source_target_pairs={{0,2},{2,0},{4,6},{6,4},{8,10},{10,8},{12,14},{14,12},{16,18},{18,... | collective-permute-start | bytes 1572872 | tf_op jit(solution)/shard_map/ppermute | solution.py:51
  275.1 20.3 %collective-permute-start.59 = (bf16[128,2048]{1,0:T(8,128)(2,1)S(1)}, bf16[128,2048]{1,0:T(8,128)(2,1)S(1)}, u32[]{:S(2)}, u32[]{:S(2)}) collective-permute-start(bf16[128,2048]{1,0:T(8,128)(2,1)S(1)} %slice.632), channel_id=1, source_target_pairs={{0,2},{2,0},{4,6},{6,4},{8,10},{10,8},{12,14},{14,12},{16,18},{18,... | collective-permute-start | bytes 1572872 | tf_op jit(solution)/shard_map/ppermute | solution.py:51
  295.5 22.4 %collective-permute-start.57 = (bf16[64,2048]{1,0:T(8,128)(2,1)S(1)}, bf16[64,2048]{1,0:T(8,128)(2,1)S(1)}, u32[]{:S(2)}, u32[]{:S(2)}) collective-permute-start(bf16[64,2048]{1,0:T(8,128)(2,1)S(1)} %pad_maximum_fusion.15), channel_id=1, source_target_pairs={{0,24},{2,26},{4,28},{6,30},{8,0},{10,2},{12,4},{14,6},{16,8},{18,... | collective-permute-start | bytes 786440 | tf_op jit(solution)/shard_map/ppermute | solution.py:51
  295.9 84.9 %collective-permute-start.62 = (bf16[64,2048]{1,0:T(8,128)(2,1)S(1)}, bf16[64,2048]{1,0:T(8,128)(2,1)S(1)}, u32[]{:S(2)}, u32[]{:S(2)}) collective-permute-start(bf16[64,2048]{1,0:T(8,128)(2,1)S(1)} %pad_maximum_fusion.16), channel_id=1, source_target_pairs={{0,8},{2,10},{4,12},{6,14},{8,16},{10,18},{12,20},{14,22},{16,24},... | collective-permute-start | bytes 786440 | tf_op jit(solution)/shard_map/ppermute | solution.py:51
  297.8 83.1 %collective-permute-start.63 = (bf16[64,2048]{1,0:T(8,128)(2,1)S(1)}, bf16[64,2048]{1,0:T(8,128)(2,1)S(1)}, u32[]{:S(2)}, u32[]{:S(2)}) collective-permute-start(bf16[64,2048]{1,0:T(8,128)(2,1)S(1)} %pad_maximum_fusion.17), channel_id=1, source_target_pairs={{0,16},{2,18},{4,20},{6,22},{8,24},{10,26},{12,28},{14,30},{16,0},... | collective-permute-start | bytes 786440 | tf_op jit(solution)/shard_map/ppermute | solution.py:51
  298.2 82.6 %collective-permute-start.64 = (bf16[64,2048]{1,0:T(8,128)(2,1)S(1)}, bf16[64,2048]{1,0:T(8,128)(2,1)S(1)}, u32[]{:S(2)}, u32[]{:S(2)}) collective-permute-start(bf16[64,2048]{1,0:T(8,128)(2,1)S(1)} %pad_maximum_fusion.18), channel_id=1, source_target_pairs={{0,24},{2,26},{4,28},{6,30},{8,0},{10,2},{12,4},{14,6},{16,8},{18,... | collective-permute-start | bytes 786440 | tf_op jit(solution)/shard_map/ppermute | solution.py:51
  380.8 24.7 %collective-permute-start.44 = (bf16[256,2048]{1,0:T(8,128)(2,1)}, bf16[256,2048]{1,0:T(8,128)(2,1)}, u32[]{:S(2)}, u32[]{:S(2)}) collective-permute-start(bf16[256,2048]{1,0:T(8,128)(2,1)} %get-tuple-element.48), channel_id=1, source_target_pairs={{0,4},{2,6},{4,0},{6,2},{8,12},{10,14},{12,8},{14,10},{16,20},{18,... | collective-permute-start | bytes 3145736 | tf_op jit(solution)/shard_map/ppermute | solution.py:51
  381.0 28.4 %collective-permute-start.46 = (bf16[256,2048]{1,0:T(8,128)(2,1)}, bf16[256,2048]{1,0:T(8,128)(2,1)}, u32[]{:S(2)}, u32[]{:S(2)}) collective-permute-start(bf16[256,2048]{1,0:T(8,128)(2,1)} %get-tuple-element.50), channel_id=1, source_target_pairs={{0,2},{2,0},{4,6},{6,4},{8,10},{10,8},{12,14},{14,12},{16,18},{18,... | collective-permute-start | bytes 3145736 | tf_op jit(solution)/shard_map/ppermute | solution.py:51
  408.2 31.3 %collective-permute-start.45 = (bf16[128,2048]{1,0:T(8,128)(2,1)}, bf16[128,2048]{1,0:T(8,128)(2,1)}, u32[]{:S(2)}, u32[]{:S(2)}) collective-permute-start(bf16[128,2048]{1,0:T(8,128)(2,1)} %slice.606), channel_id=1, source_target_pairs={{0,2},{2,0},{4,6},{6,4},{8,10},{10,8},{12,14},{14,12},{16,18},{18,... | collective-permute-start | bytes 1572872 | tf_op jit(solution)/shard_map/ppermute | solution.py:51
  411.9 28.8 %collective-permute-start.47 = (bf16[128,2048]{1,0:T(8,128)(2,1)}, bf16[128,2048]{1,0:T(8,128)(2,1)}, u32[]{:S(2)}, u32[]{:S(2)}) collective-permute-start(bf16[128,2048]{1,0:T(8,128)(2,1)} %slice.609), channel_id=1, source_target_pairs={{0,4},{2,6},{4,0},{6,2},{8,12},{10,14},{12,8},{14,10},{16,20},{18,... | collective-permute-start | bytes 1572872 | tf_op jit(solution)/shard_map/ppermute | solution.py:51
  444.8 19.7 %collective-permute-start.49 = (bf16[64,2048]{1,0:T(8,128)(2,1)}, bf16[64,2048]{1,0:T(8,128)(2,1)}, u32[]{:S(2)}, u32[]{:S(2)}) collective-permute-start(bf16[64,2048]{1,0:T(8,128)(2,1)} %pad_maximum_fusion.11), channel_id=1, source_target_pairs={{0,16},{2,18},{4,20},{6,22},{8,24},{10,26},{12,28},{14,30},{16,0},... | collective-permute-start | bytes 786440 | tf_op jit(solution)/shard_map/ppermute | solution.py:51
  447.3 22.5 %collective-permute-start.50 = (bf16[64,2048]{1,0:T(8,128)(2,1)}, bf16[64,2048]{1,0:T(8,128)(2,1)}, u32[]{:S(2)}, u32[]{:S(2)}) collective-permute-start(bf16[64,2048]{1,0:T(8,128)(2,1)} %pad_maximum_fusion.12), channel_id=1, source_target_pairs={{0,24},{2,26},{4,28},{6,30},{8,0},{10,2},{12,4},{14,6},{16,8},{18,... | collective-permute-start | bytes 786440 | tf_op jit(solution)/shard_map/ppermute | solution.py:51
  (97 other events, 1170.6 us)

commit v3 on v2

v3 whole, which is shorter than its diff:
```python
import functools

import jax
import jax.numpy as jnp
import numpy as np
from jax import lax
from jax.experimental import pallas as pl
from jax.experimental.pallas import tpu as pltpu
from jax.sharding import PartitionSpec as P

HEAD_DIM = 64
SEQ_LEN = 1104
F32 = jnp.float32
BF16 = jnp.bfloat16
MIB = 2**20


def dp_factors(size):
    if size % 8 == 0:
        return (4, 2, size // 8)
    return (1, 1, size)


class DpGrid:
    def __init__(self, size, block):
        self.size = size
        self.block = block
        self.half = block // 2
        self.factors = dp_factors(size)
        self.routes = ((2, 1), (1, 2))

    def coords(self, index):
        _, second, third = self.factors
        return (index // (second * third), (index // third) % second, index % third)

    def index(self, coords):
        _, second, third = self.factors
        return (coords[0] * second + coords[1]) * third + coords[2]

    def ahead(self, index, axis, step):
        coords = list(self.coords(index))
        coords[axis] = (coords[axis] + step) % self.factors[axis]
        return self.index(coords)

    def fetch(self, value, axis, step):
        pairs = [(self.ahead(i, axis, step), i) for i in range(self.size)]
        return lax.ppermute(value, "dp", pairs)

    def push(self, value, axis, step):
        pairs = [(i, self.ahead(i, axis, step)) for i in range(self.size)]
        return lax.ppermute(value, "dp", pairs)

    def spread(self, shard):
        with jax.named_scope("gather_z"):
            return [shard] + [self.fetch(shard, 0, s) for s in range(1, self.factors[0])]

    def middle(self, along):
        halves = []
        for part, (middle, _) in enumerate(self.routes):
            rows = slice(part * self.half, (part + 1) * self.half)
            value = jnp.concatenate([a[..., rows, :] for a in along], axis=-2)
            steps = range(1, self.factors[middle])
            with jax.named_scope("gather_middle"):
                halves.append([value] + [self.fetch(value, middle, s) for s in steps])
        return halves

    def finish(self, halves):
        pieces = []
        for (_, last), parts in zip(self.routes, halves):
            value = jnp.concatenate(parts, axis=-2)
            pieces.append(value)
            with jax.named_scope("gather_last"):
                pieces.extend(self.fetch(value, last, s) for s in range(1, self.factors[last]))
        return pieces

    def gather(self, shard):
        return self.finish(self.middle(self.spread(shard)))

    def spread_middle(self, shard):
        parts = []
        for part, (middle, _) in enumerate(self.routes):
            value = shard[..., part * self.half : (part + 1) * self.half, :]
            with jax.named_scope("gather_middle"):
                steps = range(1, self.factors[middle])
                parts.append([value] + [self.fetch(value, middle, s) for s in steps])
        return parts

    def steps(self, value, axis, steps):
        with jax.named_scope("gather_step"):
            return [self.fetch(value, axis, s) for s in steps if s < self.factors[axis]]

    def halves_of(self, along, counts):
        halves, start = [], 0
        for count in counts:
            rows = slice(start, start + count * self.half)
            start += count * self.half
            value = jnp.stack([a[..., rows, :] for a in along], axis=-3)
            lead, wide = value.shape[:-3], value.shape[-1]
            value = value.reshape(lead + (self.factors[0], count, self.half, wide))
            value = jnp.swapaxes(value, -4, -3)
            halves.append([value.reshape(lead + (-1, wide))])
        return halves

    def reduce_last(self, pieces):
        pieces, halves = list(pieces), []
        for _, last in self.routes:
            mine, pieces = pieces[: self.factors[last]], pieces[self.factors[last] :]
            with jax.named_scope("reduce_last"):
                sent = [self.push(mine[s], last, s) for s in range(1, self.factors[last])]
            halves.append([mine[0]] + sent)
        return halves

    def reduce_middle(self, halves):
        rows, out = self.factors[0] * self.half, []
        for (middle, _), parts in zip(self.routes, halves):
            cut = [
                sum(p[..., s * rows : (s + 1) * rows, :].astype(F32) for p in parts).astype(BF16)
                for s in range(self.factors[middle])
            ]
            with jax.named_scope("reduce_middle"):
                sent = [self.push(cut[s], middle, s) for s in range(1, self.factors[middle])]
            out.append([cut[0]] + sent)
        return out

    def reduce_first(self, halves):
        def along(step):
            rows = slice(step * self.half, (step + 1) * self.half)
            totals = [sum(p[..., rows, :].astype(F32) for p in parts) for parts in halves]
            return jnp.concatenate(totals, axis=-2)

        sent = [along(s).astype(BF16) for s in range(1, self.factors[0])]
        with jax.named_scope("reduce_z"):
            sent = [self.push(p, 0, s) for s, p in enumerate(sent, 1)]
        return [along(0)] + sent

    def reduce_end(self, parts):
        return sum(p.astype(F32) for p in parts)

    def scatter(self, pieces):
        return self.reduce_end(self.reduce_first(self.reduce_middle(self.reduce_last(pieces))))

    def gather_small(self, value, axes):
        for axis in axes:
            with jax.named_scope("gather_small"):
                parts = [value] + [self.fetch(value, axis, s) for s in range(1, self.factors[axis])]
            value = jnp.concatenate(parts, axis=0)
        return value

    def small_in_order(self, value):
        zeroth, second, third = self.factors
        value = value.reshape((zeroth, third, second, value.shape[1], 2, self.half))
        first_half = value[..., 0, :].transpose(3, 2, 1, 0, 4)
        second_half = value[..., 1, :].transpose(3, 1, 2, 0, 4)
        count = value.shape[3]
        return jnp.concatenate(
            [first_half.reshape(count, -1), second_half.reshape(count, -1)], axis=1
        )

    def blocks_of(self, value):
        count, full = value.shape
        second, third = self.factors[1], self.factors[2]
        first_half = value[:, : full // 2].reshape(count, second, third, self.factors[0], self.half)
        second_half = value[:, full // 2 :].reshape(count, third, second, self.factors[0], self.half)
        return jnp.concatenate(
            [first_half.transpose(2, 1, 3, 0, 4), second_half.transpose(1, 2, 3, 0, 4)], axis=-1
        )

    def reduce_small(self, value, axis):
        value = value.astype(BF16)
        total = value[0].astype(F32)
        with jax.named_scope("reduce_small"):
            for step in range(1, self.factors[axis]):
                total = total + self.push(value[step], axis, step).astype(F32)
        return total

    def piece_rows(self):
        full = self.size * self.half
        rows = []
        for _, last in self.routes:
            rows.extend([full // self.factors[last]] * self.factors[last])
        return rows

    def cut(self, value, axis=0):
        edges = np.cumsum(self.piece_rows())[:-1].tolist()
        return jnp.split(value, edges, axis=axis)

    def places(self):
        return (self.features()[:: self.half] // self.half).astype(jnp.int32)

    def features(self):
        here = self.coords(lax.axis_index("dp"))
        indices = []
        for part, (middle, last) in enumerate(self.routes):
            shape = (self.factors[last], self.factors[middle], self.factors[0], self.half)
            steps = [None, None, None]
            steps[last], steps[middle], steps[0], sub = (
                jnp.asarray(g.reshape(-1), jnp.int32) for g in np.indices(shape)
            )
            coords = [(h + s) % f for h, s, f in zip(here, steps, self.factors)]
            indices.append(self.index(coords) * self.block + part * self.half + sub)
        return jnp.concatenate(indices)


class TensorPair:
    def __init__(self, size, slot_count, local_rows):
        self.size = size
        self.relative = size == 2 and slot_count == 1
        self.local_rows = local_rows

    def swap(self, value):
        return lax.ppermute(value, "tensor", [(0, 1), (1, 0)])

    def parts(self, value):
        if self.relative:
            return [value, self.swap(value)]
        return [lax.all_gather(value, "tensor", axis=0, tiled=True)]

    def whole(self, value):
        return jnp.concatenate(self.parts(value), axis=0)

    def own(self, value):
        if self.relative:
            return value[: self.local_rows]
        start = lax.axis_index("tensor") * self.local_rows
        return lax.dynamic_slice_in_dim(value, start, self.local_rows, axis=0)

    def both(self, value):
        if self.relative:
            return value, self.swap(value)
        return lax.psum(value.astype(F32), "tensor"), jnp.zeros((1, value.shape[1]), F32)

    def own_total(self, value):
        if self.relative:
            kept = value[: self.local_rows].astype(F32)
            return kept + self.swap(value[self.local_rows :]).astype(F32)
        return lax.psum_scatter(value, "tensor", scatter_dimension=0, tiled=True).astype(F32)

    def own_both(self, value):
        if self.relative:
            return value[: self.local_rows], self.swap(value[self.local_rows :])
        total = lax.psum_scatter(value, "tensor", scatter_dimension=0, tiled=True)
        return total, jnp.zeros((1, value.shape[1]), F32)

    def small_total(self, value):
        if self.size == 2:
            return value + self.swap(value)
        return lax.psum(value, "tensor")


def join(*groups):
    flat, tree = jax.tree.flatten(groups)
    return jax.tree.unflatten(tree, lax.optimization_barrier(tuple(flat)))


def normalize(values):
    row_mean = jnp.mean(values, axis=-1, keepdims=True)
    centered = values - row_mean
    variance = jnp.mean(centered * centered, axis=-1, keepdims=True)
    inverse = lax.rsqrt(variance + 1e-05)
    return centered * inverse, inverse


def norm_input_grad(grad, gain, normed, inverse):
    scaled = grad * gain
    first = jnp.mean(scaled, axis=-1, keepdims=True)
    second = jnp.mean(scaled * normed, axis=-1, keepdims=True)
    return inverse * (scaled - first - normed * second)


def dot_nn(left, right):
    return lax.dot_general(left, right, (((1,), (0,)), ((), ())), preferred_element_type=F32)


def dot_nt(left, right):
    return lax.dot_general(left, right, (((1,), (1,)), ((), ())), preferred_element_type=F32)


def dot_tn(left, right):
    return lax.dot_general(left, right, (((0,), (0,)), ((), ())), preferred_element_type=F32)


def gelu_and_slope(values):
    cdf = 0.5 + 0.5 * lax.erf(values * (0.5**0.5))
    density = jnp.exp(-0.5 * values * values) * 0.3989422804014327
    return values * cdf, cdf + values * density


def params(limit):
    return pltpu.CompilerParams(vmem_limit_bytes=limit * MIB)


def cost(micros):
    return pl.CostEstimate(
        flops=int(micros * 1e9), transcendentals=0, bytes_accessed=int(micros * 1e6)
    )


def whole_spec(array):
    return pl.BlockSpec(array.shape, lambda *grid: (0,) * len(array.shape))


def stack_rows(refs):
    return jnp.concatenate([r[...] for r in refs], axis=0)


def head_lanes(seq, head):
    lane = lax.broadcasted_iota(jnp.int32, (seq, 2 * HEAD_DIM), 1)
    mine = (lane >= HEAD_DIM) if head else (lane < HEAD_DIM)
    return mine, lane == (0 if head else HEAD_DIM)


def head_operands(query_ref, key_ref, invalid, head):
    seq = query_ref.shape[0]
    mine, extra = head_lanes(seq, head)
    one, zero = jnp.asarray(1, BF16), jnp.asarray(0, BF16)
    scaled = query_ref[...] * jnp.asarray(HEAD_DIM**-0.5, BF16)
    query = jnp.where(mine, scaled, jnp.where(extra, one, zero))
    keys = jnp.where(mine, key_ref[...], jnp.where(extra, invalid, zero))
    return query, keys


def key_column(invalid_ref):
    seq = invalid_ref.shape[-1]
    return jnp.broadcast_to(invalid_ref[0], (2 * HEAD_DIM, seq)).T.astype(BF16)


def attend_kernel(query_ref, key_ref, value_ref, invalid_ref, mixed_ref, total_ref, turned_ref):
    seq = query_ref.shape[0]
    invalid = key_column(invalid_ref)
    values = value_ref[...].T
    for head in range(2):
        rows = slice(head * HEAD_DIM, (head + 1) * HEAD_DIM)
        query, keys = head_operands(query_ref, key_ref, invalid, head)
        with_ones = jnp.concatenate([values[rows], jnp.ones((16, seq), BF16)], axis=0)
        scores = dot_nt(keys, query)
        largest = jnp.max(scores, axis=0, keepdims=True)
        weights = jnp.exp(scores - largest)
        mixed = dot_nn(with_ones, weights.astype(BF16))
        weight_sum = mixed[HEAD_DIM : HEAD_DIM + 1]
        turned_ref[rows] = mixed[:HEAD_DIM] * (1.0 / weight_sum)
        total_ref[0, 0, head : head + 1] = largest + jnp.log(weight_sum)
    mixed_ref[...] = turned_ref[...].T.astype(BF16)


def attend_back_kernel(
    query_ref,
    key_ref,
    value_ref,
    invalid_ref,
    mixed_ref,
    total_ref,
    grad_ref,
    grad_query_ref,
    grad_key_ref,
    grad_value_ref,
    turned_ref,
    prob_ref,
    score_ref,
):
    seq = query_ref.shape[0]
    invalid = key_column(invalid_ref)
    keys_turned = key_ref[...].T
    product = mixed_ref[...].astype(F32).T * grad_ref[...].astype(F32).T
    for head in range(2):
        rows = slice(head * HEAD_DIM, (head + 1) * HEAD_DIM)
        mine, _ = head_lanes(seq, head)
        query, keys = head_operands(query_ref, key_ref, invalid, head)
        grad = jnp.where(mine, grad_ref[...], jnp.asarray(0, BF16))
        row_dot = jnp.sum(product[rows], axis=0, keepdims=True)
        for start in range(0, seq, 256):
            cut = slice(start, min(start + 256, seq))
            prob = jnp.exp(dot_nt(keys, query[cut]) - total_ref[0, 0, head : head + 1, cut])
            grad_prob = dot_nt(value_ref[...], grad[cut]) - row_dot[:, cut]
            grad_score = (prob * grad_prob).astype(BF16)
            prob_ref[:, cut] = prob.astype(BF16)
            score_ref[:, cut] = grad_score
            turned_ref[rows, cut] = dot_nn(keys_turned[rows], grad_score) * HEAD_DIM**-0.5
        grad_value = dot_nn(prob_ref[...], grad)
        grad_key = dot_nn(score_ref[...], jnp.where(mine, query, jnp.asarray(0, BF16)))
        if head == 0:
            first_value, first_key = grad_value, grad_key
    grad_value_ref[...] = (first_value + grad_value).astype(BF16)
    grad_key_ref[...] = (first_key + grad_key).astype(BF16)
    grad_query_ref[...] = turned_ref[...].T.astype(BF16)


def attend_specs():
    def columns(offset):
        return pl.BlockSpec((SEQ_LEN, 2 * HEAD_DIM), lambda s, p: (s, p + offset))

    invalid = pl.BlockSpec((1, 1, SEQ_LEN), lambda s, p: (s, 0, 0))
    total = pl.BlockSpec((1, 1, 2, SEQ_LEN), lambda s, p: (s, p, 0, 0))
    return columns, invalid, total


def attend(packed, invalid, first, count):
    slots, pairs = invalid.shape[0], packed.shape[1] // (6 * HEAD_DIM)
    columns, invalid_spec, total_spec = attend_specs()
    return pl.pallas_call(
        attend_kernel,
        grid=(slots, count),
        in_specs=[columns(first), columns(pairs + first), columns(2 * pairs + first), invalid_spec],
        out_specs=[columns(0), total_spec],
        out_shape=[
            jax.ShapeDtypeStruct((packed.shape[0], count * 2 * HEAD_DIM), BF16),
            jax.ShapeDtypeStruct((slots, count, 2, SEQ_LEN), F32),
        ],
        scratch_shapes=[pltpu.VMEM((2 * HEAD_DIM, SEQ_LEN), F32)],
        compiler_params=params(48),
        cost_estimate=cost(4 * slots * count),
        name="attend",
    )(packed, packed, packed, invalid)


def attend_back(packed, invalid, mixed, total, grad_mixed, first, count):
    slots, pairs = invalid.shape[0], packed.shape[1] // (6 * HEAD_DIM)
    columns, invalid_spec, _ = attend_specs()
    return pl.pallas_call(
        attend_back_kernel,
        grid=(slots, count),
        in_specs=[
            columns(first),
            columns(pairs + first),
            columns(2 * pairs + first),
            invalid_spec,
            columns(first),
            pl.BlockSpec((1, 1, 2, SEQ_LEN), lambda s, p: (s, p + first, 0, 0)),
            columns(first),
        ],
        out_specs=[columns(0)] * 3,
        out_shape=[jax.ShapeDtypeStruct((mixed.shape[0], count * 2 * HEAD_DIM), BF16)] * 3,
        scratch_shapes=[
            pltpu.VMEM((2 * HEAD_DIM, SEQ_LEN), F32),
            pltpu.VMEM((SEQ_LEN, SEQ_LEN), BF16),
            pltpu.VMEM((SEQ_LEN, SEQ_LEN), BF16),
        ],
        compiler_params=params(48),
        cost_estimate=cost(9 * slots * count),
        name="attend_back",
    )(packed, packed, packed, invalid, mixed, total, grad_mixed)


def joined(pieces, first, count):
    return jnp.concatenate(
        [jnp.concatenate([p[g] for p in pieces], axis=0) for g in range(first, first + count)],
        axis=1,
    )


def times_pieces(rows, pieces, first, count, fits):
    if not fits:
        return dot_nn(rows, joined(pieces, first, count)).astype(BF16)
    wide = pieces[0].shape[2]

    def kernel(rows_ref, *refs):
        weight = jnp.concatenate([r[0] for r in refs[:-1]], axis=0)
        refs[-1][...] = dot_nn(rows_ref[...], weight).astype(BF16)

    return pl.pallas_call(
        kernel,
        grid=(count,),
        in_specs=[whole_spec(rows)]
        + [pl.BlockSpec((1, p.shape[1], wide), lambda j: (first + j, 0, 0)) for p in pieces],
        out_specs=pl.BlockSpec((rows.shape[0], wide), lambda j: (0, j)),
        out_shape=jax.ShapeDtypeStruct((rows.shape[0], count * wide), BF16),
        compiler_params=params(40),
        cost_estimate=cost(2 * count),
        name="times_pieces",
    )(rows, *pieces)


def times_pieces_turned(columns, pieces, places, fits):
    count = len(columns)
    rows, wide = columns[0].shape
    if not fits:
        weight = [joined(pieces, g, 1)[:, c * wide : (c + 1) * wide] for g, c in places]
        total = dot_nt(jnp.concatenate(columns, axis=1), jnp.concatenate(weight, axis=1))
        return total.astype(BF16)
    starts = np.cumsum([0] + [p.shape[1] for p in pieces]).tolist()

    def kernel(*refs):
        lefts, weights, out_ref = refs[:count], refs[count:-1], refs[-1]
        for i, start in enumerate(starts[:-1]):
            total = 0.0
            for k in range(count):
                total = total + dot_nt(lefts[k][...], weights[i * count + k][0])
            out_ref[:, start : starts[i + 1]] = total.astype(BF16)

    def place_spec(piece, group, column):
        return pl.BlockSpec((1, piece.shape[1], wide), lambda i: (group, 0, column))

    return pl.pallas_call(
        kernel,
        grid=(1,),
        in_specs=[whole_spec(c) for c in columns] + [place_spec(p, *q) for p in pieces for q in places],
        out_specs=pl.BlockSpec((rows, starts[-1]), lambda i: (0, 0)),
        out_shape=jax.ShapeDtypeStruct((rows, starts[-1]), BF16),
        compiler_params=params(48),
        cost_estimate=cost(1 + count),
        name="times_pieces_turned",
    )(*columns, *[p for p in pieces for _ in places])


def weight_grads(lefts, rights, piece_rows, fits):
    starts = np.cumsum([0] + piece_rows).tolist()
    if not fits:
        full = jnp.stack([dot_tn(a, b).astype(BF16) for a, b in zip(lefts, rights)])
        return [full[:, s:e] for s, e in zip(starts, starts[1:])]
    count = len(rights)
    wide = rights[0].shape[1]
    names = []
    for left in lefts:
        if not any(left is other for other in names):
            names.append(left)
    which = [next(i for i, o in enumerate(names) if o is left) for left in lefts]

    def kernel(*refs):
        left_refs, right_refs = refs[: len(names)], refs[len(names) : len(names) + count]
        out_refs = refs[len(names) + count :]
        for i, (start, end) in enumerate(zip(starts, starts[1:])):
            turned = [r[:, start:end].T for r in left_refs]
            for k in range(count):
                out_refs[i][k] = dot_nn(turned[which[k]], right_refs[k][...]).astype(BF16)

    return pl.pallas_call(
        kernel,
        grid=(1,),
        in_specs=[whole_spec(a) for a in names + list(rights)],
        out_specs=[pl.BlockSpec((count, r, wide), lambda i: (0, 0, 0)) for r in piece_rows],
        out_shape=[jax.ShapeDtypeStruct((count, r, wide), BF16) for r in piece_rows],
        compiler_params=params(56),
        cost_estimate=cost(1 + 1.5 * count),
        name="weight_grads",
    )(*names, *rights)


def joined_rows(parts):
    return parts[0] if len(parts) == 1 else jnp.concatenate(parts, axis=0)


def first_norm(rows_in, gain, bias, fits):
    width = rows_in[0].shape[1]
    rows = sum(p.shape[0] for p in rows_in)

    def work(values, gain, bias):
        normed, _ = normalize(values.astype(F32))
        return (normed * gain + bias).astype(BF16)

    if not fits:
        return work(joined_rows(rows_in), gain, bias)

    def kernel(*refs):
        gain, bias, out_ref = refs[-3][...], refs[-2][...], refs[-1]
        start = 0
        for ref in refs[:-3]:
            out_ref[start : start + ref.shape[0]] = work(ref[...], gain, bias)
            start += ref.shape[0]

    return pl.pallas_call(
        kernel,
        out_shape=jax.ShapeDtypeStruct((rows, width), BF16),
        compiler_params=params(40),
        cost_estimate=cost(3),
        name="first_norm",
    )(*rows_in, gain, bias)


def second_norm(rows_in, live, mine, other, shift, gain, bias, fits):
    rows, width = mine.shape

    def work(rows_in, live, mine, other, shift, gain, bias):
        branch = mine.astype(F32) + other.astype(F32) + shift
        middle = rows_in.astype(F32) + live * branch
        normed, _ = normalize(middle)
        return middle, (normed * gain + bias).astype(BF16)

    if not fits:
        return work(joined_rows(rows_in), live, mine, other, shift, gain, bias)
    half = rows // 2

    def kernel(own_ref, next_ref, live_ref, mine_ref, other_ref, *refs):
        vectors = [r[...] for r in refs[:3]]
        for i, ref in enumerate((own_ref, next_ref)):
            cut, turned = slice(i * half, (i + 1) * half), slice((1 - i) * half, (2 - i) * half)
            refs[3][cut], refs[4][cut] = work(
                ref[...], live_ref[cut], mine_ref[cut], other_ref[turned], *vectors
            )

    return pl.pallas_call(
        kernel,
        out_shape=[
            jax.ShapeDtypeStruct((rows, width), F32),
            jax.ShapeDtypeStruct((rows, width), BF16),
        ],
        compiler_params=params(40),
        cost_estimate=cost(4),
        name="second_norm",
    )(*rows_in, live, mine, other, shift, gain, bias)


def norm_back(grad_out, live, mine, other, middle, gain, fits):
    rows, width = middle.shape

    def work(grad_out, live, mine, other, middle, gain):
        grad_out = grad_out.astype(F32)
        grad = mine.astype(F32) + other.astype(F32)
        normed, inverse = normalize(middle)
        grad_middle = grad_out + norm_input_grad(grad, gain, normed, inverse)
        grad_branch = (live * grad_middle).astype(BF16)
        sums = [grad * normed, grad, grad_branch.astype(F32), grad_out]
        sums = jnp.concatenate([jnp.sum(s, axis=0, keepdims=True) for s in sums], axis=0)
        return grad_middle, grad_branch, sums

    if not fits:
        return work(joined_rows(grad_out), live, mine, other, middle, gain)
    half = rows // 2

    def kernel(own_ref, next_ref, live_ref, mine_ref, other_ref, middle_ref, gain_ref, *refs):
        total = 0.0
        for i, ref in enumerate((own_ref, next_ref)):
            cut, turned = slice(i * half, (i + 1) * half), slice((1 - i) * half, (2 - i) * half)
            refs[0][cut], refs[1][cut], sums = work(
                ref[...],
                live_ref[cut],
                mine_ref[cut],
                other_ref[turned],
                middle_ref[cut],
                gain_ref[...],
            )
            total = total + sums
        refs[2][...] = total

    return pl.pallas_call(
        kernel,
        out_shape=[
            jax.ShapeDtypeStruct((rows, width), F32),
            jax.ShapeDtypeStruct((rows, width), BF16),
            jax.ShapeDtypeStruct((4, width), F32),
        ],
        compiler_params=params(48),
        cost_estimate=cost(7),
        name="norm_back",
    )(*grad_out, live, mine, other, middle, gain)


def first_norm_back(grad_middle, rest, mine, other, rows_in, gain, fits):
    rows, width = rows_in.shape

    def work(grad_middle, rest, mine, other, rows_in, gain):
        grad = mine.astype(F32) + other.astype(F32)
        normed, inverse = normalize(rows_in.astype(F32))
        grad_rows = grad_middle + rest.astype(F32) + norm_input_grad(grad, gain, normed, inverse)
        sums = [jnp.sum(s, axis=0, keepdims=True) for s in (grad * normed, grad)]
        return grad_rows.astype(BF16), jnp.concatenate(sums, axis=0)

    if not fits:
        return work(grad_middle, rest, mine, other, rows_in, gain)

    def kernel(*refs):
        refs[-2][...], refs[-1][...] = work(*[r[...] for r in refs[:-2]])

    own = pl.BlockSpec((rows, width), lambda i: (0, 0))
    return pl.pallas_call(
        kernel,
        grid=(1,),
        in_specs=[own] * 5 + [pl.BlockSpec((1, width), lambda i: (0, 0))],
        out_specs=[own, pl.BlockSpec((2, width), lambda i: (0, 0))],
        out_shape=[
            jax.ShapeDtypeStruct((rows, width), BF16),
            jax.ShapeDtypeStruct((2, width), F32),
        ],
        compiler_params=params(40),
        cost_estimate=cost(4),
        name="first_norm_back",
    )(grad_middle, rest, mine, other, rows_in, gain)


def feed_kernel(counts, carried, plain, scattered, places_ref, *refs):
    halves, pieces, grad_pieces = counts
    normed_ref, shift_ref, grad_refs = refs[0], refs[1], refs[2 : 2 + halves]
    refs = refs[2 + halves :]
    first_refs, second_refs, refs = refs[:pieces], refs[pieces : 2 * pieces], refs[2 * pieces :]
    before, refs = (refs[:2], refs[2:]) if carried else ((), refs)
    out_ref, grad_two_ref, shift_grad_ref = refs[:3]
    weight_grad_refs = refs[3 : 3 + grad_pieces]
    grad_ref, normed_turned, grad_turned, out_sum, grad_sum = refs[3 + grad_pieces :]
    step = pl.program_id(0)
    blocks = places_ref.shape[0]
    size = normed_ref.shape[1] // blocks

    def place(i):
        return pl.ds(pl.multiple_of(places_ref[i] * size, size), size)

    @pl.when(step == 0)
    def _():
        start = 0
        for ref in grad_refs:
            grad_ref[start : start + ref.shape[0]] = ref[...]
            start += ref.shape[0]
        if scattered:
            for i in range(blocks):
                rows = slice(i * size, (i + 1) * size)
                normed_turned[place(i)] = normed_ref[:, rows].T
                grad_turned[place(i)] = grad_ref[:, rows].T
        else:
            normed_turned[...] = normed_ref[...].T
            grad_turned[...] = grad_ref[...].T
        if carried:
            out_sum[...] = before[0][...].astype(F32)
            grad_sum[...] = before[1][...].astype(F32)
        else:
            out_sum[...] = jnp.zeros_like(out_sum)
            grad_sum[...] = jnp.zeros_like(grad_sum)

    if plain:
        first = jnp.concatenate([first_refs[0][place(i)] for i in range(blocks)], axis=0)
        second = jnp.concatenate([second_refs[0][place(i)] for i in range(blocks)], axis=0)
    else:
        first = jnp.concatenate([w[0] for w in first_refs], axis=0)
        second = jnp.concatenate([w[0] for w in second_refs], axis=0)
    hidden = dot_nn(normed_ref[...], first) + shift_ref[...]
    hidden_act, slope = gelu_and_slope(hidden)
    hidden_act = hidden_act.astype(BF16)
    grad_pre = (dot_nn(grad_ref[...], second) * slope).astype(BF16)
    out_sum[...] += dot_nt(hidden_act, second)
    grad_sum[...] += dot_nt(grad_pre, first)
    shift_grad_ref[...] = jnp.sum(grad_pre.astype(F32), axis=0, keepdims=True)
    if scattered:
        weight_grad_refs[0][...] = dot_nn(normed_turned[...], grad_pre).astype(BF16)
        weight_grad_refs[1][...] = dot_nn(grad_turned[...], hidden_act).astype(BF16)
    else:
        start = 0
        for ref in weight_grad_refs:
            rows = slice(start, start + ref.shape[2])
            ref[0, 0] = dot_nn(normed_turned[rows], grad_pre).astype(BF16)
            ref[1, 0] = dot_nn(grad_turned[rows], hidden_act).astype(BF16)
            start += ref.shape[2]

    @pl.when(step == pl.num_programs(0) - 1)
    def _():
        out_ref[...] = out_sum[...].astype(BF16)
        grad_two_ref[...] = grad_sum[...].astype(BF16)


def feed_forward(normed, grads, shift, weight, places, piece_rows, before, fits):
    rows, width = normed.shape
    plain, scattered = not isinstance(weight, list), piece_rows is None
    units = shift.shape[1]
    wide = units if plain else weight[0].shape[2]
    groups = units // wide
    if not fits:
        size = width // places.shape[0]
        order = (places[:, None] * size + jnp.arange(size)[None, :]).reshape(-1)
        if plain:
            both = jnp.take(weight, order, axis=0)
            first_w, second_w = both[:, :units], both[:, units:]
        else:
            first_w, second_w = joined(weight, 0, groups), joined(weight, groups, groups)
        grad = jnp.concatenate(grads, axis=0)
        hidden_act, slope = gelu_and_slope(dot_nn(normed, first_w) + shift)
        hidden_act = hidden_act.astype(BF16)
        grad_pre = (dot_nn(grad, second_w) * slope).astype(BF16)
        out, grad_two = dot_nt(hidden_act, second_w), dot_nt(grad_pre, first_w)
        if before:
            out, grad_two = out + before[0].astype(F32), grad_two + before[1].astype(F32)
        outs = [dot_tn(normed, grad_pre).astype(BF16), dot_tn(grad, hidden_act).astype(BF16)]
        if scattered:
            outs = [jnp.zeros_like(g).at[order].set(g) for g in outs]
        else:
            size = units // 2
            outs = jnp.stack([g[:, k * size : (k + 1) * size] for g in outs for k in range(2)])
            outs = jnp.split(outs, np.cumsum(piece_rows)[:-1].tolist(), 1)
        shift_grad = jnp.sum(grad_pre, axis=0, dtype=F32, keepdims=True)
        return [out.astype(BF16), grad_two.astype(BF16), shift_grad] + outs

    tile = min(256, units // 2)
    per = wide // tile
    pieces = [weight] if plain else weight

    def once(array):
        return pl.BlockSpec(
            array.shape, lambda j, p: (0,) * len(array.shape), pipeline_mode=pl.Buffered(1)
        )

    def weight_spec(piece, second):
        if plain:
            return pl.BlockSpec((width, tile), lambda j, p: (0, second * per + j))
        return pl.BlockSpec(
            (1, piece.shape[1], tile), lambda j, p: (second * groups + j // per, 0, j % per)
        )

    if scattered:
        grad_specs = [pl.BlockSpec((width, tile), lambda j, p: (0, j))] * 2
        grad_shapes = [jax.ShapeDtypeStruct((width, units), BF16)] * 2
    else:
        half = units // 2
        split = half // tile
        grad_specs = [
            pl.BlockSpec((2, 1, r, tile), lambda j, p: (0, j // split, 0, j % split))
            for r in piece_rows
        ]
        grad_shapes = [jax.ShapeDtypeStruct((2, 2, r, half), BF16) for r in piece_rows]
    before = tuple(before)
    outs = pl.pallas_call(
        functools.partial(
            feed_kernel,
            (len(grads), len(pieces), len(grad_shapes)),
            bool(before),
            plain,
            scattered,
        ),
        grid_spec=pltpu.PrefetchScalarGridSpec(
            num_scalar_prefetch=1,
            grid=(units // tile,),
            in_specs=[once(normed), pl.BlockSpec((1, tile), lambda j, p: (0, j))]
            + [once(g) for g in grads]
            + [weight_spec(p, 0) for p in pieces]
            + [weight_spec(p, 1) for p in pieces]
            + [once(b) for b in before],
            out_specs=[
                pl.BlockSpec((rows, width), lambda j, p: (0, 0)),
                pl.BlockSpec((rows, width), lambda j, p: (0, 0)),
                pl.BlockSpec((1, tile), lambda j, p: (0, j)),
            ]
            + grad_specs,
            scratch_shapes=[
                pltpu.VMEM((rows, width), BF16),
                pltpu.VMEM((width, rows), BF16),
                pltpu.VMEM((width, rows), BF16),
                pltpu.VMEM((rows, width), F32),
                pltpu.VMEM((rows, width), F32),
            ],
        ),
        out_shape=[
            jax.ShapeDtypeStruct((rows, width), BF16),
            jax.ShapeDtypeStruct((rows, width), BF16),
            jax.ShapeDtypeStruct((1, units), F32),
        ]
        + grad_shapes,
        compiler_params=params(60),
        cost_estimate=cost(6.3 * (units // tile)),
        name="feed_forward",
    )(places, normed, shift, *grads, *pieces, *pieces, *before)
    outs = list(outs)
    if not scattered:
        outs[3:] = [g.reshape((4,) + g.shape[2:]) for g in outs[3:]]
    return outs


def on_device(
    inputs,
    cotangent,
    slot_live,
    token_type,
    attn_norm_gain,
    attn_norm_bias,
    qkv_weight,
    proj_weight,
    proj_bias,
    mlp_norm_gain,
    mlp_norm_bias,
    fc1_weight,
    fc1_bias,
    fc2_weight,
    fc2_bias,
):
    dp_size = lax.axis_size("dp")
    tensor_size = lax.axis_size("tensor")
    local_rows, width = inputs.shape
    slot_count = slot_live.shape[0]
    whole_rows = local_rows * tensor_size
    block = fc1_weight.shape[0]
    width_here = qkv_weight.shape[2]
    hidden_here = fc1_weight.shape[1]
    hidden_block = fc1_bias.shape[0]
    hidden_cut = hidden_here // 2
    fits = whole_rows <= 2048
    grid = DpGrid(dp_size, block)
    pair = TensorPair(tensor_size, slot_count, local_rows)
    half_cut = hidden_cut // 2

    bias_columns = -(-hidden_block // block)
    bias_pad = bias_columns * block - hidden_block
    smalls = jnp.stack(
        (attn_norm_gain, attn_norm_bias, proj_bias, mlp_norm_gain, mlp_norm_bias, fc2_bias)
    )
    bias_block = jnp.pad(fc1_bias, (0, bias_pad)).reshape(bias_columns, block)
    smalls = jnp.concatenate([smalls, bias_block], axis=0)
    fc2_turned = fc2_weight.T
    cuts = slice(0, hidden_cut), slice(hidden_cut, hidden_here)
    groups = [
        w[:, start : start + half_cut]
        for w in (fc1_weight, fc2_turned)
        for start in (0, half_cut)
    ]
    first_shard = jnp.stack(groups)
    second_shard = jnp.stack(
        [
            w[:, start : start + half_cut]
            for w in (fc1_weight, fc2_turned)
            for start in (hidden_cut, hidden_cut + half_cut)
        ]
    )
    attn_shard = jnp.concatenate([qkv_weight, proj_weight.T[None]], axis=0)

    attn_along = grid.spread(attn_shard)
    smalls = grid.gather_small(smalls[None], (1, 2))
    second_parts = grid.spread_middle(second_shard)
    attn_along, smalls, second_parts, first_shard, inputs, cotangent = join(
        attn_along, smalls, second_parts, first_shard, inputs, cotangent
    )

    attn_halves = grid.middle(attn_along)
    first_along = [first_shard] + grid.steps(first_shard, 0, (1,))
    smalls = grid.gather_small(smalls, (0,))
    features, places = grid.features(), grid.places()
    select = (jnp.arange(width, dtype=jnp.int32)[:, None] == features[None, :]).astype(BF16)
    own_in = dot_nn(inputs, select).astype(BF16)
    rows_in = pair.parts(own_in)
    own_grad = dot_nn(cotangent, select)
    live_col = jnp.repeat(slot_live.astype(F32), SEQ_LEN)[:, None]
    own_live = pair.own(live_col)
    grad_mlp = pair.parts((own_live * own_grad).astype(BF16))
    rest_grad = ((1.0 - own_live) * own_grad).astype(BF16)
    valid_whole = pair.whole((token_type != 3).astype(F32))
    invalid = jnp.where(valid_whole > 0, 0.0, -1e30).reshape(slot_count, 1, SEQ_LEN)
    attn_halves, first_along = join(attn_halves, first_along)

    attn_pieces = grid.finish(attn_halves)
    first_along += grid.steps(first_along[0], 0, (2, 3))
    smalls = grid.small_in_order(smalls)
    gain_one, shift_one, proj_shift, gain_two, shift_two, fc2_shift = (
        smalls[i : i + 1].astype(F32) for i in range(6)
    )
    fc1_shift = dot_nt(smalls[6:], select).reshape(bias_columns, dp_size, block)
    fc1_shift = fc1_shift.transpose(1, 0, 2).reshape(dp_size, bias_columns * block)
    fc1_shift = fc1_shift[:, :hidden_block].reshape(1, hidden_here)
    norm_one = first_norm(rows_in, gain_one, shift_one, fits)
    attn_pieces, first_along, norm_one, second_parts, grad_mlp, invalid = join(
        attn_pieces, first_along, norm_one, second_parts, grad_mlp, invalid
    )

    first_halves = grid.middle(first_along)
    second_own = jnp.concatenate(second_parts[0] + second_parts[1], axis=-2)
    second_counts = [len(p) for p in second_parts]
    second_near = grid.steps(second_own, 0, (1, 3))
    packed = times_pieces(norm_one, attn_pieces, 0, 3, fits)
    pairs = width_here // (2 * HEAD_DIM)
    parts = 2 if pairs % 2 == 0 else 1
    share = pairs // parts
    mixed, total = attend(packed, invalid, 0, pairs)
    first_halves, second_near, second_own, mixed, total, packed, attn_pieces, norm_one = join(
        first_halves, second_near, second_own, mixed, total, packed, attn_pieces, norm_one
    )

    first_pieces = grid.finish(first_halves)
    second_far = grid.steps(second_own, 0, (2,))
    attn_out = times_pieces_turned([mixed], attn_pieces, [(3, 0)], fits)
    middle, norm_two = second_norm(
        rows_in, live_col, *pair.both(attn_out), proj_shift, gain_two, shift_two, fits
    )
    first_pieces, second_far, middle, norm_two = join(first_pieces, second_far, middle, norm_two)

    second_along = [second_own] + second_near[:1] + second_far + second_near[1:]
    second_pieces = grid.finish(grid.halves_of(second_along, second_counts))
    piece_rows = grid.piece_rows()
    shifts = [fc1_shift[:, :hidden_cut], fc1_shift[:, hidden_cut:]]
    feed_a = feed_forward(
        norm_two, grad_mlp, shifts[0], first_pieces, places, piece_rows, (), fits
    )
    second_pieces, feed_a, norm_two = join(second_pieces, feed_a, norm_two)

    last_a = grid.reduce_last(feed_a[3:])
    feed_b = feed_forward(
        norm_two, grad_mlp, shifts[1], second_pieces, places, piece_rows, feed_a[:2], fits
    )
    grad_fc1_bias = jnp.concatenate([feed_a[2], feed_b[2]], axis=1)
    last_a, feed_b = join(last_a, feed_b)
    mlp_out, grad_two = feed_b[:2]

    middle_a = grid.reduce_middle(last_a)
    grad_middle, grad_branch, sums = norm_back(
        grad_mlp, live_col, *pair.both(grad_two), middle, gain_two, fits
    )
    grad_mixed = times_pieces(grad_branch, attn_pieces, 3, 1, fits)
    middle_a, grad_mixed, pieces_b, grad_middle, grad_branch = join(
        middle_a, grad_mixed, feed_b[3:], grad_middle, grad_branch
    )

    def back(part):
        return attend_back(packed, invalid, mixed, total, grad_mixed, part * share, share)

    def grads(part, columns):
        lefts, rights = (norm_one,) * 3, tuple(columns)
        if part == 0:
            cut = width_here // parts
            lefts = lefts + (grad_branch,) * parts
            rights = rights + tuple(mixed[:, p * cut : (p + 1) * cut] for p in range(parts))
        return weight_grads(lefts, rights, piece_rows, fits)

    last_b = grid.reduce_last(pieces_b)
    first_a = grid.reduce_first(middle_a)
    columns = back(0)
    last_b, first_a, columns, grad_mixed = join(last_b, first_a, columns, grad_mixed)

    middle_b = grid.reduce_middle(last_b)
    pieces_c = grads(0, columns)
    middle_b, pieces_c, grad_mixed = join(middle_b, pieces_c, grad_mixed)

    last_c = grid.reduce_last(pieces_c)
    first_b = grid.reduce_first(middle_b)
    if parts == 2:
        more = back(1)
        last_c, first_b, more = join(last_c, first_b, more)
        columns = columns + more
    else:
        last_c, first_b = join(last_c, first_b)

    middle_c = grid.reduce_middle(last_c)
    places_c = [(j, p) for p in range(parts) for j in range(3)]
    if parts == 2:
        pieces_d = grads(1, more)
        pieces_d, columns = join(pieces_d, columns)
        last_d = grid.reduce_last(pieces_d)
    grad_one = times_pieces_turned(columns, attn_pieces, places_c, fits)
    middle_c, grad_one, mlp_out = join(middle_c, grad_one, mlp_out)

    first_c = grid.reduce_first(middle_c)
    grad_rows, sums_one = first_norm_back(
        pair.own(grad_middle), rest_grad, *pair.own_both(grad_one), own_in, gain_one, fits
    )
    sums_one = pair.small_total(sums_one)
    mlp_out = pair.own_total(mlp_out)
    first_a, first_b = grid.reduce_end(first_a), grid.reduce_end(first_b)
    if parts == 2:
        last_d, sums_one, grad_rows = join(last_d, sums_one, grad_rows)
        middle_d = grid.reduce_middle(last_d)
    bias_grads = grad_fc1_bias.astype(BF16).reshape(dp_size, hidden_block)
    bias_grads = jnp.pad(bias_grads, ((0, 0), (0, bias_pad))).reshape(dp_size, bias_columns, block)
    bias_grads = dot_nn(bias_grads.transpose(1, 0, 2).reshape(bias_columns, width), select)
    small_grads = jnp.concatenate([sums_one, sums, bias_grads], axis=0)
    small_grads = grid.blocks_of(small_grads)
    small_grads = grid.reduce_small(small_grads, 2)
    small_grads = grid.reduce_small(small_grads, 1)
    grad_inputs = dot_nt(grad_rows, select).astype(BF16)
    if parts == 2:
        first_c, middle_d, small_grads = join(first_c, middle_d, small_grads)
        first_d = grid.reduce_first(middle_d)
    else:
        first_c, small_grads = join(first_c, small_grads)
    small_grads = grid.reduce_small(small_grads, 0)
    result = pair.own(middle) + own_live * (mlp_out + fc2_shift)
    outputs = dot_nt(result.astype(BF16), select).astype(BF16)
    out_fc1 = jnp.concatenate([first_a[0], first_a[1], first_b[0], first_b[1]], axis=1)
    out_fc2 = jnp.concatenate([first_a[2], first_a[3], first_b[2], first_b[3]], axis=1)
    out_c = grid.reduce_end(first_c)
    out_qkv = out_c[:3]
    if parts == 2:
        out_qkv = jnp.concatenate([out_qkv, grid.reduce_end(first_d)], axis=2)
    out_proj = jnp.concatenate([out_c[3 + p] for p in range(parts)], axis=1)
    return (
        outputs,
        grad_inputs,
        small_grads[0],
        small_grads[1],
        out_qkv,
        out_proj.T,
        small_grads[4],
        small_grads[2],
        small_grads[3],
        out_fc1,
        small_grads[6:].reshape(-1)[:hidden_block],
        out_fc2.T,
        small_grads[5],
    )


def solution(mesh):
    in_specs = (
        P(("dp", "tensor"), None),
        P(("dp", "tensor"), None),
        P("dp"),
        P(("dp", "tensor")),
        P("dp"),
        P("dp"),
        P(None, "dp", "tensor"),
        P("tensor", "dp"),
        P("dp"),
        P("dp"),
        P("dp"),
        P("dp", "tensor"),
        P(("tensor", "dp")),
        P("tensor", "dp"),
        P("dp"),
    )
    out_specs = (
        P(("dp", "tensor"), None),
        P(("dp", "tensor"), None),
        P("dp"),
        P("dp"),
        P(None, "dp", "tensor"),
        P("tensor", "dp"),
        P("dp"),
        P("dp"),
        P("dp"),
        P("dp", "tensor"),
        P(("tensor", "dp")),
        P("tensor", "dp"),
        P("dp"),
    )
    return jax.shard_map(
        on_device, mesh=mesh, in_specs=in_specs, out_specs=out_specs, check_vma=False
    )
```

time: 481 us -> 362 us (0.75)
  the two profiles are of different devices: /device:TPU:9 before, /device:TPU:0 now
where the time goes in v3:
time: 362 us; the launch traced here: 356 us
  Pallas kernels  159 us (44%)
  starting transfers between devices  74.3 us (21%)
  waiting for transfers between devices  68 us (19%)
  local copies, waits for them, and re-layouts  21.1 us (6%)
  other arithmetic  18.3 us (5%)
  matrix products  11.9 us (3%)
    pallas_call x2, Pallas kernels, feed_forward(): pl.pallas_call(functools.partial(feed_kernel, (len(grads), len(pieces), l...  53.5 us
    ppermute x26, waiting for transfers between devices, fetch(): return lax.ppermute(value, 'dp', pairs)  49.3 us
    ppermute x33, starting transfers between devices, push(): return lax.ppermute(value, 'dp', pairs)  40.1 us
    pallas_call x2, Pallas kernels, attend_back(): pl.pallas_call(attend_back_kernel, grid=(slots, count), in_specs=[columns...  35.2 us
    ppermute x26, starting transfers between devices, fetch(): return lax.ppermute(value, 'dp', pairs)  33.4 us
    ppermute x33, waiting for transfers between devices, push(): return lax.ppermute(value, 'dp', pairs)  18.7 us
    pallas_call x1, Pallas kernels, attend(): pl.pallas_call(attend_kernel, grid=(slots, count), in_specs=[columns(firs...  16.2 us
    pallas_call x2, Pallas kernels, weight_grads(): pl.pallas_call(kernel, grid=(1,), in_specs=[whole_spec(a) for a in names...  12.8 us
  transfers between devices with their start and end apart: 67, of which 21 were waited for; matrix products, arithmetic and copies ran while one was open for 11% of the time, Pallas kernels for 42%

profile of v3, /device:TPU:0, one launch (start us, length us, event | category | flops | bytes accessed | tf_op | source)
XLA Modules:
  0.0 356.0 jit_solution(11861359640787397267)
XLA Ops:
  1.8 5.1 %collective-permute-start = (bf16[4,64,512]{2,1,0:T(8,128)(2,1)S(1)}, bf16[4,64,512]{2,1,0:T(8,128)(2,1)S(1)}, u32[]{:S(2)}, u32[]{:S(2)}) collective-permute-start(bf16[4,64,512]{2,1,0:T(8,128)(2,1)S(1)} %pad_maximum_fusion.11), channel_id=1, source_target_pairs={{8,0},{10,2},{12,4},{14,6},{16,8},{18,10},{20,12},{22,14},{24,16},... | collective-permute-start | bytes 786440 | tf_op jit(solution)/shard_map/gather_z/ppermute | solution.py:47
  18.3 2.7 collective-permute-done.5
  21.7 7.5 %collective-permute-done.1 = bf16[4,64,512]{2,1,0:T(8,128)(2,1)S(1)} collective-permute-done((bf16[4,64,512]{2,1,0:T(8,128)(2,1)S(1)}, bf16[4,64,512]{2,1,0:T(8,128)(2,1)S(1)}, u32[]{:S(2)}, u32[]{:S(2)}) %collective-permute-start.1) | collective-permute-done | bytes 262176 | tf_op jit(solution)/shard_map/gather_z/ppermute | solution.py:47
  29.2 2.8 collective-permute-start.16
  39.4 2.9 multiply_convert_fusion
  53.4 3.3 first_norm.1.rows_ref.refs_0_
  56.7 14.8 %collective-permute-done.12 = bf16[4,64,512]{2,1,0:T(8,128)(2,1)S(1)} collective-permute-done((bf16[4,64,512]{2,1,0:T(8,128)(2,1)S(1)}, bf16[4,64,512]{2,1,0:T(8,128)(2,1)S(1)}, u32[]{:S(2)}, u32[]{:S(2)}) %collective-permute-start.12) | collective-permute-done | bytes 262176 | tf_op jit(solution)/shard_map/gather_step/ppermute | solution.py:47
  77.3 5.2 %times_pieces.2.query_ref.key_ref.value_ref = bf16[1104,1536]{1,0:T(8,128)(2,1)S(1)} custom-call(bf16[1104,1024]{1,0:T(8,128)(2,1)S(1)} %first_norm.1.rows_ref.refs_0_, bf16[4,256,512]{2,1,0:T(8,128)(2,1)S(1)} %constant_dynamic-update-slice_fusion.refs_0_.refs_1_.refs_6_.refs_7_.refs_8_.refs_9_.refs_10_.refs_11_, ...), custom_call_target="tpu_custom_call" | custom-call | flops 6000000000 | bytes 6000000 | tf_op jit(solution)/shard_map/times_pieces/pallas_call | solution.py:459
  82.5 16.2 %attend.1 = (bf16[1104,512]{1,0:T(8,128)(2,1)S(1)}, f32[1,4,2,1104]{3,2,1,0:T(2,128)S(1)}) custom-call(bf16[1104,1536]{1,0:T(8,128)(2,1)S(1)} %times_pieces.2.query_ref.key_ref.value_ref, bf16[1104,1536]{1,0:T(8,128)(2,1)S(1)} %times_pieces.2.query_ref.key_ref.value_ref, bf16[1104,1536]{1,0:T(8,128)(2,1)S(1)} %times_pieces.2.query_ref.key_ref.value_ref, ...), custom_call_target="tpu_custom_call" | custom-call | flops 16000000000 | bytes 16000000 | tf_op jit(solution)/shard_map/attend/pallas_call | solution.py:399
  98.8 3.9 %times_pieces_turned.2.mine_ref = bf16[1104,1024]{1,0:T(8,128)(2,1)} custom-call(bf16[1104,512]{1,0:T(8,128)(2,1)S(1)} %get-tuple-element.241.refs_0_.mixed_ref, bf16[4,256,512]{2,1,0:T(8,128)(2,1)S(1)} %constant_dynamic-update-slice_fusion.refs_0_.refs_1_.refs_6_.refs_7_.refs_8_.refs_9_.refs_10_.refs_11_, ...), custom_call_target="tpu_custom_call" | custom-call | flops 2000000000 | bytes 2000000 | tf_op jit(solution)/shard_map/times_pieces_turned/pallas_call | solution.py:492
  112.0 4.9 %second_norm.1 = (f32[1104,1024]{1,0:T(8,128)S(1)}, bf16[1104,1024]{1,0:T(8,128)(2,1)S(1)}) custom-call(bf16[552,1024]{1,0:T(8,128)(2,1)} %fusion.12.refs_0_.own_ref.refs_4_, bf16[552,1024]{1,0:T(8,128)(2,1)} %collective-permute-done.14.refs_1_.next_ref, f32[1104,1]{1,0:T(8,128)S(1)} %broadcast_in_dim_reshape.3.live_ref, bf16[1104,1024]{1,0:T(8,128)(2,1)S(1)} %copy-done.7, ...), custom_call_target="tpu_custom_call" | custom-call | flops 4000000000 | bytes 4000000 | tf_op jit(solution)/shard_map/second_norm/pallas_call | solution.py:589
  118.4 18.1 %collective-permute-done.26 = bf16[4,128,512]{2,1,0:T(8,128)(2,1)S(1)} collective-permute-done((bf16[4,128,512]{2,1,0:T(8,128)(2,1)S(1)}, bf16[4,128,512]{2,1,0:T(8,128)(2,1)S(1)}, u32[]{:S(2)}, u32[]{:S(2)}) %collective-permute-start.26) | collective-permute-done | bytes 524320 | tf_op jit(solution)/shard_map/gather_step/ppermute | solution.py:47
  139.9 26.0 %feed_forward.2 = (bf16[1104,1024]{1,0:T(8,128)(2,1)}, bf16[1104,1024]{1,0:T(8,128)(2,1)}, f32[1,1024]{1,0:T(1,128)}, bf16[2,2,256,512]{3,2,1,0:T(8,128)(2,1)}, ...) custom-call(s32[32]{0:T(128)} %and_select_fusion.places_ref, ...), custom_call_target="tpu_custom_call" | custom-call | flops 25200001024 | bytes 25200000 | tf_op jit(solution)/shard_map/feed_forward/pallas_call | solution.py:804
  169.0 27.5 %feed_forward.3 = (bf16[1104,1024]{1,0:T(8,128)(2,1)}, bf16[1104,1024]{1,0:T(8,128)(2,1)}, f32[1,1024]{1,0:T(1,128)}, bf16[2,2,256,512]{3,2,1,0:T(8,128)(2,1)}, ...) custom-call(s32[32]{0:T(128)} %and_select_fusion.places_ref, ...), custom_call_target="tpu_custom_call" | custom-call | flops 25200001024 | bytes 25200000 | tf_op jit(solution)/shard_map/feed_forward/pallas_call | solution.py:804
  204.5 11.1 %norm_back.1 = (f32[1104,1024]{1,0:T(8,128)}, bf16[1104,1024]{1,0:T(8,128)(2,1)S(1)}, f32[4,1024]{1,0:T(4,128)S(1)}) custom-call(bf16[552,1024]{1,0:T(8,128)(2,1)} %get-tuple-element.253.refs_2_.own_ref, bf16[552,1024]{1,0:T(8,128)(2,1)} %collective-permute-done.18.refs_3_.next_ref, f32[1104,1]{1,0:T(8,128)S(1)} %copy-done.9, ...), custom_call_target="tpu_custom_call" | custom-call | flops 7000000000 | bytes 7000000 | tf_op jit(solution)/shard_map/norm_back/pallas_call | solution.py:633
  215.7 2.5 times_pieces.3.grad_ref
  218.5 2.7 collective-permute-start.39
  224.4 17.5 %attend_back.2 = (bf16[1104,256]{1,0:T(8,128)(2,1)S(1)}, bf16[1104,256]{1,0:T(8,128)(2,1)S(1)}, bf16[1104,256]{1,0:T(8,128)(2,1)S(1)}) custom-call(bf16[1104,1536]{1,0:T(8,128)(2,1)} %copy-done.28, bf16[1104,1536]{1,0:T(8,128)(2,1)} %copy-done.28, bf16[1104,1536]{1,0:T(8,128)(2,1)} %copy-done.28, f32[1,1,1104]{2,1,0:T(1,128)S(1)} %compare_select_fusion.invalid_ref, ...), custom_call_target="tpu_custom_call" | custom-call | flops 17999998976 | bytes 18000000 | tf_op jit(solution)/shard_map/attend_back/pallas_call | solution.py:418
  243.5 3.0 collective-permute-done.35
  252.4 7.5 %weight_grads.2 = (bf16[5,256,256]{2,1,0:T(8,128)(2,1)}, bf16[5,256,256]{2,1,0:T(8,128)(2,1)}, bf16[5,256,256]{2,1,0:T(8,128)(2,1)}, bf16[5,256,256]{2,1,0:T(8,128)(2,1)}) custom-call(bf16[1104,1024]{1,0:T(8,128)(2,1)} %copy-done.26, bf16[1104,1024]{1,0:T(8,128)(2,1)} %copy-done.6, bf16[1104,256]{1,0:T(8,128)(2,1)} %copy-done.10, ...), custom_call_target="tpu_custom_call" | custom-call | flops 8499999744 | bytes 8500000 | tf_op jit(solution)/shard_map/weight_grads/pallas_call | solution.py:525
  263.7 3.3 collective-permute-start.46
  270.8 17.7 %attend_back.3 = (bf16[1104,256]{1,0:T(8,128)(2,1)S(1)}, bf16[1104,256]{1,0:T(8,128)(2,1)S(1)}, bf16[1104,256]{1,0:T(8,128)(2,1)S(1)}) custom-call(bf16[1104,1536]{1,0:T(8,128)(2,1)} %copy-done.28, bf16[1104,1536]{1,0:T(8,128)(2,1)} %copy-done.28, bf16[1104,1536]{1,0:T(8,128)(2,1)} %copy-done.28, f32[1,1,1104]{2,1,0:T(1,128)S(1)} %compare_select_fusion.invalid_ref, ...), custom_call_target="tpu_custom_call" | custom-call | flops 17999998976 | bytes 18000000 | tf_op jit(solution)/shard_map/attend_back/pallas_call | solution.py:418
  291.1 5.3 %weight_grads.3 = (bf16[3,256,256]{2,1,0:T(8,128)(2,1)}, bf16[3,256,256]{2,1,0:T(8,128)(2,1)}, bf16[3,256,256]{2,1,0:T(8,128)(2,1)}, bf16[3,256,256]{2,1,0:T(8,128)(2,1)}) custom-call(bf16[1104,1024]{1,0:T(8,128)(2,1)} %copy-done.26, bf16[1104,256]{1,0:T(8,128)(2,1)} %copy-done.16, bf16[1104,256]{1,0:T(8,128)(2,1)} %copy-done.18, bf16[1104,256]{1,0:T(8,128)(2,1)} %copy-done.20), custom_call_target="tpu_custom_call" | custom-call | flops 5500000256 | bytes 5500000 | tf_op jit(solution)/shard_map/weight_grads/pallas_call | solution.py:525
  301.4 7.0 %times_pieces_turned.3 = bf16[1104,1024]{1,0:T(8,128)(2,1)} custom-call(bf16[1104,256]{1,0:T(8,128)(2,1)S(1)} %copy-done.11, bf16[1104,256]{1,0:T(8,128)(2,1)S(1)} %copy-done.13, bf16[1104,256]{1,0:T(8,128)(2,1)S(1)} %copy-done.15, bf16[1104,256]{1,0:T(8,128)(2,1)S(1)} %copy-done.17, bf16[1104,256]{1,0:T(8,128)(2,1)S(1)} %copy-done.19, ...), custom_call_target="tpu_custom_call" | custom-call | flops 7000000000 | bytes 7000000 | tf_op jit(solution)/shard_map/times_pieces_turned/pallas_call | solution.py:492
  313.0 3.2 collective-permute-start.56
  317.6 3.3 first_norm_back.1
  321.1 2.7 fusion.13
  331.7 2.6 collective-permute-done.60
  335.6 4.6 %collective-permute-done.57 = bf16[3,128,256]{2,1,0:T(8,128)(2,1)S(1)} collective-permute-done((bf16[3,128,256]{2,1,0:T(8,128)(2,1)S(1)}, bf16[3,128,256]{2,1,0:T(8,128)(2,1)S(1)}, u32[]{:S(2)}, u32[]{:S(2)}) %collective-permute-start.57) | collective-permute-done | bytes 196640 | tf_op jit(solution)/shard_map/reduce_middle/ppermute | solution.py:51
  340.4 2.6 collective-permute-start.64
  346.4 2.5 collective-permute-start.63
  351.8 2.9 collective-permute-done.66
  (430 shorter events, 109.7 us)
Async XLA Ops:
  1.8 19.9 %collective-permute-start = (bf16[4,64,512]{2,1,0:T(8,128)(2,1)S(1)}, bf16[4,64,512]{2,1,0:T(8,128)(2,1)S(1)}, u32[]{:S(2)}, u32[]{:S(2)}) collective-permute-start(bf16[4,64,512]{2,1,0:T(8,128)(2,1)S(1)} %pad_maximum_fusion.11), channel_id=1, source_target_pairs={{8,0},{10,2},{12,4},{14,6},{16,8},{18,10},{20,12},{22,14},{24,16},... | collective-permute-start | bytes 786440 | tf_op jit(solution)/shard_map/gather_z/ppermute | solution.py:47
  6.9 22.3 %collective-permute-start.1 = (bf16[4,64,512]{2,1,0:T(8,128)(2,1)S(1)}, bf16[4,64,512]{2,1,0:T(8,128)(2,1)S(1)}, u32[]{:S(2)}, u32[]{:S(2)}) collective-permute-start(bf16[4,64,512]{2,1,0:T(8,128)(2,1)S(1)} %pad_maximum_fusion.11), channel_id=1, source_target_pairs={{16,0},{18,2},{20,4},{22,6},{24,8},{26,10},{28,12},{30,14},{0,16},... | collective-permute-start | bytes 786440 | tf_op jit(solution)/shard_map/gather_z/ppermute | solution.py:47
  6.9 22.3 %collective-permute-start.2 = (bf16[4,64,512]{2,1,0:T(8,128)(2,1)S(1)}, bf16[4,64,512]{2,1,0:T(8,128)(2,1)S(1)}, u32[]{:S(2)}, u32[]{:S(2)}) collective-permute-start(bf16[4,64,512]{2,1,0:T(8,128)(2,1)S(1)} %pad_maximum_fusion.11), channel_id=1, source_target_pairs={{24,0},{26,2},{28,4},{30,6},{0,8},{2,10},{4,12},{6,14},{8,16},{10,... | collective-permute-start | bytes 786440 | tf_op jit(solution)/shard_map/gather_z/ppermute | solution.py:47
  46.4 25.2 %collective-permute-start.18 = (bf16[552,1024]{1,0:T(8,128)(2,1)}, bf16[552,1024]{1,0:T(8,128)(2,1)}, u32[]{:S(2)}, u32[]{:S(2)}) collective-permute-start(bf16[552,1024]{1,0:T(8,128)(2,1)} %get-tuple-element.253.refs_2_.own_ref), channel_id=1, source_target_pairs={{0,1},{1,0},{2,3},{3,2},{4,5},{5,4},{6,7},{7,6},{8,9},{9,8},{10,11... | collective-permute-start | bytes 3391496 | tf_op jit(solution)/shard_map/ppermute | solution.py:211
  46.6 25.6 %collective-permute-start.11 = (bf16[4,256,512]{2,1,0:T(8,128)(2,1)S(1)}, bf16[4,256,512]{2,1,0:T(8,128)(2,1)S(1)}, u32[]{:S(2)}, u32[]{:S(2)}) collective-permute-start(bf16[4,256,512]{2,1,0:T(8,128)(2,1)S(1)} %constant_dynamic-update-slice_fusion.2.refs_2_.refs_3_.refs_18_.refs_19_.refs_20_.refs_21_.refs_22, ...), channel_id=1, source_target_pairs={{2,0},{0,2},{6,4},{4,6},{10,8},{8,10},{14,12},{12,14},{18,16},{16,... | collective-permute-start | bytes 3145736 | tf_op jit(solution)/shard_map/gather_last/ppermute | solution.py:47
  48.1 25.4 %collective-permute-start.10 = (bf16[4,256,512]{2,1,0:T(8,128)(2,1)S(1)}, bf16[4,256,512]{2,1,0:T(8,128)(2,1)}, u32[]{:S(2)}, u32[]{:S(2)}) collective-permute-start(bf16[4,256,512]{2,1,0:T(8,128)(2,1)S(1)} %constant_dynamic-update-slice_fusion.refs_0_.refs_1_.refs_6_.refs_7_.refs_8_.refs_9_.refs_10_.refs_11_), channel_id=1, source_target_pairs={{4,0},{6,2},{0,4},{2,6},{12,8},{14,10},{8,12},{10,14},{20,16},{22,... | collective-permute-start | bytes 3145736 | tf_op jit(solution)/shard_map/gather_last/ppermute | solution.py:47
  51.4 20.1 %collective-permute-start.12 = (bf16[4,64,512]{2,1,0:T(8,128)(2,1)S(1)}, bf16[4,64,512]{2,1,0:T(8,128)(2,1)S(1)}, u32[]{:S(2)}, u32[]{:S(2)}) collective-permute-start(bf16[4,64,512]{2,1,0:T(8,128)(2,1)S(1)} %pad_maximum_fusion.13), channel_id=1, source_target_pairs={{16,0},{18,2},{20,4},{22,6},{24,8},{26,10},{28,12},{30,14},{0,16},... | collective-permute-start | bytes 786440 | tf_op jit(solution)/shard_map/gather_step/ppermute | solution.py:47
  51.7 19.9 %collective-permute-start.13 = (bf16[4,64,512]{2,1,0:T(8,128)(2,1)S(1)}, bf16[4,64,512]{2,1,0:T(8,128)(2,1)S(1)}, u32[]{:S(2)}, u32[]{:S(2)}) collective-permute-start(bf16[4,64,512]{2,1,0:T(8,128)(2,1)S(1)} %pad_maximum_fusion.13), channel_id=1, source_target_pairs={{24,0},{26,2},{28,4},{30,6},{0,8},{2,10},{4,12},{6,14},{8,16},{10,... | collective-permute-start | bytes 786440 | tf_op jit(solution)/shard_map/gather_step/ppermute | solution.py:47
  73.6 25.1 %collective-permute-start.22 = (bf16[4,128,512]{2,1,0:T(8,128)(2,1)S(1)}, bf16[4,128,512]{2,1,0:T(8,128)(2,1)S(1)}, u32[]{:S(2)}, u32[]{:S(2)}) collective-permute-start(bf16[4,128,512]{2,1,0:T(8,128)(2,1)S(1)} %constant_dynamic-update-slice_fusion.6), channel_id=1, source_target_pairs={{8,0},{10,2},{12,4},{14,6},{16,8},{18,10},{20,12},{22,14},{24,16},... | collective-permute-start | bytes 1572872 | tf_op jit(solution)/shard_map/gather_step/ppermute | solution.py:47
  75.2 23.6 %collective-permute-start.23 = (bf16[4,128,512]{2,1,0:T(8,128)(2,1)S(1)}, bf16[4,128,512]{2,1,0:T(8,128)(2,1)S(1)}, u32[]{:S(2)}, u32[]{:S(2)}) collective-permute-start(bf16[4,128,512]{2,1,0:T(8,128)(2,1)S(1)} %constant_dynamic-update-slice_fusion.6), channel_id=1, source_target_pairs={{24,0},{26,2},{28,4},{30,6},{0,8},{2,10},{4,12},{6,14},{8,16},{10,... | collective-permute-start | bytes 1572872 | tf_op jit(solution)/shard_map/gather_step/ppermute | solution.py:47
  76.0 22.8 %collective-permute-start.21 = (bf16[4,128,512]{2,1,0:T(8,128)(2,1)S(1)}, bf16[4,128,512]{2,1,0:T(8,128)(2,1)S(1)}, u32[]{:S(2)}, u32[]{:S(2)}) collective-permute-start(bf16[4,128,512]{2,1,0:T(8,128)(2,1)S(1)} %pad_maximum_fusion.5), channel_id=1, source_target_pairs={{4,0},{6,2},{0,4},{2,6},{12,8},{14,10},{8,12},{10,14},{20,16},{22,... | collective-permute-start | bytes 1572872 | tf_op jit(solution)/shard_map/gather_middle/ppermute | solution.py:47
  76.7 22.2 %collective-permute-start.20 = (bf16[4,128,512]{2,1,0:T(8,128)(2,1)S(1)}, bf16[4,128,512]{2,1,0:T(8,128)(2,1)S(1)}, u32[]{:S(2)}, u32[]{:S(2)}) collective-permute-start(bf16[4,128,512]{2,1,0:T(8,128)(2,1)S(1)} %pad_maximum_fusion.4), channel_id=1, source_target_pairs={{2,0},{0,2},{6,4},{4,6},{10,8},{8,10},{14,12},{12,14},{18,16},{16,... | collective-permute-start | bytes 1572872 | tf_op jit(solution)/shard_map/gather_middle/ppermute | solution.py:47
  107.3 29.2 %collective-permute-start.25 = (bf16[4,256,512]{2,1,0:T(8,128)(2,1)S(1)}, bf16[4,256,512]{2,1,0:T(8,128)(2,1)S(1)}, u32[]{:S(2)}, u32[]{:S(2)}) collective-permute-start(bf16[4,256,512]{2,1,0:T(8,128)(2,1)S(1)} %constant_dynamic-update-slice_fusion.12.refs_6_.refs_10_), channel_id=1, source_target_pairs={{2,0},{0,2},{6,4},{4,6},{10,8},{8,10},{14,12},{12,14},{18,16},{16,... | collective-permute-start | bytes 3145736 | tf_op jit(solution)/shard_map/gather_last/ppermute | solution.py:47
  109.0 27.5 %collective-permute-start.24 = (bf16[4,256,512]{2,1,0:T(8,128)(2,1)S(1)}, bf16[4,256,512]{2,1,0:T(8,128)(2,1)}, u32[]{:S(2)}, u32[]{:S(2)}) collective-permute-start(bf16[4,256,512]{2,1,0:T(8,128)(2,1)S(1)} %constant_dynamic-update-slice_fusion.10.refs_4_.refs_8_), channel_id=1, source_target_pairs={{4,0},{6,2},{0,4},{2,6},{12,8},{14,10},{8,12},{10,14},{20,16},{22,... | collective-permute-start | bytes 3145736 | tf_op jit(solution)/shard_map/gather_last/ppermute | solution.py:47
  110.6 25.9 %collective-permute-start.26 = (bf16[4,128,512]{2,1,0:T(8,128)(2,1)S(1)}, bf16[4,128,512]{2,1,0:T(8,128)(2,1)S(1)}, u32[]{:S(2)}, u32[]{:S(2)}) collective-permute-start(bf16[4,128,512]{2,1,0:T(8,128)(2,1)S(1)} %copy-done.36), channel_id=1, source_target_pairs={{16,0},{18,2},{20,4},{22,6},{24,8},{26,10},{28,12},{30,14},{0,16},... | collective-permute-start | bytes 1572872 | tf_op jit(solution)/shard_map/gather_step/ppermute | solution.py:47
  137.8 28.1 %collective-permute-start.29 = (bf16[4,256,512]{2,1,0:T(8,128)(2,1)}, bf16[4,256,512]{2,1,0:T(8,128)(2,1)}, u32[]{:S(2)}, u32[]{:S(2)}) collective-permute-start(bf16[4,256,512]{2,1,0:T(8,128)(2,1)} %bitcast.43.refs_6_.refs_10_), channel_id=1, source_target_pairs={{2,0},{0,2},{6,4},{4,6},{10,8},{8,10},{14,12},{12,14},{18,16},{16,... | collective-permute-start | bytes 3145736 | tf_op jit(solution)/shard_map/gather_last/ppermute | solution.py:47
  139.4 26.5 %collective-permute-start.28 = (bf16[4,256,512]{2,1,0:T(8,128)(2,1)}, bf16[4,256,512]{2,1,0:T(8,128)(2,1)}, u32[]{:S(2)}, u32[]{:S(2)}) collective-permute-start(bf16[4,256,512]{2,1,0:T(8,128)(2,1)} %bitcast.32.refs_4_.refs_8_), channel_id=1, source_target_pairs={{4,0},{6,2},{0,4},{2,6},{12,8},{14,10},{8,12},{10,14},{20,16},{22,... | collective-permute-start | bytes 3145736 | tf_op jit(solution)/shard_map/gather_last/ppermute | solution.py:47
  165.9 30.6 %collective-permute-start.30 = (bf16[4,256,512]{2,1,0:T(8,128)(2,1)}, bf16[4,256,512]{2,1,0:T(8,128)(2,1)}, u32[]{:S(2)}, u32[]{:S(2)}) collective-permute-start(bf16[4,256,512]{2,1,0:T(8,128)(2,1)} %bitcast.191), channel_id=1, source_target_pairs={{0,4},{2,6},{4,0},{6,2},{8,12},{10,14},{12,8},{14,10},{16,20},{18,... | collective-permute-start | bytes 3145736 | tf_op jit(solution)/shard_map/reduce_last/ppermute | solution.py:51
  167.5 29.0 %collective-permute-start.31 = (bf16[4,256,512]{2,1,0:T(8,128)(2,1)}, bf16[4,256,512]{2,1,0:T(8,128)(2,1)}, u32[]{:S(2)}, u32[]{:S(2)}) collective-permute-start(bf16[4,256,512]{2,1,0:T(8,128)(2,1)} %bitcast.190), channel_id=1, source_target_pairs={{0,2},{2,0},{4,6},{6,4},{8,10},{10,8},{12,14},{14,12},{16,18},{18,... | collective-permute-start | bytes 3145736 | tf_op jit(solution)/shard_map/reduce_last/ppermute | solution.py:51
  218.5 24.6 %collective-permute-start.39 = (bf16[4,64,512]{2,1,0:T(8,128)(2,1)S(1)}, bf16[4,64,512]{2,1,0:T(8,128)(2,1)S(1)}, u32[]{:S(2)}, u32[]{:S(2)}) collective-permute-start(bf16[4,64,512]{2,1,0:T(8,128)(2,1)S(1)} %pad_maximum_fusion.16), channel_id=1, source_target_pairs={{0,24},{2,26},{4,28},{6,30},{8,0},{10,2},{12,4},{14,6},{16,8},{18,... | collective-permute-start | bytes 786440 | tf_op jit(solution)/shard_map/reduce_z/ppermute | solution.py:51
  221.2 22.3 %collective-permute-start.38 = (bf16[4,64,512]{2,1,0:T(8,128)(2,1)S(1)}, bf16[4,64,512]{2,1,0:T(8,128)(2,1)S(1)}, u32[]{:S(2)}, u32[]{:S(2)}) collective-permute-start(bf16[4,64,512]{2,1,0:T(8,128)(2,1)S(1)} %pad_maximum_fusion.15), channel_id=1, source_target_pairs={{0,16},{2,18},{4,20},{6,22},{8,24},{10,26},{12,28},{14,30},{16,0},... | collective-permute-start | bytes 786440 | tf_op jit(solution)/shard_map/reduce_z/ppermute | solution.py:51
  221.3 22.2 %collective-permute-start.37 = (bf16[4,64,512]{2,1,0:T(8,128)(2,1)S(1)}, bf16[4,64,512]{2,1,0:T(8,128)(2,1)S(1)}, u32[]{:S(2)}, u32[]{:S(2)}) collective-permute-start(bf16[4,64,512]{2,1,0:T(8,128)(2,1)S(1)} %pad_maximum_fusion.14), channel_id=1, source_target_pairs={{0,8},{2,10},{4,12},{6,14},{8,16},{10,18},{12,20},{14,22},{16,24},... | collective-permute-start | bytes 786440 | tf_op jit(solution)/shard_map/reduce_z/ppermute | solution.py:51
  221.9 24.6 %collective-permute-start.35 = (bf16[4,256,512]{2,1,0:T(8,128)(2,1)}, bf16[4,256,512]{2,1,0:T(8,128)(2,1)S(1)}, u32[]{:S(2)}, u32[]{:S(2)}) collective-permute-start(bf16[4,256,512]{2,1,0:T(8,128)(2,1)} %bitcast.51), channel_id=1, source_target_pairs={{0,4},{2,6},{4,0},{6,2},{8,12},{10,14},{12,8},{14,10},{16,20},{18,... | collective-permute-start | bytes 3145736 | tf_op jit(solution)/shard_map/reduce_last/ppermute | solution.py:51
  222.9 24.4 %collective-permute-start.36 = (bf16[4,256,512]{2,1,0:T(8,128)(2,1)}, bf16[4,256,512]{2,1,0:T(8,128)(2,1)S(1)}, u32[]{:S(2)}, u32[]{:S(2)}) collective-permute-start(bf16[4,256,512]{2,1,0:T(8,128)(2,1)} %bitcast.53), channel_id=1, source_target_pairs={{0,2},{2,0},{4,6},{6,4},{8,10},{10,8},{12,14},{14,12},{16,18},{18,... | collective-permute-start | bytes 3145736 | tf_op jit(solution)/shard_map/reduce_last/ppermute | solution.py:51
  263.7 27.4 %collective-permute-start.46 = (bf16[4,64,512]{2,1,0:T(8,128)(2,1)S(1)}, bf16[4,64,512]{2,1,0:T(8,128)(2,1)S(1)}, u32[]{:S(2)}, u32[]{:S(2)}) collective-permute-start(bf16[4,64,512]{2,1,0:T(8,128)(2,1)S(1)} %pad_maximum_fusion.19), channel_id=1, source_target_pairs={{0,24},{2,26},{4,28},{6,30},{8,0},{10,2},{12,4},{14,6},{16,8},{18,... | collective-permute-start | bytes 786440 | tf_op jit(solution)/shard_map/reduce_z/ppermute | solution.py:51
  267.0 24.1 %collective-permute-start.45 = (bf16[4,64,512]{2,1,0:T(8,128)(2,1)S(1)}, bf16[4,64,512]{2,1,0:T(8,128)(2,1)S(1)}, u32[]{:S(2)}, u32[]{:S(2)}) collective-permute-start(bf16[4,64,512]{2,1,0:T(8,128)(2,1)S(1)} %pad_maximum_fusion.18), channel_id=1, source_target_pairs={{0,16},{2,18},{4,20},{6,22},{8,24},{10,26},{12,28},{14,30},{16,0},... | collective-permute-start | bytes 786440 | tf_op jit(solution)/shard_map/reduce_z/ppermute | solution.py:51
  267.6 23.5 %collective-permute-start.44 = (bf16[4,64,512]{2,1,0:T(8,128)(2,1)S(1)}, bf16[4,64,512]{2,1,0:T(8,128)(2,1)S(1)}, u32[]{:S(2)}, u32[]{:S(2)}) collective-permute-start(bf16[4,64,512]{2,1,0:T(8,128)(2,1)S(1)} %pad_maximum_fusion.17), channel_id=1, source_target_pairs={{0,8},{2,10},{4,12},{6,14},{8,16},{10,18},{12,20},{14,22},{16,24},... | collective-permute-start | bytes 786440 | tf_op jit(solution)/shard_map/reduce_z/ppermute | solution.py:51
  268.3 22.8 %collective-permute-start.42 = (bf16[5,256,256]{2,1,0:T(8,128)(2,1)S(1)}, bf16[5,256,256]{2,1,0:T(8,128)(2,1)S(1)}, u32[]{:S(2)}, u32[]{:S(2)}) collective-permute-start(bf16[5,256,256]{2,1,0:T(8,128)(2,1)S(1)} %copy-done.80), channel_id=1, source_target_pairs={{0,4},{2,6},{4,0},{6,2},{8,12},{10,14},{12,8},{14,10},{16,20},{18,... | collective-permute-start | bytes 1966088 | tf_op jit(solution)/shard_map/reduce_last/ppermute | solution.py:51
  269.3 21.8 %collective-permute-start.43 = (bf16[5,256,256]{2,1,0:T(8,128)(2,1)S(1)}, bf16[5,256,256]{2,1,0:T(8,128)(2,1)S(1)}, u32[]{:S(2)}, u32[]{:S(2)}) collective-permute-start(bf16[5,256,256]{2,1,0:T(8,128)(2,1)S(1)} %copy-done.79), channel_id=1, source_target_pairs={{0,2},{2,0},{4,6},{6,4},{8,10},{10,8},{12,14},{14,12},{16,18},{18,... | collective-permute-start | bytes 1966088 | tf_op jit(solution)/shard_map/reduce_last/ppermute | solution.py:51
  298.7 25.5 %collective-permute-start.50 = (bf16[3,256,256]{2,1,0:T(8,128)(2,1)S(1)}, bf16[3,256,256]{2,1,0:T(8,128)(2,1)S(1)}, u32[]{:S(2)}, u32[]{:S(2)}) collective-permute-start(bf16[3,256,256]{2,1,0:T(8,128)(2,1)S(1)} %copy-done.82), channel_id=1, source_target_pairs={{0,4},{2,6},{4,0},{6,2},{8,12},{10,14},{12,8},{14,10},{16,20},{18,... | collective-permute-start | bytes 1179656 | tf_op jit(solution)/shard_map/reduce_last/ppermute | solution.py:51
  299.7 24.5 %collective-permute-start.51 = (bf16[3,256,256]{2,1,0:T(8,128)(2,1)S(1)}, bf16[3,256,256]{2,1,0:T(8,128)(2,1)S(1)}, u32[]{:S(2)}, u32[]{:S(2)}) collective-permute-start(bf16[3,256,256]{2,1,0:T(8,128)(2,1)S(1)} %copy-done.81), channel_id=1, source_target_pairs={{0,2},{2,0},{4,6},{6,4},{8,10},{10,8},{12,14},{14,12},{16,18},{18,... | collective-permute-start | bytes 1179656 | tf_op jit(solution)/shard_map/reduce_last/ppermute | solution.py:51
  313.0 22.5 %collective-permute-start.56 = (bf16[5,64,256]{2,1,0:T(8,128)(2,1)S(1)}, bf16[5,64,256]{2,1,0:T(8,128)(2,1)S(1)}, u32[]{:S(2)}, u32[]{:S(2)}) collective-permute-start(bf16[5,64,256]{2,1,0:T(8,128)(2,1)S(1)} %pad_maximum_fusion.22), channel_id=1, source_target_pairs={{0,24},{2,26},{4,28},{6,30},{8,0},{10,2},{12,4},{14,6},{16,8},{18,... | collective-permute-start | bytes 491528 | tf_op jit(solution)/shard_map/reduce_z/ppermute | solution.py:51
  (122 other events, 1288.8 us)

commit v4 on v3

--- a/solution.py
+++ b/solution.py
@@ -122,16 +122,21 @@
             out.append([cut[0]] + sent)
         return out
 
-    def reduce_first(self, halves):
+    def first_pieces(self, halves):
         def along(step):
             rows = slice(step * self.half, (step + 1) * self.half)
             totals = [sum(p[..., rows, :].astype(F32) for p in parts) for parts in halves]
             return jnp.concatenate(totals, axis=-2)
 
-        sent = [along(s).astype(BF16) for s in range(1, self.factors[0])]
+        return [along(0)] + [along(s).astype(BF16) for s in range(1, self.factors[0])]
+
+    def send_first(self, pieces, steps):
         with jax.named_scope("reduce_z"):
-            sent = [self.push(p, 0, s) for s, p in enumerate(sent, 1)]
-        return [along(0)] + sent
+            return [self.push(pieces[s], 0, s) for s in steps if s < len(pieces)]
+
+    def reduce_first(self, halves):
+        pieces = self.first_pieces(halves)
+        return pieces[:1] + self.send_first(pieces, (1, 2, 3))
 
     def reduce_end(self, parts):
         return sum(p.astype(F32) for p in parts)
@@ -148,9 +153,9 @@
 
     def small_in_order(self, value):
         zeroth, second, third = self.factors
-        value = value.reshape((zeroth, third, second, value.shape[1], 2, self.half))
-        first_half = value[..., 0, :].transpose(3, 2, 1, 0, 4)
-        second_half = value[..., 1, :].transpose(3, 1, 2, 0, 4)
+        value = value.reshape((third, second, zeroth, value.shape[1], 2, self.half))
+        first_half = value[..., 0, :].transpose(3, 1, 0, 2, 4)
+        second_half = value[..., 1, :].transpose(3, 0, 1, 2, 4)
         count = value.shape[3]
         return jnp.concatenate(
             [first_half.reshape(count, -1), second_half.reshape(count, -1)], axis=1
@@ -235,9 +240,10 @@
             return kept + self.swap(value[self.local_rows :]).astype(F32)
         return lax.psum_scatter(value, "tensor", scatter_dimension=0, tiled=True).astype(F32)
 
-    def own_both(self, value):
+    def own_both(self, halves):
         if self.relative:
-            return value[: self.local_rows], self.swap(value[self.local_rows :])
+            return halves[0], self.swap(halves[1])
+        value = jnp.concatenate(halves, axis=0)
         total = lax.psum_scatter(value, "tensor", scatter_dimension=0, tiled=True)
         return total, jnp.zeros((1, value.shape[1]), F32)
 
@@ -414,7 +420,7 @@
 
 def attend_back(packed, invalid, mixed, total, grad_mixed, first, count):
     slots, pairs = invalid.shape[0], packed.shape[1] // (6 * HEAD_DIM)
-    columns, invalid_spec, _ = attend_specs()
+    columns, invalid_spec, total_spec = attend_specs()
     return pl.pallas_call(
         attend_back_kernel,
         grid=(slots, count),
@@ -423,8 +429,8 @@
             columns(pairs + first),
             columns(2 * pairs + first),
             invalid_spec,
-            columns(first),
-            pl.BlockSpec((1, 1, 2, SEQ_LEN), lambda s, p: (s, p + first, 0, 0)),
+            columns(0),
+            total_spec,
             columns(first),
         ],
         out_specs=[columns(0)] * 3,
@@ -469,36 +475,43 @@
     )(rows, *pieces)
 
 
-def times_pieces_turned(columns, pieces, places, fits):
+def times_pieces_turned(columns, pieces, places, fits, cuts=1):
     count = len(columns)
     rows, wide = columns[0].shape
     if not fits:
         weight = [joined(pieces, g, 1)[:, c * wide : (c + 1) * wide] for g, c in places]
         total = dot_nt(jnp.concatenate(columns, axis=1), jnp.concatenate(weight, axis=1))
-        return total.astype(BF16)
+        return jnp.split(total.astype(BF16), cuts) if cuts > 1 else total.astype(BF16)
     starts = np.cumsum([0] + [p.shape[1] for p in pieces]).tolist()
 
     def kernel(*refs):
-        lefts, weights, out_ref = refs[:count], refs[count:-1], refs[-1]
-        for i, start in enumerate(starts[:-1]):
-            total = 0.0
-            for k in range(count):
-                total = total + dot_nt(lefts[k][...], weights[i * count + k][0])
-            out_ref[:, start : starts[i + 1]] = total.astype(BF16)
+        lefts, weights, out_refs = refs[:count], refs[count:-cuts], refs[-cuts:]
+        left = jnp.concatenate([r[...] for r in lefts], axis=1)
+        weight = jnp.concatenate(
+            [
+                jnp.concatenate([r[0] for r in weights[i * count : (i + 1) * count]], axis=1)
+                for i in range(len(pieces))
+            ],
+            axis=0,
+        )
+        for k, out_ref in enumerate(out_refs):
+            cut = slice(k * rows // cuts, (k + 1) * rows // cuts)
+            out_ref[...] = dot_nt(left[cut], weight).astype(BF16)
 
     def place_spec(piece, group, column):
         return pl.BlockSpec((1, piece.shape[1], wide), lambda i: (group, 0, column))
 
-    return pl.pallas_call(
+    outs = pl.pallas_call(
         kernel,
         grid=(1,),
         in_specs=[whole_spec(c) for c in columns] + [place_spec(p, *q) for p in pieces for q in places],
-        out_specs=pl.BlockSpec((rows, starts[-1]), lambda i: (0, 0)),
-        out_shape=jax.ShapeDtypeStruct((rows, starts[-1]), BF16),
+        out_specs=[pl.BlockSpec((rows // cuts, starts[-1]), lambda i: (0, 0))] * cuts,
+        out_shape=[jax.ShapeDtypeStruct((rows // cuts, starts[-1]), BF16)] * cuts,
         compiler_params=params(48),
         cost_estimate=cost(1 + count),
         name="times_pieces_turned",
     )(*columns, *[p for p in pieces for _ in places])
+    return outs if cuts > 1 else outs[0]
 
 
 def weight_grads(lefts, rights, piece_rows, fits):
@@ -517,10 +530,11 @@
     def kernel(*refs):
         left_refs, right_refs = refs[: len(names)], refs[len(names) : len(names) + count]
         out_refs = refs[len(names) + count :]
-        for i, (start, end) in enumerate(zip(starts, starts[1:])):
-            turned = [r[:, start:end].T for r in left_refs]
-            for k in range(count):
-                out_refs[i][k] = dot_nn(turned[which[k]], right_refs[k][...]).astype(BF16)
+        turned = [r[...].T for r in left_refs]
+        for k in range(count):
+            product = dot_nn(turned[which[k]], right_refs[k][...]).astype(BF16)
+            for i, (start, end) in enumerate(zip(starts, starts[1:])):
+                out_refs[i][k] = product[start:end]
 
     return pl.pallas_call(
         kernel,
@@ -578,16 +592,25 @@
         return work(joined_rows(rows_in), live, mine, other, shift, gain, bias)
     half = rows // 2
 
-    def kernel(own_ref, next_ref, live_ref, mine_ref, other_ref, *refs):
-        vectors = [r[...] for r in refs[:3]]
-        for i, ref in enumerate((own_ref, next_ref)):
-            cut, turned = slice(i * half, (i + 1) * half), slice((1 - i) * half, (2 - i) * half)
-            refs[3][cut], refs[4][cut] = work(
-                ref[...], live_ref[cut], mine_ref[cut], other_ref[turned], *vectors
-            )
+    def kernel(own_ref, next_ref, *refs):
+        rows_in = jnp.where(pl.program_id(0) == 0, own_ref[...], next_ref[...])
+        refs[-2][...], refs[-1][...] = work(rows_in, *[r[...] for r in refs[:-2]])
+
+    def block(columns, place=lambda i: i):
+        return pl.BlockSpec((half, columns), lambda i: (place(i), 0))
 
     return pl.pallas_call(
         kernel,
+        grid=(2,),
+        in_specs=[
+            block(width, lambda i: 0),
+            block(width, lambda i: 0),
+            block(1),
+            block(width),
+            block(width, lambda i: 1 - i),
+        ]
+        + [whole_spec(shift)] * 3,
+        out_specs=[block(width), block(width)],
         out_shape=[
             jax.ShapeDtypeStruct((rows, width), F32),
             jax.ShapeDtypeStruct((rows, width), BF16),
@@ -616,28 +639,46 @@
     half = rows // 2
 
     def kernel(own_ref, next_ref, live_ref, mine_ref, other_ref, middle_ref, gain_ref, *refs):
-        total = 0.0
-        for i, ref in enumerate((own_ref, next_ref)):
-            cut, turned = slice(i * half, (i + 1) * half), slice((1 - i) * half, (2 - i) * half)
-            refs[0][cut], refs[1][cut], sums = work(
-                ref[...],
-                live_ref[cut],
-                mine_ref[cut],
-                other_ref[turned],
-                middle_ref[cut],
-                gain_ref[...],
-            )
-            total = total + sums
-        refs[2][...] = total
+        step = pl.program_id(0)
+        grad = jnp.where(step == 0, own_ref[...], next_ref[...])
+        rest = [r[...] for r in (live_ref, mine_ref, other_ref, middle_ref, gain_ref)]
+        grad_middle, refs[1][...], sums = work(grad, *rest)
+
+        @pl.when(step == 0)
+        def _():
+            refs[0][...] = grad_middle
+            refs[2][...] = sums
+
+        @pl.when(step == 1)
+        def _():
+            refs[2][...] += sums
+
+    def block(columns, place=lambda i: i):
+        return pl.BlockSpec((half, columns), lambda i: (place(i), 0))
 
     return pl.pallas_call(
         kernel,
+        grid=(2,),
+        in_specs=[
+            block(width, lambda i: 0),
+            block(width, lambda i: 0),
+            block(1),
+            block(width),
+            block(width, lambda i: 1 - i),
+            block(width),
+            whole_spec(gain),
+        ],
+        out_specs=[
+            block(width, lambda i: 0),
+            block(width),
+            pl.BlockSpec((4, width), lambda i: (0, 0)),
+        ],
         out_shape=[
-            jax.ShapeDtypeStruct((rows, width), F32),
+            jax.ShapeDtypeStruct((half, width), F32),
             jax.ShapeDtypeStruct((rows, width), BF16),
             jax.ShapeDtypeStruct((4, width), F32),
         ],
-        compiler_params=params(48),
+        compiler_params=params(40),
         cost_estimate=cost(7),
         name="norm_back",
     )(*grad_out, live, mine, other, middle, gain)
@@ -705,12 +746,6 @@
         else:
             normed_turned[...] = normed_ref[...].T
             grad_turned[...] = grad_ref[...].T
-        if carried:
-            out_sum[...] = before[0][...].astype(F32)
-            grad_sum[...] = before[1][...].astype(F32)
-        else:
-            out_sum[...] = jnp.zeros_like(out_sum)
-            grad_sum[...] = jnp.zeros_like(grad_sum)
 
     if plain:
         first = jnp.concatenate([first_refs[0][place(i)] for i in range(blocks)], axis=0)
@@ -722,24 +757,40 @@
     hidden_act, slope = gelu_and_slope(hidden)
     hidden_act = hidden_act.astype(BF16)
     grad_pre = (dot_nn(grad_ref[...], second) * slope).astype(BF16)
-    out_sum[...] += dot_nt(hidden_act, second)
-    grad_sum[...] += dot_nt(grad_pre, first)
     shift_grad_ref[...] = jnp.sum(grad_pre.astype(F32), axis=0, keepdims=True)
+    last = pl.num_programs(0) - 1
+    products = (
+        (out_sum, out_ref, hidden_act, second, before[:1]),
+        (grad_sum, grad_two_ref, grad_pre, first, before[1:]),
+    )
+
+    @pl.when(step == 0)
+    def _():
+        for sum_ref, _, left, right, start in products:
+            product = dot_nt(left, right)
+            sum_ref[...] = product + start[0][...].astype(F32) if carried else product
+
+    @pl.when((step > 0) & (step < last))
+    def _():
+        for sum_ref, _, left, right, _ in products:
+            sum_ref[...] += dot_nt(left, right)
+
+    @pl.when(step == last)
+    def _():
+        for sum_ref, end_ref, left, right, _ in products:
+            end_ref[...] = (sum_ref[...] + dot_nt(left, right)).astype(BF16)
+
     if scattered:
         weight_grad_refs[0][...] = dot_nn(normed_turned[...], grad_pre).astype(BF16)
         weight_grad_refs[1][...] = dot_nn(grad_turned[...], hidden_act).astype(BF16)
     else:
-        start = 0
-        for ref in weight_grad_refs:
-            rows = slice(start, start + ref.shape[2])
-            ref[0, 0] = dot_nn(normed_turned[rows], grad_pre).astype(BF16)
-            ref[1, 0] = dot_nn(grad_turned[rows], hidden_act).astype(BF16)
-            start += ref.shape[2]
-
-    @pl.when(step == pl.num_programs(0) - 1)
-    def _():
-        out_ref[...] = out_sum[...].astype(BF16)
-        grad_two_ref[...] = grad_sum[...].astype(BF16)
+        for k, (left, right) in enumerate(
+            ((normed_turned, grad_pre), (grad_turned, hidden_act))
+        ):
+            product, start = dot_nn(left[...], right).astype(BF16), 0
+            for ref in weight_grad_refs:
+                ref[k, 0] = product[start : start + ref.shape[2]]
+                start += ref.shape[2]
 
 
 def feed_forward(normed, grads, shift, weight, places, piece_rows, before, fits):
@@ -773,7 +824,7 @@
         shift_grad = jnp.sum(grad_pre, axis=0, dtype=F32, keepdims=True)
         return [out.astype(BF16), grad_two.astype(BF16), shift_grad] + outs
 
-    tile = min(256, units // 2)
+    tile = units // 2
     per = wide // tile
     pieces = [weight] if plain else weight
 
@@ -837,8 +888,8 @@
             jax.ShapeDtypeStruct((1, units), F32),
         ]
         + grad_shapes,
-        compiler_params=params(60),
-        cost_estimate=cost(6.3 * (units // tile)),
+        compiler_params=params(52),
+        cost_estimate=cost(25),
         name="feed_forward",
     )(places, normed, shift, *grads, *pieces, *pieces, *before)
     outs = list(outs)
@@ -902,20 +953,26 @@
         ]
     )
     attn_shard = jnp.concatenate([qkv_weight, proj_weight.T[None]], axis=0)
+    count = smalls.shape[0]
+    spare = ((0, 3), (0, 0), (0, width_here - block))
+    attn_shard = jnp.concatenate([attn_shard, jnp.pad(smalls[None], spare)], axis=1)
 
     attn_along = grid.spread(attn_shard)
-    smalls = grid.gather_small(smalls[None], (1, 2))
+    smalls = jnp.stack([a[0, block:, :block] for a in attn_along])
     second_parts = grid.spread_middle(second_shard)
     attn_along, smalls, second_parts, first_shard, inputs, cotangent = join(
         attn_along, smalls, second_parts, first_shard, inputs, cotangent
     )
 
     attn_halves = grid.middle(attn_along)
-    first_along = [first_shard] + grid.steps(first_shard, 0, (1,))
-    smalls = grid.gather_small(smalls, (0,))
+    smalls = grid.gather_small(smalls, (1, 2))
+    second_own = jnp.concatenate(second_parts[0] + second_parts[1], axis=-2)
+    second_counts = [len(p) for p in second_parts]
     features, places = grid.features(), grid.places()
     select = (jnp.arange(width, dtype=jnp.int32)[:, None] == features[None, :]).astype(BF16)
     own_in = dot_nn(inputs, select).astype(BF16)
+    own_in, first_shard = join(own_in, first_shard)
+    first_along = [first_shard] + grid.steps(first_shard, 0, (1,))
     rows_in = pair.parts(own_in)
     own_grad = dot_nn(cotangent, select)
     live_col = jnp.repeat(slot_live.astype(F32), SEQ_LEN)[:, None]
@@ -924,7 +981,9 @@
     rest_grad = ((1.0 - own_live) * own_grad).astype(BF16)
     valid_whole = pair.whole((token_type != 3).astype(F32))
     invalid = jnp.where(valid_whole > 0, 0.0, -1e30).reshape(slot_count, 1, SEQ_LEN)
-    attn_halves, first_along = join(attn_halves, first_along)
+    attn_halves, first_along, second_own, smalls = join(
+        attn_halves, first_along, second_own, smalls
+    )
 
     attn_pieces = grid.finish(attn_halves)
     first_along += grid.steps(first_along[0], 0, (2, 3))
@@ -936,32 +995,37 @@
     fc1_shift = fc1_shift.transpose(1, 0, 2).reshape(dp_size, bias_columns * block)
     fc1_shift = fc1_shift[:, :hidden_block].reshape(1, hidden_here)
     norm_one = first_norm(rows_in, gain_one, shift_one, fits)
-    attn_pieces, first_along, norm_one, second_parts, grad_mlp, invalid = join(
-        attn_pieces, first_along, norm_one, second_parts, grad_mlp, invalid
+    attn_pieces, first_along, norm_one, second_own, grad_mlp, invalid = join(
+        attn_pieces, first_along, norm_one, second_own, grad_mlp, invalid
     )
 
     first_halves = grid.middle(first_along)
-    second_own = jnp.concatenate(second_parts[0] + second_parts[1], axis=-2)
-    second_counts = [len(p) for p in second_parts]
-    second_near = grid.steps(second_own, 0, (1, 3))
+    second_along = [second_own] + grid.steps(second_own, 0, (1,))
     packed = times_pieces(norm_one, attn_pieces, 0, 3, fits)
     pairs = width_here // (2 * HEAD_DIM)
     parts = 2 if pairs % 2 == 0 else 1
     share = pairs // parts
-    mixed, total = attend(packed, invalid, 0, pairs)
-    first_halves, second_near, second_own, mixed, total, packed, attn_pieces, norm_one = join(
-        first_halves, second_near, second_own, mixed, total, packed, attn_pieces, norm_one
+    forward = [attend(packed, invalid, 0, share)]
+    first_halves, second_along, forward, packed, attn_pieces, norm_one = join(
+        first_halves, second_along, forward, packed, attn_pieces, norm_one
     )
 
     first_pieces = grid.finish(first_halves)
-    second_far = grid.steps(second_own, 0, (2,))
-    attn_out = times_pieces_turned([mixed], attn_pieces, [(3, 0)], fits)
+    second_along += grid.steps(second_along[0], 0, (2,))
+    if parts == 2:
+        forward = forward + [attend(packed, invalid, share, share)]
+    mixed = [f[0] for f in forward]
+    attn_out = times_pieces_turned(mixed, attn_pieces, [(3, p) for p in range(parts)], fits)
+    first_pieces, second_along, attn_out = join(first_pieces, second_along, attn_out)
+
+    second_along += grid.steps(second_along[0], 0, (3,))
     middle, norm_two = second_norm(
         rows_in, live_col, *pair.both(attn_out), proj_shift, gain_two, shift_two, fits
     )
-    first_pieces, second_far, middle, norm_two = join(first_pieces, second_far, middle, norm_two)
-
-    second_along = [second_own] + second_near[:1] + second_far + second_near[1:]
+    first_pieces, second_along, middle, norm_two = join(
+        first_pieces, second_along, middle, norm_two
+    )
+
     second_pieces = grid.finish(grid.halves_of(second_along, second_counts))
     piece_rows = grid.piece_rows()
     shifts = [fc1_shift[:, :hidden_cut], fc1_shift[:, hidden_cut:]]
@@ -982,59 +1046,62 @@
     grad_middle, grad_branch, sums = norm_back(
         grad_mlp, live_col, *pair.both(grad_two), middle, gain_two, fits
     )
+    grad_branch, pieces_b = join(grad_branch, feed_b[3:])
+    last_b = grid.reduce_last(pieces_b)
     grad_mixed = times_pieces(grad_branch, attn_pieces, 3, 1, fits)
-    middle_a, grad_mixed, pieces_b, grad_middle, grad_branch = join(
-        middle_a, grad_mixed, feed_b[3:], grad_middle, grad_branch
-    )
+    middle_a, grad_mixed, mlp_out = join(middle_a, grad_mixed, mlp_out)
 
     def back(part):
-        return attend_back(packed, invalid, mixed, total, grad_mixed, part * share, share)
+        return attend_back(packed, invalid, *forward[part], grad_mixed, part * share, share)
 
     def grads(part, columns):
         lefts, rights = (norm_one,) * 3, tuple(columns)
         if part == 0:
-            cut = width_here // parts
-            lefts = lefts + (grad_branch,) * parts
-            rights = rights + tuple(mixed[:, p * cut : (p + 1) * cut] for p in range(parts))
+            lefts, rights = lefts + (grad_branch,) * parts, rights + tuple(mixed)
         return weight_grads(lefts, rights, piece_rows, fits)
 
-    last_b = grid.reduce_last(pieces_b)
-    first_a = grid.reduce_first(middle_a)
+    pieces_a = grid.first_pieces(middle_a)
+    first_a = grid.send_first(pieces_a, (1, 3))
     columns = back(0)
-    last_b, first_a, columns, grad_mixed = join(last_b, first_a, columns, grad_mixed)
+    mlp_out = pair.own_total(mlp_out)
+    last_b, first_a, pieces_a, columns, grad_mixed, mlp_out = join(
+        last_b, first_a, pieces_a, columns, grad_mixed, mlp_out
+    )
 
     middle_b = grid.reduce_middle(last_b)
+    first_a = pieces_a[:1] + first_a + grid.send_first(pieces_a, (2,))
     pieces_c = grads(0, columns)
-    middle_b, pieces_c, grad_mixed = join(middle_b, pieces_c, grad_mixed)
+    middle_b, pieces_c, grad_mixed, first_a = join(middle_b, pieces_c, grad_mixed, first_a)
 
     last_c = grid.reduce_last(pieces_c)
-    first_b = grid.reduce_first(middle_b)
+    pieces_b = grid.first_pieces(middle_b)
+    first_b = grid.send_first(pieces_b, (1, 3))
+    pieces_d, places_c = (), [(j, p) for p in range(parts) for j in range(3)]
     if parts == 2:
         more = back(1)
-        last_c, first_b, more = join(last_c, first_b, more)
+        last_c, first_b, pieces_b, more = join(last_c, first_b, pieces_b, more)
         columns = columns + more
-    else:
-        last_c, first_b = join(last_c, first_b)
+        pieces_d = grads(1, more)
 
     middle_c = grid.reduce_middle(last_c)
-    places_c = [(j, p) for p in range(parts) for j in range(3)]
-    if parts == 2:
-        pieces_d = grads(1, more)
-        pieces_d, columns = join(pieces_d, columns)
-        last_d = grid.reduce_last(pieces_d)
-    grad_one = times_pieces_turned(columns, attn_pieces, places_c, fits)
-    middle_c, grad_one, mlp_out = join(middle_c, grad_one, mlp_out)
-
+    first_b = pieces_b[:1] + first_b + grid.send_first(pieces_b, (2,))
+    grad_one = times_pieces_turned(columns, attn_pieces, places_c, fits, 2)
+    middle_c, first_b, pieces_d, grad_one = join(middle_c, first_b, pieces_d, grad_one)
+
+    last_d = grid.reduce_last(pieces_d) if parts == 2 else ()
     first_c = grid.reduce_first(middle_c)
     grad_rows, sums_one = first_norm_back(
-        pair.own(grad_middle), rest_grad, *pair.own_both(grad_one), own_in, gain_one, fits
+        grad_middle if fits else pair.own(grad_middle),
+        rest_grad,
+        *pair.own_both(grad_one),
+        own_in,
+        gain_one,
+        fits,
     )
     sums_one = pair.small_total(sums_one)
-    mlp_out = pair.own_total(mlp_out)
-    first_a, first_b = grid.reduce_end(first_a), grid.reduce_end(first_b)
-    if parts == 2:
-        last_d, sums_one, grad_rows = join(last_d, sums_one, grad_rows)
-        middle_d = grid.reduce_middle(last_d)
+    last_d, sums_one, grad_rows = join(last_d, sums_one, grad_rows)
+
+    middle_d = grid.reduce_middle(last_d) if parts == 2 else ()
     bias_grads = grad_fc1_bias.astype(BF16).reshape(dp_size, hidden_block)
     bias_grads = jnp.pad(bias_grads, ((0, 0), (0, bias_pad))).reshape(dp_size, bias_columns, block)
     bias_grads = dot_nn(bias_grads.transpose(1, 0, 2).reshape(bias_columns, width), select)
@@ -1042,21 +1109,31 @@
     small_grads = grid.blocks_of(small_grads)
     small_grads = grid.reduce_small(small_grads, 2)
     small_grads = grid.reduce_small(small_grads, 1)
+    middle_d, small_grads, first_c, grad_rows, mlp_out = join(
+        middle_d, small_grads, first_c, grad_rows, mlp_out
+    )
+
+    if parts == 2:
+        count, lanes = small_grads.shape[1], middle_d[0][0].shape[2]
+        spare = ((0, 2), (0, 0), (0, lanes - block))
+        pieces_d = [
+            jnp.concatenate([p, jnp.pad(g.astype(p.dtype)[None], spare)], axis=1)
+            for p, g in zip(grid.first_pieces(middle_d), small_grads)
+        ]
+        sum_d = grid.reduce_end(pieces_d[:1] + grid.send_first(pieces_d, (1, 2, 3)))
+        sum_d, small_grads = sum_d[:, :block], sum_d[0, block:, :block]
+    else:
+        small_grads = grid.reduce_small(small_grads, 0)
     grad_inputs = dot_nt(grad_rows, select).astype(BF16)
-    if parts == 2:
-        first_c, middle_d, small_grads = join(first_c, middle_d, small_grads)
-        first_d = grid.reduce_first(middle_d)
-    else:
-        first_c, small_grads = join(first_c, small_grads)
-    small_grads = grid.reduce_small(small_grads, 0)
     result = pair.own(middle) + own_live * (mlp_out + fc2_shift)
     outputs = dot_nt(result.astype(BF16), select).astype(BF16)
+    first_a, first_b = grid.reduce_end(first_a), grid.reduce_end(first_b)
     out_fc1 = jnp.concatenate([first_a[0], first_a[1], first_b[0], first_b[1]], axis=1)
     out_fc2 = jnp.concatenate([first_a[2], first_a[3], first_b[2], first_b[3]], axis=1)
     out_c = grid.reduce_end(first_c)
     out_qkv = out_c[:3]
     if parts == 2:
-        out_qkv = jnp.concatenate([out_qkv, grid.reduce_end(first_d)], axis=2)
+        out_qkv = jnp.concatenate([out_qkv, sum_d], axis=2)
     out_proj = jnp.concatenate([out_c[3 + p] for p in range(parts)], axis=1)
     return (
         outputs,

time: 362 us -> 348 us (0.961)
  Pallas kernels: 159 us -> 148 us
    pallas_call x2, Pallas kernels: 53.5 us -> 46.2 us  [feed_forward(): pl.pallas_call(functools.partial(feed_kernel, (len(grads), len(pieces), l...]
    slice x4 -> x5, local copies, waits for them, and re-layouts: 5.22 us -> 0.11 us  [the longest x1 0.09 us: small_in_order(): second_half = value[..., 1, :].transpose(3, 0, 1, 2, 4)]
    unnamed x184 -> x167, local copies, waits for them, and re-layouts: 8.11 us -> 12.5 us
    ppermute x33 -> x30, starting transfers between devices: 40.1 us -> 35.9 us  [push(): return lax.ppermute(value, 'dp', pairs)]
    pallas_call x2, Pallas kernels: 16 us -> 12.4 us  [the longest x1 7.76 us: norm_back(): pl.pallas_call(kernel, grid=(2,), in_specs=[block(width, lambda i: 0), bl...]
    ppermute x26 -> x23, starting transfers between devices: 33.4 us -> 37 us  [fetch(): return lax.ppermute(value, 'dp', pairs)]
    ppermute x33 -> x30, waiting for transfers between devices: 18.7 us -> 15.7 us  [push(): return lax.ppermute(value, 'dp', pairs)]
    ppermute x26 -> x23, waiting for transfers between devices: 49.3 us -> 47.8 us  [fetch(): return lax.ppermute(value, 'dp', pairs)]
  transfers between devices with their start and end apart: 67 -> 61, of which waited for: 21 -> 20; matrix products, arithmetic and copies ran while one was open for 11% -> 9% of each run, Pallas kernels for 42% -> 43%
where the time goes in v4:
time: 348 us; the launch traced here: 342 us
  Pallas kernels  148 us (43%)
  starting transfers between devices  73.3 us (21%)
  waiting for transfers between devices  67 us (19%)
  local copies, waits for them, and re-layouts  19.1 us (5%)
  other arithmetic  18.1 us (5%)
  matrix products  13.5 us (4%)
    ppermute x23, waiting for transfers between devices, fetch(): return lax.ppermute(value, 'dp', pairs)  47.8 us
    pallas_call x2, Pallas kernels, feed_forward(): pl.pallas_call(functools.partial(feed_kernel, (len(grads), len(pieces), l...  46.2 us
    ppermute x23, starting transfers between devices, fetch(): return lax.ppermute(value, 'dp', pairs)  37 us
    ppermute x30, starting transfers between devices, push(): return lax.ppermute(value, 'dp', pairs)  35.9 us
    pallas_call x2, Pallas kernels, attend_back(): pl.pallas_call(attend_back_kernel, grid=(slots, count), in_specs=[columns...  35.4 us
    pallas_call x2, Pallas kernels, attend(): pl.pallas_call(attend_kernel, grid=(slots, count), in_specs=[columns(firs...  16.2 us
    ppermute x30, waiting for transfers between devices, push(): return lax.ppermute(value, 'dp', pairs)  15.7 us
    pallas_call x2, Pallas kernels, weight_grads(): pl.pallas_call(kernel, grid=(1,), in_specs=[whole_spec(a) for a in names...  13.3 us
  transfers between devices with their start and end apart: 61, of which 20 were waited for; matrix products, arithmetic and copies ran while one was open for 9% of the time, Pallas kernels for 43%

profile of v4, /device:TPU:0, one launch (start us, length us, event | category | flops | bytes accessed | tf_op | source)
XLA Modules:
  0.0 341.9 jit_solution(13125921381539043158)
XLA Ops:
  3.3 3.1 collective-permute-start.2
  6.4 2.6 collective-permute-start.1
  16.4 11.8 %collective-permute-done.1 = bf16[4,72,512]{2,1,0:T(8,128)(2,1)S(1)} collective-permute-done((bf16[4,72,512]{2,1,0:T(8,128)(2,1)S(1)}, bf16[4,72,512]{2,1,0:T(8,128)(2,1)S(1)}, u32[]{:S(2)}, u32[]{:S(2)}) %collective-permute-start.1) | collective-permute-done | bytes 294944 | tf_op jit(solution)/shard_map/gather_z/ppermute | solution.py:47
  36.3 7.8 %collective-permute-start.7 = (bf16[4,64,512]{2,1,0:T(8,128)(2,1)S(1)}, bf16[4,64,512]{2,1,0:T(8,128)(2,1)S(1)}, u32[]{:S(2)}, u32[]{:S(2)}) collective-permute-start(bf16[4,64,512]{2,1,0:T(8,128)(2,1)S(1)} %pad_maximum_fusion.13), channel_id=1, source_target_pairs={{8,0},{10,2},{12,4},{14,6},{16,8},{18,10},{20,12},{22,14},{24,16},... | collective-permute-start | bytes 786440 | tf_op jit(solution)/shard_map/gather_step/ppermute | solution.py:47
  44.1 2.9 multiply_convert_fusion
  57.2 3.2 first_norm.1.rows_ref.refs_0_
  60.5 5.1 %collective-permute-done.13 = bf16[4,64,512]{2,1,0:T(8,128)(2,1)S(1)} collective-permute-done((bf16[4,64,512]{2,1,0:T(8,128)(2,1)S(1)}, bf16[4,64,512]{2,1,0:T(8,128)(2,1)S(1)}, u32[]{:S(2)}, u32[]{:S(2)}) %collective-permute-start.13) | collective-permute-done | bytes 262176 | tf_op jit(solution)/shard_map/gather_step/ppermute | solution.py:47
  65.6 10.1 %collective-permute-done.12 = bf16[4,64,512]{2,1,0:T(8,128)(2,1)S(1)} collective-permute-done((bf16[4,64,512]{2,1,0:T(8,128)(2,1)S(1)}, bf16[4,64,512]{2,1,0:T(8,128)(2,1)S(1)}, u32[]{:S(2)}, u32[]{:S(2)}) %collective-permute-start.12) | collective-permute-done | bytes 262176 | tf_op jit(solution)/shard_map/gather_step/ppermute | solution.py:47
  81.9 5.2 %times_pieces.2.query_ref.key_ref.value_ref = bf16[1104,1536]{1,0:T(8,128)(2,1)S(1)} custom-call(bf16[1104,1024]{1,0:T(8,128)(2,1)S(1)} %first_norm.1.rows_ref.refs_0_, bf16[4,256,512]{2,1,0:T(8,128)(2,1)S(1)} %constant_dynamic-update-slice_fusion.refs_0_.refs_2_.refs_3_.refs_6_.refs_7_.refs_8_.refs_9_.refs_10_.refs_11_, ...), custom_call_target="tpu_custom_call" | custom-call | flops 6000000000 | bytes 6000000 | tf_op jit(solution)/shard_map/times_pieces/pallas_call | solution.py:465
  87.1 8.1 %attend.2 = (bf16[1104,256]{1,0:T(8,128)(2,1)S(1)}, f32[1,2,2,1104]{3,2,1,0:T(2,128)S(1)}) custom-call(bf16[1104,1536]{1,0:T(8,128)(2,1)S(1)} %times_pieces.2.query_ref.key_ref.value_ref, bf16[1104,1536]{1,0:T(8,128)(2,1)S(1)} %times_pieces.2.query_ref.key_ref.value_ref, bf16[1104,1536]{1,0:T(8,128)(2,1)S(1)} %times_pieces.2.query_ref.key_ref.value_ref, ...), custom_call_target="tpu_custom_call" | custom-call | flops 8000000000 | bytes 8000000 | tf_op jit(solution)/shard_map/attend/pallas_call | solution.py:405
  100.1 8.1 %attend.3 = (bf16[1104,256]{1,0:T(8,128)(2,1)S(1)}, f32[1,2,2,1104]{3,2,1,0:T(2,128)S(1)}) custom-call(bf16[1104,1536]{1,0:T(8,128)(2,1)S(1)} %times_pieces.2.query_ref.key_ref.value_ref, bf16[1104,1536]{1,0:T(8,128)(2,1)S(1)} %times_pieces.2.query_ref.key_ref.value_ref, bf16[1104,1536]{1,0:T(8,128)(2,1)S(1)} %times_pieces.2.query_ref.key_ref.value_ref, ...), custom_call_target="tpu_custom_call" | custom-call | flops 8000000000 | bytes 8000000 | tf_op jit(solution)/shard_map/attend/pallas_call | solution.py:405
  108.3 3.9 %times_pieces_turned.2.refs_1_ = bf16[1104,1024]{1,0:T(8,128)(2,1)} custom-call(bf16[1104,256]{1,0:T(8,128)(2,1)S(1)} %get-tuple-element.263.refs_0_.mixed_ref.refs_5_, bf16[1104,256]{1,0:T(8,128)(2,1)S(1)} %get-tuple-element.265.refs_1_.refs_6_.mixed_ref, ...), custom_call_target="tpu_custom_call" | custom-call | flops 3000000000 | bytes 3000000 | tf_op jit(solution)/shard_map/times_pieces_turned/pallas_call | solution.py:504
  112.2 10.2 %collective-permute-done.22 = bf16[4,128,512]{2,1,0:T(8,128)(2,1)S(1)} collective-permute-done((bf16[4,128,512]{2,1,0:T(8,128)(2,1)S(1)}, bf16[4,128,512]{2,1,0:T(8,128)(2,1)S(1)}, u32[]{:S(2)}, u32[]{:S(2)}) %collective-permute-start.22) | collective-permute-done | bytes 524320 | tf_op jit(solution)/shard_map/gather_step/ppermute | solution.py:47
  126.8 3.1 collective-permute-done.24.refs_2_
  131.8 4.6 %second_norm.1 = (f32[1104,1024]{1,0:T(8,128)S(1)}, bf16[1104,1024]{1,0:T(8,128)(2,1)S(1)}) custom-call(bf16[552,1024]{1,0:T(8,128)(2,1)} %fusion.12.refs_0_.own_ref.refs_4_, bf16[552,1024]{1,0:T(8,128)(2,1)} %collective-permute-done.14.refs_1_.next_ref, f32[1104,1]{1,0:T(8,128)S(1)} %broadcast_in_dim_reshape.3.refs_0_.live_ref, ...), custom_call_target="tpu_custom_call" | custom-call | flops 4000000000 | bytes 4000000 | tf_op jit(solution)/shard_map/second_norm/pallas_call | solution.py:602
  137.8 5.3 %collective-permute-done.23 = bf16[4,128,512]{2,1,0:T(8,128)(2,1)S(1)} collective-permute-done((bf16[4,128,512]{2,1,0:T(8,128)(2,1)}, bf16[4,128,512]{2,1,0:T(8,128)(2,1)S(1)}, u32[]{:S(2)}, u32[]{:S(2)}) %collective-permute-start.23) | collective-permute-done | bytes 524320 | tf_op jit(solution)/shard_map/gather_step/ppermute | solution.py:47
  145.0 22.3 %feed_forward.2 = (bf16[1104,1024]{1,0:T(8,128)(2,1)}, bf16[1104,1024]{1,0:T(8,128)(2,1)}, f32[1,1024]{1,0:T(1,128)S(1)}, bf16[2,2,256,512]{3,2,1,0:T(8,128)(2,1...) custom-call(s32[32]{0:T(128)S(1)} %and_select_fusion.places_ref, ...), custom_call_target="tpu_custom_call" | custom-call | flops 24999999488 | bytes 25000000 | tf_op jit(solution)/shard_map/feed_forward/pallas_call | solution.py:855
  171.2 23.8 %feed_forward.3 = (bf16[1104,1024]{1,0:T(8,128)(2,1)}, bf16[1104,1024]{1,0:T(8,128)(2,1)}, f32[1,1024]{1,0:T(1,128)S(1)}, bf16[2,2,256,512]{3,2,1,0:T(8,128)(2,1...) custom-call(s32[32]{0:T(128)S(1)} %and_select_fusion.places_ref, ...), custom_call_target="tpu_custom_call" | custom-call | flops 24999999488 | bytes 25000000 | tf_op jit(solution)/shard_map/feed_forward/pallas_call | solution.py:855
  202.5 7.8 %norm_back.1 = (f32[552,1024]{1,0:T(8,128)S(1)}, bf16[1104,1024]{1,0:T(8,128)(2,1)S(1)}, f32[4,1024]{1,0:T(4,128)S(1)}) custom-call(bf16[552,1024]{1,0:T(8,128)(2,1)} %get-tuple-element.281.refs_2_.own_ref, bf16[552,1024]{1,0:T(8,128)(2,1)} %collective-permute-done.15.refs_3_.next_ref, f32[1104,1]{1,0:T(8,128)S(1)} %copy-done.10, ...), custom_call_target="tpu_custom_call" | custom-call | flops 7000000000 | bytes 7000000 | tf_op jit(solution)/shard_map/norm_back/pallas_call | solution.py:659
  217.1 3.9 %collective-permute-start.35 = (bf16[4,64,512]{2,1,0:T(8,128)(2,1)S(1)}, bf16[4,64,512]{2,1,0:T(8,128)(2,1)S(1)}, u32[]{:S(2)}, u32[]{:S(2)}) collective-permute-start(bf16[4,64,512]{2,1,0:T(8,128)(2,1)S(1)} %pad_maximum_fusion.15), channel_id=1, source_target_pairs={{0,24},{2,26},{4,28},{6,30},{8,0},{10,2},{12,4},{14,6},{16,8},{18,... | collective-permute-start | bytes 786440 | tf_op jit(solution)/shard_map/reduce_z/ppermute | solution.py:51
  221.1 17.5 %attend_back.2 = (bf16[1104,256]{1,0:T(8,128)(2,1)S(1)}, bf16[1104,256]{1,0:T(8,128)(2,1)S(1)}, bf16[1104,256]{1,0:T(8,128)(2,1)S(1)}) custom-call(bf16[1104,1536]{1,0:T(8,128)(2,1)} %copy-done.34, bf16[1104,1536]{1,0:T(8,128)(2,1)} %copy-done.34, bf16[1104,1536]{1,0:T(8,128)(2,1)} %copy-done.34, f32[1,1,1104]{2,1,0:T(1,128)S(1)} %compare_select_fusion.invalid_ref, ...), custom_call_target="tpu_custom_call" | custom-call | flops 17999998976 | bytes 18000000 | tf_op jit(solution)/shard_map/attend_back/pallas_call | solution.py:424
  244.5 8.0 %weight_grads.2 = (bf16[5,256,256]{2,1,0:T(8,128)(2,1)}, bf16[5,256,256]{2,1,0:T(8,128)(2,1)}, bf16[5,256,256]{2,1,0:T(8,128)(2,1)}, bf16[5,256,256]{2,1,0:T(8,128)(2,1)}) custom-call(bf16[1104,1024]{1,0:T(8,128)(2,1)} %copy-done.30, bf16[1104,1024]{1,0:T(8,128)(2,1)} %copy-done.5, bf16[1104,256]{1,0:T(8,128)(2,1)} %copy-done.15, ...), custom_call_target="tpu_custom_call" | custom-call | flops 8499999744 | bytes 8500000 | tf_op jit(solution)/shard_map/weight_grads/pallas_call | solution.py:539
  253.5 3.2 collective-permute-done.37
  258.4 3.8 %collective-permute-start.43 = (bf16[4,64,512]{2,1,0:T(8,128)(2,1)S(1)}, bf16[4,64,512]{2,1,0:T(8,128)(2,1)S(1)}, u32[]{:S(2)}, u32[]{:S(2)}) collective-permute-start(bf16[4,64,512]{2,1,0:T(8,128)(2,1)S(1)} %pad_maximum_fusion.18), channel_id=1, source_target_pairs={{0,24},{2,26},{4,28},{6,30},{8,0},{10,2},{12,4},{14,6},{16,8},{18,... | collective-permute-start | bytes 786440 | tf_op jit(solution)/shard_map/reduce_z/ppermute | solution.py:51
  263.8 17.9 %attend_back.3 = (bf16[1104,256]{1,0:T(8,128)(2,1)S(1)}, bf16[1104,256]{1,0:T(8,128)(2,1)S(1)}, bf16[1104,256]{1,0:T(8,128)(2,1)S(1)}) custom-call(bf16[1104,1536]{1,0:T(8,128)(2,1)} %copy-done.34, bf16[1104,1536]{1,0:T(8,128)(2,1)} %copy-done.34, bf16[1104,1536]{1,0:T(8,128)(2,1)} %copy-done.34, f32[1,1,1104]{2,1,0:T(1,128)S(1)} %compare_select_fusion.invalid_ref, ...), custom_call_target="tpu_custom_call" | custom-call | flops 17999998976 | bytes 18000000 | tf_op jit(solution)/shard_map/attend_back/pallas_call | solution.py:424
  286.2 6.6 %times_pieces_turned.3 = (bf16[552,1024]{1,0:T(8,128)(2,1)}, bf16[552,1024]{1,0:T(8,128)(2,1)}) custom-call(bf16[1104,256]{1,0:T(8,128)(2,1)S(1)} %copy-done.16, bf16[1104,256]{1,0:T(8,128)(2,1)S(1)} %copy-done.18, bf16[1104,256]{1,0:T(8,128)(2,1)S(1)} %copy-done.20, bf16[1104,256]{1,0:T(8,128)(2,1)S(1)} %get-tuple-element.381.refs_1_.refs_3_, ...), custom_call_target="tpu_custom_call" | custom-call | flops 7000000000 | bytes 7000000 | tf_op jit(solution)/shard_map/times_pieces_turned/pallas_call | solution.py:504
  292.7 5.3 %weight_grads.3 = (bf16[3,256,256]{2,1,0:T(8,128)(2,1)}, bf16[3,256,256]{2,1,0:T(8,128)(2,1)}, bf16[3,256,256]{2,1,0:T(8,128)(2,1)}, bf16[3,256,256]{2,1,0:T(8,128)(2,1)}) custom-call(bf16[1104,1024]{1,0:T(8,128)(2,1)} %copy-done.30, bf16[1104,256]{1,0:T(8,128)(2,1)} %copy-done.21, bf16[1104,256]{1,0:T(8,128)(2,1)} %copy-done.22, bf16[1104,256]{1,0:T(8,128)(2,1)} %copy-done.23), custom_call_target="tpu_custom_call" | custom-call | flops 5500000256 | bytes 5500000 | tf_op jit(solution)/shard_map/weight_grads/pallas_call | solution.py:539
  305.9 3.3 first_norm_back.1
  310.5 2.9 collective-permute-start.57
  322.9 4.3 %collective-permute-done.52 = bf16[3,128,256]{2,1,0:T(8,128)(2,1)S(1)} collective-permute-done((bf16[3,128,256]{2,1,0:T(8,128)(2,1)S(1)}, bf16[3,128,256]{2,1,0:T(8,128)(2,1)S(1)}, u32[]{:S(2)}, u32[]{:S(2)}) %collective-permute-start.52) | collective-permute-done | bytes 196640 | tf_op jit(solution)/shard_map/reduce_middle/ppermute | solution.py:51
  328.3 2.4 fusion.14
  334.3 4.2 %fusion.13 = bf16[552,1024]{1,0:T(8,128)(2,1)} fusion(s32[1024]{0:T(1024)S(1)} %copy-done.67, f32[552,1024]{1,0:T(8,128)S(1)} %copy-done.35, f32[1104,1024]{1,0:T(8,128)} %copy-done.28, f32[1024]{0:T(1024)S(1)} %bitcast.173, f32[]{:T(128)} %bitcast.22), kind=kOutput, calls=%fused_computation.18 | convolution fusion | flops 1161502720 | bytes 5661184 | tf_op jit(solution)/shard_map/dot_general | solution.py:281
  (405 shorter events, 106.5 us)
Async XLA Ops:
  6.4 21.8 %collective-permute-start.1 = (bf16[4,72,512]{2,1,0:T(8,128)(2,1)S(1)}, bf16[4,72,512]{2,1,0:T(8,128)(2,1)S(1)}, u32[]{:S(2)}, u32[]{:S(2)}) collective-permute-start(bf16[4,72,512]{2,1,0:T(8,128)(2,1)S(1)} %fusion.18), channel_id=1, source_target_pairs={{16,0},{18,2},{20,4},{22,6},{24,8},{26,10},{28,12},{30,14},{0,16},... | collective-permute-start | bytes 884744 | tf_op jit(solution)/shard_map/gather_z/ppermute | solution.py:47
  9.0 19.2 %collective-permute-start = (bf16[4,72,512]{2,1,0:T(8,128)(2,1)S(1)}, bf16[4,72,512]{2,1,0:T(8,128)(2,1)S(1)}, u32[]{:S(2)}, u32[]{:S(2)}) collective-permute-start(bf16[4,72,512]{2,1,0:T(8,128)(2,1)S(1)} %fusion.18), channel_id=1, source_target_pairs={{8,0},{10,2},{12,4},{14,6},{16,8},{18,10},{20,12},{22,14},{24,16},... | collective-permute-start | bytes 884744 | tf_op jit(solution)/shard_map/gather_z/ppermute | solution.py:47
  12.2 16.0 %collective-permute-start.4 = (bf16[4,32,512]{2,1,0:T(8,128)(2,1)S(1)}, bf16[4,32,512]{2,1,0:T(8,128)(2,1)S(1)}, u32[]{:S(2)}, u32[]{:S(2)}) collective-permute-start(bf16[4,32,512]{2,1,0:T(8,128)(2,1)S(1)} %get-tuple-element.231), channel_id=1, source_target_pairs={{4,0},{6,2},{0,4},{2,6},{12,8},{14,10},{8,12},{10,14},{20,16},{22,... | collective-permute-start | bytes 393224 | tf_op jit(solution)/shard_map/gather_middle/ppermute | solution.py:47
  29.0 18.0 %collective-permute-start.8 = (bf16[4,8,64]{2,1,0:T(8,128)(2,1)S(1)}, bf16[4,8,64]{2,1,0:T(8,128)(2,1)S(1)}, u32[]{:S(2)}, u32[]{:S(2)}) collective-permute-start(bf16[4,8,64]{2,1,0:T(8,128)(2,1)S(1)} %pad_maximum_fusion.26), channel_id=1, source_target_pairs={{4,0},{6,2},{0,4},{2,6},{12,8},{14,10},{8,12},{10,14},{20,16},{22,... | collective-permute-start | bytes 12296 | tf_op jit(solution)/shard_map/gather_small/ppermute | solution.py:47
  31.7 19.2 %collective-permute-start.5 = (bf16[4,128,512]{2,1,0:T(8,128)(2,1)S(1)}, bf16[4,128,512]{2,1,0:T(8,128)(2,1)S(1)}, u32[]{:S(2)}, u32[]{:S(2)}) collective-permute-start(bf16[4,128,512]{2,1,0:T(8,128)(2,1)S(1)} %pad_maximum_fusion.2), channel_id=1, source_target_pairs={{2,0},{0,2},{6,4},{4,6},{10,8},{8,10},{14,12},{12,14},{18,16},{16,... | collective-permute-start | bytes 1572872 | tf_op jit(solution)/shard_map/gather_middle/ppermute | solution.py:47
  33.3 17.6 %collective-permute-start.6 = (bf16[4,128,512]{2,1,0:T(8,128)(2,1)S(1)}, bf16[4,128,512]{2,1,0:T(8,128)(2,1)S(1)}, u32[]{:S(2)}, u32[]{:S(2)}) collective-permute-start(bf16[4,128,512]{2,1,0:T(8,128)(2,1)S(1)} %pad_maximum_fusion.3), channel_id=1, source_target_pairs={{4,0},{6,2},{0,4},{2,6},{12,8},{14,10},{8,12},{10,14},{20,16},{22,... | collective-permute-start | bytes 1572872 | tf_op jit(solution)/shard_map/gather_middle/ppermute | solution.py:47
  50.9 24.8 %collective-permute-start.15 = (bf16[552,1024]{1,0:T(8,128)(2,1)}, bf16[552,1024]{1,0:T(8,128)(2,1)}, u32[]{:S(2)}, u32[]{:S(2)}) collective-permute-start(bf16[552,1024]{1,0:T(8,128)(2,1)} %get-tuple-element.281.refs_2_.own_ref), channel_id=1, source_target_pairs={{0,1},{1,0},{2,3},{3,2},{4,5},{5,4},{6,7},{7,6},{8,9},{9,8},{10,11... | collective-permute-start | bytes 3391496 | tf_op jit(solution)/shard_map/ppermute | solution.py:216
  51.6 25.6 %collective-permute-start.11 = (bf16[4,256,512]{2,1,0:T(8,128)(2,1)S(1)}, bf16[4,256,512]{2,1,0:T(8,128)(2,1)S(1)}, u32[]{:S(2)}, u32[]{:S(2)}) collective-permute-start(bf16[4,256,512]{2,1,0:T(8,128)(2,1)S(1)} %constant_dynamic-update-slice_fusion.2.refs_2_.refs_6_.refs_7_.refs_18_.refs_19_.refs_20_.refs_21_, ...), channel_id=1, source_target_pairs={{2,0},{0,2},{6,4},{4,6},{10,8},{8,10},{14,12},{12,14},{18,16},{16,... | collective-permute-start | bytes 3145736 | tf_op jit(solution)/shard_map/gather_last/ppermute | solution.py:47
  52.3 25.5 %collective-permute-start.10 = (bf16[4,256,512]{2,1,0:T(8,128)(2,1)S(1)}, bf16[4,256,512]{2,1,0:T(8,128)(2,1)}, u32[]{:S(2)}, u32[]{:S(2)}) collective-permute-start(bf16[4,256,512]{2,1,0:T(8,128)(2,1)S(1)} %constant_dynamic-update-slice_fusion.refs_0_.refs_2_.refs_3_.refs_6_.refs_7_.refs_8_.refs_9_.refs_10_., ...), channel_id=1, source_target_pairs={{4,0},{6,2},{0,4},{2,6},{12,8},{14,10},{8,12},{10,14},{20,16},{22,... | collective-permute-start | bytes 3145736 | tf_op jit(solution)/shard_map/gather_last/ppermute | solution.py:47
  56.6 19.0 %collective-permute-start.12 = (bf16[4,64,512]{2,1,0:T(8,128)(2,1)S(1)}, bf16[4,64,512]{2,1,0:T(8,128)(2,1)S(1)}, u32[]{:S(2)}, u32[]{:S(2)}) collective-permute-start(bf16[4,64,512]{2,1,0:T(8,128)(2,1)S(1)} %pad_maximum_fusion.13), channel_id=1, source_target_pairs={{16,0},{18,2},{20,4},{22,6},{24,8},{26,10},{28,12},{30,14},{0,16},... | collective-permute-start | bytes 786440 | tf_op jit(solution)/shard_map/gather_step/ppermute | solution.py:47
  77.9 17.3 %collective-permute-start.17 = (bf16[4,128,512]{2,1,0:T(8,128)(2,1)S(1)}, bf16[4,128,512]{2,1,0:T(8,128)(2,1)S(1)}, u32[]{:S(2)}, u32[]{:S(2)}) collective-permute-start(bf16[4,128,512]{2,1,0:T(8,128)(2,1)S(1)} %pad_maximum_fusion.5), channel_id=1, source_target_pairs={{2,0},{0,2},{6,4},{4,6},{10,8},{8,10},{14,12},{12,14},{18,16},{16,... | collective-permute-start | bytes 1572872 | tf_op jit(solution)/shard_map/gather_middle/ppermute | solution.py:47
  79.5 15.7 %collective-permute-start.18 = (bf16[4,128,512]{2,1,0:T(8,128)(2,1)S(1)}, bf16[4,128,512]{2,1,0:T(8,128)(2,1)S(1)}, u32[]{:S(2)}, u32[]{:S(2)}) collective-permute-start(bf16[4,128,512]{2,1,0:T(8,128)(2,1)S(1)} %pad_maximum_fusion.6), channel_id=1, source_target_pairs={{4,0},{6,2},{0,4},{2,6},{12,8},{14,10},{8,12},{10,14},{20,16},{22,... | collective-permute-start | bytes 1572872 | tf_op jit(solution)/shard_map/gather_middle/ppermute | solution.py:47
  95.4 27.7 %collective-permute-start.21 = (bf16[4,256,512]{2,1,0:T(8,128)(2,1)S(1)}, bf16[4,256,512]{2,1,0:T(8,128)(2,1)S(1)}, u32[]{:S(2)}, u32[]{:S(2)}) collective-permute-start(bf16[4,256,512]{2,1,0:T(8,128)(2,1)S(1)} %constant_dynamic-update-slice_fusion.8.refs_6_.refs_10_), channel_id=1, source_target_pairs={{2,0},{0,2},{6,4},{4,6},{10,8},{8,10},{14,12},{12,14},{18,16},{16,... | collective-permute-start | bytes 3145736 | tf_op jit(solution)/shard_map/gather_last/ppermute | solution.py:47
  97.0 26.1 %collective-permute-start.20 = (bf16[4,256,512]{2,1,0:T(8,128)(2,1)S(1)}, bf16[4,256,512]{2,1,0:T(8,128)(2,1)S(1)}, u32[]{:S(2)}, u32[]{:S(2)}) collective-permute-start(bf16[4,256,512]{2,1,0:T(8,128)(2,1)S(1)} %constant_dynamic-update-slice_fusion.6.refs_4_.refs_8_), channel_id=1, source_target_pairs={{4,0},{6,2},{0,4},{2,6},{12,8},{14,10},{8,12},{10,14},{20,16},{22,... | collective-permute-start | bytes 3145736 | tf_op jit(solution)/shard_map/gather_last/ppermute | solution.py:47
  98.6 23.7 %collective-permute-start.22 = (bf16[4,128,512]{2,1,0:T(8,128)(2,1)S(1)}, bf16[4,128,512]{2,1,0:T(8,128)(2,1)S(1)}, u32[]{:S(2)}, u32[]{:S(2)}) collective-permute-start(bf16[4,128,512]{2,1,0:T(8,128)(2,1)S(1)} %copy-done.37), channel_id=1, source_target_pairs={{16,0},{18,2},{20,4},{22,6},{24,8},{26,10},{28,12},{30,14},{0,16},... | collective-permute-start | bytes 1572872 | tf_op jit(solution)/shard_map/gather_step/ppermute | solution.py:47
  126.3 16.8 %collective-permute-start.23 = (bf16[4,128,512]{2,1,0:T(8,128)(2,1)}, bf16[4,128,512]{2,1,0:T(8,128)(2,1)S(1)}, u32[]{:S(2)}, u32[]{:S(2)}) collective-permute-start(bf16[4,128,512]{2,1,0:T(8,128)(2,1)} %pad_maximum_fusion.4), channel_id=1, source_target_pairs={{24,0},{26,2},{28,4},{30,6},{0,8},{2,10},{4,12},{6,14},{8,16},{10,... | collective-permute-start | bytes 1572872 | tf_op jit(solution)/shard_map/gather_step/ppermute | solution.py:47
  143.5 24.8 %collective-permute-start.25 = (bf16[4,256,512]{2,1,0:T(8,128)(2,1)S(1)}, bf16[4,256,512]{2,1,0:T(8,128)(2,1)S(1)}, u32[]{:S(2)}, u32[]{:S(2)}) collective-permute-start(bf16[4,256,512]{2,1,0:T(8,128)(2,1)S(1)} %bitcast.147), channel_id=1, source_target_pairs={{4,0},{6,2},{0,4},{2,6},{12,8},{14,10},{8,12},{10,14},{20,16},{22,... | collective-permute-start | bytes 3145736 | tf_op jit(solution)/shard_map/gather_last/ppermute | solution.py:47
  144.4 24.6 %collective-permute-start.26 = (bf16[4,256,512]{2,1,0:T(8,128)(2,1)S(1)}, bf16[4,256,512]{2,1,0:T(8,128)(2,1)S(1)}, u32[]{:S(2)}, u32[]{:S(2)}) collective-permute-start(bf16[4,256,512]{2,1,0:T(8,128)(2,1)S(1)} %bitcast.150), channel_id=1, source_target_pairs={{2,0},{0,2},{6,4},{4,6},{10,8},{8,10},{14,12},{12,14},{18,16},{16,... | collective-permute-start | bytes 3145736 | tf_op jit(solution)/shard_map/gather_last/ppermute | solution.py:47
  168.9 27.2 %collective-permute-start.27 = (bf16[4,256,512]{2,1,0:T(8,128)(2,1)}, bf16[4,256,512]{2,1,0:T(8,128)(2,1)S(1)}, u32[]{:S(2)}, u32[]{:S(2)}) collective-permute-start(bf16[4,256,512]{2,1,0:T(8,128)(2,1)} %bitcast.181), channel_id=1, source_target_pairs={{0,4},{2,6},{4,0},{6,2},{8,12},{10,14},{12,8},{14,10},{16,20},{18,... | collective-permute-start | bytes 3145736 | tf_op jit(solution)/shard_map/reduce_last/ppermute | solution.py:51
  170.3 25.8 %collective-permute-start.28 = (bf16[4,256,512]{2,1,0:T(8,128)(2,1)}, bf16[4,256,512]{2,1,0:T(8,128)(2,1)S(1)}, u32[]{:S(2)}, u32[]{:S(2)}) collective-permute-start(bf16[4,256,512]{2,1,0:T(8,128)(2,1)} %bitcast.180), channel_id=1, source_target_pairs={{0,2},{2,0},{4,6},{6,4},{8,10},{10,8},{12,14},{14,12},{16,18},{18,... | collective-permute-start | bytes 3145736 | tf_op jit(solution)/shard_map/reduce_last/ppermute | solution.py:51
  210.3 30.3 %collective-permute-start.30 = (bf16[4,256,512]{2,1,0:T(8,128)(2,1)}, bf16[4,256,512]{2,1,0:T(8,128)(2,1)}, u32[]{:S(2)}, u32[]{:S(2)}) collective-permute-start(bf16[4,256,512]{2,1,0:T(8,128)(2,1)} %bitcast.51), channel_id=1, source_target_pairs={{0,4},{2,6},{4,0},{6,2},{8,12},{10,14},{12,8},{14,10},{16,20},{18,... | collective-permute-start | bytes 3145736 | tf_op jit(solution)/shard_map/reduce_last/ppermute | solution.py:51
  211.7 28.9 %collective-permute-start.31 = (bf16[4,256,512]{2,1,0:T(8,128)(2,1)}, bf16[4,256,512]{2,1,0:T(8,128)(2,1)S(1)}, u32[]{:S(2)}, u32[]{:S(2)}) collective-permute-start(bf16[4,256,512]{2,1,0:T(8,128)(2,1)} %bitcast.53), channel_id=1, source_target_pairs={{0,2},{2,0},{4,6},{6,4},{8,10},{10,8},{12,14},{14,12},{16,18},{18,... | collective-permute-start | bytes 3145736 | tf_op jit(solution)/shard_map/reduce_last/ppermute | solution.py:51
  217.0 23.6 %collective-permute-start.34 = (bf16[4,64,512]{2,1,0:T(8,128)(2,1)S(1)}, bf16[4,64,512]{2,1,0:T(8,128)(2,1)S(1)}, u32[]{:S(2)}, u32[]{:S(2)}) collective-permute-start(bf16[4,64,512]{2,1,0:T(8,128)(2,1)S(1)} %pad_maximum_fusion.14), channel_id=1, source_target_pairs={{0,8},{2,10},{4,12},{6,14},{8,16},{10,18},{12,20},{14,22},{16,24},... | collective-permute-start | bytes 786440 | tf_op jit(solution)/shard_map/reduce_z/ppermute | solution.py:51
  217.1 23.5 %collective-permute-start.35 = (bf16[4,64,512]{2,1,0:T(8,128)(2,1)S(1)}, bf16[4,64,512]{2,1,0:T(8,128)(2,1)S(1)}, u32[]{:S(2)}, u32[]{:S(2)}) collective-permute-start(bf16[4,64,512]{2,1,0:T(8,128)(2,1)S(1)} %pad_maximum_fusion.15), channel_id=1, source_target_pairs={{0,24},{2,26},{4,28},{6,30},{8,0},{10,2},{12,4},{14,6},{16,8},{18,... | collective-permute-start | bytes 786440 | tf_op jit(solution)/shard_map/reduce_z/ppermute | solution.py:51
  221.0 17.7 %collective-permute-start.36 = (bf16[552,1024]{1,0:T(8,128)(2,1)S(1)}, bf16[552,1024]{1,0:T(8,128)(2,1)S(1)}, u32[]{:S(2)}, u32[]{:S(2)}) collective-permute-start(bf16[552,1024]{1,0:T(8,128)(2,1)S(1)} %slice.612), channel_id=1, source_target_pairs={{0,1},{1,0},{2,3},{3,2},{4,5},{5,4},{6,7},{7,6},{8,9},{9,8},{10,11... | collective-permute-start | bytes 3391496 | tf_op jit(solution)/shard_map/ppermute | solution.py:216
  258.2 23.9 %collective-permute-start.42 = (bf16[4,64,512]{2,1,0:T(8,128)(2,1)S(1)}, bf16[4,64,512]{2,1,0:T(8,128)(2,1)S(1)}, u32[]{:S(2)}, u32[]{:S(2)}) collective-permute-start(bf16[4,64,512]{2,1,0:T(8,128)(2,1)S(1)} %pad_maximum_fusion.17), channel_id=1, source_target_pairs={{0,8},{2,10},{4,12},{6,14},{8,16},{10,18},{12,20},{14,22},{16,24},... | collective-permute-start | bytes 786440 | tf_op jit(solution)/shard_map/reduce_z/ppermute | solution.py:51
  258.4 23.7 %collective-permute-start.43 = (bf16[4,64,512]{2,1,0:T(8,128)(2,1)S(1)}, bf16[4,64,512]{2,1,0:T(8,128)(2,1)S(1)}, u32[]{:S(2)}, u32[]{:S(2)}) collective-permute-start(bf16[4,64,512]{2,1,0:T(8,128)(2,1)S(1)} %pad_maximum_fusion.18), channel_id=1, source_target_pairs={{0,24},{2,26},{4,28},{6,30},{8,0},{10,2},{12,4},{14,6},{16,8},{18,... | collective-permute-start | bytes 786440 | tf_op jit(solution)/shard_map/reduce_z/ppermute | solution.py:51
  262.1 20.0 %collective-permute-start.40 = (bf16[5,256,256]{2,1,0:T(8,128)(2,1)S(1)}, bf16[5,256,256]{2,1,0:T(8,128)(2,1)S(1)}, u32[]{:S(2)}, u32[]{:S(2)}) collective-permute-start(bf16[5,256,256]{2,1,0:T(8,128)(2,1)S(1)} %copy-done.79), channel_id=1, source_target_pairs={{0,4},{2,6},{4,0},{6,2},{8,12},{10,14},{12,8},{14,10},{16,20},{18,... | collective-permute-start | bytes 1966088 | tf_op jit(solution)/shard_map/reduce_last/ppermute | solution.py:51
  262.8 19.3 %collective-permute-start.41 = (bf16[5,256,256]{2,1,0:T(8,128)(2,1)S(1)}, bf16[5,256,256]{2,1,0:T(8,128)(2,1)S(1)}, u32[]{:S(2)}, u32[]{:S(2)}) collective-permute-start(bf16[5,256,256]{2,1,0:T(8,128)(2,1)S(1)} %copy-done.78), channel_id=1, source_target_pairs={{0,2},{2,0},{4,6},{6,4},{8,10},{10,8},{12,14},{14,12},{16,18},{18,... | collective-permute-start | bytes 1966088 | tf_op jit(solution)/shard_map/reduce_last/ppermute | solution.py:51
  282.1 15.9 %collective-permute-start.46 = (bf16[4,64,512]{2,1,0:T(8,128)(2,1)S(1)}, bf16[4,64,512]{2,1,0:T(8,128)(2,1)S(1)}, u32[]{:S(2)}, u32[]{:S(2)}) collective-permute-start(bf16[4,64,512]{2,1,0:T(8,128)(2,1)S(1)} %pad_maximum_fusion.19), channel_id=1, source_target_pairs={{0,16},{2,18},{4,20},{6,22},{8,24},{10,26},{12,28},{14,30},{16,0},... | collective-permute-start | bytes 786440 | tf_op jit(solution)/shard_map/reduce_z/ppermute | solution.py:51
  300.7 22.2 %collective-permute-start.55 = (bf16[5,64,256]{2,1,0:T(8,128)(2,1)}, bf16[5,64,256]{2,1,0:T(8,128)(2,1)}, u32[]{:S(2)}, u32[]{:S(2)}) collective-permute-start(bf16[5,64,256]{2,1,0:T(8,128)(2,1)} %pad_maximum_fusion.20), channel_id=1, source_target_pairs={{0,8},{2,10},{4,12},{6,14},{8,16},{10,18},{12,20},{14,22},{16,24},... | collective-permute-start | bytes 491528 | tf_op jit(solution)/shard_map/reduce_z/ppermute | solution.py:51
  301.4 21.4 %collective-permute-start.56 = (bf16[5,64,256]{2,1,0:T(8,128)(2,1)}, bf16[5,64,256]{2,1,0:T(8,128)(2,1)}, u32[]{:S(2)}, u32[]{:S(2)}) collective-permute-start(bf16[5,64,256]{2,1,0:T(8,128)(2,1)} %pad_maximum_fusion.21), channel_id=1, source_target_pairs={{0,16},{2,18},{4,20},{6,22},{8,24},{10,26},{12,28},{14,30},{16,0},... | collective-permute-start | bytes 491528 | tf_op jit(solution)/shard_map/reduce_z/ppermute | solution.py:51
  (111 other events, 1182.9 us)

commit v5 on v4

--- a/solution.py
+++ b/solution.py
@@ -412,7 +412,7 @@
             jax.ShapeDtypeStruct((slots, count, 2, SEQ_LEN), F32),
         ],
         scratch_shapes=[pltpu.VMEM((2 * HEAD_DIM, SEQ_LEN), F32)],
-        compiler_params=params(48),
+        compiler_params=params(14),
         cost_estimate=cost(4 * slots * count),
         name="attend",
     )(packed, packed, packed, invalid)
@@ -420,7 +420,7 @@
 
 def attend_back(packed, invalid, mixed, total, grad_mixed, first, count):
     slots, pairs = invalid.shape[0], packed.shape[1] // (6 * HEAD_DIM)
-    columns, invalid_spec, total_spec = attend_specs()
+    columns, invalid_spec, _ = attend_specs()
     return pl.pallas_call(
         attend_back_kernel,
         grid=(slots, count),
@@ -429,8 +429,8 @@
             columns(pairs + first),
             columns(2 * pairs + first),
             invalid_spec,
-            columns(0),
-            total_spec,
+            columns(first),
+            pl.BlockSpec((1, 1, 2, SEQ_LEN), lambda s, p: (s, p + first, 0, 0)),
             columns(first),
         ],
         out_specs=[columns(0)] * 3,
@@ -440,7 +440,7 @@
             pltpu.VMEM((SEQ_LEN, SEQ_LEN), BF16),
             pltpu.VMEM((SEQ_LEN, SEQ_LEN), BF16),
         ],
-        compiler_params=params(48),
+        compiler_params=params(22),
         cost_estimate=cost(9 * slots * count),
         name="attend_back",
     )(packed, packed, packed, invalid, mixed, total, grad_mixed)
@@ -469,7 +469,7 @@
         + [pl.BlockSpec((1, p.shape[1], wide), lambda j: (first + j, 0, 0)) for p in pieces],
         out_specs=pl.BlockSpec((rows.shape[0], wide), lambda j: (0, j)),
         out_shape=jax.ShapeDtypeStruct((rows.shape[0], count * wide), BF16),
-        compiler_params=params(40),
+        compiler_params=params(12),
         cost_estimate=cost(2 * count),
         name="times_pieces",
     )(rows, *pieces)
@@ -507,7 +507,7 @@
         in_specs=[whole_spec(c) for c in columns] + [place_spec(p, *q) for p in pieces for q in places],
         out_specs=[pl.BlockSpec((rows // cuts, starts[-1]), lambda i: (0, 0))] * cuts,
         out_shape=[jax.ShapeDtypeStruct((rows // cuts, starts[-1]), BF16)] * cuts,
-        compiler_params=params(48),
+        compiler_params=params(16),
         cost_estimate=cost(1 + count),
         name="times_pieces_turned",
     )(*columns, *[p for p in pieces for _ in places])
@@ -515,12 +515,14 @@
 
 
 def weight_grads(lefts, rights, piece_rows, fits):
+    wide = rights[0].shape[1]
+    rights = [r if isinstance(r, tuple) else (r, 0) for r in rights]
     starts = np.cumsum([0] + piece_rows).tolist()
     if not fits:
-        full = jnp.stack([dot_tn(a, b).astype(BF16) for a, b in zip(lefts, rights)])
+        blocks = [a[:, c * wide : (c + 1) * wide] for a, c in rights]
+        full = jnp.stack([dot_tn(a, b).astype(BF16) for a, b in zip(lefts, blocks)])
         return [full[:, s:e] for s, e in zip(starts, starts[1:])]
     count = len(rights)
-    wide = rights[0].shape[1]
     names = []
     for left in lefts:
         if not any(left is other for other in names):
@@ -539,13 +541,14 @@
     return pl.pallas_call(
         kernel,
         grid=(1,),
-        in_specs=[whole_spec(a) for a in names + list(rights)],
+        in_specs=[whole_spec(a) for a in names]
+        + [pl.BlockSpec((a.shape[0], wide), lambda i, c=c: (0, c)) for a, c in rights],
         out_specs=[pl.BlockSpec((count, r, wide), lambda i: (0, 0, 0)) for r in piece_rows],
         out_shape=[jax.ShapeDtypeStruct((count, r, wide), BF16) for r in piece_rows],
-        compiler_params=params(56),
+        compiler_params=params(20),
         cost_estimate=cost(1 + 1.5 * count),
         name="weight_grads",
-    )(*names, *rights)
+    )(*names, *[a for a, _ in rights])
 
 
 def joined_rows(parts):
@@ -573,7 +576,7 @@
     return pl.pallas_call(
         kernel,
         out_shape=jax.ShapeDtypeStruct((rows, width), BF16),
-        compiler_params=params(40),
+        compiler_params=params(12),
         cost_estimate=cost(3),
         name="first_norm",
     )(*rows_in, gain, bias)
@@ -612,7 +615,7 @@
         + [whole_spec(shift)] * 3,
         out_specs=[block(width), block(width)],
         out_shape=[
-            jax.ShapeDtypeStruct((rows, width), F32),
+            pltpu.HBM((rows, width), F32),
             jax.ShapeDtypeStruct((rows, width), BF16),
         ],
         compiler_params=params(40),
@@ -678,7 +681,7 @@
             jax.ShapeDtypeStruct((rows, width), BF16),
             jax.ShapeDtypeStruct((4, width), F32),
         ],
-        compiler_params=params(40),
+        compiler_params=params(44),
         cost_estimate=cost(7),
         name="norm_back",
     )(*grad_out, live, mine, other, middle, gain)
@@ -710,7 +713,7 @@
             jax.ShapeDtypeStruct((rows, width), BF16),
             jax.ShapeDtypeStruct((2, width), F32),
         ],
-        compiler_params=params(40),
+        compiler_params=params(14),
         cost_estimate=cost(4),
         name="first_norm_back",
     )(grad_middle, rest, mine, other, rows_in, gain)
@@ -769,11 +772,6 @@
         for sum_ref, _, left, right, start in products:
             product = dot_nt(left, right)
             sum_ref[...] = product + start[0][...].astype(F32) if carried else product
-
-    @pl.when((step > 0) & (step < last))
-    def _():
-        for sum_ref, _, left, right, _ in products:
-            sum_ref[...] += dot_nt(left, right)
 
     @pl.when(step == last)
     def _():
@@ -850,7 +848,7 @@
             pl.BlockSpec((2, 1, r, tile), lambda j, p: (0, j // split, 0, j % split))
             for r in piece_rows
         ]
-        grad_shapes = [jax.ShapeDtypeStruct((2, 2, r, half), BF16) for r in piece_rows]
+        grad_shapes = [pltpu.HBM((2, 2, r, half), BF16) for r in piece_rows]
     before = tuple(before)
     outs = pl.pallas_call(
         functools.partial(
@@ -888,7 +886,7 @@
             jax.ShapeDtypeStruct((1, units), F32),
         ]
         + grad_shapes,
-        compiler_params=params(52),
+        compiler_params=params(44),
         cost_estimate=cost(25),
         name="feed_forward",
     )(places, normed, shift, *grads, *pieces, *pieces, *before)
@@ -1005,17 +1003,14 @@
     pairs = width_here // (2 * HEAD_DIM)
     parts = 2 if pairs % 2 == 0 else 1
     share = pairs // parts
-    forward = [attend(packed, invalid, 0, share)]
-    first_halves, second_along, forward, packed, attn_pieces, norm_one = join(
-        first_halves, second_along, forward, packed, attn_pieces, norm_one
+    first_halves, second_along, packed, attn_pieces, norm_one = join(
+        first_halves, second_along, packed, attn_pieces, norm_one
     )
 
     first_pieces = grid.finish(first_halves)
     second_along += grid.steps(second_along[0], 0, (2,))
-    if parts == 2:
-        forward = forward + [attend(packed, invalid, share, share)]
-    mixed = [f[0] for f in forward]
-    attn_out = times_pieces_turned(mixed, attn_pieces, [(3, p) for p in range(parts)], fits)
+    mixed, total = attend(packed, invalid, 0, pairs)
+    attn_out = times_pieces_turned([mixed], attn_pieces, [(3, 0)], fits)
     first_pieces, second_along, attn_out = join(first_pieces, second_along, attn_out)
 
     second_along += grid.steps(second_along[0], 0, (3,))
@@ -1052,12 +1047,16 @@
     middle_a, grad_mixed, mlp_out = join(middle_a, grad_mixed, mlp_out)
 
     def back(part):
-        return attend_back(packed, invalid, *forward[part], grad_mixed, part * share, share)
+        packed_late, mixed_late, total_late, late = join(packed, mixed, total, grad_mixed)
+        return attend_back(
+            packed_late, invalid, mixed_late, total_late, late, part * share, share
+        )
 
     def grads(part, columns):
         lefts, rights = (norm_one,) * 3, tuple(columns)
         if part == 0:
-            lefts, rights = lefts + (grad_branch,) * parts, rights + tuple(mixed)
+            lefts = lefts + (grad_branch,) * parts
+            rights = rights + tuple((mixed, p) for p in range(parts))
         return weight_grads(lefts, rights, piece_rows, fits)
 
     pieces_a = grid.first_pieces(middle_a)
@@ -1107,10 +1106,12 @@
     bias_grads = dot_nn(bias_grads.transpose(1, 0, 2).reshape(bias_columns, width), select)
     small_grads = jnp.concatenate([sums_one, sums, bias_grads], axis=0)
     small_grads = grid.blocks_of(small_grads)
+    small_grads, grad_rows, _ = join(small_grads, grad_rows, [m[0] for m in middle_d])
+    grad_inputs = dot_nt(grad_rows, select).astype(BF16)
     small_grads = grid.reduce_small(small_grads, 2)
     small_grads = grid.reduce_small(small_grads, 1)
-    middle_d, small_grads, first_c, grad_rows, mlp_out = join(
-        middle_d, small_grads, first_c, grad_rows, mlp_out
+    middle_d, small_grads, first_c, grad_inputs, mlp_out = join(
+        middle_d, small_grads, first_c, grad_inputs, mlp_out
     )
 
     if parts == 2:
@@ -1124,7 +1125,6 @@
         sum_d, small_grads = sum_d[:, :block], sum_d[0, block:, :block]
     else:
         small_grads = grid.reduce_small(small_grads, 0)
-    grad_inputs = dot_nt(grad_rows, select).astype(BF16)
     result = pair.own(middle) + own_live * (mlp_out + fc2_shift)
     outputs = dot_nt(result.astype(BF16), select).astype(BF16)
     first_a, first_b = grid.reduce_end(first_a), grid.reduce_end(first_b)

time: 348 us -> 337 us (0.968)
  Pallas kernels: 148 us -> 138 us
    pallas_call x2, Pallas kernels: 13.3 us -> 5.95 us  [weight_grads(): pl.pallas_call(kernel, grid=(1,), in_specs=[whole_spec(a) for a in names]...]
    ppermute x30, waiting for transfers between devices: 15.7 us -> 22 us  [push(): return lax.ppermute(value, 'dp', pairs)]
    unnamed x167 -> x117, local copies, waits for them, and re-layouts: 12.5 us -> 9.08 us
    pallas_call x2 -> x1, Pallas kernels: 16.2 us -> 16.2 us  [attend(): pl.pallas_call(attend_kernel, grid=(slots, count), in_specs=[columns(firs...]
  transfers between devices with their start and end apart: 61 -> 61, of which waited for: 20 -> 24; matrix products, arithmetic and copies ran while one was open for 9% -> 10% of each run, Pallas kernels for 43% -> 42%
where the time goes in v5:
time: 337 us; the launch traced here: 331 us
  Pallas kernels  138 us (41%)
  starting transfers between devices  74.6 us (22%)
  waiting for transfers between devices  67.8 us (20%)
  local copies, waits for them, and re-layouts  20.3 us (6%)
  other arithmetic  15.8 us (5%)
  matrix products  11.7 us (3%)
    pallas_call x2, Pallas kernels, feed_forward(): pl.pallas_call(functools.partial(feed_kernel, (len(grads), len(pieces), l...  45 us
    ppermute x23, waiting for transfers between devices, fetch(): return lax.ppermute(value, 'dp', pairs)  44.7 us
    ppermute x23, starting transfers between devices, fetch(): return lax.ppermute(value, 'dp', pairs)  39.3 us
    ppermute x30, starting transfers between devices, push(): return lax.ppermute(value, 'dp', pairs)  35 us
    pallas_call x2, Pallas kernels, attend_back(): pl.pallas_call(attend_back_kernel, grid=(slots, count), in_specs=[columns...  34 us
    ppermute x30, waiting for transfers between devices, push(): return lax.ppermute(value, 'dp', pairs)  22 us
    pallas_call x1, Pallas kernels, attend(): pl.pallas_call(attend_kernel, grid=(slots, count), in_specs=[columns(firs...  16.2 us
    unnamed x117, local copies, waits for them, and re-layouts  9.08 us
  transfers between devices with their start and end apart: 61, of which 24 were waited for; matrix products, arithmetic and copies ran while one was open for 10% of the time, Pallas kernels for 42%

profile of v5, /device:TPU:0, one launch (start us, length us, event | category | flops | bytes accessed | tf_op | source)
XLA Modules:
  0.0 330.7 jit_solution(4601458294358868267)
XLA Ops:
  3.3 3.1 collective-permute-start.2
  6.4 2.6 collective-permute-start.1
  16.4 11.8 %collective-permute-done.1 = bf16[4,72,512]{2,1,0:T(8,128)(2,1)S(1)} collective-permute-done((bf16[4,72,512]{2,1,0:T(8,128)(2,1)S(1)}, bf16[4,72,512]{2,1,0:T(8,128)(2,1)S(1)}, u32[]{:S(2)}, u32[]{:S(2)}) %collective-permute-start.1) | collective-permute-done | bytes 294944 | tf_op jit(solution)/shard_map/gather_z/ppermute | solution.py:47
  34.3 2.4 fusion.12.refs_0_.own_ref.refs_4_
  36.7 7.8 %collective-permute-start.7 = (bf16[4,64,512]{2,1,0:T(8,128)(2,1)S(1)}, bf16[4,64,512]{2,1,0:T(8,128)(2,1)S(1)}, u32[]{:S(2)}, u32[]{:S(2)}) collective-permute-start(bf16[4,64,512]{2,1,0:T(8,128)(2,1)S(1)} %pad_maximum_fusion.13), channel_id=1, source_target_pairs={{8,0},{10,2},{12,4},{14,6},{16,8},{18,10},{20,12},{22,14},{24,16},... | collective-permute-start | bytes 786440 | tf_op jit(solution)/shard_map/gather_step/ppermute | solution.py:47
  44.6 2.8 multiply_convert_fusion
  59.1 3.2 first_norm.1.rows_ref.refs_0_
  62.4 5.0 %collective-permute-done.13 = bf16[4,64,512]{2,1,0:T(8,128)(2,1)S(1)} collective-permute-done((bf16[4,64,512]{2,1,0:T(8,128)(2,1)S(1)}, bf16[4,64,512]{2,1,0:T(8,128)(2,1)S(1)}, u32[]{:S(2)}, u32[]{:S(2)}) %collective-permute-start.13) | collective-permute-done | bytes 262176 | tf_op jit(solution)/shard_map/gather_step/ppermute | solution.py:47
  67.3 10.1 %collective-permute-done.12 = bf16[4,64,512]{2,1,0:T(8,128)(2,1)S(1)} collective-permute-done((bf16[4,64,512]{2,1,0:T(8,128)(2,1)S(1)}, bf16[4,64,512]{2,1,0:T(8,128)(2,1)S(1)}, u32[]{:S(2)}, u32[]{:S(2)}) %collective-permute-start.12) | collective-permute-done | bytes 262176 | tf_op jit(solution)/shard_map/gather_step/ppermute | solution.py:47
  82.6 5.2 %times_pieces.2.query_ref.key_ref.value_ref = bf16[1104,1536]{1,0:T(8,128)(2,1)S(1)} custom-call(bf16[1104,1024]{1,0:T(8,128)(2,1)S(1)} %first_norm.1.rows_ref.refs_0_, bf16[4,256,512]{2,1,0:T(8,128)(2,1)S(1)} %constant_dynamic-update-slice_fusion.refs_0_.refs_1_.refs_6_.refs_7_.refs_8_.refs_9_.refs_10_.refs_11_, ...), custom_call_target="tpu_custom_call" | custom-call | flops 6000000000 | bytes 6000000 | tf_op jit(solution)/shard_map/times_pieces/pallas_call | solution.py:465
  87.9 3.7 %collective-permute-done.17 = bf16[4,128,512]{2,1,0:T(8,128)(2,1)S(1)} collective-permute-done((bf16[4,128,512]{2,1,0:T(8,128)(2,1)S(1)}, bf16[4,128,512]{2,1,0:T(8,128)(2,1)S(1)}, u32[]{:S(2)}, u32[]{:S(2)}) %collective-permute-start.17) | collective-permute-done | bytes 524320 | tf_op jit(solution)/shard_map/gather_middle/ppermute | solution.py:47
  97.7 16.2 %attend.1 = (bf16[1104,512]{1,0:T(8,128)(2,1)S(1)}, f32[1,4,2,1104]{3,2,1,0:T(2,128)S(1)}) custom-call(bf16[1104,1536]{1,0:T(8,128)(2,1)S(1)} %times_pieces.2.query_ref.key_ref.value_ref, bf16[1104,1536]{1,0:T(8,128)(2,1)S(1)} %times_pieces.2.query_ref.key_ref.value_ref, bf16[1104,1536]{1,0:T(8,128)(2,1)S(1)} %times_pieces.2.query_ref.key_ref.value_ref, ...), custom_call_target="tpu_custom_call" | custom-call | flops 16000000000 | bytes 16000000 | tf_op jit(solution)/shard_map/attend/pallas_call | solution.py:405
  114.0 3.9 %times_pieces_turned.2.refs_1_ = bf16[1104,1024]{1,0:T(8,128)(2,1)} custom-call(bf16[1104,512]{1,0:T(8,128)(2,1)S(1)} %get-tuple-element.377.refs_0_.mixed_ref.refs_5_.refs_6_, bf16[4,256,512]{2,1,0:T(8,128)(2,1)S(1)} %constant_dynamic-update-slice_fusion.refs_0_.refs_1_.refs_6_.refs_7_.refs_8_.refs_9_.refs_10_.refs_11_, ...), custom_call_target="tpu_custom_call" | custom-call | flops 2000000000 | bytes 2000000 | tf_op jit(solution)/shard_map/times_pieces_turned/pallas_call | solution.py:504
  121.9 3.0 collective-permute-start.23
  125.6 5.8 %second_norm.1 = (f32[1104,1024]{1,0:T(8,128)}, bf16[1104,1024]{1,0:T(8,128)(2,1)S(1)}) custom-call(bf16[552,1024]{1,0:T(8,128)(2,1)} %fusion.12.refs_0_.own_ref.refs_4_, bf16[552,1024]{1,0:T(8,128)(2,1)} %collective-permute-done.14.refs_1_.next_ref, f32[1104,1]{1,0:T(8,128)S(1)} %broadcast_in_dim_reshape.3.refs_0_.live_ref, ...), custom_call_target="tpu_custom_call" | custom-call | flops 4000000000 | bytes 4000000 | tf_op jit(solution)/shard_map/second_norm/pallas_call | solution.py:605
  131.4 7.0 %collective-permute-done.23 = bf16[4,128,512]{2,1,0:T(8,128)(2,1)S(1)} collective-permute-done((bf16[4,128,512]{2,1,0:T(8,128)(2,1)}, bf16[4,128,512]{2,1,0:T(8,128)(2,1)S(1)}, u32[]{:S(2)}, u32[]{:S(2)}) %collective-permute-start.23) | collective-permute-done | bytes 524320 | tf_op jit(solution)/shard_map/gather_step/ppermute | solution.py:47
  141.3 21.6 %feed_forward.2 = (bf16[1104,1024]{1,0:T(8,128)(2,1)S(1)}, bf16[1104,1024]{1,0:T(8,128)(2,1)}, f32[1,1024]{1,0:T(1,128)S(1)}, bf16[2,2,256,512]{3,2,1,0:T(8,128)...) custom-call(s32[32]{0:T(128)S(1)} %and_select_fusion.places_ref, ...), custom_call_target="tpu_custom_call" | custom-call | flops 24999999488 | bytes 25000000 | tf_op jit(solution)/shard_map/feed_forward/pallas_call | solution.py:853
  166.1 23.4 %feed_forward.3 = (bf16[1104,1024]{1,0:T(8,128)(2,1)S(1)}, bf16[1104,1024]{1,0:T(8,128)(2,1)}, f32[1,1024]{1,0:T(1,128)S(1)}, bf16[2,2,256,512]{3,2,1,0:T(8,128)...) custom-call(s32[32]{0:T(128)S(1)} %and_select_fusion.places_ref, ...), custom_call_target="tpu_custom_call" | custom-call | flops 24999999488 | bytes 25000000 | tf_op jit(solution)/shard_map/feed_forward/pallas_call | solution.py:853
  197.4 7.8 %norm_back.1 = (f32[552,1024]{1,0:T(8,128)S(1)}, bf16[1104,1024]{1,0:T(8,128)(2,1)S(1)}, f32[4,1024]{1,0:T(4,128)S(1)}) custom-call(bf16[552,1024]{1,0:T(8,128)(2,1)} %get-tuple-element.284.refs_2_.own_ref, bf16[552,1024]{1,0:T(8,128)(2,1)} %collective-permute-done.15.refs_3_.next_ref, f32[1104,1]{1,0:T(8,128)S(1)} %copy-done.7, ...), custom_call_target="tpu_custom_call" | custom-call | flops 7000000000 | bytes 7000000 | tf_op jit(solution)/shard_map/norm_back/pallas_call | solution.py:662
  207.1 2.4 times_pieces.3.grad_ref
  213.0 2.8 collective-permute-start.35
  216.0 17.0 %attend_back.2 = (bf16[1104,256]{1,0:T(8,128)(2,1)S(1)}, bf16[1104,256]{1,0:T(8,128)(2,1)S(1)}, bf16[1104,256]{1,0:T(8,128)(2,1)S(1)}) custom-call(bf16[1104,1536]{1,0:T(8,128)(2,1)S(1)} %copy-done.24, bf16[1104,1536]{1,0:T(8,128)(2,1)S(1)} %copy-done.24, bf16[1104,1536]{1,0:T(8,128)(2,1)S(1)} %copy-done.24, ...), custom_call_target="tpu_custom_call" | custom-call | flops 17999998976 | bytes 18000000 | tf_op jit(solution)/shard_map/attend_back/pallas_call | solution.py:424
  238.1 3.6 %weight_grads.2 = (bf16[5,256,256]{2,1,0:T(8,128)(2,1)S(1)}, bf16[5,256,256]{2,1,0:T(8,128)(2,1)S(1)}, bf16[5,256,256]{2,1,0:T(8,128)(2,1)S(1)}, bf16[5,256,256]{2,1,0:T(8,128)(2,1)S(1)}) custom-call(bf16[1104,1024]{1,0:T(8,128)(2,1)S(1)} %copy-done.21, bf16[1104,1024]{1,0:T(8,128)(2,1)S(1)} %get-tuple-element.334.rows_ref.refs_1_, ...), custom_call_target="tpu_custom_call" | custom-call | flops 8499999744 | bytes 8500000 | tf_op jit(solution)/shard_map/weight_grads/pallas_call | solution.py:541
  241.8 7.2 %collective-permute-done.39 = bf16[4,64,512]{2,1,0:T(8,128)(2,1)S(1)} collective-permute-done((bf16[4,64,512]{2,1,0:T(8,128)(2,1)S(1)}, bf16[4,64,512]{2,1,0:T(8,128)(2,1)S(1)}, u32[]{:S(2)}, u32[]{:S(2)}) %collective-permute-start.39) | collective-permute-done | bytes 262176 | tf_op jit(solution)/shard_map/reduce_z/ppermute | solution.py:51
  251.2 3.9 %collective-permute-start.43 = (bf16[4,64,512]{2,1,0:T(8,128)(2,1)S(1)}, bf16[4,64,512]{2,1,0:T(8,128)(2,1)S(1)}, u32[]{:S(2)}, u32[]{:S(2)}) collective-permute-start(bf16[4,64,512]{2,1,0:T(8,128)(2,1)S(1)} %pad_maximum_fusion.18), channel_id=1, source_target_pairs={{0,24},{2,26},{4,28},{6,30},{8,0},{10,2},{12,4},{14,6},{16,8},{18,... | collective-permute-start | bytes 786440 | tf_op jit(solution)/shard_map/reduce_z/ppermute | solution.py:51
  257.4 17.0 %attend_back.3 = (bf16[1104,256]{1,0:T(8,128)(2,1)S(1)}, bf16[1104,256]{1,0:T(8,128)(2,1)S(1)}, bf16[1104,256]{1,0:T(8,128)(2,1)S(1)}) custom-call(bf16[1104,1536]{1,0:T(8,128)(2,1)S(1)} %copy-done.24, bf16[1104,1536]{1,0:T(8,128)(2,1)S(1)} %copy-done.24, bf16[1104,1536]{1,0:T(8,128)(2,1)S(1)} %copy-done.24, ...), custom_call_target="tpu_custom_call" | custom-call | flops 17999998976 | bytes 18000000 | tf_op jit(solution)/shard_map/attend_back/pallas_call | solution.py:424
  277.4 5.0 %times_pieces_turned.3 = (bf16[552,1024]{1,0:T(8,128)(2,1)S(1)}, bf16[552,1024]{1,0:T(8,128)(2,1)S(1)}) custom-call(bf16[1104,256]{1,0:T(8,128)(2,1)S(1)} %get-tuple-element.355.refs_2_.refs_0_, bf16[1104,256]{1,0:T(8,128)(2,1)S(1)} %get-tuple-element.356.refs_3_.refs_1_, bf16[1104,256]{1,0:T(8,128)(2,1)S(1)} %get-tuple-element.357.refs_4_.refs_2_, ...), custom_call_target="tpu_custom_call" | custom-call | flops 7000000000 | bytes 7000000 | tf_op jit(solution)/shard_map/times_pieces_turned/pallas_call | solution.py:504
  289.5 2.8 collective-permute-start.56
  294.2 3.3 first_norm_back.1
  310.0 2.4 fusion.13
  313.7 4.8 %collective-permute-done.52 = bf16[3,128,256]{2,1,0:T(8,128)(2,1)S(1)} collective-permute-done((bf16[3,128,256]{2,1,0:T(8,128)(2,1)S(1)}, bf16[3,128,256]{2,1,0:T(8,128)(2,1)S(1)}, u32[]{:S(2)}, u32[]{:S(2)}) %collective-permute-start.52) | collective-permute-done | bytes 196640 | tf_op jit(solution)/shard_map/reduce_middle/ppermute | solution.py:51
  322.7 2.5 fusion.14
  (354 shorter events, 106.8 us)
Async XLA Ops:
  6.4 21.8 %collective-permute-start.1 = (bf16[4,72,512]{2,1,0:T(8,128)(2,1)S(1)}, bf16[4,72,512]{2,1,0:T(8,128)(2,1)S(1)}, u32[]{:S(2)}, u32[]{:S(2)}) collective-permute-start(bf16[4,72,512]{2,1,0:T(8,128)(2,1)S(1)} %fusion.18), channel_id=1, source_target_pairs={{16,0},{18,2},{20,4},{22,6},{24,8},{26,10},{28,12},{30,14},{0,16},... | collective-permute-start | bytes 884744 | tf_op jit(solution)/shard_map/gather_z/ppermute | solution.py:47
  8.9 19.2 %collective-permute-start = (bf16[4,72,512]{2,1,0:T(8,128)(2,1)S(1)}, bf16[4,72,512]{2,1,0:T(8,128)(2,1)S(1)}, u32[]{:S(2)}, u32[]{:S(2)}) collective-permute-start(bf16[4,72,512]{2,1,0:T(8,128)(2,1)S(1)} %fusion.18), channel_id=1, source_target_pairs={{8,0},{10,2},{12,4},{14,6},{16,8},{18,10},{20,12},{22,14},{24,16},... | collective-permute-start | bytes 884744 | tf_op jit(solution)/shard_map/gather_z/ppermute | solution.py:47
  12.2 16.0 %collective-permute-start.4 = (bf16[4,32,512]{2,1,0:T(8,128)(2,1)S(1)}, bf16[4,32,512]{2,1,0:T(8,128)(2,1)S(1)}, u32[]{:S(2)}, u32[]{:S(2)}) collective-permute-start(bf16[4,32,512]{2,1,0:T(8,128)(2,1)S(1)} %get-tuple-element.237), channel_id=1, source_target_pairs={{4,0},{6,2},{0,4},{2,6},{12,8},{14,10},{8,12},{10,14},{20,16},{22,... | collective-permute-start | bytes 393224 | tf_op jit(solution)/shard_map/gather_middle/ppermute | solution.py:47
  13.8 15.0 %collective-permute-start.3 = (bf16[4,32,512]{2,1,0:T(8,128)(2,1)S(1)}, bf16[4,32,512]{2,1,0:T(8,128)(2,1)S(1)}, u32[]{:S(2)}, u32[]{:S(2)}) collective-permute-start(bf16[4,32,512]{2,1,0:T(8,128)(2,1)S(1)} %get-tuple-element.235), channel_id=1, source_target_pairs={{2,0},{0,2},{6,4},{4,6},{10,8},{8,10},{14,12},{12,14},{18,16},{16,... | collective-permute-start | bytes 393224 | tf_op jit(solution)/shard_map/gather_middle/ppermute | solution.py:47
  29.5 17.8 %collective-permute-start.8 = (bf16[4,8,64]{2,1,0:T(8,128)(2,1)S(1)}, bf16[4,8,64]{2,1,0:T(8,128)(2,1)S(1)}, u32[]{:S(2)}, u32[]{:S(2)}) collective-permute-start(bf16[4,8,64]{2,1,0:T(8,128)(2,1)S(1)} %pad_maximum_fusion.27), channel_id=1, source_target_pairs={{4,0},{6,2},{0,4},{2,6},{12,8},{14,10},{8,12},{10,14},{20,16},{22,... | collective-permute-start | bytes 12296 | tf_op jit(solution)/shard_map/gather_small/ppermute | solution.py:47
  32.2 19.1 %collective-permute-start.5 = (bf16[4,128,512]{2,1,0:T(8,128)(2,1)S(1)}, bf16[4,128,512]{2,1,0:T(8,128)(2,1)S(1)}, u32[]{:S(2)}, u32[]{:S(2)}) collective-permute-start(bf16[4,128,512]{2,1,0:T(8,128)(2,1)S(1)} %pad_maximum_fusion.2), channel_id=1, source_target_pairs={{2,0},{0,2},{6,4},{4,6},{10,8},{8,10},{14,12},{12,14},{18,16},{16,... | collective-permute-start | bytes 1572872 | tf_op jit(solution)/shard_map/gather_middle/ppermute | solution.py:47
  33.8 17.5 %collective-permute-start.6 = (bf16[4,128,512]{2,1,0:T(8,128)(2,1)S(1)}, bf16[4,128,512]{2,1,0:T(8,128)(2,1)S(1)}, u32[]{:S(2)}, u32[]{:S(2)}) collective-permute-start(bf16[4,128,512]{2,1,0:T(8,128)(2,1)S(1)} %pad_maximum_fusion.3), channel_id=1, source_target_pairs={{4,0},{6,2},{0,4},{2,6},{12,8},{14,10},{8,12},{10,14},{20,16},{22,... | collective-permute-start | bytes 1572872 | tf_op jit(solution)/shard_map/gather_middle/ppermute | solution.py:47
  51.2 26.3 %collective-permute-start.15 = (bf16[552,1024]{1,0:T(8,128)(2,1)}, bf16[552,1024]{1,0:T(8,128)(2,1)}, u32[]{:S(2)}, u32[]{:S(2)}) collective-permute-start(bf16[552,1024]{1,0:T(8,128)(2,1)} %get-tuple-element.284.refs_2_.own_ref), channel_id=1, source_target_pairs={{0,1},{1,0},{2,3},{3,2},{4,5},{5,4},{6,7},{7,6},{8,9},{9,8},{10,11... | collective-permute-start | bytes 3391496 | tf_op jit(solution)/shard_map/ppermute | solution.py:216
  52.0 25.6 %collective-permute-start.11 = (bf16[4,256,512]{2,1,0:T(8,128)(2,1)S(1)}, bf16[4,256,512]{2,1,0:T(8,128)(2,1)S(1)}, u32[]{:S(2)}, u32[]{:S(2)}) collective-permute-start(bf16[4,256,512]{2,1,0:T(8,128)(2,1)S(1)} %constant_dynamic-update-slice_fusion.2.refs_2_.refs_3_.refs_18_.refs_19_.refs_20_.refs_21_.refs_22, ...), channel_id=1, source_target_pairs={{2,0},{0,2},{6,4},{4,6},{10,8},{8,10},{14,12},{12,14},{18,16},{16,... | collective-permute-start | bytes 3145736 | tf_op jit(solution)/shard_map/gather_last/ppermute | solution.py:47
  52.7 25.5 %collective-permute-start.10 = (bf16[4,256,512]{2,1,0:T(8,128)(2,1)S(1)}, bf16[4,256,512]{2,1,0:T(8,128)(2,1)}, u32[]{:S(2)}, u32[]{:S(2)}) collective-permute-start(bf16[4,256,512]{2,1,0:T(8,128)(2,1)S(1)} %constant_dynamic-update-slice_fusion.refs_0_.refs_1_.refs_6_.refs_7_.refs_8_.refs_9_.refs_10_.refs_11_), channel_id=1, source_target_pairs={{4,0},{6,2},{0,4},{2,6},{12,8},{14,10},{8,12},{10,14},{20,16},{22,... | collective-permute-start | bytes 3145736 | tf_op jit(solution)/shard_map/gather_last/ppermute | solution.py:47
  58.6 18.9 %collective-permute-start.12 = (bf16[4,64,512]{2,1,0:T(8,128)(2,1)S(1)}, bf16[4,64,512]{2,1,0:T(8,128)(2,1)S(1)}, u32[]{:S(2)}, u32[]{:S(2)}) collective-permute-start(bf16[4,64,512]{2,1,0:T(8,128)(2,1)S(1)} %pad_maximum_fusion.13), channel_id=1, source_target_pairs={{16,0},{18,2},{20,4},{22,6},{24,8},{26,10},{28,12},{30,14},{0,16},... | collective-permute-start | bytes 786440 | tf_op jit(solution)/shard_map/gather_step/ppermute | solution.py:47
  94.7 23.9 %collective-permute-start.22 = (bf16[4,128,512]{2,1,0:T(8,128)(2,1)S(1)}, bf16[4,128,512]{2,1,0:T(8,128)(2,1)S(1)}, u32[]{:S(2)}, u32[]{:S(2)}) collective-permute-start(bf16[4,128,512]{2,1,0:T(8,128)(2,1)S(1)} %copy-done.27), channel_id=1, source_target_pairs={{16,0},{18,2},{20,4},{22,6},{24,8},{26,10},{28,12},{30,14},{0,16},... | collective-permute-start | bytes 1572872 | tf_op jit(solution)/shard_map/gather_step/ppermute | solution.py:47
  95.3 23.3 %collective-permute-start.21 = (bf16[4,256,512]{2,1,0:T(8,128)(2,1)S(1)}, bf16[4,256,512]{2,1,0:T(8,128)(2,1)S(1)}, u32[]{:S(2)}, u32[]{:S(2)}) collective-permute-start(bf16[4,256,512]{2,1,0:T(8,128)(2,1)S(1)} %constant_dynamic-update-slice_fusion.8.refs_6_.refs_10_), channel_id=1, source_target_pairs={{2,0},{0,2},{6,4},{4,6},{10,8},{8,10},{14,12},{12,14},{18,16},{16,... | collective-permute-start | bytes 3145736 | tf_op jit(solution)/shard_map/gather_last/ppermute | solution.py:47
  96.1 23.5 %collective-permute-start.20 = (bf16[4,256,512]{2,1,0:T(8,128)(2,1)S(1)}, bf16[4,256,512]{2,1,0:T(8,128)(2,1)S(1)}, u32[]{:S(2)}, u32[]{:S(2)}) collective-permute-start(bf16[4,256,512]{2,1,0:T(8,128)(2,1)S(1)} %constant_dynamic-update-slice_fusion.6.refs_4_.refs_8_), channel_id=1, source_target_pairs={{4,0},{6,2},{0,4},{2,6},{12,8},{14,10},{8,12},{10,14},{20,16},{22,... | collective-permute-start | bytes 3145736 | tf_op jit(solution)/shard_map/gather_last/ppermute | solution.py:47
  121.9 16.5 %collective-permute-start.23 = (bf16[4,128,512]{2,1,0:T(8,128)(2,1)}, bf16[4,128,512]{2,1,0:T(8,128)(2,1)S(1)}, u32[]{:S(2)}, u32[]{:S(2)}) collective-permute-start(bf16[4,128,512]{2,1,0:T(8,128)(2,1)} %pad_maximum_fusion.4), channel_id=1, source_target_pairs={{24,0},{26,2},{28,4},{30,6},{0,8},{2,10},{4,12},{6,14},{8,16},{10,... | collective-permute-start | bytes 1572872 | tf_op jit(solution)/shard_map/gather_step/ppermute | solution.py:47
  138.8 25.5 %collective-permute-start.25 = (bf16[4,256,512]{2,1,0:T(8,128)(2,1)S(1)}, bf16[4,256,512]{2,1,0:T(8,128)(2,1)S(1)}, u32[]{:S(2)}, u32[]{:S(2)}) collective-permute-start(bf16[4,256,512]{2,1,0:T(8,128)(2,1)S(1)} %bitcast.143), channel_id=1, source_target_pairs={{4,0},{6,2},{0,4},{2,6},{12,8},{14,10},{8,12},{10,14},{20,16},{22,... | collective-permute-start | bytes 3145736 | tf_op jit(solution)/shard_map/gather_last/ppermute | solution.py:47
  139.5 24.8 %collective-permute-start.26 = (bf16[4,256,512]{2,1,0:T(8,128)(2,1)S(1)}, bf16[4,256,512]{2,1,0:T(8,128)(2,1)S(1)}, u32[]{:S(2)}, u32[]{:S(2)}) collective-permute-start(bf16[4,256,512]{2,1,0:T(8,128)(2,1)S(1)} %bitcast.146), channel_id=1, source_target_pairs={{2,0},{0,2},{6,4},{4,6},{10,8},{8,10},{14,12},{12,14},{18,16},{16,... | collective-permute-start | bytes 3145736 | tf_op jit(solution)/shard_map/gather_last/ppermute | solution.py:47
  164.3 26.6 %collective-permute-start.27 = (bf16[4,256,512]{2,1,0:T(8,128)(2,1)}, bf16[4,256,512]{2,1,0:T(8,128)(2,1)}, u32[]{:S(2)}, u32[]{:S(2)}) collective-permute-start(bf16[4,256,512]{2,1,0:T(8,128)(2,1)} %bitcast.179), channel_id=1, source_target_pairs={{0,4},{2,6},{4,0},{6,2},{8,12},{10,14},{12,8},{14,10},{16,20},{18,... | collective-permute-start | bytes 3145736 | tf_op jit(solution)/shard_map/reduce_last/ppermute | solution.py:51
  165.5 25.3 %collective-permute-start.28 = (bf16[4,256,512]{2,1,0:T(8,128)(2,1)}, bf16[4,256,512]{2,1,0:T(8,128)(2,1)S(1)}, u32[]{:S(2)}, u32[]{:S(2)}) collective-permute-start(bf16[4,256,512]{2,1,0:T(8,128)(2,1)} %bitcast.178), channel_id=1, source_target_pairs={{0,2},{2,0},{4,6},{6,4},{8,10},{10,8},{12,14},{14,12},{16,18},{18,... | collective-permute-start | bytes 3145736 | tf_op jit(solution)/shard_map/reduce_last/ppermute | solution.py:51
  196.5 14.9 %collective-permute-start.33 = (bf16[4,128,512]{2,1,0:T(8,128)(2,1)S(1)}, bf16[4,128,512]{2,1,0:T(8,128)(2,1)S(1)}, u32[]{:S(2)}, u32[]{:S(2)}) collective-permute-start(bf16[4,128,512]{2,1,0:T(8,128)(2,1)S(1)} %get-tuple-element.449), channel_id=1, source_target_pairs={{0,4},{2,6},{4,0},{6,2},{8,12},{10,14},{12,8},{14,10},{16,20},{18,... | collective-permute-start | bytes 1572872 | tf_op jit(solution)/shard_map/reduce_middle/ppermute | solution.py:51
  205.2 29.7 %collective-permute-start.30 = (bf16[4,256,512]{2,1,0:T(8,128)(2,1)}, bf16[4,256,512]{2,1,0:T(8,128)(2,1)S(1)}, u32[]{:S(2)}, u32[]{:S(2)}) collective-permute-start(bf16[4,256,512]{2,1,0:T(8,128)(2,1)} %bitcast.51), channel_id=1, source_target_pairs={{0,4},{2,6},{4,0},{6,2},{8,12},{10,14},{12,8},{14,10},{16,20},{18,... | collective-permute-start | bytes 3145736 | tf_op jit(solution)/shard_map/reduce_last/ppermute | solution.py:51
  206.5 28.4 %collective-permute-start.31 = (bf16[4,256,512]{2,1,0:T(8,128)(2,1)}, bf16[4,256,512]{2,1,0:T(8,128)(2,1)S(1)}, u32[]{:S(2)}, u32[]{:S(2)}) collective-permute-start(bf16[4,256,512]{2,1,0:T(8,128)(2,1)} %bitcast.53), channel_id=1, source_target_pairs={{0,2},{2,0},{4,6},{6,4},{8,10},{10,8},{12,14},{14,12},{16,18},{18,... | collective-permute-start | bytes 3145736 | tf_op jit(solution)/shard_map/reduce_last/ppermute | solution.py:51
  211.8 23.1 %collective-permute-start.34 = (bf16[4,64,512]{2,1,0:T(8,128)(2,1)S(1)}, bf16[4,64,512]{2,1,0:T(8,128)(2,1)S(1)}, u32[]{:S(2)}, u32[]{:S(2)}) collective-permute-start(bf16[4,64,512]{2,1,0:T(8,128)(2,1)S(1)} %pad_maximum_fusion.14), channel_id=1, source_target_pairs={{0,8},{2,10},{4,12},{6,14},{8,16},{10,18},{12,20},{14,22},{16,24},... | collective-permute-start | bytes 786440 | tf_op jit(solution)/shard_map/reduce_z/ppermute | solution.py:51
  213.0 21.9 %collective-permute-start.35 = (bf16[4,64,512]{2,1,0:T(8,128)(2,1)S(1)}, bf16[4,64,512]{2,1,0:T(8,128)(2,1)S(1)}, u32[]{:S(2)}, u32[]{:S(2)}) collective-permute-start(bf16[4,64,512]{2,1,0:T(8,128)(2,1)S(1)} %pad_maximum_fusion.15), channel_id=1, source_target_pairs={{0,24},{2,26},{4,28},{6,30},{8,0},{10,2},{12,4},{14,6},{16,8},{18,... | collective-permute-start | bytes 786440 | tf_op jit(solution)/shard_map/reduce_z/ppermute | solution.py:51
  215.9 17.2 %collective-permute-start.36 = (bf16[552,1024]{1,0:T(8,128)(2,1)S(1)}, bf16[552,1024]{1,0:T(8,128)(2,1)S(1)}, u32[]{:S(2)}, u32[]{:S(2)}) collective-permute-start(bf16[552,1024]{1,0:T(8,128)(2,1)S(1)} %slice.610), channel_id=1, source_target_pairs={{0,1},{1,0},{2,3},{3,2},{4,5},{5,4},{6,7},{7,6},{8,9},{9,8},{10,11... | collective-permute-start | bytes 3391496 | tf_op jit(solution)/shard_map/ppermute | solution.py:216
  251.1 23.5 %collective-permute-start.42 = (bf16[4,64,512]{2,1,0:T(8,128)(2,1)S(1)}, bf16[4,64,512]{2,1,0:T(8,128)(2,1)S(1)}, u32[]{:S(2)}, u32[]{:S(2)}) collective-permute-start(bf16[4,64,512]{2,1,0:T(8,128)(2,1)S(1)} %pad_maximum_fusion.17), channel_id=1, source_target_pairs={{0,8},{2,10},{4,12},{6,14},{8,16},{10,18},{12,20},{14,22},{16,24},... | collective-permute-start | bytes 786440 | tf_op jit(solution)/shard_map/reduce_z/ppermute | solution.py:51
  251.2 23.4 %collective-permute-start.43 = (bf16[4,64,512]{2,1,0:T(8,128)(2,1)S(1)}, bf16[4,64,512]{2,1,0:T(8,128)(2,1)S(1)}, u32[]{:S(2)}, u32[]{:S(2)}) collective-permute-start(bf16[4,64,512]{2,1,0:T(8,128)(2,1)S(1)} %pad_maximum_fusion.18), channel_id=1, source_target_pairs={{0,24},{2,26},{4,28},{6,30},{8,0},{10,2},{12,4},{14,6},{16,8},{18,... | collective-permute-start | bytes 786440 | tf_op jit(solution)/shard_map/reduce_z/ppermute | solution.py:51
  255.1 19.6 %collective-permute-start.40 = (bf16[5,256,256]{2,1,0:T(8,128)(2,1)S(1)}, bf16[5,256,256]{2,1,0:T(8,128)(2,1)S(1)}, u32[]{:S(2)}, u32[]{:S(2)}) collective-permute-start(bf16[5,256,256]{2,1,0:T(8,128)(2,1)S(1)} %get-tuple-element.368), channel_id=1, source_target_pairs={{0,4},{2,6},{4,0},{6,2},{8,12},{10,14},{12,8},{14,10},{16,20},{18,... | collective-permute-start | bytes 1966088 | tf_op jit(solution)/shard_map/reduce_last/ppermute | solution.py:51
  256.4 18.3 %collective-permute-start.41 = (bf16[5,256,256]{2,1,0:T(8,128)(2,1)S(1)}, bf16[5,256,256]{2,1,0:T(8,128)(2,1)S(1)}, u32[]{:S(2)}, u32[]{:S(2)}) collective-permute-start(bf16[5,256,256]{2,1,0:T(8,128)(2,1)S(1)} %get-tuple-element.370), channel_id=1, source_target_pairs={{0,2},{2,0},{4,6},{6,4},{8,10},{10,8},{12,14},{14,12},{16,18},{18,... | collective-permute-start | bytes 1966088 | tf_op jit(solution)/shard_map/reduce_last/ppermute | solution.py:51
  288.8 24.9 %collective-permute-start.55 = (bf16[5,64,256]{2,1,0:T(8,128)(2,1)}, bf16[5,64,256]{2,1,0:T(8,128)(2,1)S(1)}, u32[]{:S(2)}, u32[]{:S(2)}) collective-permute-start(bf16[5,64,256]{2,1,0:T(8,128)(2,1)} %pad_maximum_fusion.20), channel_id=1, source_target_pairs={{0,8},{2,10},{4,12},{6,14},{8,16},{10,18},{12,20},{14,22},{16,24},... | collective-permute-start | bytes 491528 | tf_op jit(solution)/shard_map/reduce_z/ppermute | solution.py:51
  289.5 24.2 %collective-permute-start.56 = (bf16[5,64,256]{2,1,0:T(8,128)(2,1)}, bf16[5,64,256]{2,1,0:T(8,128)(2,1)S(1)}, u32[]{:S(2)}, u32[]{:S(2)}) collective-permute-start(bf16[5,64,256]{2,1,0:T(8,128)(2,1)} %pad_maximum_fusion.21), channel_id=1, source_target_pairs={{0,16},{2,18},{4,20},{6,22},{8,24},{10,26},{12,28},{14,30},{16,0},... | collective-permute-start | bytes 491528 | tf_op jit(solution)/shard_map/reduce_z/ppermute | solution.py:51
  298.7 15.0 %collective-permute-start.57 = (bf16[5,64,256]{2,1,0:T(8,128)(2,1)}, bf16[5,64,256]{2,1,0:T(8,128)(2,1)S(1)}, u32[]{:S(2)}, u32[]{:S(2)}) collective-permute-start(bf16[5,64,256]{2,1,0:T(8,128)(2,1)} %pad_maximum_fusion.22), channel_id=1, source_target_pairs={{0,24},{2,26},{4,28},{6,30},{8,0},{10,2},{12,4},{14,6},{16,8},{18,... | collective-permute-start | bytes 491528 | tf_op jit(solution)/shard_map/reduce_z/ppermute | solution.py:51
  (84 other events, 921.6 us)

commit v6 on v5

--- a/solution.py
+++ b/solution.py
@@ -233,12 +233,6 @@
         if self.relative:
             return value, self.swap(value)
         return lax.psum(value.astype(F32), "tensor"), jnp.zeros((1, value.shape[1]), F32)
-
-    def own_total(self, value):
-        if self.relative:
-            kept = value[: self.local_rows].astype(F32)
-            return kept + self.swap(value[self.local_rows :]).astype(F32)
-        return lax.psum_scatter(value, "tensor", scatter_dimension=0, tiled=True).astype(F32)
 
     def own_both(self, halves):
         if self.relative:
@@ -360,8 +354,6 @@
     grad_key_ref,
     grad_value_ref,
     turned_ref,
-    prob_ref,
-    score_ref,
 ):
     seq = query_ref.shape[0]
     invalid = key_column(invalid_ref)
@@ -373,16 +365,12 @@
         query, keys = head_operands(query_ref, key_ref, invalid, head)
         grad = jnp.where(mine, grad_ref[...], jnp.asarray(0, BF16))
         row_dot = jnp.sum(product[rows], axis=0, keepdims=True)
-        for start in range(0, seq, 256):
-            cut = slice(start, min(start + 256, seq))
-            prob = jnp.exp(dot_nt(keys, query[cut]) - total_ref[0, 0, head : head + 1, cut])
-            grad_prob = dot_nt(value_ref[...], grad[cut]) - row_dot[:, cut]
-            grad_score = (prob * grad_prob).astype(BF16)
-            prob_ref[:, cut] = prob.astype(BF16)
-            score_ref[:, cut] = grad_score
-            turned_ref[rows, cut] = dot_nn(keys_turned[rows], grad_score) * HEAD_DIM**-0.5
-        grad_value = dot_nn(prob_ref[...], grad)
-        grad_key = dot_nn(score_ref[...], jnp.where(mine, query, jnp.asarray(0, BF16)))
+        prob = jnp.exp(dot_nt(keys, query) - total_ref[0, 0, head : head + 1])
+        grad_prob = dot_nt(value_ref[...], grad) - row_dot
+        grad_score = (prob * grad_prob).astype(BF16)
+        turned_ref[rows] = dot_nn(keys_turned[rows], grad_score) * HEAD_DIM**-0.5
+        grad_value = dot_nn(prob.astype(BF16), grad)
+        grad_key = dot_nn(grad_score, jnp.where(mine, query, jnp.asarray(0, BF16)))
         if head == 0:
             first_value, first_key = grad_value, grad_key
     grad_value_ref[...] = (first_value + grad_value).astype(BF16)
@@ -437,10 +425,8 @@
         out_shape=[jax.ShapeDtypeStruct((mixed.shape[0], count * 2 * HEAD_DIM), BF16)] * 3,
         scratch_shapes=[
             pltpu.VMEM((2 * HEAD_DIM, SEQ_LEN), F32),
-            pltpu.VMEM((SEQ_LEN, SEQ_LEN), BF16),
-            pltpu.VMEM((SEQ_LEN, SEQ_LEN), BF16),
         ],
-        compiler_params=params(22),
+        compiler_params=params(36),
         cost_estimate=cost(9 * slots * count),
         name="attend_back",
     )(packed, packed, packed, invalid, mixed, total, grad_mixed)
@@ -881,8 +867,8 @@
             ],
         ),
         out_shape=[
-            jax.ShapeDtypeStruct((rows, width), BF16),
-            jax.ShapeDtypeStruct((rows, width), BF16),
+            pltpu.HBM((rows, width), BF16),
+            pltpu.HBM((rows, width), BF16),
             jax.ShapeDtypeStruct((1, units), F32),
         ]
         + grad_shapes,
@@ -1062,7 +1048,7 @@
     pieces_a = grid.first_pieces(middle_a)
     first_a = grid.send_first(pieces_a, (1, 3))
     columns = back(0)
-    mlp_out = pair.own_total(mlp_out)
+    mlp_out = pair.own_both(jnp.split(mlp_out, 2) if pair.relative else [mlp_out])
     last_b, first_a, pieces_a, columns, grad_mixed, mlp_out = join(
         last_b, first_a, pieces_a, columns, grad_mixed, mlp_out
     )
@@ -1125,6 +1111,7 @@
         sum_d, small_grads = sum_d[:, :block], sum_d[0, block:, :block]
     else:
         small_grads = grid.reduce_small(small_grads, 0)
+    mlp_out = sum(m.astype(F32) for m in mlp_out)
     result = pair.own(middle) + own_live * (mlp_out + fc2_shift)
     outputs = dot_nt(result.astype(BF16), select).astype(BF16)
     first_a, first_b = grid.reduce_end(first_a), grid.reduce_end(first_b)

time: 337 us -> 333 us (0.988)
  Pallas kernels: 138 us -> 134 us
    unnamed x117 -> x115, local copies, waits for them, and re-layouts: 9.08 us -> 7.31 us
  transfers between devices with their start and end apart: 61 -> 61, of which waited for: 24 -> 28; matrix products, arithmetic and copies ran while one was open for 10% -> 10% of each run, Pallas kernels for 42% -> 41%
where the time goes in v6:
time: 333 us; the launch traced here: 327 us
  Pallas kernels  134 us (40%)
  starting transfers between devices  74.8 us (22%)
  waiting for transfers between devices  69.5 us (21%)
  local copies, waits for them, and re-layouts  19.8 us (6%)
  other arithmetic  13.9 us (4%)
  matrix products  11.9 us (4%)
    ppermute x23, waiting for transfers between devices, fetch(): return lax.ppermute(value, 'dp', pairs)  46.6 us
    pallas_call x2, Pallas kernels, feed_forward(): pl.pallas_call(functools.partial(feed_kernel, (len(grads), len(pieces), l...  43.7 us
    ppermute x23, starting transfers between devices, fetch(): return lax.ppermute(value, 'dp', pairs)  39.3 us
    ppermute x30, starting transfers between devices, push(): return lax.ppermute(value, 'dp', pairs)  35.4 us
    pallas_call x2, Pallas kernels, attend_back(): pl.pallas_call(attend_back_kernel, grid=(slots, count), in_specs=[columns...  31.6 us
    ppermute x30, waiting for transfers between devices, push(): return lax.ppermute(value, 'dp', pairs)  21.9 us
    pallas_call x1, Pallas kernels, attend(): pl.pallas_call(attend_kernel, grid=(slots, count), in_specs=[columns(firs...  16.2 us
    pallas_call x2, Pallas kernels, times_pieces_turned(): pl.pallas_call(kernel, grid=(1,), in_specs=[whole_spec(c) for c in column...  8.86 us
  transfers between devices with their start and end apart: 61, of which 28 were waited for; matrix products, arithmetic and copies ran while one was open for 10% of the time, Pallas kernels for 41%

profile of v6, /device:TPU:0, one launch (start us, length us, event | category | flops | bytes accessed | tf_op | source)
XLA Modules:
  0.0 326.6 jit_solution(4522972784113215556)
XLA Ops:
  3.3 3.1 collective-permute-start.2
  6.4 2.6 collective-permute-start.1
  16.4 11.8 %collective-permute-done.1 = bf16[4,72,512]{2,1,0:T(8,128)(2,1)S(1)} collective-permute-done((bf16[4,72,512]{2,1,0:T(8,128)(2,1)S(1)}, bf16[4,72,512]{2,1,0:T(8,128)(2,1)S(1)}, u32[]{:S(2)}, u32[]{:S(2)}) %collective-permute-start.1) | collective-permute-done | bytes 294944 | tf_op jit(solution)/shard_map/gather_z/ppermute | solution.py:47
  34.3 2.4 fusion.12.refs_0_.own_ref.refs_4_
  36.7 7.8 %collective-permute-start.7 = (bf16[4,64,512]{2,1,0:T(8,128)(2,1)S(1)}, bf16[4,64,512]{2,1,0:T(8,128)(2,1)S(1)}, u32[]{:S(2)}, u32[]{:S(2)}) collective-permute-start(bf16[4,64,512]{2,1,0:T(8,128)(2,1)S(1)} %pad_maximum_fusion.13), channel_id=1, source_target_pairs={{8,0},{10,2},{12,4},{14,6},{16,8},{18,10},{20,12},{22,14},{24,16},... | collective-permute-start | bytes 786440 | tf_op jit(solution)/shard_map/gather_step/ppermute | solution.py:47
  44.6 2.8 multiply_convert_fusion
  48.8 2.4 collective-permute-done.9
  59.1 3.2 first_norm.1.rows_ref.refs_0_
  62.4 5.0 %collective-permute-done.13 = bf16[4,64,512]{2,1,0:T(8,128)(2,1)S(1)} collective-permute-done((bf16[4,64,512]{2,1,0:T(8,128)(2,1)S(1)}, bf16[4,64,512]{2,1,0:T(8,128)(2,1)S(1)}, u32[]{:S(2)}, u32[]{:S(2)}) %collective-permute-start.13) | collective-permute-done | bytes 262176 | tf_op jit(solution)/shard_map/gather_step/ppermute | solution.py:47
  67.3 10.1 %collective-permute-done.12 = bf16[4,64,512]{2,1,0:T(8,128)(2,1)S(1)} collective-permute-done((bf16[4,64,512]{2,1,0:T(8,128)(2,1)S(1)}, bf16[4,64,512]{2,1,0:T(8,128)(2,1)S(1)}, u32[]{:S(2)}, u32[]{:S(2)}) %collective-permute-start.12) | collective-permute-done | bytes 262176 | tf_op jit(solution)/shard_map/gather_step/ppermute | solution.py:47
  82.6 5.2 %times_pieces.2.query_ref.key_ref.value_ref = bf16[1104,1536]{1,0:T(8,128)(2,1)S(1)} custom-call(bf16[1104,1024]{1,0:T(8,128)(2,1)S(1)} %first_norm.1.rows_ref.refs_0_, bf16[4,256,512]{2,1,0:T(8,128)(2,1)S(1)} %constant_dynamic-update-slice_fusion.refs_0_.refs_1_.refs_6_.refs_7_.refs_8_.refs_9_.refs_10_.refs_11_, ...), custom_call_target="tpu_custom_call" | custom-call | flops 6000000000 | bytes 6000000 | tf_op jit(solution)/shard_map/times_pieces/pallas_call | solution.py:451
  87.9 3.7 %collective-permute-done.17 = bf16[4,128,512]{2,1,0:T(8,128)(2,1)S(1)} collective-permute-done((bf16[4,128,512]{2,1,0:T(8,128)(2,1)S(1)}, bf16[4,128,512]{2,1,0:T(8,128)(2,1)S(1)}, u32[]{:S(2)}, u32[]{:S(2)}) %collective-permute-start.17) | collective-permute-done | bytes 524320 | tf_op jit(solution)/shard_map/gather_middle/ppermute | solution.py:47
  97.7 16.2 %attend.1 = (bf16[1104,512]{1,0:T(8,128)(2,1)S(1)}, f32[1,4,2,1104]{3,2,1,0:T(2,128)S(1)}) custom-call(bf16[1104,1536]{1,0:T(8,128)(2,1)S(1)} %times_pieces.2.query_ref.key_ref.value_ref, bf16[1104,1536]{1,0:T(8,128)(2,1)S(1)} %times_pieces.2.query_ref.key_ref.value_ref, bf16[1104,1536]{1,0:T(8,128)(2,1)S(1)} %times_pieces.2.query_ref.key_ref.value_ref, ...), custom_call_target="tpu_custom_call" | custom-call | flops 16000000000 | bytes 16000000 | tf_op jit(solution)/shard_map/attend/pallas_call | solution.py:393
  114.0 3.9 %times_pieces_turned.2.refs_1_ = bf16[1104,1024]{1,0:T(8,128)(2,1)} custom-call(bf16[1104,512]{1,0:T(8,128)(2,1)S(1)} %get-tuple-element.379.refs_0_.mixed_ref.refs_5_.refs_6_, bf16[4,256,512]{2,1,0:T(8,128)(2,1)S(1)} %constant_dynamic-update-slice_fusion.refs_0_.refs_1_.refs_6_.refs_7_.refs_8_.refs_9_.refs_10_.refs_11_, ...), custom_call_target="tpu_custom_call" | custom-call | flops 2000000000 | bytes 2000000 | tf_op jit(solution)/shard_map/times_pieces_turned/pallas_call | solution.py:490
  121.9 3.0 collective-permute-start.23
  125.6 5.8 %second_norm.1 = (f32[1104,1024]{1,0:T(8,128)}, bf16[1104,1024]{1,0:T(8,128)(2,1)S(1)}) custom-call(bf16[552,1024]{1,0:T(8,128)(2,1)} %fusion.12.refs_0_.own_ref.refs_4_, bf16[552,1024]{1,0:T(8,128)(2,1)} %collective-permute-done.14.refs_1_.next_ref, f32[1104,1]{1,0:T(8,128)S(1)} %broadcast_in_dim_reshape.3.refs_0_.live_ref, ...), custom_call_target="tpu_custom_call" | custom-call | flops 4000000000 | bytes 4000000 | tf_op jit(solution)/shard_map/second_norm/pallas_call | solution.py:591
  131.4 7.0 %collective-permute-done.23 = bf16[4,128,512]{2,1,0:T(8,128)(2,1)S(1)} collective-permute-done((bf16[4,128,512]{2,1,0:T(8,128)(2,1)}, bf16[4,128,512]{2,1,0:T(8,128)(2,1)S(1)}, u32[]{:S(2)}, u32[]{:S(2)}) %collective-permute-start.23) | collective-permute-done | bytes 524320 | tf_op jit(solution)/shard_map/gather_step/ppermute | solution.py:47
  141.3 20.9 %feed_forward.2 = (bf16[1104,1024]{1,0:T(8,128)(2,1)}, bf16[1104,1024]{1,0:T(8,128)(2,1)}, f32[1,1024]{1,0:T(1,128)S(1)}, bf16[2,2,256,512]{3,2,1,0:T(8,128)(2,1...) custom-call(s32[32]{0:T(128)S(1)} %and_select_fusion.places_ref, ...), custom_call_target="tpu_custom_call" | custom-call | flops 24999999488 | bytes 25000000 | tf_op jit(solution)/shard_map/feed_forward/pallas_call | solution.py:839
  166.1 22.8 %feed_forward.3 = (bf16[1104,1024]{1,0:T(8,128)(2,1)}, bf16[1104,1024]{1,0:T(8,128)(2,1)}, f32[1,1024]{1,0:T(1,128)S(1)}, bf16[2,2,256,512]{3,2,1,0:T(8,128)(2,1...) custom-call(s32[32]{0:T(128)S(1)} %and_select_fusion.places_ref, ...), custom_call_target="tpu_custom_call" | custom-call | flops 24999999488 | bytes 25000000 | tf_op jit(solution)/shard_map/feed_forward/pallas_call | solution.py:839
  195.6 7.8 %norm_back.1 = (f32[552,1024]{1,0:T(8,128)S(1)}, bf16[1104,1024]{1,0:T(8,128)(2,1)S(1)}, f32[4,1024]{1,0:T(4,128)S(1)}) custom-call(bf16[552,1024]{1,0:T(8,128)(2,1)} %get-tuple-element.286.refs_2_.own_ref, bf16[552,1024]{1,0:T(8,128)(2,1)} %collective-permute-done.15.refs_3_.next_ref, f32[1104,1]{1,0:T(8,128)S(1)} %copy-done.5, ...), custom_call_target="tpu_custom_call" | custom-call | flops 7000000000 | bytes 7000000 | tf_op jit(solution)/shard_map/norm_back/pallas_call | solution.py:648
  211.0 2.8 collective-permute-start.35
  215.0 15.8 %attend_back.2 = (bf16[1104,256]{1,0:T(8,128)(2,1)S(1)}, bf16[1104,256]{1,0:T(8,128)(2,1)S(1)}, bf16[1104,256]{1,0:T(8,128)(2,1)S(1)}) custom-call(bf16[1104,1536]{1,0:T(8,128)(2,1)S(1)} %copy-done.21, bf16[1104,1536]{1,0:T(8,128)(2,1)S(1)} %copy-done.21, bf16[1104,1536]{1,0:T(8,128)(2,1)S(1)} %copy-done.21, ...), custom_call_target="tpu_custom_call" | custom-call | flops 17999998976 | bytes 18000000 | tf_op jit(solution)/shard_map/attend_back/pallas_call | solution.py:412
  235.6 3.6 %weight_grads.2 = (bf16[5,256,256]{2,1,0:T(8,128)(2,1)S(1)}, bf16[5,256,256]{2,1,0:T(8,128)(2,1)S(1)}, bf16[5,256,256]{2,1,0:T(8,128)(2,1)S(1)}, bf16[5,256,256]{2,1,0:T(8,128)(2,1)S(1)}) custom-call(bf16[1104,1024]{1,0:T(8,128)(2,1)S(1)} %copy-done.19, bf16[1104,1024]{1,0:T(8,128)(2,1)S(1)} %get-tuple-element.336.rows_ref.refs_1_, ...), custom_call_target="tpu_custom_call" | custom-call | flops 8499999744 | bytes 8500000 | tf_op jit(solution)/shard_map/weight_grads/pallas_call | solution.py:527
  239.2 5.8 %collective-permute-done.39 = bf16[4,64,512]{2,1,0:T(8,128)(2,1)S(1)} collective-permute-done((bf16[4,64,512]{2,1,0:T(8,128)(2,1)S(1)}, bf16[4,64,512]{2,1,0:T(8,128)(2,1)S(1)}, u32[]{:S(2)}, u32[]{:S(2)}) %collective-permute-start.39) | collective-permute-done | bytes 262176 | tf_op jit(solution)/shard_map/reduce_z/ppermute | solution.py:51
  248.5 3.9 %collective-permute-start.43 = (bf16[4,64,512]{2,1,0:T(8,128)(2,1)S(1)}, bf16[4,64,512]{2,1,0:T(8,128)(2,1)S(1)}, u32[]{:S(2)}, u32[]{:S(2)}) collective-permute-start(bf16[4,64,512]{2,1,0:T(8,128)(2,1)S(1)} %pad_maximum_fusion.18), channel_id=1, source_target_pairs={{0,24},{2,26},{4,28},{6,30},{8,0},{10,2},{12,4},{14,6},{16,8},{18,... | collective-permute-start | bytes 786440 | tf_op jit(solution)/shard_map/reduce_z/ppermute | solution.py:51
  254.6 15.8 %attend_back.3 = (bf16[1104,256]{1,0:T(8,128)(2,1)S(1)}, bf16[1104,256]{1,0:T(8,128)(2,1)S(1)}, bf16[1104,256]{1,0:T(8,128)(2,1)S(1)}) custom-call(bf16[1104,1536]{1,0:T(8,128)(2,1)S(1)} %copy-done.21, bf16[1104,1536]{1,0:T(8,128)(2,1)S(1)} %copy-done.21, bf16[1104,1536]{1,0:T(8,128)(2,1)S(1)} %copy-done.21, ...), custom_call_target="tpu_custom_call" | custom-call | flops 17999998976 | bytes 18000000 | tf_op jit(solution)/shard_map/attend_back/pallas_call | solution.py:412
  273.1 5.0 %times_pieces_turned.3 = (bf16[552,1024]{1,0:T(8,128)(2,1)S(1)}, bf16[552,1024]{1,0:T(8,128)(2,1)S(1)}) custom-call(bf16[1104,256]{1,0:T(8,128)(2,1)S(1)} %get-tuple-element.357.refs_2_.refs_0_, bf16[1104,256]{1,0:T(8,128)(2,1)S(1)} %get-tuple-element.358.refs_3_.refs_1_, bf16[1104,256]{1,0:T(8,128)(2,1)S(1)} %get-tuple-element.359.refs_4_.refs_2_, ...), custom_call_target="tpu_custom_call" | custom-call | flops 7000000000 | bytes 7000000 | tf_op jit(solution)/shard_map/times_pieces_turned/pallas_call | solution.py:490
  285.1 3.0 collective-permute-start.56
  289.9 3.3 %first_norm_back.1 = (bf16[552,1024]{1,0:T(8,128)(2,1)S(1)}, f32[2,1024]{1,0:T(2,128)S(1)}) custom-call(f32[552,1024]{1,0:T(8,128)S(1)} %get-tuple-element.406.refs_0_, bf16[552,1024]{1,0:T(8,128)(2,1)S(1)} %copy-done.17, bf16[552,1024]{1,0:T(8,128)(2,1)S(1)} %get-tuple-element.407.refs_2_, bf16[552,1024]{1,0:T(8,128)(2,1)S(1)} %collective-permute-done.49.refs_3_, ...), custom_call_target="tpu_custom_call" | custom-call | flops 4000000000 | bytes 4000000 | tf_op jit(solution)/shard_map/first_norm_back/pallas_call | solution.py:693
  306.2 2.4 fusion.13
  309.9 4.7 %collective-permute-done.52 = bf16[3,128,256]{2,1,0:T(8,128)(2,1)S(1)} collective-permute-done((bf16[3,128,256]{2,1,0:T(8,128)(2,1)S(1)}, bf16[3,128,256]{2,1,0:T(8,128)(2,1)S(1)}, u32[]{:S(2)}, u32[]{:S(2)}) %collective-permute-start.52) | collective-permute-done | bytes 196640 | tf_op jit(solution)/shard_map/reduce_middle/ppermute | solution.py:51
  318.2 2.7 fusion.14
  (351 shorter events, 107.5 us)
Async XLA Ops:
  6.4 21.8 %collective-permute-start.1 = (bf16[4,72,512]{2,1,0:T(8,128)(2,1)S(1)}, bf16[4,72,512]{2,1,0:T(8,128)(2,1)S(1)}, u32[]{:S(2)}, u32[]{:S(2)}) collective-permute-start(bf16[4,72,512]{2,1,0:T(8,128)(2,1)S(1)} %fusion.18), channel_id=1, source_target_pairs={{16,0},{18,2},{20,4},{22,6},{24,8},{26,10},{28,12},{30,14},{0,16},... | collective-permute-start | bytes 884744 | tf_op jit(solution)/shard_map/gather_z/ppermute | solution.py:47
  8.9 19.2 %collective-permute-start = (bf16[4,72,512]{2,1,0:T(8,128)(2,1)S(1)}, bf16[4,72,512]{2,1,0:T(8,128)(2,1)S(1)}, u32[]{:S(2)}, u32[]{:S(2)}) collective-permute-start(bf16[4,72,512]{2,1,0:T(8,128)(2,1)S(1)} %fusion.18), channel_id=1, source_target_pairs={{8,0},{10,2},{12,4},{14,6},{16,8},{18,10},{20,12},{22,14},{24,16},... | collective-permute-start | bytes 884744 | tf_op jit(solution)/shard_map/gather_z/ppermute | solution.py:47
  12.2 16.0 %collective-permute-start.4 = (bf16[4,32,512]{2,1,0:T(8,128)(2,1)S(1)}, bf16[4,32,512]{2,1,0:T(8,128)(2,1)S(1)}, u32[]{:S(2)}, u32[]{:S(2)}) collective-permute-start(bf16[4,32,512]{2,1,0:T(8,128)(2,1)S(1)} %get-tuple-element.239), channel_id=1, source_target_pairs={{4,0},{6,2},{0,4},{2,6},{12,8},{14,10},{8,12},{10,14},{20,16},{22,... | collective-permute-start | bytes 393224 | tf_op jit(solution)/shard_map/gather_middle/ppermute | solution.py:47
  13.8 15.0 %collective-permute-start.3 = (bf16[4,32,512]{2,1,0:T(8,128)(2,1)S(1)}, bf16[4,32,512]{2,1,0:T(8,128)(2,1)S(1)}, u32[]{:S(2)}, u32[]{:S(2)}) collective-permute-start(bf16[4,32,512]{2,1,0:T(8,128)(2,1)S(1)} %get-tuple-element.237), channel_id=1, source_target_pairs={{2,0},{0,2},{6,4},{4,6},{10,8},{8,10},{14,12},{12,14},{18,16},{16,... | collective-permute-start | bytes 393224 | tf_op jit(solution)/shard_map/gather_middle/ppermute | solution.py:47
  29.5 17.8 %collective-permute-start.8 = (bf16[4,8,64]{2,1,0:T(8,128)(2,1)S(1)}, bf16[4,8,64]{2,1,0:T(8,128)(2,1)S(1)}, u32[]{:S(2)}, u32[]{:S(2)}) collective-permute-start(bf16[4,8,64]{2,1,0:T(8,128)(2,1)S(1)} %pad_maximum_fusion.27), channel_id=1, source_target_pairs={{4,0},{6,2},{0,4},{2,6},{12,8},{14,10},{8,12},{10,14},{20,16},{22,... | collective-permute-start | bytes 12296 | tf_op jit(solution)/shard_map/gather_small/ppermute | solution.py:47
  32.2 19.1 %collective-permute-start.5 = (bf16[4,128,512]{2,1,0:T(8,128)(2,1)S(1)}, bf16[4,128,512]{2,1,0:T(8,128)(2,1)S(1)}, u32[]{:S(2)}, u32[]{:S(2)}) collective-permute-start(bf16[4,128,512]{2,1,0:T(8,128)(2,1)S(1)} %pad_maximum_fusion.2), channel_id=1, source_target_pairs={{2,0},{0,2},{6,4},{4,6},{10,8},{8,10},{14,12},{12,14},{18,16},{16,... | collective-permute-start | bytes 1572872 | tf_op jit(solution)/shard_map/gather_middle/ppermute | solution.py:47
  33.8 17.5 %collective-permute-start.6 = (bf16[4,128,512]{2,1,0:T(8,128)(2,1)S(1)}, bf16[4,128,512]{2,1,0:T(8,128)(2,1)S(1)}, u32[]{:S(2)}, u32[]{:S(2)}) collective-permute-start(bf16[4,128,512]{2,1,0:T(8,128)(2,1)S(1)} %pad_maximum_fusion.3), channel_id=1, source_target_pairs={{4,0},{6,2},{0,4},{2,6},{12,8},{14,10},{8,12},{10,14},{20,16},{22,... | collective-permute-start | bytes 1572872 | tf_op jit(solution)/shard_map/gather_middle/ppermute | solution.py:47
  51.2 26.3 %collective-permute-start.15 = (bf16[552,1024]{1,0:T(8,128)(2,1)}, bf16[552,1024]{1,0:T(8,128)(2,1)}, u32[]{:S(2)}, u32[]{:S(2)}) collective-permute-start(bf16[552,1024]{1,0:T(8,128)(2,1)} %get-tuple-element.286.refs_2_.own_ref), channel_id=1, source_target_pairs={{0,1},{1,0},{2,3},{3,2},{4,5},{5,4},{6,7},{7,6},{8,9},{9,8},{10,11... | collective-permute-start | bytes 3391496 | tf_op jit(solution)/shard_map/ppermute | solution.py:216
  52.0 25.6 %collective-permute-start.11 = (bf16[4,256,512]{2,1,0:T(8,128)(2,1)S(1)}, bf16[4,256,512]{2,1,0:T(8,128)(2,1)S(1)}, u32[]{:S(2)}, u32[]{:S(2)}) collective-permute-start(bf16[4,256,512]{2,1,0:T(8,128)(2,1)S(1)} %constant_dynamic-update-slice_fusion.2.refs_2_.refs_3_.refs_18_.refs_19_.refs_20_.refs_21_.refs_22, ...), channel_id=1, source_target_pairs={{2,0},{0,2},{6,4},{4,6},{10,8},{8,10},{14,12},{12,14},{18,16},{16,... | collective-permute-start | bytes 3145736 | tf_op jit(solution)/shard_map/gather_last/ppermute | solution.py:47
  52.7 25.5 %collective-permute-start.10 = (bf16[4,256,512]{2,1,0:T(8,128)(2,1)S(1)}, bf16[4,256,512]{2,1,0:T(8,128)(2,1)}, u32[]{:S(2)}, u32[]{:S(2)}) collective-permute-start(bf16[4,256,512]{2,1,0:T(8,128)(2,1)S(1)} %constant_dynamic-update-slice_fusion.refs_0_.refs_1_.refs_6_.refs_7_.refs_8_.refs_9_.refs_10_.refs_11_), channel_id=1, source_target_pairs={{4,0},{6,2},{0,4},{2,6},{12,8},{14,10},{8,12},{10,14},{20,16},{22,... | collective-permute-start | bytes 3145736 | tf_op jit(solution)/shard_map/gather_last/ppermute | solution.py:47
  58.6 18.9 %collective-permute-start.12 = (bf16[4,64,512]{2,1,0:T(8,128)(2,1)S(1)}, bf16[4,64,512]{2,1,0:T(8,128)(2,1)S(1)}, u32[]{:S(2)}, u32[]{:S(2)}) collective-permute-start(bf16[4,64,512]{2,1,0:T(8,128)(2,1)S(1)} %pad_maximum_fusion.13), channel_id=1, source_target_pairs={{16,0},{18,2},{20,4},{22,6},{24,8},{26,10},{28,12},{30,14},{0,16},... | collective-permute-start | bytes 786440 | tf_op jit(solution)/shard_map/gather_step/ppermute | solution.py:47
  94.7 23.9 %collective-permute-start.22 = (bf16[4,128,512]{2,1,0:T(8,128)(2,1)S(1)}, bf16[4,128,512]{2,1,0:T(8,128)(2,1)S(1)}, u32[]{:S(2)}, u32[]{:S(2)}) collective-permute-start(bf16[4,128,512]{2,1,0:T(8,128)(2,1)S(1)} %copy-done.23), channel_id=1, source_target_pairs={{16,0},{18,2},{20,4},{22,6},{24,8},{26,10},{28,12},{30,14},{0,16},... | collective-permute-start | bytes 1572872 | tf_op jit(solution)/shard_map/gather_step/ppermute | solution.py:47
  95.3 23.3 %collective-permute-start.21 = (bf16[4,256,512]{2,1,0:T(8,128)(2,1)S(1)}, bf16[4,256,512]{2,1,0:T(8,128)(2,1)S(1)}, u32[]{:S(2)}, u32[]{:S(2)}) collective-permute-start(bf16[4,256,512]{2,1,0:T(8,128)(2,1)S(1)} %constant_dynamic-update-slice_fusion.8.refs_6_.refs_10_), channel_id=1, source_target_pairs={{2,0},{0,2},{6,4},{4,6},{10,8},{8,10},{14,12},{12,14},{18,16},{16,... | collective-permute-start | bytes 3145736 | tf_op jit(solution)/shard_map/gather_last/ppermute | solution.py:47
  96.1 23.5 %collective-permute-start.20 = (bf16[4,256,512]{2,1,0:T(8,128)(2,1)S(1)}, bf16[4,256,512]{2,1,0:T(8,128)(2,1)S(1)}, u32[]{:S(2)}, u32[]{:S(2)}) collective-permute-start(bf16[4,256,512]{2,1,0:T(8,128)(2,1)S(1)} %constant_dynamic-update-slice_fusion.6.refs_4_.refs_8_), channel_id=1, source_target_pairs={{4,0},{6,2},{0,4},{2,6},{12,8},{14,10},{8,12},{10,14},{20,16},{22,... | collective-permute-start | bytes 3145736 | tf_op jit(solution)/shard_map/gather_last/ppermute | solution.py:47
  121.9 16.5 %collective-permute-start.23 = (bf16[4,128,512]{2,1,0:T(8,128)(2,1)}, bf16[4,128,512]{2,1,0:T(8,128)(2,1)S(1)}, u32[]{:S(2)}, u32[]{:S(2)}) collective-permute-start(bf16[4,128,512]{2,1,0:T(8,128)(2,1)} %pad_maximum_fusion.4), channel_id=1, source_target_pairs={{24,0},{26,2},{28,4},{30,6},{0,8},{2,10},{4,12},{6,14},{8,16},{10,... | collective-permute-start | bytes 1572872 | tf_op jit(solution)/shard_map/gather_step/ppermute | solution.py:47
  138.8 24.8 %collective-permute-start.25 = (bf16[4,256,512]{2,1,0:T(8,128)(2,1)S(1)}, bf16[4,256,512]{2,1,0:T(8,128)(2,1)S(1)}, u32[]{:S(2)}, u32[]{:S(2)}) collective-permute-start(bf16[4,256,512]{2,1,0:T(8,128)(2,1)S(1)} %bitcast.143), channel_id=1, source_target_pairs={{4,0},{6,2},{0,4},{2,6},{12,8},{14,10},{8,12},{10,14},{20,16},{22,... | collective-permute-start | bytes 3145736 | tf_op jit(solution)/shard_map/gather_last/ppermute | solution.py:47
  139.5 24.6 %collective-permute-start.26 = (bf16[4,256,512]{2,1,0:T(8,128)(2,1)S(1)}, bf16[4,256,512]{2,1,0:T(8,128)(2,1)S(1)}, u32[]{:S(2)}, u32[]{:S(2)}) collective-permute-start(bf16[4,256,512]{2,1,0:T(8,128)(2,1)S(1)} %bitcast.146), channel_id=1, source_target_pairs={{2,0},{0,2},{6,4},{4,6},{10,8},{8,10},{14,12},{12,14},{18,16},{16,... | collective-permute-start | bytes 3145736 | tf_op jit(solution)/shard_map/gather_last/ppermute | solution.py:47
  164.1 24.8 %collective-permute-start.27 = (bf16[4,256,512]{2,1,0:T(8,128)(2,1)}, bf16[4,256,512]{2,1,0:T(8,128)(2,1)}, u32[]{:S(2)}, u32[]{:S(2)}) collective-permute-start(bf16[4,256,512]{2,1,0:T(8,128)(2,1)} %bitcast.179), channel_id=1, source_target_pairs={{0,4},{2,6},{4,0},{6,2},{8,12},{10,14},{12,8},{14,10},{16,20},{18,... | collective-permute-start | bytes 3145736 | tf_op jit(solution)/shard_map/reduce_last/ppermute | solution.py:51
  165.6 23.5 %collective-permute-start.28 = (bf16[4,256,512]{2,1,0:T(8,128)(2,1)}, bf16[4,256,512]{2,1,0:T(8,128)(2,1)S(1)}, u32[]{:S(2)}, u32[]{:S(2)}) collective-permute-start(bf16[4,256,512]{2,1,0:T(8,128)(2,1)} %bitcast.178), channel_id=1, source_target_pairs={{0,2},{2,0},{4,6},{6,4},{8,10},{10,8},{12,14},{14,12},{16,18},{18,... | collective-permute-start | bytes 3145736 | tf_op jit(solution)/shard_map/reduce_last/ppermute | solution.py:51
  194.5 14.9 %collective-permute-start.33 = (bf16[4,128,512]{2,1,0:T(8,128)(2,1)S(1)}, bf16[4,128,512]{2,1,0:T(8,128)(2,1)S(1)}, u32[]{:S(2)}, u32[]{:S(2)}) collective-permute-start(bf16[4,128,512]{2,1,0:T(8,128)(2,1)S(1)} %get-tuple-element.455), channel_id=1, source_target_pairs={{0,4},{2,6},{4,0},{6,2},{8,12},{10,14},{12,8},{14,10},{16,20},{18,... | collective-permute-start | bytes 1572872 | tf_op jit(solution)/shard_map/reduce_middle/ppermute | solution.py:51
  203.4 27.6 %collective-permute-start.30 = (bf16[4,256,512]{2,1,0:T(8,128)(2,1)}, bf16[4,256,512]{2,1,0:T(8,128)(2,1)S(1)}, u32[]{:S(2)}, u32[]{:S(2)}) collective-permute-start(bf16[4,256,512]{2,1,0:T(8,128)(2,1)} %bitcast.51), channel_id=1, source_target_pairs={{0,4},{2,6},{4,0},{6,2},{8,12},{10,14},{12,8},{14,10},{16,20},{18,... | collective-permute-start | bytes 3145736 | tf_op jit(solution)/shard_map/reduce_last/ppermute | solution.py:51
  204.5 26.5 %collective-permute-start.31 = (bf16[4,256,512]{2,1,0:T(8,128)(2,1)}, bf16[4,256,512]{2,1,0:T(8,128)(2,1)S(1)}, u32[]{:S(2)}, u32[]{:S(2)}) collective-permute-start(bf16[4,256,512]{2,1,0:T(8,128)(2,1)} %bitcast.53), channel_id=1, source_target_pairs={{0,2},{2,0},{4,6},{6,4},{8,10},{10,8},{12,14},{14,12},{16,18},{18,... | collective-permute-start | bytes 3145736 | tf_op jit(solution)/shard_map/reduce_last/ppermute | solution.py:51
  209.8 21.2 %collective-permute-start.34 = (bf16[4,64,512]{2,1,0:T(8,128)(2,1)S(1)}, bf16[4,64,512]{2,1,0:T(8,128)(2,1)S(1)}, u32[]{:S(2)}, u32[]{:S(2)}) collective-permute-start(bf16[4,64,512]{2,1,0:T(8,128)(2,1)S(1)} %pad_maximum_fusion.14), channel_id=1, source_target_pairs={{0,8},{2,10},{4,12},{6,14},{8,16},{10,18},{12,20},{14,22},{16,24},... | collective-permute-start | bytes 786440 | tf_op jit(solution)/shard_map/reduce_z/ppermute | solution.py:51
  211.0 20.0 %collective-permute-start.35 = (bf16[4,64,512]{2,1,0:T(8,128)(2,1)S(1)}, bf16[4,64,512]{2,1,0:T(8,128)(2,1)S(1)}, u32[]{:S(2)}, u32[]{:S(2)}) collective-permute-start(bf16[4,64,512]{2,1,0:T(8,128)(2,1)S(1)} %pad_maximum_fusion.15), channel_id=1, source_target_pairs={{0,24},{2,26},{4,28},{6,30},{8,0},{10,2},{12,4},{14,6},{16,8},{18,... | collective-permute-start | bytes 786440 | tf_op jit(solution)/shard_map/reduce_z/ppermute | solution.py:51
  215.0 16.0 %collective-permute-start.36 = (bf16[552,1024]{1,0:T(8,128)(2,1)S(1)}, bf16[552,1024]{1,0:T(8,128)(2,1)S(1)}, u32[]{:S(2)}, u32[]{:S(2)}) collective-permute-start(bf16[552,1024]{1,0:T(8,128)(2,1)S(1)} %get-tuple-element.449), channel_id=1, source_target_pairs={{0,1},{1,0},{2,3},{3,2},{4,5},{5,4},{6,7},{7,6},{8,9},{9,8},{10,11... | collective-permute-start | bytes 3391496 | tf_op jit(solution)/shard_map/ppermute | solution.py:216
  248.4 22.3 %collective-permute-start.42 = (bf16[4,64,512]{2,1,0:T(8,128)(2,1)S(1)}, bf16[4,64,512]{2,1,0:T(8,128)(2,1)S(1)}, u32[]{:S(2)}, u32[]{:S(2)}) collective-permute-start(bf16[4,64,512]{2,1,0:T(8,128)(2,1)S(1)} %pad_maximum_fusion.17), channel_id=1, source_target_pairs={{0,8},{2,10},{4,12},{6,14},{8,16},{10,18},{12,20},{14,22},{16,24},... | collective-permute-start | bytes 786440 | tf_op jit(solution)/shard_map/reduce_z/ppermute | solution.py:51
  248.5 22.3 %collective-permute-start.43 = (bf16[4,64,512]{2,1,0:T(8,128)(2,1)S(1)}, bf16[4,64,512]{2,1,0:T(8,128)(2,1)S(1)}, u32[]{:S(2)}, u32[]{:S(2)}) collective-permute-start(bf16[4,64,512]{2,1,0:T(8,128)(2,1)S(1)} %pad_maximum_fusion.18), channel_id=1, source_target_pairs={{0,24},{2,26},{4,28},{6,30},{8,0},{10,2},{12,4},{14,6},{16,8},{18,... | collective-permute-start | bytes 786440 | tf_op jit(solution)/shard_map/reduce_z/ppermute | solution.py:51
  252.3 18.4 %collective-permute-start.40 = (bf16[5,256,256]{2,1,0:T(8,128)(2,1)S(1)}, bf16[5,256,256]{2,1,0:T(8,128)(2,1)S(1)}, u32[]{:S(2)}, u32[]{:S(2)}) collective-permute-start(bf16[5,256,256]{2,1,0:T(8,128)(2,1)S(1)} %get-tuple-element.370), channel_id=1, source_target_pairs={{0,4},{2,6},{4,0},{6,2},{8,12},{10,14},{12,8},{14,10},{16,20},{18,... | collective-permute-start | bytes 1966088 | tf_op jit(solution)/shard_map/reduce_last/ppermute | solution.py:51
  253.9 16.9 %collective-permute-start.41 = (bf16[5,256,256]{2,1,0:T(8,128)(2,1)S(1)}, bf16[5,256,256]{2,1,0:T(8,128)(2,1)S(1)}, u32[]{:S(2)}, u32[]{:S(2)}) collective-permute-start(bf16[5,256,256]{2,1,0:T(8,128)(2,1)S(1)} %get-tuple-element.372), channel_id=1, source_target_pairs={{0,2},{2,0},{4,6},{6,4},{8,10},{10,8},{12,14},{14,12},{16,18},{18,... | collective-permute-start | bytes 1966088 | tf_op jit(solution)/shard_map/reduce_last/ppermute | solution.py:51
  284.4 25.5 %collective-permute-start.55 = (bf16[5,64,256]{2,1,0:T(8,128)(2,1)}, bf16[5,64,256]{2,1,0:T(8,128)(2,1)S(1)}, u32[]{:S(2)}, u32[]{:S(2)}) collective-permute-start(bf16[5,64,256]{2,1,0:T(8,128)(2,1)} %pad_maximum_fusion.20), channel_id=1, source_target_pairs={{0,8},{2,10},{4,12},{6,14},{8,16},{10,18},{12,20},{14,22},{16,24},... | collective-permute-start | bytes 491528 | tf_op jit(solution)/shard_map/reduce_z/ppermute | solution.py:51
  285.1 24.8 %collective-permute-start.56 = (bf16[5,64,256]{2,1,0:T(8,128)(2,1)}, bf16[5,64,256]{2,1,0:T(8,128)(2,1)S(1)}, u32[]{:S(2)}, u32[]{:S(2)}) collective-permute-start(bf16[5,64,256]{2,1,0:T(8,128)(2,1)} %pad_maximum_fusion.21), channel_id=1, source_target_pairs={{0,16},{2,18},{4,20},{6,22},{8,24},{10,26},{12,28},{14,30},{16,0},... | collective-permute-start | bytes 491528 | tf_op jit(solution)/shard_map/reduce_z/ppermute | solution.py:51
  294.4 15.4 %collective-permute-start.57 = (bf16[5,64,256]{2,1,0:T(8,128)(2,1)}, bf16[5,64,256]{2,1,0:T(8,128)(2,1)S(1)}, u32[]{:S(2)}, u32[]{:S(2)}) collective-permute-start(bf16[5,64,256]{2,1,0:T(8,128)(2,1)} %pad_maximum_fusion.22), channel_id=1, source_target_pairs={{0,24},{2,26},{4,28},{6,30},{8,0},{10,2},{12,4},{14,6},{16,8},{18,... | collective-permute-start | bytes 491528 | tf_op jit(solution)/shard_map/reduce_z/ppermute | solution.py:51
  (83 other events, 914.8 us)

commit v7 on v6

--- a/solution.py
+++ b/solution.py
@@ -705,7 +705,7 @@
     )(grad_middle, rest, mine, other, rows_in, gain)
 
 
-def feed_kernel(counts, carried, plain, scattered, places_ref, *refs):
+def feed_kernel(counts, carried, *refs):
     halves, pieces, grad_pieces = counts
     normed_ref, shift_ref, grad_refs = refs[0], refs[1], refs[2 : 2 + halves]
     refs = refs[2 + halves :]
@@ -715,33 +715,17 @@
     weight_grad_refs = refs[3 : 3 + grad_pieces]
     grad_ref, normed_turned, grad_turned, out_sum, grad_sum = refs[3 + grad_pieces :]
     step = pl.program_id(0)
-    blocks = places_ref.shape[0]
-    size = normed_ref.shape[1] // blocks
-
-    def place(i):
-        return pl.ds(pl.multiple_of(places_ref[i] * size, size), size)
-
     @pl.when(step == 0)
     def _():
         start = 0
         for ref in grad_refs:
             grad_ref[start : start + ref.shape[0]] = ref[...]
             start += ref.shape[0]
-        if scattered:
-            for i in range(blocks):
-                rows = slice(i * size, (i + 1) * size)
-                normed_turned[place(i)] = normed_ref[:, rows].T
-                grad_turned[place(i)] = grad_ref[:, rows].T
-        else:
-            normed_turned[...] = normed_ref[...].T
-            grad_turned[...] = grad_ref[...].T
-
-    if plain:
-        first = jnp.concatenate([first_refs[0][place(i)] for i in range(blocks)], axis=0)
-        second = jnp.concatenate([second_refs[0][place(i)] for i in range(blocks)], axis=0)
-    else:
-        first = jnp.concatenate([w[0] for w in first_refs], axis=0)
-        second = jnp.concatenate([w[0] for w in second_refs], axis=0)
+        normed_turned[...] = normed_ref[...].T
+        grad_turned[...] = grad_ref[...].T
+
+    first = jnp.concatenate([w[0] for w in first_refs], axis=0)
+    second = jnp.concatenate([w[0] for w in second_refs], axis=0)
     hidden = dot_nn(normed_ref[...], first) + shift_ref[...]
     hidden_act, slope = gelu_and_slope(hidden)
     hidden_act = hidden_act.astype(BF16)
@@ -764,10 +748,7 @@
         for sum_ref, end_ref, left, right, _ in products:
             end_ref[...] = (sum_ref[...] + dot_nt(left, right)).astype(BF16)
 
-    if scattered:
-        weight_grad_refs[0][...] = dot_nn(normed_turned[...], grad_pre).astype(BF16)
-        weight_grad_refs[1][...] = dot_nn(grad_turned[...], hidden_act).astype(BF16)
-    else:
+    if True:
         for k, (left, right) in enumerate(
             ((normed_turned, grad_pre), (grad_turned, hidden_act))
         ):
@@ -814,24 +795,24 @@
 
     def once(array):
         return pl.BlockSpec(
-            array.shape, lambda j, p: (0,) * len(array.shape), pipeline_mode=pl.Buffered(1)
+            array.shape, lambda j: (0,) * len(array.shape), pipeline_mode=pl.Buffered(1)
         )
 
     def weight_spec(piece, second):
         if plain:
-            return pl.BlockSpec((width, tile), lambda j, p: (0, second * per + j))
+            return pl.BlockSpec((width, tile), lambda j: (0, second * per + j))
         return pl.BlockSpec(
-            (1, piece.shape[1], tile), lambda j, p: (second * groups + j // per, 0, j % per)
+            (1, piece.shape[1], tile), lambda j: (second * groups + j // per, 0, j % per)
         )
 
     if scattered:
-        grad_specs = [pl.BlockSpec((width, tile), lambda j, p: (0, j))] * 2
+        grad_specs = [pl.BlockSpec((width, tile), lambda j: (0, j))] * 2
         grad_shapes = [jax.ShapeDtypeStruct((width, units), BF16)] * 2
     else:
         half = units // 2
         split = half // tile
         grad_specs = [
-            pl.BlockSpec((2, 1, r, tile), lambda j, p: (0, j // split, 0, j % split))
+            pl.BlockSpec((2, 1, r, tile), lambda j: (0, j // split, 0, j % split))
             for r in piece_rows
         ]
         grad_shapes = [pltpu.HBM((2, 2, r, half), BF16) for r in piece_rows]
@@ -841,21 +822,19 @@
             feed_kernel,
             (len(grads), len(pieces), len(grad_shapes)),
             bool(before),
-            plain,
-            scattered,
         ),
         grid_spec=pltpu.PrefetchScalarGridSpec(
-            num_scalar_prefetch=1,
+            num_scalar_prefetch=0,
             grid=(units // tile,),
-            in_specs=[once(normed), pl.BlockSpec((1, tile), lambda j, p: (0, j))]
+            in_specs=[once(normed), pl.BlockSpec((1, tile), lambda j: (0, j))]
             + [once(g) for g in grads]
             + [weight_spec(p, 0) for p in pieces]
             + [weight_spec(p, 1) for p in pieces]
             + [once(b) for b in before],
             out_specs=[
-                pl.BlockSpec((rows, width), lambda j, p: (0, 0)),
-                pl.BlockSpec((rows, width), lambda j, p: (0, 0)),
-                pl.BlockSpec((1, tile), lambda j, p: (0, j)),
+                pl.BlockSpec((rows, width), lambda j: (0, 0)),
+                pl.BlockSpec((rows, width), lambda j: (0, 0)),
+                pl.BlockSpec((1, tile), lambda j: (0, j)),
             ]
             + grad_specs,
             scratch_shapes=[
@@ -875,7 +854,7 @@
         compiler_params=params(44),
         cost_estimate=cost(25),
         name="feed_forward",
-    )(places, normed, shift, *grads, *pieces, *pieces, *before)
+    )(normed, shift, *grads, *pieces, *pieces, *before)
     outs = list(outs)
     if not scattered:
         outs[3:] = [g.reshape((4,) + g.shape[2:]) for g in outs[3:]]

time: 333 us -> 332 us (level)
  no operation moved by 1% of the time
where the time goes in v7:
time: 332 us; the launch traced here: 326 us
  Pallas kernels  133 us (40%)
  starting transfers between devices  73.8 us (22%)
  waiting for transfers between devices  71.2 us (21%)
  local copies, waits for them, and re-layouts  19.7 us (6%)
  other arithmetic  13.9 us (4%)
  matrix products  11.9 us (4%)
    ppermute x23, waiting for transfers between devices, fetch(): return lax.ppermute(value, 'dp', pairs)  46.9 us
    pallas_call x2, Pallas kernels, feed_forward(): pl.pallas_call(functools.partial(feed_kernel, (len(grads), len(pieces), l...  42.6 us
    ppermute x23, starting transfers between devices, fetch(): return lax.ppermute(value, 'dp', pairs)  39.3 us
    ppermute x30, starting transfers between devices, push(): return lax.ppermute(value, 'dp', pairs)  34.4 us
    pallas_call x2, Pallas kernels, attend_back(): pl.pallas_call(attend_back_kernel, grid=(slots, count), in_specs=[columns...  31.6 us
    ppermute x30, waiting for transfers between devices, push(): return lax.ppermute(value, 'dp', pairs)  23.1 us
    pallas_call x1, Pallas kernels, attend(): pl.pallas_call(attend_kernel, grid=(slots, count), in_specs=[columns(firs...  16.2 us
    pallas_call x2, Pallas kernels, times_pieces_turned(): pl.pallas_call(kernel, grid=(1,), in_specs=[whole_spec(c) for c in column...  8.86 us
  transfers between devices with their start and end apart: 61, of which 28 were waited for; matrix products, arithmetic and copies ran while one was open for 10% of the time, Pallas kernels for 41%

profile of v7, /device:TPU:0, one launch (start us, length us, event | category | flops | bytes accessed | tf_op | source)
XLA Modules:
  0.0 326.1 jit_solution(9995023005625075602)
XLA Ops:
  3.3 3.1 collective-permute-start.2
  6.4 2.6 collective-permute-start.1
  16.4 11.8 %collective-permute-done.1 = bf16[4,72,512]{2,1,0:T(8,128)(2,1)S(1)} collective-permute-done((bf16[4,72,512]{2,1,0:T(8,128)(2,1)S(1)}, bf16[4,72,512]{2,1,0:T(8,128)(2,1)S(1)}, u32[]{:S(2)}, u32[]{:S(2)}) %collective-permute-start.1) | collective-permute-done | bytes 294944 | tf_op jit(solution)/shard_map/gather_z/ppermute | solution.py:47
  34.3 2.4 fusion.12.refs_0_.own_ref.refs_4_
  36.7 7.8 %collective-permute-start.7 = (bf16[4,64,512]{2,1,0:T(8,128)(2,1)S(1)}, bf16[4,64,512]{2,1,0:T(8,128)(2,1)S(1)}, u32[]{:S(2)}, u32[]{:S(2)}) collective-permute-start(bf16[4,64,512]{2,1,0:T(8,128)(2,1)S(1)} %pad_maximum_fusion.13), channel_id=1, source_target_pairs={{8,0},{10,2},{12,4},{14,6},{16,8},{18,10},{20,12},{22,14},{24,16},... | collective-permute-start | bytes 786440 | tf_op jit(solution)/shard_map/gather_step/ppermute | solution.py:47
  44.6 2.8 multiply_convert_fusion
  48.8 2.4 collective-permute-done.9
  59.1 3.2 first_norm.1.rows_ref.refs_0_
  62.4 5.0 %collective-permute-done.13 = bf16[4,64,512]{2,1,0:T(8,128)(2,1)S(1)} collective-permute-done((bf16[4,64,512]{2,1,0:T(8,128)(2,1)S(1)}, bf16[4,64,512]{2,1,0:T(8,128)(2,1)S(1)}, u32[]{:S(2)}, u32[]{:S(2)}) %collective-permute-start.13) | collective-permute-done | bytes 262176 | tf_op jit(solution)/shard_map/gather_step/ppermute | solution.py:47
  67.3 10.1 %collective-permute-done.12 = bf16[4,64,512]{2,1,0:T(8,128)(2,1)S(1)} collective-permute-done((bf16[4,64,512]{2,1,0:T(8,128)(2,1)S(1)}, bf16[4,64,512]{2,1,0:T(8,128)(2,1)S(1)}, u32[]{:S(2)}, u32[]{:S(2)}) %collective-permute-start.12) | collective-permute-done | bytes 262176 | tf_op jit(solution)/shard_map/gather_step/ppermute | solution.py:47
  82.6 5.2 %times_pieces.2.query_ref.key_ref.value_ref = bf16[1104,1536]{1,0:T(8,128)(2,1)S(1)} custom-call(bf16[1104,1024]{1,0:T(8,128)(2,1)S(1)} %first_norm.1.rows_ref.refs_0_, bf16[4,256,512]{2,1,0:T(8,128)(2,1)S(1)} %constant_dynamic-update-slice_fusion.refs_0_.refs_1_.refs_6_.refs_7_.refs_8_.refs_9_.refs_10_.refs_11_, ...), custom_call_target="tpu_custom_call" | custom-call | flops 6000000000 | bytes 6000000 | tf_op jit(solution)/shard_map/times_pieces/pallas_call | solution.py:451
  87.9 3.7 %collective-permute-done.17 = bf16[4,128,512]{2,1,0:T(8,128)(2,1)S(1)} collective-permute-done((bf16[4,128,512]{2,1,0:T(8,128)(2,1)S(1)}, bf16[4,128,512]{2,1,0:T(8,128)(2,1)S(1)}, u32[]{:S(2)}, u32[]{:S(2)}) %collective-permute-start.17) | collective-permute-done | bytes 524320 | tf_op jit(solution)/shard_map/gather_middle/ppermute | solution.py:47
  97.7 16.2 %attend.1 = (bf16[1104,512]{1,0:T(8,128)(2,1)S(1)}, f32[1,4,2,1104]{3,2,1,0:T(2,128)S(1)}) custom-call(bf16[1104,1536]{1,0:T(8,128)(2,1)S(1)} %times_pieces.2.query_ref.key_ref.value_ref, bf16[1104,1536]{1,0:T(8,128)(2,1)S(1)} %times_pieces.2.query_ref.key_ref.value_ref, bf16[1104,1536]{1,0:T(8,128)(2,1)S(1)} %times_pieces.2.query_ref.key_ref.value_ref, ...), custom_call_target="tpu_custom_call" | custom-call | flops 16000000000 | bytes 16000000 | tf_op jit(solution)/shard_map/attend/pallas_call | solution.py:393
  114.0 3.9 %times_pieces_turned.2.refs_1_ = bf16[1104,1024]{1,0:T(8,128)(2,1)} custom-call(bf16[1104,512]{1,0:T(8,128)(2,1)S(1)} %get-tuple-element.379.refs_0_.mixed_ref.refs_5_.refs_6_, bf16[4,256,512]{2,1,0:T(8,128)(2,1)S(1)} %constant_dynamic-update-slice_fusion.refs_0_.refs_1_.refs_6_.refs_7_.refs_8_.refs_9_.refs_10_.refs_11_, ...), custom_call_target="tpu_custom_call" | custom-call | flops 2000000000 | bytes 2000000 | tf_op jit(solution)/shard_map/times_pieces_turned/pallas_call | solution.py:490
  121.7 3.0 collective-permute-start.23
  125.6 5.8 %second_norm.1 = (f32[1104,1024]{1,0:T(8,128)}, bf16[1104,1024]{1,0:T(8,128)(2,1)S(1)}) custom-call(bf16[552,1024]{1,0:T(8,128)(2,1)} %fusion.12.refs_0_.own_ref.refs_4_, bf16[552,1024]{1,0:T(8,128)(2,1)} %collective-permute-done.14.refs_1_.next_ref, f32[1104,1]{1,0:T(8,128)S(1)} %broadcast_in_dim_reshape.3.refs_0_.live_ref, ...), custom_call_target="tpu_custom_call" | custom-call | flops 4000000000 | bytes 4000000 | tf_op jit(solution)/shard_map/second_norm/pallas_call | solution.py:591
  131.4 6.9 %collective-permute-done.23 = bf16[4,128,512]{2,1,0:T(8,128)(2,1)S(1)} collective-permute-done((bf16[4,128,512]{2,1,0:T(8,128)(2,1)}, bf16[4,128,512]{2,1,0:T(8,128)(2,1)S(1)}, u32[]{:S(2)}, u32[]{:S(2)}) %collective-permute-start.23) | collective-permute-done | bytes 524320 | tf_op jit(solution)/shard_map/gather_step/ppermute | solution.py:47
  141.2 20.5 %feed_forward.2 = (bf16[1104,1024]{1,0:T(8,128)(2,1)}, bf16[1104,1024]{1,0:T(8,128)(2,1)}, f32[1,1024]{1,0:T(1,128)S(1)}, bf16[2,2,256,512]{3,2,1,0:T(8,128)(2,1...) custom-call(bf16[1104,1024]{1,0:T(8,128)(2,1)S(1)} %get-tuple-element.308.re, ...), custom_call_target="tpu_custom_call" | custom-call | flops 24999999488 | bytes 25000000 | tf_op jit(solution)/shard_map/feed_forward/pallas_call | solution.py:820
  166.0 22.1 %feed_forward.3 = (bf16[1104,1024]{1,0:T(8,128)(2,1)}, bf16[1104,1024]{1,0:T(8,128)(2,1)}, f32[1,1024]{1,0:T(1,128)S(1)}, bf16[2,2,256,512]{3,2,1,0:T(8,128)(2,1...) custom-call(bf16[1104,1024]{1,0:T(8,128)(2,1)S(1)} %get-tuple-element.308.re, ...), custom_call_target="tpu_custom_call" | custom-call | flops 24999999488 | bytes 25000000 | tf_op jit(solution)/shard_map/feed_forward/pallas_call | solution.py:820
  195.5 7.8 %norm_back.1 = (f32[552,1024]{1,0:T(8,128)S(1)}, bf16[1104,1024]{1,0:T(8,128)(2,1)S(1)}, f32[4,1024]{1,0:T(4,128)S(1)}) custom-call(bf16[552,1024]{1,0:T(8,128)(2,1)} %get-tuple-element.286.refs_2_.own_ref, bf16[552,1024]{1,0:T(8,128)(2,1)} %collective-permute-done.15.refs_3_.next_ref, f32[1104,1]{1,0:T(8,128)S(1)} %copy-done.5, ...), custom_call_target="tpu_custom_call" | custom-call | flops 7000000000 | bytes 7000000 | tf_op jit(solution)/shard_map/norm_back/pallas_call | solution.py:648
  210.2 2.8 collective-permute-start.35
  214.3 15.8 %attend_back.2 = (bf16[1104,256]{1,0:T(8,128)(2,1)S(1)}, bf16[1104,256]{1,0:T(8,128)(2,1)S(1)}, bf16[1104,256]{1,0:T(8,128)(2,1)S(1)}) custom-call(bf16[1104,1536]{1,0:T(8,128)(2,1)S(1)} %copy-done.21, bf16[1104,1536]{1,0:T(8,128)(2,1)S(1)} %copy-done.21, bf16[1104,1536]{1,0:T(8,128)(2,1)S(1)} %copy-done.21, ...), custom_call_target="tpu_custom_call" | custom-call | flops 17999998976 | bytes 18000000 | tf_op jit(solution)/shard_map/attend_back/pallas_call | solution.py:412
  234.8 3.6 %weight_grads.2 = (bf16[5,256,256]{2,1,0:T(8,128)(2,1)S(1)}, bf16[5,256,256]{2,1,0:T(8,128)(2,1)S(1)}, bf16[5,256,256]{2,1,0:T(8,128)(2,1)S(1)}, bf16[5,256,256]{2,1,0:T(8,128)(2,1)S(1)}) custom-call(bf16[1104,1024]{1,0:T(8,128)(2,1)S(1)} %copy-done.19, bf16[1104,1024]{1,0:T(8,128)(2,1)S(1)} %get-tuple-element.336.rows_ref.refs_1_, ...), custom_call_target="tpu_custom_call" | custom-call | flops 8499999744 | bytes 8500000 | tf_op jit(solution)/shard_map/weight_grads/pallas_call | solution.py:527
  238.4 5.8 %collective-permute-done.39 = bf16[4,64,512]{2,1,0:T(8,128)(2,1)S(1)} collective-permute-done((bf16[4,64,512]{2,1,0:T(8,128)(2,1)S(1)}, bf16[4,64,512]{2,1,0:T(8,128)(2,1)S(1)}, u32[]{:S(2)}, u32[]{:S(2)}) %collective-permute-start.39) | collective-permute-done | bytes 262176 | tf_op jit(solution)/shard_map/reduce_z/ppermute | solution.py:51
  248.3 3.9 %collective-permute-start.43 = (bf16[4,64,512]{2,1,0:T(8,128)(2,1)S(1)}, bf16[4,64,512]{2,1,0:T(8,128)(2,1)S(1)}, u32[]{:S(2)}, u32[]{:S(2)}) collective-permute-start(bf16[4,64,512]{2,1,0:T(8,128)(2,1)S(1)} %pad_maximum_fusion.18), channel_id=1, source_target_pairs={{0,24},{2,26},{4,28},{6,30},{8,0},{10,2},{12,4},{14,6},{16,8},{18,... | collective-permute-start | bytes 786440 | tf_op jit(solution)/shard_map/reduce_z/ppermute | solution.py:51
  254.5 15.8 %attend_back.3 = (bf16[1104,256]{1,0:T(8,128)(2,1)S(1)}, bf16[1104,256]{1,0:T(8,128)(2,1)S(1)}, bf16[1104,256]{1,0:T(8,128)(2,1)S(1)}) custom-call(bf16[1104,1536]{1,0:T(8,128)(2,1)S(1)} %copy-done.21, bf16[1104,1536]{1,0:T(8,128)(2,1)S(1)} %copy-done.21, bf16[1104,1536]{1,0:T(8,128)(2,1)S(1)} %copy-done.21, ...), custom_call_target="tpu_custom_call" | custom-call | flops 17999998976 | bytes 18000000 | tf_op jit(solution)/shard_map/attend_back/pallas_call | solution.py:412
  272.9 5.0 %times_pieces_turned.3 = (bf16[552,1024]{1,0:T(8,128)(2,1)S(1)}, bf16[552,1024]{1,0:T(8,128)(2,1)S(1)}) custom-call(bf16[1104,256]{1,0:T(8,128)(2,1)S(1)} %get-tuple-element.357.refs_2_.refs_0_, bf16[1104,256]{1,0:T(8,128)(2,1)S(1)} %get-tuple-element.358.refs_3_.refs_1_, bf16[1104,256]{1,0:T(8,128)(2,1)S(1)} %get-tuple-element.359.refs_4_.refs_2_, ...), custom_call_target="tpu_custom_call" | custom-call | flops 7000000000 | bytes 7000000 | tf_op jit(solution)/shard_map/times_pieces_turned/pallas_call | solution.py:490
  285.0 3.0 collective-permute-start.56
  289.8 3.3 %first_norm_back.1 = (bf16[552,1024]{1,0:T(8,128)(2,1)S(1)}, f32[2,1024]{1,0:T(2,128)S(1)}) custom-call(f32[552,1024]{1,0:T(8,128)S(1)} %get-tuple-element.406.refs_0_, bf16[552,1024]{1,0:T(8,128)(2,1)S(1)} %copy-done.17, bf16[552,1024]{1,0:T(8,128)(2,1)S(1)} %get-tuple-element.407.refs_2_, bf16[552,1024]{1,0:T(8,128)(2,1)S(1)} %collective-permute-done.49.refs_3_, ...), custom_call_target="tpu_custom_call" | custom-call | flops 4000000000 | bytes 4000000 | tf_op jit(solution)/shard_map/first_norm_back/pallas_call | solution.py:693
  305.5 2.4 fusion.13
  309.6 4.8 %collective-permute-done.52 = bf16[3,128,256]{2,1,0:T(8,128)(2,1)S(1)} collective-permute-done((bf16[3,128,256]{2,1,0:T(8,128)(2,1)S(1)}, bf16[3,128,256]{2,1,0:T(8,128)(2,1)S(1)}, u32[]{:S(2)}, u32[]{:S(2)}) %collective-permute-start.52) | collective-permute-done | bytes 196640 | tf_op jit(solution)/shard_map/reduce_middle/ppermute | solution.py:51
  317.7 2.7 fusion.14
  (349 shorter events, 108.2 us)
Async XLA Ops:
  6.4 21.8 %collective-permute-start.1 = (bf16[4,72,512]{2,1,0:T(8,128)(2,1)S(1)}, bf16[4,72,512]{2,1,0:T(8,128)(2,1)S(1)}, u32[]{:S(2)}, u32[]{:S(2)}) collective-permute-start(bf16[4,72,512]{2,1,0:T(8,128)(2,1)S(1)} %fusion.18), channel_id=1, source_target_pairs={{16,0},{18,2},{20,4},{22,6},{24,8},{26,10},{28,12},{30,14},{0,16},... | collective-permute-start | bytes 884744 | tf_op jit(solution)/shard_map/gather_z/ppermute | solution.py:47
  8.9 19.2 %collective-permute-start = (bf16[4,72,512]{2,1,0:T(8,128)(2,1)S(1)}, bf16[4,72,512]{2,1,0:T(8,128)(2,1)S(1)}, u32[]{:S(2)}, u32[]{:S(2)}) collective-permute-start(bf16[4,72,512]{2,1,0:T(8,128)(2,1)S(1)} %fusion.18), channel_id=1, source_target_pairs={{8,0},{10,2},{12,4},{14,6},{16,8},{18,10},{20,12},{22,14},{24,16},... | collective-permute-start | bytes 884744 | tf_op jit(solution)/shard_map/gather_z/ppermute | solution.py:47
  12.2 16.0 %collective-permute-start.4 = (bf16[4,32,512]{2,1,0:T(8,128)(2,1)S(1)}, bf16[4,32,512]{2,1,0:T(8,128)(2,1)S(1)}, u32[]{:S(2)}, u32[]{:S(2)}) collective-permute-start(bf16[4,32,512]{2,1,0:T(8,128)(2,1)S(1)} %get-tuple-element.239), channel_id=1, source_target_pairs={{4,0},{6,2},{0,4},{2,6},{12,8},{14,10},{8,12},{10,14},{20,16},{22,... | collective-permute-start | bytes 393224 | tf_op jit(solution)/shard_map/gather_middle/ppermute | solution.py:47
  13.8 15.0 %collective-permute-start.3 = (bf16[4,32,512]{2,1,0:T(8,128)(2,1)S(1)}, bf16[4,32,512]{2,1,0:T(8,128)(2,1)S(1)}, u32[]{:S(2)}, u32[]{:S(2)}) collective-permute-start(bf16[4,32,512]{2,1,0:T(8,128)(2,1)S(1)} %get-tuple-element.237), channel_id=1, source_target_pairs={{2,0},{0,2},{6,4},{4,6},{10,8},{8,10},{14,12},{12,14},{18,16},{16,... | collective-permute-start | bytes 393224 | tf_op jit(solution)/shard_map/gather_middle/ppermute | solution.py:47
  29.5 17.8 %collective-permute-start.8 = (bf16[4,8,64]{2,1,0:T(8,128)(2,1)S(1)}, bf16[4,8,64]{2,1,0:T(8,128)(2,1)S(1)}, u32[]{:S(2)}, u32[]{:S(2)}) collective-permute-start(bf16[4,8,64]{2,1,0:T(8,128)(2,1)S(1)} %pad_maximum_fusion.27), channel_id=1, source_target_pairs={{4,0},{6,2},{0,4},{2,6},{12,8},{14,10},{8,12},{10,14},{20,16},{22,... | collective-permute-start | bytes 12296 | tf_op jit(solution)/shard_map/gather_small/ppermute | solution.py:47
  32.2 19.1 %collective-permute-start.5 = (bf16[4,128,512]{2,1,0:T(8,128)(2,1)S(1)}, bf16[4,128,512]{2,1,0:T(8,128)(2,1)S(1)}, u32[]{:S(2)}, u32[]{:S(2)}) collective-permute-start(bf16[4,128,512]{2,1,0:T(8,128)(2,1)S(1)} %pad_maximum_fusion.2), channel_id=1, source_target_pairs={{2,0},{0,2},{6,4},{4,6},{10,8},{8,10},{14,12},{12,14},{18,16},{16,... | collective-permute-start | bytes 1572872 | tf_op jit(solution)/shard_map/gather_middle/ppermute | solution.py:47
  33.8 17.5 %collective-permute-start.6 = (bf16[4,128,512]{2,1,0:T(8,128)(2,1)S(1)}, bf16[4,128,512]{2,1,0:T(8,128)(2,1)S(1)}, u32[]{:S(2)}, u32[]{:S(2)}) collective-permute-start(bf16[4,128,512]{2,1,0:T(8,128)(2,1)S(1)} %pad_maximum_fusion.3), channel_id=1, source_target_pairs={{4,0},{6,2},{0,4},{2,6},{12,8},{14,10},{8,12},{10,14},{20,16},{22,... | collective-permute-start | bytes 1572872 | tf_op jit(solution)/shard_map/gather_middle/ppermute | solution.py:47
  51.2 26.3 %collective-permute-start.15 = (bf16[552,1024]{1,0:T(8,128)(2,1)}, bf16[552,1024]{1,0:T(8,128)(2,1)}, u32[]{:S(2)}, u32[]{:S(2)}) collective-permute-start(bf16[552,1024]{1,0:T(8,128)(2,1)} %get-tuple-element.286.refs_2_.own_ref), channel_id=1, source_target_pairs={{0,1},{1,0},{2,3},{3,2},{4,5},{5,4},{6,7},{7,6},{8,9},{9,8},{10,11... | collective-permute-start | bytes 3391496 | tf_op jit(solution)/shard_map/ppermute | solution.py:216
  52.0 25.6 %collective-permute-start.11 = (bf16[4,256,512]{2,1,0:T(8,128)(2,1)S(1)}, bf16[4,256,512]{2,1,0:T(8,128)(2,1)S(1)}, u32[]{:S(2)}, u32[]{:S(2)}) collective-permute-start(bf16[4,256,512]{2,1,0:T(8,128)(2,1)S(1)} %constant_dynamic-update-slice_fusion.2.refs_2_.refs_3_.refs_18_.refs_19_.refs_20_.refs_21_.refs_22, ...), channel_id=1, source_target_pairs={{2,0},{0,2},{6,4},{4,6},{10,8},{8,10},{14,12},{12,14},{18,16},{16,... | collective-permute-start | bytes 3145736 | tf_op jit(solution)/shard_map/gather_last/ppermute | solution.py:47
  52.7 25.5 %collective-permute-start.10 = (bf16[4,256,512]{2,1,0:T(8,128)(2,1)S(1)}, bf16[4,256,512]{2,1,0:T(8,128)(2,1)}, u32[]{:S(2)}, u32[]{:S(2)}) collective-permute-start(bf16[4,256,512]{2,1,0:T(8,128)(2,1)S(1)} %constant_dynamic-update-slice_fusion.refs_0_.refs_1_.refs_6_.refs_7_.refs_8_.refs_9_.refs_10_.refs_11_), channel_id=1, source_target_pairs={{4,0},{6,2},{0,4},{2,6},{12,8},{14,10},{8,12},{10,14},{20,16},{22,... | collective-permute-start | bytes 3145736 | tf_op jit(solution)/shard_map/gather_last/ppermute | solution.py:47
  58.6 18.9 %collective-permute-start.12 = (bf16[4,64,512]{2,1,0:T(8,128)(2,1)S(1)}, bf16[4,64,512]{2,1,0:T(8,128)(2,1)S(1)}, u32[]{:S(2)}, u32[]{:S(2)}) collective-permute-start(bf16[4,64,512]{2,1,0:T(8,128)(2,1)S(1)} %pad_maximum_fusion.13), channel_id=1, source_target_pairs={{16,0},{18,2},{20,4},{22,6},{24,8},{26,10},{28,12},{30,14},{0,16},... | collective-permute-start | bytes 786440 | tf_op jit(solution)/shard_map/gather_step/ppermute | solution.py:47
  94.7 23.9 %collective-permute-start.22 = (bf16[4,128,512]{2,1,0:T(8,128)(2,1)S(1)}, bf16[4,128,512]{2,1,0:T(8,128)(2,1)S(1)}, u32[]{:S(2)}, u32[]{:S(2)}) collective-permute-start(bf16[4,128,512]{2,1,0:T(8,128)(2,1)S(1)} %copy-done.23), channel_id=1, source_target_pairs={{16,0},{18,2},{20,4},{22,6},{24,8},{26,10},{28,12},{30,14},{0,16},... | collective-permute-start | bytes 1572872 | tf_op jit(solution)/shard_map/gather_step/ppermute | solution.py:47
  95.3 23.3 %collective-permute-start.21 = (bf16[4,256,512]{2,1,0:T(8,128)(2,1)S(1)}, bf16[4,256,512]{2,1,0:T(8,128)(2,1)S(1)}, u32[]{:S(2)}, u32[]{:S(2)}) collective-permute-start(bf16[4,256,512]{2,1,0:T(8,128)(2,1)S(1)} %constant_dynamic-update-slice_fusion.8.refs_6_.refs_10_), channel_id=1, source_target_pairs={{2,0},{0,2},{6,4},{4,6},{10,8},{8,10},{14,12},{12,14},{18,16},{16,... | collective-permute-start | bytes 3145736 | tf_op jit(solution)/shard_map/gather_last/ppermute | solution.py:47
  96.1 23.5 %collective-permute-start.20 = (bf16[4,256,512]{2,1,0:T(8,128)(2,1)S(1)}, bf16[4,256,512]{2,1,0:T(8,128)(2,1)S(1)}, u32[]{:S(2)}, u32[]{:S(2)}) collective-permute-start(bf16[4,256,512]{2,1,0:T(8,128)(2,1)S(1)} %constant_dynamic-update-slice_fusion.6.refs_4_.refs_8_), channel_id=1, source_target_pairs={{4,0},{6,2},{0,4},{2,6},{12,8},{14,10},{8,12},{10,14},{20,16},{22,... | collective-permute-start | bytes 3145736 | tf_op jit(solution)/shard_map/gather_last/ppermute | solution.py:47
  121.7 16.5 %collective-permute-start.23 = (bf16[4,128,512]{2,1,0:T(8,128)(2,1)}, bf16[4,128,512]{2,1,0:T(8,128)(2,1)S(1)}, u32[]{:S(2)}, u32[]{:S(2)}) collective-permute-start(bf16[4,128,512]{2,1,0:T(8,128)(2,1)} %pad_maximum_fusion.4), channel_id=1, source_target_pairs={{24,0},{26,2},{28,4},{30,6},{0,8},{2,10},{4,12},{6,14},{8,16},{10,... | collective-permute-start | bytes 1572872 | tf_op jit(solution)/shard_map/gather_step/ppermute | solution.py:47
  138.6 24.8 %collective-permute-start.25 = (bf16[4,256,512]{2,1,0:T(8,128)(2,1)S(1)}, bf16[4,256,512]{2,1,0:T(8,128)(2,1)S(1)}, u32[]{:S(2)}, u32[]{:S(2)}) collective-permute-start(bf16[4,256,512]{2,1,0:T(8,128)(2,1)S(1)} %bitcast.143), channel_id=1, source_target_pairs={{4,0},{6,2},{0,4},{2,6},{12,8},{14,10},{8,12},{10,14},{20,16},{22,... | collective-permute-start | bytes 3145736 | tf_op jit(solution)/shard_map/gather_last/ppermute | solution.py:47
  139.4 24.6 %collective-permute-start.26 = (bf16[4,256,512]{2,1,0:T(8,128)(2,1)S(1)}, bf16[4,256,512]{2,1,0:T(8,128)(2,1)S(1)}, u32[]{:S(2)}, u32[]{:S(2)}) collective-permute-start(bf16[4,256,512]{2,1,0:T(8,128)(2,1)S(1)} %bitcast.146), channel_id=1, source_target_pairs={{2,0},{0,2},{6,4},{4,6},{10,8},{8,10},{14,12},{12,14},{18,16},{16,... | collective-permute-start | bytes 3145736 | tf_op jit(solution)/shard_map/gather_last/ppermute | solution.py:47
  163.9 24.1 %collective-permute-start.27 = (bf16[4,256,512]{2,1,0:T(8,128)(2,1)}, bf16[4,256,512]{2,1,0:T(8,128)(2,1)}, u32[]{:S(2)}, u32[]{:S(2)}) collective-permute-start(bf16[4,256,512]{2,1,0:T(8,128)(2,1)} %bitcast.179), channel_id=1, source_target_pairs={{0,4},{2,6},{4,0},{6,2},{8,12},{10,14},{12,8},{14,10},{16,20},{18,... | collective-permute-start | bytes 3145736 | tf_op jit(solution)/shard_map/reduce_last/ppermute | solution.py:51
  165.4 23.5 %collective-permute-start.28 = (bf16[4,256,512]{2,1,0:T(8,128)(2,1)}, bf16[4,256,512]{2,1,0:T(8,128)(2,1)S(1)}, u32[]{:S(2)}, u32[]{:S(2)}) collective-permute-start(bf16[4,256,512]{2,1,0:T(8,128)(2,1)} %bitcast.178), channel_id=1, source_target_pairs={{0,2},{2,0},{4,6},{6,4},{8,10},{10,8},{12,14},{14,12},{16,18},{18,... | collective-permute-start | bytes 3145736 | tf_op jit(solution)/shard_map/reduce_last/ppermute | solution.py:51
  193.8 14.9 %collective-permute-start.33 = (bf16[4,128,512]{2,1,0:T(8,128)(2,1)S(1)}, bf16[4,128,512]{2,1,0:T(8,128)(2,1)S(1)}, u32[]{:S(2)}, u32[]{:S(2)}) collective-permute-start(bf16[4,128,512]{2,1,0:T(8,128)(2,1)S(1)} %get-tuple-element.455), channel_id=1, source_target_pairs={{0,4},{2,6},{4,0},{6,2},{8,12},{10,14},{12,8},{14,10},{16,20},{18,... | collective-permute-start | bytes 1572872 | tf_op jit(solution)/shard_map/reduce_middle/ppermute | solution.py:51
  203.3 27.0 %collective-permute-start.30 = (bf16[4,256,512]{2,1,0:T(8,128)(2,1)}, bf16[4,256,512]{2,1,0:T(8,128)(2,1)S(1)}, u32[]{:S(2)}, u32[]{:S(2)}) collective-permute-start(bf16[4,256,512]{2,1,0:T(8,128)(2,1)} %bitcast.51), channel_id=1, source_target_pairs={{0,4},{2,6},{4,0},{6,2},{8,12},{10,14},{12,8},{14,10},{16,20},{18,... | collective-permute-start | bytes 3145736 | tf_op jit(solution)/shard_map/reduce_last/ppermute | solution.py:51
  203.8 26.5 %collective-permute-start.31 = (bf16[4,256,512]{2,1,0:T(8,128)(2,1)}, bf16[4,256,512]{2,1,0:T(8,128)(2,1)S(1)}, u32[]{:S(2)}, u32[]{:S(2)}) collective-permute-start(bf16[4,256,512]{2,1,0:T(8,128)(2,1)} %bitcast.53), channel_id=1, source_target_pairs={{0,2},{2,0},{4,6},{6,4},{8,10},{10,8},{12,14},{14,12},{16,18},{18,... | collective-permute-start | bytes 3145736 | tf_op jit(solution)/shard_map/reduce_last/ppermute | solution.py:51
  209.1 21.2 %collective-permute-start.34 = (bf16[4,64,512]{2,1,0:T(8,128)(2,1)S(1)}, bf16[4,64,512]{2,1,0:T(8,128)(2,1)S(1)}, u32[]{:S(2)}, u32[]{:S(2)}) collective-permute-start(bf16[4,64,512]{2,1,0:T(8,128)(2,1)S(1)} %pad_maximum_fusion.14), channel_id=1, source_target_pairs={{0,8},{2,10},{4,12},{6,14},{8,16},{10,18},{12,20},{14,22},{16,24},... | collective-permute-start | bytes 786440 | tf_op jit(solution)/shard_map/reduce_z/ppermute | solution.py:51
  210.2 20.0 %collective-permute-start.35 = (bf16[4,64,512]{2,1,0:T(8,128)(2,1)S(1)}, bf16[4,64,512]{2,1,0:T(8,128)(2,1)S(1)}, u32[]{:S(2)}, u32[]{:S(2)}) collective-permute-start(bf16[4,64,512]{2,1,0:T(8,128)(2,1)S(1)} %pad_maximum_fusion.15), channel_id=1, source_target_pairs={{0,24},{2,26},{4,28},{6,30},{8,0},{10,2},{12,4},{14,6},{16,8},{18,... | collective-permute-start | bytes 786440 | tf_op jit(solution)/shard_map/reduce_z/ppermute | solution.py:51
  214.3 16.0 %collective-permute-start.36 = (bf16[552,1024]{1,0:T(8,128)(2,1)S(1)}, bf16[552,1024]{1,0:T(8,128)(2,1)S(1)}, u32[]{:S(2)}, u32[]{:S(2)}) collective-permute-start(bf16[552,1024]{1,0:T(8,128)(2,1)S(1)} %get-tuple-element.449), channel_id=1, source_target_pairs={{0,1},{1,0},{2,3},{3,2},{4,5},{5,4},{6,7},{7,6},{8,9},{9,8},{10,11... | collective-permute-start | bytes 3391496 | tf_op jit(solution)/shard_map/ppermute | solution.py:216
  248.2 22.3 %collective-permute-start.42 = (bf16[4,64,512]{2,1,0:T(8,128)(2,1)S(1)}, bf16[4,64,512]{2,1,0:T(8,128)(2,1)S(1)}, u32[]{:S(2)}, u32[]{:S(2)}) collective-permute-start(bf16[4,64,512]{2,1,0:T(8,128)(2,1)S(1)} %pad_maximum_fusion.17), channel_id=1, source_target_pairs={{0,8},{2,10},{4,12},{6,14},{8,16},{10,18},{12,20},{14,22},{16,24},... | collective-permute-start | bytes 786440 | tf_op jit(solution)/shard_map/reduce_z/ppermute | solution.py:51
  248.3 22.2 %collective-permute-start.43 = (bf16[4,64,512]{2,1,0:T(8,128)(2,1)S(1)}, bf16[4,64,512]{2,1,0:T(8,128)(2,1)S(1)}, u32[]{:S(2)}, u32[]{:S(2)}) collective-permute-start(bf16[4,64,512]{2,1,0:T(8,128)(2,1)S(1)} %pad_maximum_fusion.18), channel_id=1, source_target_pairs={{0,24},{2,26},{4,28},{6,30},{8,0},{10,2},{12,4},{14,6},{16,8},{18,... | collective-permute-start | bytes 786440 | tf_op jit(solution)/shard_map/reduce_z/ppermute | solution.py:51
  252.2 18.4 %collective-permute-start.40 = (bf16[5,256,256]{2,1,0:T(8,128)(2,1)S(1)}, bf16[5,256,256]{2,1,0:T(8,128)(2,1)S(1)}, u32[]{:S(2)}, u32[]{:S(2)}) collective-permute-start(bf16[5,256,256]{2,1,0:T(8,128)(2,1)S(1)} %get-tuple-element.370), channel_id=1, source_target_pairs={{0,4},{2,6},{4,0},{6,2},{8,12},{10,14},{12,8},{14,10},{16,20},{18,... | collective-permute-start | bytes 1966088 | tf_op jit(solution)/shard_map/reduce_last/ppermute | solution.py:51
  253.1 17.5 %collective-permute-start.41 = (bf16[5,256,256]{2,1,0:T(8,128)(2,1)S(1)}, bf16[5,256,256]{2,1,0:T(8,128)(2,1)S(1)}, u32[]{:S(2)}, u32[]{:S(2)}) collective-permute-start(bf16[5,256,256]{2,1,0:T(8,128)(2,1)S(1)} %get-tuple-element.372), channel_id=1, source_target_pairs={{0,2},{2,0},{4,6},{6,4},{8,10},{10,8},{12,14},{14,12},{16,18},{18,... | collective-permute-start | bytes 1966088 | tf_op jit(solution)/shard_map/reduce_last/ppermute | solution.py:51
  284.3 25.4 %collective-permute-start.55 = (bf16[5,64,256]{2,1,0:T(8,128)(2,1)}, bf16[5,64,256]{2,1,0:T(8,128)(2,1)S(1)}, u32[]{:S(2)}, u32[]{:S(2)}) collective-permute-start(bf16[5,64,256]{2,1,0:T(8,128)(2,1)} %pad_maximum_fusion.20), channel_id=1, source_target_pairs={{0,8},{2,10},{4,12},{6,14},{8,16},{10,18},{12,20},{14,22},{16,24},... | collective-permute-start | bytes 491528 | tf_op jit(solution)/shard_map/reduce_z/ppermute | solution.py:51
  285.0 24.7 %collective-permute-start.56 = (bf16[5,64,256]{2,1,0:T(8,128)(2,1)}, bf16[5,64,256]{2,1,0:T(8,128)(2,1)S(1)}, u32[]{:S(2)}, u32[]{:S(2)}) collective-permute-start(bf16[5,64,256]{2,1,0:T(8,128)(2,1)} %pad_maximum_fusion.21), channel_id=1, source_target_pairs={{0,16},{2,18},{4,20},{6,22},{8,24},{10,26},{12,28},{14,30},{16,0},... | collective-permute-start | bytes 491528 | tf_op jit(solution)/shard_map/reduce_z/ppermute | solution.py:51
  294.3 15.3 %collective-permute-start.57 = (bf16[5,64,256]{2,1,0:T(8,128)(2,1)}, bf16[5,64,256]{2,1,0:T(8,128)(2,1)S(1)}, u32[]{:S(2)}, u32[]{:S(2)}) collective-permute-start(bf16[5,64,256]{2,1,0:T(8,128)(2,1)} %pad_maximum_fusion.22), channel_id=1, source_target_pairs={{0,24},{2,26},{4,28},{6,30},{8,0},{10,2},{12,4},{14,6},{16,8},{18,... | collective-permute-start | bytes 491528 | tf_op jit(solution)/shard_map/reduce_z/ppermute | solution.py:51
  (83 other events, 913.5 us)
